TPU v7x, 32 devices: a whole 2x2x4 slice. The times are simulated.
32 devices in a mesh: row: 8 (over z, core), col: 4 (over y, x).
Axes of the slice: x: 2, y: 2, z: 4, core: 2. Of those that a mesh axis runs over, the one named last changes fastest.
Arguments:
- tokens: bfloat16 [2, 2048, 2048], P(None, 'row', 'col'), may hold values from -6 to 6
- routes: int32 [2, 2048, 4], P(None, 'row'), may hold values from 0 to 7, all different within a row; in each aligned block of 256 rows (0 to 255, 256 to 511, ..., all dimensions but the last counted through in order) at most 170 rows name the same one
- route_weights: float32 [2, 2048, 4], P(None, 'row'), may hold values from 0.1 to 0.6
- group_ids: int32 [2, 16], P(None, 'row'), may hold values from 0 to 1
- first_gain: bfloat16 [2048], P('row'), may hold values from 0.099609375 to 1.8984375
- query_weight: bfloat16 [2048, 2048], P('row', 'col'), may hold values from -0.125 to 0.125
- key_weight: bfloat16 [2048, 2048], P('row', 'col'), may hold values from -0.125 to 0.125
- value_weight: bfloat16 [2048, 2048], P('row', 'col'), may hold values from -0.125 to 0.125
- output_weight: bfloat16 [2048, 2048], P('col', 'row'), may hold values from -0.5 to 0.5
- second_gain: bfloat16 [2048], P('row'), may hold values from 0.099609375 to 1.8984375
- shared_gate: bfloat16 [2048, 5632], P('row', 'col'), may hold values from -0.125 to 0.125
- shared_up: bfloat16 [2048, 5632], P('row', 'col'), may hold values from -0.125 to 0.125
- shared_down: bfloat16 [5632, 2048], P('col', 'row'), may hold values from -0.15625 to 0.15625
- shared_logit: bfloat16 [2048], P('row'), may hold values from -0.125 to 0.125
- expert_gate: bfloat16 [2048, 8, 1408], P('row', 'col'), may hold values from -0.125 to 0.125
- expert_up: bfloat16 [2048, 8, 1408], P('row', 'col'), may hold values from -0.125 to 0.125
- expert_down: bfloat16 [8, 1408, 2048], P('col', None, 'row'), may hold values from -0.3125 to 0.3125
- cotangent: bfloat16 [2, 2048, 2048], P(None, 'row', 'col'), may hold values from -6 to 6
Outputs:
- result: bfloat16 [2, 2048, 2048], P(None, 'row', 'col')
- token_grad: float32 [2, 2048, 2048], P(None, 'row', 'col')
- first_gain_grad: float32 [2048], P('row')
- query_grad: float32 [2048, 2048], P('row', 'col')
- key_grad: float32 [2048, 2048], P('row', 'col')
- value_grad: float32 [2048, 2048], P('row', 'col')
- output_grad: float32 [2048, 2048], P('col', 'row')
- second_gain_grad: float32 [2048], P('row')
- shared_gate_grad: float32 [2048, 5632], P('row', 'col')
- shared_up_grad: float32 [2048, 5632], P('row', 'col')
- shared_down_grad: float32 [5632, 2048], P('col', 'row')
- shared_logit_grad: float32 [2048], P('row')
- expert_gate_grad: float32 [2048, 8, 1408], P('row', 'col')
- expert_up_grad: float32 [2048, 8, 1408], P('row', 'col')
- expert_down_grad: float32 [8, 1408, 2048], P('col', None, 'row')
Inputs may be any that keep to these rules, and one draw needn't show every extreme that they name: `routes`: within the 256 rows of one device in one micro-batch no expert is named by more than 170 rows, and in every draw some expert is named by exactly 170 rows of some device; each row names 4 different experts. `group_ids`: each continuation follows one of the 2 prompts of its own device block and micro-batch.
All inputs are finite; a program needn't handle non-finite values.
Results may differ from a plain program's by a relative error of at most 0.025.
Values may be sent and summed in bfloat16 or wider, within the bound.
No kernel may reach another device: no remote copies, remote signals or barrier semaphores. Data moves between devices by JAX's collectives and lax.ppermute only.
A program may use at most 256 MiB of HBM per device.

v0:
```python
import math

import jax
import jax.numpy as jnp
from jax import lax
from jax.sharding import PartitionSpec as P

HEAD_DIM = 128
EXPERTS = 8
PROMPTS = 2
CONTS = 2
CONT_LEN = 64
PROMPT_LEN = 64
CAP = 170


epsilon = 1e-06
rope_base = 1000000.0
masked_score = -1000000000.0


def block_layout(groups, row_count):
    token_index = jnp.arange(row_count, dtype=jnp.int32)
    prompt_rows = PROMPTS * PROMPT_LEN
    is_prompt = token_index < prompt_rows
    cont_offset = jnp.maximum(token_index - prompt_rows, 0)
    cont_number = cont_offset // CONT_LEN
    segment = jnp.where(is_prompt, token_index // PROMPT_LEN, PROMPTS + cont_number)
    position = jnp.where(is_prompt, token_index % PROMPT_LEN, PROMPT_LEN + cont_offset % CONT_LEN)
    cont_picks = (cont_number[:, None] == jnp.arange(CONTS, dtype=jnp.int32)[None, :]).astype(
        jnp.int32
    )
    source = jnp.where(is_prompt, segment, jnp.sum(cont_picks * groups[None, :], axis=1))
    same_segment = (segment[:, None] == segment[None, :]) & (position[None, :] <= position[:, None])
    context = (
        jnp.logical_not(is_prompt)[:, None]
        & is_prompt[None, :]
        & (source[:, None] == segment[None, :])
    )
    return (same_segment | context, position)


def rotary_tables(position):
    half_dim = HEAD_DIM // 2
    frequency = rope_base ** (-(2.0 * jnp.arange(half_dim, dtype=jnp.float32)) / HEAD_DIM)
    angles = position.astype(jnp.float32)[:, None] * frequency[None, :]
    return (jnp.cos(angles), jnp.sin(angles))


def rotate(values, cosine, sine_rows):
    half_dim = HEAD_DIM // 2
    first_half = values[..., :half_dim]
    second = values[..., half_dim:]
    cos_rows = cosine[:, None, :]
    sin_rows = sine_rows[:, None, :]
    return jnp.concatenate(
        [first_half * cos_rows - second * sin_rows, second * cos_rows + first_half * sin_rows],
        axis=-1,
    )


def rotate_back(values, cosine, sine_rows):
    half_dim = HEAD_DIM // 2
    first_half = values[..., :half_dim]
    second = values[..., half_dim:]
    cos_rows = cosine[:, None, :]
    sin_rows = sine_rows[:, None, :]
    return jnp.concatenate(
        [first_half * cos_rows + second * sin_rows, second * cos_rows - first_half * sin_rows],
        axis=-1,
    )


def score_block(query_rot, key_rot, allowed):
    raw_scores = jnp.einsum("qhd,khd->hqk", query_rot, key_rot, preferred_element_type=jnp.float32)
    return jnp.where(allowed[None], raw_scores * (1.0 / math.sqrt(HEAD_DIM)), masked_score)


def swiglu_back(act_grad, gate_pre, up_pre):
    sigma = jax.nn.sigmoid(gate_pre)
    gate_grad = act_grad * up_pre * sigma * (1.0 + gate_pre * (1.0 - sigma))
    up_grad = act_grad * gate_pre * sigma
    return (gate_grad.astype(jnp.bfloat16), up_grad.astype(jnp.bfloat16))


def norm_back(normed_grad, inputs, scale, gain):
    unit_rows = inputs * scale
    weighted = normed_grad * gain
    rows_grad = scale * (
        weighted - unit_rows * jnp.mean(weighted * unit_rows, axis=-1, keepdims=True)
    )
    return (rows_grad, jnp.sum(normed_grad * unit_rows, axis=0))


def dispatch(route_rows, route_share, row_count, expert_start, local_experts):
    labels = jnp.arange(EXPERTS, dtype=jnp.int32)
    route_hits = (route_rows[:, :, None] == labels[None, None, :]).astype(jnp.int32)
    chosen = jnp.sum(route_hits, axis=1)
    before = jnp.cumsum(chosen, axis=0) - chosen
    slot_place = jnp.sum(route_hits * before[:, None, :], axis=2)
    slot_of = route_rows * CAP + slot_place
    token_ids = jnp.broadcast_to(jnp.arange(row_count, dtype=jnp.int32)[:, None], route_rows.shape)
    slot_owner = (
        jnp.full((EXPERTS * CAP,), row_count, jnp.int32)
        .at[slot_of.reshape(-1)]
        .set(token_ids.reshape(-1))
    )
    slot_share = (
        jnp.zeros((EXPERTS * CAP,), jnp.float32)
        .at[slot_of.reshape(-1)]
        .set(route_share.reshape(-1))
    )
    local_slots = local_experts * CAP
    first_slot = expert_start * CAP
    local_owner = lax.dynamic_slice_in_dim(slot_owner, first_slot, local_slots, 0)
    local_share = lax.dynamic_slice_in_dim(slot_share, first_slot, local_slots, 0)
    return (local_owner, local_share)


def forward_pass(
    rows_in, route_rows, route_share, groups, blocks, col_start, local_width, expert_start
):
    (
        first_gain,
        query_weight,
        key_weight,
        value_weight,
        output_weight,
        second_gain,
        shared_gate,
        shared_up,
        shared_down,
        shared_logit,
        expert_gate,
        expert_up,
        expert_down,
    ) = blocks
    inputs = rows_in.astype(jnp.float32)
    row_count = inputs.shape[0]
    local_experts = expert_gate.shape[1]
    first_scale = lax.rsqrt(jnp.mean(inputs * inputs, axis=-1, keepdims=True) + epsilon)
    first_normed = (inputs * first_scale * first_gain).astype(jnp.bfloat16)
    queries = jnp.dot(first_normed, query_weight, preferred_element_type=jnp.float32)
    key_rows = jnp.dot(first_normed, key_weight, preferred_element_type=jnp.float32)
    value_rows = jnp.dot(first_normed, value_weight, preferred_element_type=jnp.float32)
    allowed, position = block_layout(groups, row_count)
    cosine, sine_rows = rotary_tables(position)
    head_shape = (row_count, local_width // HEAD_DIM, HEAD_DIM)
    query_rot = rotate(queries.reshape(head_shape), cosine, sine_rows).astype(jnp.bfloat16)
    key_rot = rotate(key_rows.reshape(head_shape), cosine, sine_rows).astype(jnp.bfloat16)
    value_low = value_rows.reshape(head_shape).astype(jnp.bfloat16)
    scores = score_block(query_rot, key_rot, allowed)
    row_peak = jnp.max(scores, axis=-1, keepdims=True)
    exp_scores = jnp.exp(scores - row_peak)
    exp_total = jnp.sum(exp_scores, axis=-1, keepdims=True)
    probabilities = exp_scores / exp_total
    log_total = row_peak + jnp.log(exp_total)
    mixed_heads = (
        jnp.einsum(
            "hqk,khd->qhd",
            probabilities.astype(jnp.bfloat16),
            value_low,
            preferred_element_type=jnp.float32,
        )
        .reshape(row_count, local_width)
        .astype(jnp.bfloat16)
    )
    partial_attn = jnp.dot(mixed_heads, output_weight, preferred_element_type=jnp.float32)
    attention = lax.psum(partial_attn.astype(jnp.bfloat16), "col").astype(jnp.float32)
    hidden = inputs + attention
    second_scale = lax.rsqrt(jnp.mean(hidden * hidden, axis=-1, keepdims=True) + epsilon)
    second_normed = (hidden * second_scale * second_gain).astype(jnp.bfloat16)
    gate_pre = jnp.dot(second_normed, shared_gate, preferred_element_type=jnp.float32)
    up_pre = jnp.dot(second_normed, shared_up, preferred_element_type=jnp.float32)
    shared_act = (jax.nn.silu(gate_pre) * up_pre).astype(jnp.bfloat16)
    shared_out = jnp.dot(shared_act, shared_down, preferred_element_type=jnp.float32)
    shared_prob = jax.nn.sigmoid(
        jnp.dot(second_normed, shared_logit, preferred_element_type=jnp.float32)
    )
    local_owner, local_share = dispatch(
        route_rows, route_share, row_count, expert_start, local_experts
    )
    padded = jnp.concatenate(
        [second_normed, jnp.zeros((1, second_normed.shape[1]), jnp.bfloat16)], axis=0
    )
    expert_rows = padded[local_owner].reshape(local_experts, CAP, -1)
    expert_gate_pre = jnp.einsum(
        "ecd,def->ecf", expert_rows, expert_gate, preferred_element_type=jnp.float32
    )
    expert_up_pre = jnp.einsum(
        "ecd,def->ecf", expert_rows, expert_up, preferred_element_type=jnp.float32
    )
    expert_act = (jax.nn.silu(expert_gate_pre) * expert_up_pre).astype(jnp.bfloat16)
    expert_out = jnp.einsum(
        "ecf,efd->ecd", expert_act, expert_down, preferred_element_type=jnp.float32
    )
    weighted_out = expert_out.reshape(local_experts * CAP, -1) * local_share[:, None]
    routed = (
        jnp.zeros((row_count + 1, weighted_out.shape[1]), jnp.float32)
        .at[local_owner]
        .add(weighted_out)[:row_count]
    )
    ffn_partial = shared_prob[:, None] * shared_out + routed
    ffn_share = lax.psum_scatter(
        ffn_partial.astype(jnp.bfloat16), "col", scatter_dimension=1, tiled=True
    ).astype(jnp.float32)
    hidden_share = lax.dynamic_slice_in_dim(hidden, col_start, local_width, 1)
    result_rows = (hidden_share + ffn_share).astype(jnp.bfloat16)
    kept_state = (
        inputs,
        first_scale,
        first_normed,
        query_rot,
        key_rot,
        value_low,
        allowed,
        cosine,
        sine_rows,
        log_total,
        mixed_heads,
        hidden,
        second_scale,
        second_normed,
        gate_pre,
        up_pre,
        shared_act,
        shared_out,
        shared_prob,
        local_owner,
        local_share,
        expert_rows,
        expert_gate_pre,
        expert_up_pre,
        expert_act,
    )
    return (kept_state, result_rows)


def backward_pass(kept_state, grad_rows, blocks, col_start, local_width):
    (
        inputs,
        first_scale,
        first_normed,
        query_rot,
        key_rot,
        value_low,
        allowed,
        cosine,
        sine_rows,
        log_total,
        mixed_heads,
        hidden,
        second_scale,
        second_normed,
        gate_pre,
        up_pre,
        shared_act,
        shared_out,
        shared_prob,
        local_owner,
        local_share,
        expert_rows,
        expert_gate_pre,
        expert_up_pre,
        expert_act,
    ) = kept_state
    (
        first_gain,
        query_weight,
        key_weight,
        value_weight,
        output_weight,
        second_gain,
        shared_gate,
        shared_up,
        shared_down,
        shared_logit,
        expert_gate,
        expert_up,
        expert_down,
    ) = blocks
    row_count = inputs.shape[0]
    local_experts = expert_gate.shape[1]
    grad_out = grad_rows.astype(jnp.float32)
    shared_grad_out = (shared_prob[:, None] * grad_out).astype(jnp.bfloat16)
    padded_grad = jnp.concatenate(
        [grad_out, jnp.zeros((1, grad_out.shape[1]), jnp.float32)], axis=0
    )
    expert_grad_out = (
        (padded_grad[local_owner] * local_share[:, None])
        .astype(jnp.bfloat16)
        .reshape(local_experts, CAP, -1)
    )
    prob_part = jnp.sum(grad_out * shared_out, axis=-1)
    shared_down_term = jnp.einsum(
        "tf,td->fd", shared_act, shared_grad_out, preferred_element_type=jnp.float32
    )
    shared_act_grad = jnp.einsum(
        "td,fd->tf", shared_grad_out, shared_down, preferred_element_type=jnp.float32
    )
    gate_grad_s, up_grad_s = swiglu_back(shared_act_grad, gate_pre, up_pre)
    shared_gate_term = jnp.einsum(
        "td,tf->df", second_normed, gate_grad_s, preferred_element_type=jnp.float32
    )
    shared_up_term = jnp.einsum(
        "td,tf->df", second_normed, up_grad_s, preferred_element_type=jnp.float32
    )
    expert_down_term = jnp.einsum(
        "ecf,ecd->efd", expert_act, expert_grad_out, preferred_element_type=jnp.float32
    )
    expert_act_grad = jnp.einsum(
        "ecd,efd->ecf", expert_grad_out, expert_down, preferred_element_type=jnp.float32
    )
    gate_grad_e, up_grad_e = swiglu_back(expert_act_grad, expert_gate_pre, expert_up_pre)
    expert_gate_term = jnp.einsum(
        "ecd,ecf->def", expert_rows, gate_grad_e, preferred_element_type=jnp.float32
    )
    expert_up_term = jnp.einsum(
        "ecd,ecf->def", expert_rows, up_grad_e, preferred_element_type=jnp.float32
    )
    expert_rows_grad = jnp.einsum(
        "ecf,def->ecd", gate_grad_e, expert_gate, preferred_element_type=jnp.float32
    )
    expert_rows_grad = expert_rows_grad + jnp.einsum(
        "ecf,def->ecd", up_grad_e, expert_up, preferred_element_type=jnp.float32
    )
    normed_part = jnp.einsum(
        "tf,df->td", gate_grad_s, shared_gate, preferred_element_type=jnp.float32
    )
    normed_part = normed_part + jnp.einsum(
        "tf,df->td", up_grad_s, shared_up, preferred_element_type=jnp.float32
    )
    routed_back = (
        jnp.zeros((row_count + 1, normed_part.shape[1]), jnp.float32)
        .at[local_owner]
        .add(expert_rows_grad.reshape(local_experts * CAP, -1))[:row_count]
    )
    normed_part = normed_part + routed_back
    normed_sum, prob_sum = (
        lax.psum(normed_part.astype(jnp.bfloat16), "col").astype(jnp.float32),
        lax.psum(prob_part.astype(jnp.bfloat16), "col").astype(jnp.float32),
    )
    logit_grad = prob_sum * shared_prob * (1.0 - shared_prob)
    normed_grad_2 = normed_sum + logit_grad[:, None] * shared_logit[None, :]
    logit_term = jnp.dot(logit_grad, second_normed, preferred_element_type=jnp.float32)
    hidden_part, second_gain_term = norm_back(normed_grad_2, hidden, second_scale, second_gain)
    hidden_grad = grad_out + hidden_part
    attn_grad = hidden_grad.astype(jnp.bfloat16)
    output_term = jnp.einsum(
        "tc,td->cd", mixed_heads, attn_grad, preferred_element_type=jnp.float32
    )
    head_shape = (row_count, local_width // HEAD_DIM, HEAD_DIM)
    mixed_grad = (
        jnp.einsum("td,cd->tc", attn_grad, output_weight, preferred_element_type=jnp.float32)
        .astype(jnp.bfloat16)
        .reshape(head_shape)
    )
    scores = score_block(query_rot, key_rot, allowed)
    probabilities = jnp.exp(scores - log_total)
    prob_grad = jnp.einsum(
        "qhd,khd->hqk", mixed_grad, value_low, preferred_element_type=jnp.float32
    )
    value_grad_h = (
        jnp.einsum(
            "hqk,qhd->khd",
            probabilities.astype(jnp.bfloat16),
            mixed_grad,
            preferred_element_type=jnp.float32,
        )
        .astype(jnp.bfloat16)
        .reshape(row_count, local_width)
    )
    center = jnp.sum(prob_grad * probabilities, axis=-1, keepdims=True)
    score_grad = (probabilities * (prob_grad - center) * (1.0 / math.sqrt(HEAD_DIM))).astype(
        jnp.bfloat16
    )
    query_grad_h = (
        rotate_back(
            jnp.einsum("hqk,khd->qhd", score_grad, key_rot, preferred_element_type=jnp.float32),
            cosine,
            sine_rows,
        )
        .astype(jnp.bfloat16)
        .reshape(row_count, local_width)
    )
    key_grad_h = (
        rotate_back(
            jnp.einsum("hqk,qhd->khd", score_grad, query_rot, preferred_element_type=jnp.float32),
            cosine,
            sine_rows,
        )
        .astype(jnp.bfloat16)
        .reshape(row_count, local_width)
    )
    query_term = jnp.einsum(
        "td,tc->dc", first_normed, query_grad_h, preferred_element_type=jnp.float32
    )
    key_term = jnp.einsum("td,tc->dc", first_normed, key_grad_h, preferred_element_type=jnp.float32)
    value_term = jnp.einsum(
        "td,tc->dc", first_normed, value_grad_h, preferred_element_type=jnp.float32
    )
    first_part = jnp.einsum(
        "tc,dc->td", query_grad_h, query_weight, preferred_element_type=jnp.float32
    )
    first_part = first_part + jnp.einsum(
        "tc,dc->td", key_grad_h, key_weight, preferred_element_type=jnp.float32
    )
    first_part = first_part + jnp.einsum(
        "tc,dc->td", value_grad_h, value_weight, preferred_element_type=jnp.float32
    )
    normed_grad_1 = lax.psum(first_part.astype(jnp.bfloat16), "col").astype(jnp.float32)
    rows_part, first_gain_term = norm_back(normed_grad_1, inputs, first_scale, first_gain)
    token_rows = lax.dynamic_slice_in_dim(hidden_grad + rows_part, col_start, local_width, 1)
    grad_terms = (
        first_gain_term,
        query_term,
        key_term,
        value_term,
        output_term,
        second_gain_term,
        shared_gate_term,
        shared_up_term,
        shared_down_term,
        logit_term,
        expert_gate_term,
        expert_up_term,
        expert_down_term,
    )
    return (token_rows, grad_terms)


def shards(
    tokens,
    routes,
    route_weights,
    group_ids,
    first_gain,
    query_weight,
    key_weight,
    value_weight,
    output_weight,
    second_gain,
    shared_gate,
    shared_up,
    shared_down,
    shared_logit,
    expert_gate,
    expert_up,
    expert_down,
    cotangent,
):
    local_width = query_weight.shape[1]
    col_start = lax.axis_index("col") * local_width
    expert_start = lax.axis_index("col") * expert_gate.shape[1]
    full_tokens, full_cotangent = (
        lax.all_gather(tokens, "col", axis=2, tiled=True),
        lax.all_gather(cotangent, "col", axis=2, tiled=True),
    )
    totals = None
    results = []
    input_grads = []
    for batch_index in range(tokens.shape[0]):
        forward_blocks = (
            lax.all_gather(first_gain, "row", axis=0, tiled=True),
            lax.all_gather(query_weight, "row", axis=0, tiled=True),
            lax.all_gather(key_weight, "row", axis=0, tiled=True),
            lax.all_gather(value_weight, "row", axis=0, tiled=True),
            lax.all_gather(output_weight, "row", axis=1, tiled=True),
            lax.all_gather(second_gain, "row", axis=0, tiled=True),
            lax.all_gather(shared_gate, "row", axis=0, tiled=True),
            lax.all_gather(shared_up, "row", axis=0, tiled=True),
            lax.all_gather(shared_down, "row", axis=1, tiled=True),
            lax.all_gather(shared_logit, "row", axis=0, tiled=True),
            lax.all_gather(expert_gate, "row", axis=0, tiled=True),
            lax.all_gather(expert_up, "row", axis=0, tiled=True),
            lax.all_gather(expert_down, "row", axis=2, tiled=True),
        )
        kept_state, result_rows = forward_pass(
            full_tokens[batch_index],
            routes[batch_index],
            route_weights[batch_index],
            group_ids[batch_index],
            forward_blocks,
            col_start,
            local_width,
            expert_start,
        )
        backward_blocks = (
            lax.all_gather(first_gain, "row", axis=0, tiled=True),
            lax.all_gather(query_weight, "row", axis=0, tiled=True),
            lax.all_gather(key_weight, "row", axis=0, tiled=True),
            lax.all_gather(value_weight, "row", axis=0, tiled=True),
            lax.all_gather(output_weight, "row", axis=1, tiled=True),
            lax.all_gather(second_gain, "row", axis=0, tiled=True),
            lax.all_gather(shared_gate, "row", axis=0, tiled=True),
            lax.all_gather(shared_up, "row", axis=0, tiled=True),
            lax.all_gather(shared_down, "row", axis=1, tiled=True),
            lax.all_gather(shared_logit, "row", axis=0, tiled=True),
            lax.all_gather(expert_gate, "row", axis=0, tiled=True),
            lax.all_gather(expert_up, "row", axis=0, tiled=True),
            lax.all_gather(expert_down, "row", axis=2, tiled=True),
        )
        token_rows, grad_terms = backward_pass(
            kept_state, full_cotangent[batch_index], backward_blocks, col_start, local_width
        )
        results.append(result_rows)
        input_grads.append(token_rows)
        if totals is None:
            totals = tuple(grad_terms)
        else:
            totals = tuple(
                (left_term + right_term for left_term, right_term in zip(totals, grad_terms))
            )
    totals = (
        lax.psum_scatter(
            totals[0].astype(jnp.bfloat16), "row", scatter_dimension=0, tiled=True
        ).astype(jnp.float32),
        lax.psum_scatter(
            totals[1].astype(jnp.bfloat16), "row", scatter_dimension=0, tiled=True
        ).astype(jnp.float32),
        lax.psum_scatter(
            totals[2].astype(jnp.bfloat16), "row", scatter_dimension=0, tiled=True
        ).astype(jnp.float32),
        lax.psum_scatter(
            totals[3].astype(jnp.bfloat16), "row", scatter_dimension=0, tiled=True
        ).astype(jnp.float32),
        lax.psum_scatter(
            totals[4].astype(jnp.bfloat16), "row", scatter_dimension=1, tiled=True
        ).astype(jnp.float32),
        lax.psum_scatter(
            totals[5].astype(jnp.bfloat16), "row", scatter_dimension=0, tiled=True
        ).astype(jnp.float32),
        lax.psum_scatter(
            totals[6].astype(jnp.bfloat16), "row", scatter_dimension=0, tiled=True
        ).astype(jnp.float32),
        lax.psum_scatter(
            totals[7].astype(jnp.bfloat16), "row", scatter_dimension=0, tiled=True
        ).astype(jnp.float32),
        lax.psum_scatter(
            totals[8].astype(jnp.bfloat16), "row", scatter_dimension=1, tiled=True
        ).astype(jnp.float32),
        lax.psum_scatter(
            totals[9].astype(jnp.bfloat16), "row", scatter_dimension=0, tiled=True
        ).astype(jnp.float32),
        lax.psum_scatter(
            totals[10].astype(jnp.bfloat16), "row", scatter_dimension=0, tiled=True
        ).astype(jnp.float32),
        lax.psum_scatter(
            totals[11].astype(jnp.bfloat16), "row", scatter_dimension=0, tiled=True
        ).astype(jnp.float32),
        lax.psum_scatter(
            totals[12].astype(jnp.bfloat16), "row", scatter_dimension=2, tiled=True
        ).astype(jnp.float32),
    )
    return (
        jnp.stack(results),
        jnp.stack(input_grads),
        totals[0],
        totals[1],
        totals[2],
        totals[3],
        totals[4],
        totals[5],
        totals[6],
        totals[7],
        totals[8],
        totals[9],
        totals[10],
        totals[11],
        totals[12],
    )


def solution(mesh):
    return jax.shard_map(
        shards,
        mesh=mesh,
        in_specs=(
            P(None, "row", "col"),
            P(None, "row", None),
            P(None, "row", None),
            P(None, "row"),
            P("row"),
            P("row", "col"),
            P("row", "col"),
            P("row", "col"),
            P("col", "row"),
            P("row"),
            P("row", "col"),
            P("row", "col"),
            P("col", "row"),
            P("row"),
            P("row", "col", None),
            P("row", "col", None),
            P("col", None, "row"),
            P(None, "row", "col"),
        ),
        out_specs=(
            P(None, "row", "col"),
            P(None, "row", "col"),
            P("row"),
            P("row", "col"),
            P("row", "col"),
            P("row", "col"),
            P("col", "row"),
            P("row"),
            P("row", "col"),
            P("row", "col"),
            P("col", "row"),
            P("row"),
            P("row", "col", None),
            P("row", "col", None),
            P("col", None, "row"),
        ),
        check_vma=False,
    )
```

profile of v0, /device:TPU:0, one launch (start us, length us, event | category | flops | bytes accessed | tf_op | source)
XLA Modules:
  0.0 1808.7 jit_solution(10773522638501020359)
XLA Ops:
  25.5 22.1 %all-gather.16.cloned.1.call-done = bf16[2,256,2048]{2,1,0:T(8,128)(2,1)} async-done(((bf16[2,256,512]{2,1,0:T(8,128)(2,1)}), bf16[2,256,2048]{2,1,0:T(8,128)(2,1)}) %all-gather.16.cloned.1.call-update) | async-done | bytes 2097168 | tf_op jit(solution)/shard_map/all_gather | solution.py:456
  49.7 28.7 %all-gather.18.cloned.1.call-done = bf16[2048,512]{1,0:T(8,128)(2,1)} async-done(((bf16[256,512]{1,0:T(8,128)(2,1)}), bf16[2048,512]{1,0:T(8,128)(2,1)}) %all-gather.18.cloned.1.call-update) | async-done | bytes 2097168 | tf_op jit(solution)/shard_map/all_gather | solution.py:467
  82.3 26.3 %all-gather.22.cloned.1.call-done = bf16[2048,512]{1,0:T(8,128)(2,1)} async-done(((bf16[256,512]{1,0:T(8,128)(2,1)}), bf16[2048,512]{1,0:T(8,128)(2,1)}) %all-gather.22.cloned.1.call-update) | async-done | bytes 2097168 | tf_op jit(solution)/shard_map/all_gather | solution.py:466
  112.5 26.1 %all-gather.20.cloned.1.call-done = bf16[2048,512]{1,0:T(8,128)(2,1)} async-done(((bf16[256,512]{1,0:T(8,128)(2,1)}), bf16[2048,512]{1,0:T(8,128)(2,1)}) %all-gather.20.cloned.1.call-update) | async-done | bytes 2097168 | tf_op jit(solution)/shard_map/all_gather | solution.py:465
  155.2 14.9 all-gather.24.cloned.1.call-done
  244.5 35.1 %all-reduce.20.cloned.1.call-done = (bf16[256,2048]{1,0:T(8,128)(2,1)}, bf16[256,2048]{1,0:T(8,128)(2,1)}) async-done(((bf16[256,2048]{1,0:T(8,128)(2,1)}, bf16[256,2048]{1,0:T(8,128)(2,1)}), (bf16[256,2048]{1,0:T(8,128)(2,1)}, bf16[256,2048]{1,0:T(8,128)(2,1)})) %all-reduce.20.cloned.1.call-update) | async-done | bytes 2097168 | tf_op jit(solution)/shard_map/psum | solution.py:169
  299.5 42.2 %all-gather.26.cloned.1.call-done = bf16[2048,1408]{1,0:T(8,128)(2,1)} async-done(((bf16[256,1408]{1,0:T(8,128)(2,1)}), bf16[2048,1408]{1,0:T(8,128)(2,1)}) %all-gather.26.cloned.1.call-update) | async-done | bytes 5767184 | tf_op jit(solution)/shard_map/all_gather | solution.py:470
  347.5 54.9 %all-gather.28.cloned.1.call-done = bf16[2048,1408]{1,0:T(8,128)(2,1)} async-done(((bf16[256,1408]{1,0:T(8,128)(2,1)}), bf16[2048,1408]{1,0:T(8,128)(2,1)}) %all-gather.28.cloned.1.call-update) | async-done | bytes 5767184 | tf_op jit(solution)/shard_map/all_gather | solution.py:471
  408.8 54.5 %all-gather.30.cloned.1.call-done = bf16[1408,2048]{1,0:T(8,128)(2,1)} async-done(((bf16[1408,256]{1,0:T(8,128)(2,1)}), bf16[1408,2048]{1,0:T(8,128)(2,1)}) %all-gather.30.cloned.1.call-update) | async-done | bytes 5767184 | tf_op jit(solution)/shard_map/all_gather | solution.py:472
  513.1 58.7 %all-gather.34.cloned.1.call-done = bf16[2048,2,1408]{2,0,1:T(8,128)(2,1)} async-done(((bf16[256,2,1408]{2,0,1:T(8,128)(2,1)}), bf16[2048,2,1408]{2,0,1:T(8,128)(2,1)}) %all-gather.34.cloned.1.call-update) | async-done | bytes 11534352 | tf_op jit(solution)/shard_map/all_gather | solution.py:475
  578.5 101.7 %all-gather.32.cloned.1.call-done = bf16[2048,2,1408]{2,0,1:T(8,128)(2,1)} async-done(((bf16[256,2,1408]{2,0,1:T(8,128)(2,1)}), bf16[2048,2,1408]{2,0,1:T(8,128)(2,1)}) %all-gather.32.cloned.1.call-update) | async-done | bytes 11534352 | tf_op jit(solution)/shard_map/all_gather | solution.py:474
  688.1 100.4 %all-gather.36.cloned.1.call-done = bf16[2,1408,2048]{2,1,0:T(8,128)(2,1)} async-done(((bf16[2,1408,256]{2,1,0:T(8,128)(2,1)}), bf16[2,1408,2048]{2,1,0:T(8,128)(2,1)}) %all-gather.36.cloned.1.call-update) | async-done | bytes 11534352 | tf_op jit(solution)/shard_map/all_gather | solution.py:476
  1035.0 15.4 add_convert_fusion
  1113.1 41.3 %reduce-scatter.25.cloned.1.call-done = bf16[256,1408]{1,0:T(8,128)(2,1)} async-done(((bf16[2048,1408]{1,0:T(8,128)(2,1)}), bf16[256,1408]{1,0:T(8,128)(2,1)}) %reduce-scatter.25.cloned.1.call-update) | async-done | bytes 720912 | tf_op jit(solution)/shard_map/reduce_scatter | solution.py:533
  1156.7 26.8 %reduce-scatter.15.cloned.1.call-done = bf16[256,512]{1,0:T(8,128)(2,1)} async-done(((bf16[256,2048]{1,0:T(8,128)(2,1)}), bf16[256,512]{1,0:T(8,128)(2,1)}) %reduce-scatter.15.cloned.1.call-update) | async-done | bytes 262160 | tf_op jit(solution)/shard_map/reduce_scatter | solution.py:204
  1184.8 29.7 %reduce-scatter.13.cloned.1.call-done = bf16[256,512]{1,0:T(8,128)(2,1)} async-done(((bf16[256,2048]{1,0:T(8,128)(2,1)}), bf16[256,512]{1,0:T(8,128)(2,1)}) %reduce-scatter.13.cloned.1.call-update) | async-done | bytes 262160 | tf_op jit(solution)/shard_map/reduce_scatter | solution.py:204
  1216.5 70.4 %all-reduce.16.cloned.1.call-done = (bf16[256,2048]{1,0:T(8,128)(2,1)}, bf16[256,2048]{1,0:T(8,128)(2,1)}) async-done(((bf16[256,2048]{1,0:T(8,128)(2,1)}, bf16[256,2048]{1,0:T(8,128)(2,1)}), (bf16[256,2048]{1,0:T(8,128)(2,1)}, bf16[256,2048]{1,0:T(8,128)(2,1)})) %all-reduce.16.cloned.1.call-update) | async-done | bytes 2097168 | tf_op jit(solution)/shard_map/psum | solution.py:411
  1292.9 28.8 %all-reduce.7 = (bf16[2048]{0:T(1024)(128)(2,1)S(1)}, bf16[2048]{0:T(1024)(128)(2,1)S(1)}, bf16[2048]{0:T(1024)(128)(2,1)S(1)}) all-reduce(bf16[2048]{0:T(1024)(128)(2,1)S(1)} %add_convert_fusion.18, bf16[2048]{0:T(1024)(128)(2,1)S(1)} %add_convert_fusion.17, ...), channel_id=4, replica_groups=mesh['row'=8,'col'=4] {'row'}, use_global_device_ids=true, to_apply=%region_46.47.clone | all-reduce | flops 6144 | bytes 24576
  1329.6 33.0 %reduce-scatter.19.cloned.1.call-done = bf16[256,512]{1,0:T(8,128)(2,1)} async-done(((bf16[2048,512]{1,0:T(8,128)(2,1)}), bf16[256,512]{1,0:T(8,128)(2,1)}) %reduce-scatter.19.cloned.1.call-update) | async-done | bytes 262160 | tf_op jit(solution)/shard_map/reduce_scatter | solution.py:521
  1364.4 35.2 %reduce-scatter.17.cloned.1.call-done = bf16[256,512]{1,0:T(8,128)(2,1)} async-done(((bf16[2048,512]{1,0:T(8,128)(2,1)}), bf16[256,512]{1,0:T(8,128)(2,1)}) %reduce-scatter.17.cloned.1.call-update) | async-done | bytes 262160 | tf_op jit(solution)/shard_map/reduce_scatter | solution.py:518
  1401.4 35.0 %reduce-scatter.23.cloned.1.call-done = bf16[512,256]{1,0:T(8,128)(2,1)} async-done(((bf16[512,2048]{1,0:T(8,128)(2,1)}), bf16[512,256]{1,0:T(8,128)(2,1)}) %reduce-scatter.23.cloned.1.call-update) | async-done | bytes 262160 | tf_op jit(solution)/shard_map/reduce_scatter | solution.py:527
  1438.1 118.4 %reduce-scatter.35.cloned.1.call-done = bf16[2,1408,256]{2,1,0:T(8,128)(2,1)} async-done(((bf16[2,1408,2048]{2,1,0:T(8,128)(2,1)}), bf16[2,1408,256]{2,1,0:T(8,128)(2,1)}) %reduce-scatter.35.cloned.1.call-update) | async-done | bytes 1441808 | tf_op jit(solution)/shard_map/reduce_scatter | solution.py:551
  1559.7 116.7 %reduce-scatter.33.cloned.1.call-done = bf16[256,2,1408]{0,2,1:T(8,128)(2,1)} async-done(((bf16[2048,2,1408]{0,2,1:T(8,128)(2,1)}), bf16[256,2,1408]{0,2,1:T(8,128)(2,1)}) %reduce-scatter.33.cloned.1.call-update) | async-done | bytes 1441808 | tf_op jit(solution)/shard_map/reduce_scatter | solution.py:548
  1681.5 114.9 %reduce-scatter.31.cloned.1.call-done = bf16[256,2,1408]{0,2,1:T(8,128)(2,1)} async-done(((bf16[2048,2,1408]{0,2,1:T(8,128)(2,1)}), bf16[256,2,1408]{0,2,1:T(8,128)(2,1)}) %reduce-scatter.31.cloned.1.call-update) | async-done | bytes 1441808 | tf_op jit(solution)/shard_map/reduce_scatter | solution.py:545
  (585 shorter events, 560.0 us)
Async XLA Ops:
  9.4 129.2 %all-gather.20.cloned.1.call-start = ((), (), s32[]{:S(2)}) async-start(), calls=%async_computation.14 | async-start | bytes 2359296 | tf_op jit(solution)/shard_map/all_gather | solution.py:465
  10.0 160.1 %all-gather.24.cloned.1.call-start = ((), (), s32[]{:S(2)}) async-start(), calls=%async_computation.16 | async-start | bytes 2359296 | tf_op jit(solution)/shard_map/all_gather | solution.py:468
  10.6 214.9 %all-gather.38.cloned.1.call-start = ((), (), s32[]{:S(2)}) async-start(), calls=%async_computation.25 | async-start | bytes 2621440 | tf_op jit(solution)/shard_map/all_gather | solution.py:457
  11.2 268.4 %all-reduce.20.cloned.1.call-start = ((), (), s32[]{:S(2)}) async-start(), calls=%async_computation.38 | async-start | bytes 4194304 | tf_op jit(solution)/shard_map/psum | solution.py:169
  175.3 166.3 %all-gather.26.cloned.1.call-start = ((), (), s32[]{:S(2)}) async-start(), calls=%async_computation.17 | async-start | bytes 6488064 | tf_op jit(solution)/shard_map/all_gather | solution.py:470
  176.0 226.3 %all-gather.28.cloned.1.call-start = ((), (), s32[]{:S(2)}) async-start(), calls=%async_computation.18 | async-start | bytes 6488064 | tf_op jit(solution)/shard_map/all_gather | solution.py:471
  176.8 286.5 %all-gather.30.cloned.1.call-start = ((), (), s32[]{:S(2)}) async-start(), calls=%async_computation.19 | async-start | bytes 6488064 | tf_op jit(solution)/shard_map/all_gather | solution.py:472
  177.4 394.4 %all-gather.34.cloned.1.call-start = ((), (), s32[]{:S(2)}) async-start(), calls=%async_computation.21 | async-start | bytes 12976128 | tf_op jit(solution)/shard_map/all_gather | solution.py:475
  178.7 501.4 %all-gather.32.cloned.1.call-start = ((), (), s32[]{:S(2)}) async-start(), calls=%async_computation.20 | async-start | bytes 12976128 | tf_op jit(solution)/shard_map/all_gather | solution.py:474
  180.6 607.9 %all-gather.36.cloned.1.call-start = ((), (), s32[]{:S(2)}) async-start(), calls=%async_computation.22 | async-start | bytes 12976128 | tf_op jit(solution)/shard_map/all_gather | solution.py:476
  181.4 775.3 %all-reduce.18.cloned.1.call-start = ((), (), s32[]{:S(2)}) async-start(), calls=%async_computation.37 | async-start | bytes 4194304 | tf_op jit(solution)/shard_map/psum | solution.py:340
  888.8 219.7 %reduce-scatter.29.cloned.1.call-start = ((), (), s32[]{:S(2)}) async-start(), calls=%async_computation.32 | async-start | bytes 6488064 | tf_op jit(solution)/shard_map/reduce_scatter | solution.py:539
  896.6 214.2 %reduce-scatter.27.cloned.1.call-start = ((), (), s32[]{:S(2)}) async-start(), calls=%async_computation.31 | async-start | bytes 6488064 | tf_op jit(solution)/shard_map/reduce_scatter | solution.py:536
  904.2 250.3 %reduce-scatter.25.cloned.1.call-start = ((), (), s32[]{:S(2)}) async-start(), calls=%async_computation.30 | async-start | bytes 6488064 | tf_op jit(solution)/shard_map/reduce_scatter | solution.py:533
  911.4 272.1 %reduce-scatter.15.cloned.1.call-start = ((), (), s32[]{:S(2)}) async-start(), calls=%async_computation.24 | async-start | bytes 1310720 | tf_op jit(solution)/shard_map/reduce_scatter | solution.py:204
  930.7 283.8 %reduce-scatter.13.cloned.1.call-start = ((), (), s32[]{:S(2)}) async-start(), calls=%async_computation.23 | async-start | bytes 1310720 | tf_op jit(solution)/shard_map/reduce_scatter | solution.py:204
  951.6 335.3 %all-reduce.16.cloned.1.call-start = ((), (), s32[]{:S(2)}) async-start(), calls=%async_computation.36 | async-start | bytes 4194304 | tf_op jit(solution)/shard_map/psum | solution.py:411
  1003.8 324.0 %reduce-scatter.21.cloned.1.call-start = ((), (), s32[]{:S(2)}) async-start(), calls=%async_computation.28 | async-start | bytes 2359296 | tf_op jit(solution)/shard_map/reduce_scatter | solution.py:524
  1007.6 354.9 %reduce-scatter.19.cloned.1.call-start = ((), (), s32[]{:S(2)}) async-start(), calls=%async_computation.27 | async-start | bytes 2359296 | tf_op jit(solution)/shard_map/reduce_scatter | solution.py:521
  1011.9 387.7 %reduce-scatter.17.cloned.1.call-start = ((), (), s32[]{:S(2)}) async-start(), calls=%async_computation.26 | async-start | bytes 2359296 | tf_op jit(solution)/shard_map/reduce_scatter | solution.py:518
  1015.0 421.3 %reduce-scatter.23.cloned.1.call-start = ((), (), s32[]{:S(2)}) async-start(), calls=%async_computation.29 | async-start | bytes 2359296 | tf_op jit(solution)/shard_map/reduce_scatter | solution.py:527
  1020.5 536.1 %reduce-scatter.35.cloned.1.call-start = ((), (), s32[]{:S(2)}) async-start(), calls=%async_computation.35 | async-start | bytes 12976128 | tf_op jit(solution)/shard_map/reduce_scatter | solution.py:551
  1050.4 626.0 %reduce-scatter.33.cloned.1.call-start = ((), (), s32[]{:S(2)}) async-start(), calls=%async_computation.34 | async-start | bytes 12976128 | tf_op jit(solution)/shard_map/reduce_scatter | solution.py:548
  1077.4 718.9 %reduce-scatter.31.cloned.1.call-start = ((), (), s32[]{:S(2)}) async-start(), calls=%async_computation.33 | async-start | bytes 12976128 | tf_op jit(solution)/shard_map/reduce_scatter | solution.py:545
  (155 other events, 4463.8 us)
Sparse Core Ops, SparseCore 0:
  9.8 37.7 all-gather.15
  49.2 29.1 all-gather.17
  80.0 28.5 all-gather.21
  140.1 29.9 all-gather.23
  171.8 34.0 all-gather.37
  210.1 69.4 all-reduce.19
  281.2 60.3 all-gather.25
  343.3 59.0 all-gather.27
  403.8 59.4 all-gather.29
  465.5 106.2 all-gather.33
  573.8 106.2 all-gather.31
  681.7 106.7 all-gather.35
  888.9 67.6 all-reduce.17
  958.8 64.7 reduce-scatter.28
  1025.7 63.2 reduce-scatter.26
  1091.2 63.2 reduce-scatter.24
  1217.4 69.4 all-reduce.15
  1289.2 36.3 reduce-scatter.20
  1327.8 34.6 reduce-scatter.18
  1364.9 34.6 reduce-scatter.16
  1401.7 34.6 reduce-scatter.22
  1438.7 117.8 reduce-scatter.34
  1558.7 117.6 reduce-scatter.32
  1678.6 117.6 reduce-scatter.30
  (3 shorter events, 82.6 us)
where the time goes:
time: 1820 us; the launch traced here: 1810 us
  waiting for transfers between devices  1200 us (66%)
  matrix products  321 us (18%)
  local copies, waits for them, and re-layouts  103 us (6%)
  other arithmetic  93.3 us (5%)
  blocking collectives  73.4 us (4%)
    reduce_scatter x1, waiting for transfers between devices, shards(): lax.psum_scatter(totals[12].astype(jnp.bfloat16), 'row', scatter_dimensio...  118 us
    reduce_scatter x1, waiting for transfers between devices, shards(): lax.psum_scatter(totals[11].astype(jnp.bfloat16), 'row', scatter_dimensio...  117 us
    reduce_scatter x1, waiting for transfers between devices, shards(): lax.psum_scatter(totals[10].astype(jnp.bfloat16), 'row', scatter_dimensio...  115 us
    all_gather x1, waiting for transfers between devices, shards(): lax.all_gather(expert_gate, 'row', axis=0, tiled=True)  102 us
    all_gather x1, waiting for transfers between devices, shards(): lax.all_gather(expert_down, 'row', axis=2, tiled=True)  100 us
    psum x1, waiting for transfers between devices, backward_pass(): lax.psum(first_part.astype(jnp.bfloat16), 'col').astype(jnp.float32)  70.4 us
    all_gather x1, waiting for transfers between devices, shards(): lax.all_gather(expert_up, 'row', axis=0, tiled=True)  58.7 us
    reduce_scatter x2, waiting for transfers between devices, forward_pass(): lax.psum_scatter(ffn_partial.astype(jnp.bfloat16), 'col', scatter_dimensi...  56.5 us
  transfers between devices with their start and end apart: 27, of which 23 were waited for; matrix products, arithmetic and copies ran while one was open for 22% of the time, Pallas kernels for 0%

commit v1 on v0

v1 whole, which is shorter than its diff:
```python
import functools
import math

import jax
import jax.numpy as jnp
from jax import lax
from jax.experimental import pallas as pl
from jax.experimental.pallas import tpu as pltpu
from jax.sharding import Mesh, PartitionSpec as P

HEAD_DIM = 128
EXPERTS = 8
PROMPTS = 2
CONTS = 2
CONT_LEN = 64
PROMPT_LEN = 64

epsilon = 1e-06
rope_base = 1000000.0
masked_score = -1000000000.0

F32 = jnp.float32
BF16 = jnp.bfloat16
COL = ("y", "x")
ROW = ("g", "k")
ALL = ("g", "k", "y", "x")


def block_layout(groups, row_count):
    token_index = jnp.arange(row_count, dtype=jnp.int32)
    prompt_rows = PROMPTS * PROMPT_LEN
    is_prompt = token_index < prompt_rows
    cont_offset = jnp.maximum(token_index - prompt_rows, 0)
    cont_number = cont_offset // CONT_LEN
    segment = jnp.where(is_prompt, token_index // PROMPT_LEN, PROMPTS + cont_number)
    position = jnp.where(is_prompt, token_index % PROMPT_LEN, PROMPT_LEN + cont_offset % CONT_LEN)
    cont_picks = (cont_number[:, None] == jnp.arange(CONTS, dtype=jnp.int32)[None, :]).astype(
        jnp.int32
    )
    source = jnp.where(
        is_prompt[None], segment[None], jnp.sum(cont_picks[None] * groups[:, None, :], axis=2)
    )
    same_segment = (segment[:, None] == segment[None, :]) & (position[None, :] <= position[:, None])
    context = (
        jnp.logical_not(is_prompt)[None, :, None]
        & is_prompt[None, None, :]
        & (source[:, :, None] == segment[None, None, :])
    )
    return (same_segment[None] | context, position)


def rotary_tables(position):
    half_dim = HEAD_DIM // 2
    frequency = rope_base ** (-(2.0 * jnp.arange(half_dim, dtype=F32)) / HEAD_DIM)
    angles = position.astype(F32)[:, None] * frequency[None, :]
    cosine = jnp.cos(angles)
    sine = jnp.sin(angles)
    return (cosine[None, :, None, :], sine[None, :, None, :])


def rotate(values, cosine, sine):
    first, second = jnp.split(values, 2, axis=-1)
    return jnp.concatenate([first * cosine - second * sine, second * cosine + first * sine], -1)


def dot(left, right, dims):
    return lax.dot_general(left, right, (dims, ((), ())), preferred_element_type=F32)


TILE = 256
PARTS = 2
EXTRA = 16


def ffn_kernel(sizes, meta, rows_ref, cot_ref, mix_ref, logit_ref, *refs):
    n_g, f_pad, f_shared, f_routed, local_experts, d_own = sizes
    blocks = refs[: 2 * n_g]
    out_ref, normed_ref, act_ref, gate_ref, up_ref = refs[2 * n_g : 2 * n_g + 5]
    w_gu, w_down, sems = refs[2 * n_g + 5 :]
    g_at, k_at = meta[0], meta[1]

    @pl.when((pl.program_id(0) == 0) & (pl.program_id(1) == 0))
    def _():
        copies = []
        for half in range(2):
            for shift in range(n_g):
                column = 2 * (g_at ^ shift) + (k_at ^ half)
                lanes = pl.ds(pl.multiple_of(column * d_own, d_own), d_own)
                source = blocks[half * n_g + shift]
                for kind, target in enumerate(
                    (w_gu.at[:f_pad, lanes], w_gu.at[f_pad : 2 * f_pad, lanes], w_down.at[:, lanes])
                ):
                    copies.append(
                        pltpu.make_async_copy(
                            source.at[kind], target, sems.at[(half * n_g + shift) * 3 + kind]
                        )
                    )
        for copy in copies:
            copy.start()
        w_gu[2 * f_pad :, :] = logit_ref[...]
        for copy in copies:
            copy.wait()

    rows = rows_ref[...]
    count = rows.shape[0]
    cot = jnp.concatenate(
        [cot_ref[c, 0, :, 0].reshape(count, -1) for c in range(cot_ref.shape[0])], axis=1
    )
    minor = ((1,), (1,))
    pre = dot(w_gu[...], rows, minor)
    down_back = dot(w_down[...], cot, minor)
    gate_pre, up_pre = pre[:f_pad], pre[f_pad : 2 * f_pad]
    prob = jax.nn.sigmoid(pre[2 * f_pad : 2 * f_pad + 1])
    pieces = [jnp.broadcast_to(prob, (f_shared, count))]
    for e in range(local_experts):
        pieces.append(jnp.broadcast_to(mix_ref[0, e : e + 1, :], (f_routed, count)))
    rest = f_pad - f_shared - local_experts * f_routed
    if rest:
        pieces.append(jnp.zeros((rest, count), F32))
    scale = jnp.concatenate(pieces, axis=0)
    sigma = jax.nn.sigmoid(gate_pre)
    silu = gate_pre * sigma
    act = silu * up_pre
    prob_part = jnp.sum(act[:f_shared] * down_back[:f_shared], axis=0, keepdims=True)
    act_grad = down_back * scale
    act_low = (act * scale).astype(BF16)
    gate_low = (act_grad * up_pre * sigma * (1.0 + gate_pre * (1.0 - sigma))).astype(BF16)
    up_low = (act_grad * silu).astype(BF16)
    logit_part = prob_part * prob * (1.0 - prob)
    logit_high = logit_part.astype(BF16).astype(F32)
    logit_rows = jnp.concatenate(
        [logit_high, logit_part - logit_high, jnp.zeros((EXTRA - 2, count), F32)], axis=0
    ).astype(BF16)
    act_ref[...] = act_low
    gate_ref[:f_pad, :] = gate_low
    gate_ref[f_pad:, :] = logit_rows
    up_ref[...] = up_low
    major = ((0,), (0,))
    out_ref[...] = dot(act_low, w_down[...], major).astype(BF16)
    both = jnp.concatenate([gate_low, up_low, logit_rows], axis=0)
    normed_ref[...] = dot(both, w_gu[...], major).astype(BF16)


def ffn_pass(sizes, meta, rows, cot, mix, logit, blocks, part):
    n_g, f_pad, _, _, local_experts, d_own = sizes
    total, dim = rows.shape
    n_c, _, _, parts, sub, cw = cot.shape
    take = min(TILE // sub, n_c)
    tile = take * sub
    steps = n_c // take
    flat = lambda i, j, m: (i * steps + j, 0)
    wide = lambda i, j, m: (0, i * steps + j)
    any_spec = pl.BlockSpec(memory_space=pl.ANY)
    return pl.pallas_call(
        functools.partial(ffn_kernel, sizes),
        grid_spec=pltpu.PrefetchScalarGridSpec(
            num_scalar_prefetch=1,
            grid=(n_g, steps),
            in_specs=[
                pl.BlockSpec((tile, dim), flat),
                pl.BlockSpec((n_c, 1, take, 1, sub, cw), lambda i, j, m: (0, i, j, part, 0, 0)),
                pl.BlockSpec((1, 8, tile), lambda i, j, m: (i * steps + j, 0, 0)),
                pl.BlockSpec((EXTRA, dim), lambda i, j, m: (0, 0)),
            ]
            + [any_spec] * (2 * n_g),
            out_specs=[
                pl.BlockSpec((tile, dim), flat),
                pl.BlockSpec((tile, dim), flat),
                pl.BlockSpec((f_pad, tile), wide),
                pl.BlockSpec((f_pad + EXTRA, tile), wide),
                pl.BlockSpec((f_pad, tile), wide),
            ],
            scratch_shapes=[
                pltpu.VMEM((2 * f_pad + EXTRA, dim), BF16),
                pltpu.VMEM((f_pad, dim), BF16),
                pltpu.SemaphoreType.DMA((6 * n_g,)),
            ],
        ),
        out_shape=[
            jax.ShapeDtypeStruct((total, dim), BF16),
            jax.ShapeDtypeStruct((total, dim), BF16),
            jax.ShapeDtypeStruct((f_pad, total), BF16),
            jax.ShapeDtypeStruct((f_pad + EXTRA, total), BF16),
            jax.ShapeDtypeStruct((f_pad, total), BF16),
        ],
        compiler_params=pltpu.CompilerParams(
            dimension_semantics=("arbitrary", "arbitrary"), vmem_limit_bytes=60 * 1024 * 1024
        ),
        cost_estimate=pl.CostEstimate(
            flops=12 * total * dim * f_pad,
            bytes_accessed=8 * total * dim + 6 * total * f_pad + 6 * f_pad * dim,
            transcendentals=total * f_pad,
        ),
        name="ffn_pass",
    )(meta, rows, cot, mix.reshape(-1, tile, 8).transpose(0, 2, 1), logit, *blocks)


def grad_kernel(parts, f_pad, meta, *refs):
    total = None
    for left, right in zip(refs[:parts], refs[parts : 2 * parts]):
        value = right[...].reshape(left.shape[1], -1)
        term = dot(left[...], value, ((1,), (0,)))
        total = term if total is None else total + term
    refs[2 * parts][0, 0] = total[:f_pad].astype(BF16)
    if len(refs) > 2 * parts + 1:
        refs[2 * parts + 1][...] = jnp.broadcast_to(
            total[f_pad : f_pad + 1] + total[f_pad + 1 : f_pad + 2], refs[2 * parts + 1].shape
        )


def weight_grad(sizes, meta, lefts, rights, cot):
    n_g, f_pad, _, _, _, d_own = sizes
    parts = len(lefts)
    f_rows, part_rows = lefts[0].shape
    dim = 2 * n_g * d_own
    if cot:
        n_c, _, _, _, sub, cw = rights[0].shape
        per = cw // d_own
        right_specs = [
            pl.BlockSpec(
                (1, n_g, n_c, 1, sub, d_own),
                functools.partial(lambda part, j, m: (j // per, 0, 0, part, 0, j % per), part),
            )
            for part in range(parts)
        ]
    else:
        right_specs = [pl.BlockSpec((part_rows, d_own), lambda j, m: (0, j))] * parts
    out_specs = [
        pl.BlockSpec(
            (1, 1, f_pad, d_own), lambda j, m: ((j % 2) ^ m[1], (j // 2) ^ m[0], 0, 0)
        )
    ]
    out_shape = [jax.ShapeDtypeStruct((2, n_g, f_pad, d_own), BF16)]
    if f_rows > f_pad:
        out_specs.append(pl.BlockSpec((8, d_own), lambda j, m: (0, j)))
        out_shape.append(jax.ShapeDtypeStruct((8, dim), F32))
    return pl.pallas_call(
        functools.partial(grad_kernel, parts, f_pad),
        grid_spec=pltpu.PrefetchScalarGridSpec(
            num_scalar_prefetch=1,
            grid=(2 * n_g,),
            in_specs=[pl.BlockSpec((f_rows, part_rows), lambda j, m: (0, 0))] * parts + right_specs,
            out_specs=out_specs,
        ),
        out_shape=out_shape,
        compiler_params=pltpu.CompilerParams(
            dimension_semantics=("arbitrary",), vmem_limit_bytes=48 * 1024 * 1024
        ),
        cost_estimate=pl.CostEstimate(
            flops=2 * parts * part_rows * dim * f_rows,
            bytes_accessed=2 * parts * part_rows * (dim + f_rows) + 2 * f_pad * dim,
            transcendentals=0,
        ),
        name="weight_grad",
    )(meta, *lefts, *rights)


def norm_back(normed_grad, unit_rows, scale, gain):
    weighted = normed_grad * gain
    rows_grad = scale * (
        weighted - unit_rows * jnp.mean(weighted * unit_rows, axis=-1, keepdims=True)
    )
    return (rows_grad, jnp.sum(normed_grad * unit_rows, axis=0))


def swap(value, axis):
    return lax.ppermute(value, axis, [(0, 1), (1, 0)])


def shift_chips(value, shift, n_g):
    if shift == 0:
        return value
    return lax.ppermute(value, "g", [(i, i ^ shift) for i in range(n_g)])


def col_gather(value, count):
    spread = jnp.broadcast_to(value[None], (count,) + value.shape)
    return lax.all_to_all(spread, COL, 0, 0, tiled=True)


def col_sum(partial, count):
    parts = partial.astype(BF16).reshape((count, -1) + partial.shape[1:])
    return jnp.sum(lax.all_to_all(parts, COL, 0, 0, tiled=True).astype(F32), axis=0)


def rows_to_features(rows, count):
    row_count, width = rows.shape
    parts = rows.reshape(row_count, count, width // count).transpose(1, 0, 2)
    moved = lax.all_to_all(parts, COL, 0, 0, tiled=True)
    blocks = moved.reshape(2, row_count * count // 2, width // count)
    return lax.all_to_all(blocks, "k", 0, 0, tiled=True)


def shards(
    tokens,
    routes,
    route_weights,
    group_ids,
    first_gain,
    query_weight,
    key_weight,
    value_weight,
    output_weight,
    second_gain,
    shared_gate,
    shared_up,
    shared_down,
    shared_logit,
    expert_gate,
    expert_up,
    expert_down,
    cotangent,
):
    n_g = lax.axis_size("g")
    n_c = lax.axis_size("y") * lax.axis_size("x")
    n_row = 2 * n_g
    at_g, at_k = lax.axis_index("g"), lax.axis_index("k")
    at_c = lax.axis_index(COL)
    block = tokens.shape[1]
    dim = query_weight.shape[0] * n_row
    d_own = query_weight.shape[0]
    width = query_weight.shape[1]
    heads = width // HEAD_DIM
    local_experts = expert_gate.shape[1]
    span = 2 * block
    total = n_g * span
    own_rows = span // n_c
    pick = lambda array, index, axis=0: lax.dynamic_index_in_dim(array, index, axis, keepdims=False)

    labels = jnp.arange(EXPERTS, dtype=jnp.int32)
    mixing = jnp.sum(
        jnp.where(
            routes[:, None] == labels[None, :, None, None], route_weights[:, None], 0.0
        ),
        axis=-1,
    )
    small = jnp.concatenate(
        [
            mixing.reshape(2 * EXPERTS, block),
            jnp.zeros((8, block), F32)
            .at[0, :d_own].set(first_gain.astype(F32))
            .at[1, :d_own].set(second_gain.astype(F32))
            .at[2, :d_own].set(shared_logit.astype(F32))
            .at[3, : 2 * CONTS].set(group_ids.astype(F32).reshape(-1)),
        ],
        axis=0,
    )
    small_all = lax.all_gather(small, ROW, axis=0, tiled=False)
    gain_1 = small_all[:, 16, :d_own].reshape(dim)
    gain_2 = small_all[:, 17, :d_own].reshape(dim)
    logit_w = small_all[:, 18, :d_own].reshape(dim)
    groups_all = small_all[:, 19, : 2 * CONTS].reshape(n_g, 2, 2, CONTS)
    groups = pick(pick(groups_all, at_g), at_k, 1).astype(jnp.int32)
    mixing_all = small_all[:, : 2 * EXPERTS].reshape(n_row, 2, EXPERTS, block)
    mixing_own = lax.dynamic_slice_in_dim(
        pick(mixing_all, at_k, 1), at_c * local_experts, local_experts, 1
    )
    mixing_own = mixing_own.transpose(0, 2, 1).reshape(total, local_experts)

    token_part = lax.all_to_all(tokens, "k", 0, 0, tiled=True).reshape(span, -1)
    cot_part = lax.all_to_all(cotangent, "k", 0, 0, tiled=True).reshape(span, -1)

    qkv = lax.all_gather(
        jnp.concatenate([query_weight, key_weight, value_weight], axis=1), ROW, axis=0, tiled=True
    )
    out_w = lax.all_gather(output_weight, ROW, axis=1, tiled=True)
    inputs = col_gather(token_part, n_c).reshape(n_c, span, -1).transpose(1, 0, 2)
    inputs = inputs.reshape(span, dim).astype(F32)

    f_shared = shared_gate.shape[1] // n_g
    f_routed = expert_gate.shape[2] // n_g
    f_all = f_shared + local_experts * f_routed
    f_pad = -(-f_all // 16) * 16
    sizes = (n_g, f_pad, f_shared, f_routed, local_experts, d_own)
    meta = jnp.stack([at_g, at_k]).astype(jnp.int32)

    def slices(shared, routed):
        parts = [
            shared.reshape(n_g, f_shared, d_own),
            routed.reshape(local_experts, n_g, f_routed, d_own)
            .transpose(1, 0, 2, 3)
            .reshape(n_g, -1, d_own),
        ]
        if f_pad > f_all:
            parts.append(jnp.zeros((n_g, f_pad - f_all, d_own), BF16))
        return jnp.concatenate(parts, axis=1)

    weight_slices = jnp.stack(
        [
            slices(shared_gate.T, expert_gate.transpose(1, 2, 0)),
            slices(shared_up.T, expert_up.transpose(1, 2, 0)),
            slices(shared_down, expert_down),
        ],
        axis=1,
    )
    own_blocks = [
        shift_chips(pick(weight_slices, at_g ^ shift), shift, n_g) for shift in range(n_g)
    ]
    weight_blocks = own_blocks + [swap(value, "k") for value in own_blocks]

    first_scale = lax.rsqrt(jnp.mean(inputs * inputs, axis=-1, keepdims=True) + epsilon)
    normed_1 = (inputs * first_scale * gain_1).astype(BF16)
    projected = dot(normed_1, qkv, ((1,), (0,)))
    allowed, position = block_layout(groups, block)
    cosine, sine = rotary_tables(position)
    head_shape = (2, block, heads, HEAD_DIM)
    query_rot = rotate(projected[:, :width].reshape(head_shape), cosine, sine).astype(BF16)
    key_rot = rotate(projected[:, width : 2 * width].reshape(head_shape), cosine, sine).astype(BF16)
    value_low = projected[:, 2 * width :].reshape(head_shape).astype(BF16)

    def einsum(form, left, right):
        return jnp.einsum(form, left, right, preferred_element_type=F32)

    scores = jnp.where(
        allowed[:, None],
        einsum("bqhd,bkhd->bhqk", query_rot, key_rot) * (1.0 / math.sqrt(HEAD_DIM)),
        masked_score,
    )
    peak = jnp.max(scores, axis=-1, keepdims=True)
    exp_scores = jnp.exp(scores - peak)
    probabilities = exp_scores / jnp.sum(exp_scores, axis=-1, keepdims=True)
    prob_low = probabilities.astype(BF16)
    mixed = einsum("bhqk,bkhd->bqhd", prob_low, value_low).astype(BF16).reshape(span, width)
    attention = col_sum(dot(mixed, out_w, ((1,), (0,))), n_c)

    own_inputs = lax.dynamic_slice_in_dim(inputs, at_c * own_rows, own_rows, 0)
    hidden = own_inputs + attention
    second_scale = lax.rsqrt(jnp.mean(hidden * hidden, axis=-1, keepdims=True) + epsilon)
    unit_2 = hidden * second_scale
    normed_own = (unit_2 * gain_2).astype(BF16)
    sub = own_rows // PARTS
    normed_parts = [
        lax.all_gather(
            normed_own[part * sub : (part + 1) * sub], ("g",) + COL, axis=0, tiled=True
        )
        for part in range(PARTS)
    ]

    cot_rows = lax.all_gather(cot_part, "g", axis=0, tiled=True)
    cot_all = col_gather(cot_rows, n_c).reshape(n_c, n_g, n_c, PARTS, sub, dim // n_c)
    own_cot = pick(pick(cot_all, at_g, 1), at_c, 1).reshape(n_c, own_rows, -1)
    own_cot = own_cot.transpose(1, 0, 2).reshape(own_rows, dim)

    logit_low = jnp.zeros((EXTRA, dim), BF16).at[:2].set(logit_w.astype(BF16)[None])
    mixing_parts = mixing_own.reshape(n_g, n_c, PARTS, sub, local_experts)
    mixing_parts = jnp.pad(mixing_parts, ((0, 0),) * 4 + ((0, 8 - local_experts),))
    passes = [
        ffn_pass(
            sizes,
            meta,
            normed_parts[part],
            cot_all,
            mixing_parts[:, :, part].reshape(-1, 8),
            logit_low,
            weight_blocks,
            part,
        )
        for part in range(PARTS)
    ]

    def scatter_axis(value, axis, at):
        size = lax.axis_size(axis)
        index = lax.axis_index(axis)
        if size == 2:
            other = swap(pick(value, 1 - index, at), axis)
            return (pick(value, index, at).astype(F32) + other.astype(F32)).astype(BF16)
        moved = lax.all_to_all(value, axis, at, at, tiled=True)
        return jnp.sum(moved.astype(F32), axis=at).astype(BF16)

    def scatter_cols(partial):
        part = partial.reshape(n_g, lax.axis_size("y"), 2, sub, dim)
        left, right = part[..., : dim // 2], part[..., dim // 2 :]
        left, right = scatter_axis(left, "x", 2), scatter_axis(right, "y", 1)
        left, right = scatter_axis(left, "y", 1), scatter_axis(right, "x", 1)
        return jnp.concatenate([left, right], axis=-1)

    def scatter_rows(partial):
        part = scatter_cols(partial)
        return jnp.sum(lax.all_to_all(part, "g", 0, 0, tiled=True).astype(F32), axis=0)

    normed_grad_2 = jnp.concatenate([scatter_rows(parts[1]) for parts in passes], axis=0)
    hidden_part, gain_2_sum = norm_back(normed_grad_2, unit_2, second_scale, gain_2)
    hidden_grad = own_cot.astype(F32) + hidden_part
    attn_grad = col_gather(hidden_grad.astype(BF16), n_c).reshape(span, dim)

    def return_slices(grad):
        other = swap(grad[1], "k")
        both = (grad[0].astype(F32) + other.astype(F32)).astype(BF16)
        moved = [shift_chips(both[shift], shift, n_g) for shift in range(n_g)]
        moved = jnp.stack(moved)
        moved = jnp.stack([pick(moved, at_g ^ source) for source in range(n_g)])
        shared = moved[:, :f_shared].reshape(n_g * f_shared, d_own)
        routed = moved[:, f_shared:f_all].reshape(n_g, local_experts, f_routed, d_own)
        routed = routed.transpose(1, 0, 2, 3).reshape(local_experts, n_g * f_routed, d_own)
        return (shared, routed)

    gate_blocks, logit_sum = weight_grad(
        sizes, meta, [parts[3] for parts in passes], normed_parts, False
    )
    (up_blocks,) = weight_grad(sizes, meta, [parts[4] for parts in passes], normed_parts, False)
    (down_blocks,) = weight_grad(
        sizes, meta, [parts[2] for parts in passes], [cot_all] * PARTS, True
    )
    gate_s, gate_e = return_slices(gate_blocks)
    up_s, up_e = return_slices(up_blocks)
    down_s, down_e = return_slices(down_blocks)
    logit_sum = logit_sum[0]

    out_rows = jnp.concatenate([scatter_rows(parts[0]) for parts in passes], axis=0)
    result = rows_to_features((hidden + out_rows).astype(BF16), n_c)

    out_grad = dot(attn_grad, mixed, ((0,), (0,)))
    mixed_grad = dot(attn_grad, out_w, ((1,), (1,))).astype(BF16).reshape(head_shape)
    prob_grad = einsum("bqhd,bkhd->bhqk", mixed_grad, value_low)
    value_grad = einsum("bhqk,bqhd->bkhd", prob_low, mixed_grad).astype(BF16)
    center = jnp.sum(prob_grad * probabilities, axis=-1, keepdims=True)
    score_grad = (probabilities * (prob_grad - center) * (1.0 / math.sqrt(HEAD_DIM))).astype(BF16)
    query_grad = rotate(einsum("bhqk,bkhd->bqhd", score_grad, key_rot), cosine, -sine).astype(BF16)
    key_grad = rotate(einsum("bhqk,bqhd->bkhd", score_grad, query_rot), cosine, -sine).astype(BF16)
    qkv_grad = jnp.concatenate(
        [part.reshape(span, width) for part in (query_grad, key_grad, value_grad)], axis=1
    )
    qkv_sum = dot(normed_1, qkv_grad, ((0,), (0,)))
    normed_grad_1 = col_sum(dot(qkv_grad, qkv, ((1,), (1,))), n_c)
    own_scale = lax.dynamic_slice_in_dim(first_scale, at_c * own_rows, own_rows, 0)
    rows_part, gain_1_sum = norm_back(normed_grad_1, own_inputs * own_scale, own_scale, gain_1)
    token_grad = rows_to_features((hidden_grad + rows_part).astype(BF16), n_c).astype(F32)

    sums = jnp.stack([gain_1_sum, gain_2_sum, logit_sum]).reshape(3, n_row, d_own)
    sums = jnp.broadcast_to(sums.transpose(1, 0, 2)[:, None], (n_row, n_c, 3, d_own))
    sums = lax.all_to_all(sums.reshape(n_row * n_c, 3, d_own), ALL, 0, 0, tiled=True)
    sums = jnp.sum(sums, axis=0)

    out_w_grad = lax.psum_scatter(out_grad.astype(BF16), ROW, scatter_dimension=0, tiled=True)
    qkv_own = lax.psum_scatter(qkv_sum.astype(BF16), ROW, scatter_dimension=0, tiled=True)
    qkv_own = qkv_own.astype(F32)
    return (
        result,
        token_grad,
        sums[0],
        qkv_own[:, :width],
        qkv_own[:, width : 2 * width],
        qkv_own[:, 2 * width :],
        out_w_grad.T.astype(F32),
        sums[1],
        gate_s.T.astype(F32),
        up_s.T.astype(F32),
        down_s.astype(F32),
        sums[2],
        gate_e.transpose(2, 0, 1).astype(F32),
        up_e.transpose(2, 0, 1).astype(F32),
        down_e.astype(F32),
    )


def solution(mesh):
    n_row, n_col = mesh.shape["row"], mesh.shape["col"]
    inner = Mesh(mesh.devices.reshape(n_row // 2, 2, n_col // 2, 2), ALL)
    return jax.shard_map(
        shards,
        mesh=inner,
        in_specs=(
            P(None, ROW, COL),
            P(None, ROW, None),
            P(None, ROW, None),
            P(None, ROW),
            P(ROW),
            P(ROW, COL),
            P(ROW, COL),
            P(ROW, COL),
            P(COL, ROW),
            P(ROW),
            P(ROW, COL),
            P(ROW, COL),
            P(COL, ROW),
            P(ROW),
            P(ROW, COL, None),
            P(ROW, COL, None),
            P(COL, None, ROW),
            P(None, ROW, COL),
        ),
        out_specs=(
            P(None, ROW, COL),
            P(None, ROW, COL),
            P(ROW),
            P(ROW, COL),
            P(ROW, COL),
            P(ROW, COL),
            P(COL, ROW),
            P(ROW),
            P(ROW, COL),
            P(ROW, COL),
            P(COL, ROW),
            P(ROW),
            P(ROW, COL, None),
            P(ROW, COL, None),
            P(COL, None, ROW),
        ),
        check_vma=False,
    )
```

time: 1820 us -> 1090 us (0.60)
  waiting for transfers between devices: 1200 us -> 501 us
  matrix products: 321 us -> 47.8 us
  starting transfers between devices: 2.65 us -> 159 us
  Pallas kernels: 0 us -> 138 us
  blocking collectives: 73.4 us -> 24.6 us
  other arithmetic: 93.3 us -> 75.1 us
    reduce_scatter x12 -> x2, waiting for transfers between devices: 551 us -> 0.01 us  [the longest x1 0.01 us: shards(): lax.psum_scatter(out_grad.astype(BF16), ROW, scatter_dimension=0, tiled=T...]
    all_gather x12 -> x5, waiting for transfers between devices: 530 us -> 58.1 us  [the longest x1 25.7 us: shards(): lax.all_gather(jnp.concatenate([query_weight, key_weight, value_weight],...]
    ppermute x0 -> x35, waiting for transfers between devices: none -> 352 us  [the longest x12 287 us: shift_chips(): return lax.ppermute(value, 'g', [(i, i ^ shift) for i in range(n_g)])]
    dot_general x76 -> x11, matrix products: 321 us -> 45.3 us  [the longest x6 32 us: dot(): lax.dot_general(left, right, (dims, ((), ())), preferred_element_type=F32)]
    pallas_call x0 -> x5, Pallas kernels: none -> 138 us  [the longest x2 97.6 us: ffn_pass(): pl.pallas_call(functools.partial(ffn_kernel, sizes), grid_spec=pltpu.Pref...]
    psum x3 -> x0, waiting for transfers between devices: 110 us -> none  [the longest x1 70.4 us: backward_pass(): lax.psum(first_part.astype(jnp.bfloat16), 'col').astype(jnp.float32)]
    ppermute x0 -> x35, starting transfers between devices: none -> 99.3 us  [the longest x12 80.8 us: shift_chips(): return lax.ppermute(value, 'g', [(i, i ^ shift) for i in range(n_g)])]
    all_to_all x0 -> x14, waiting for transfers between devices: none -> 89.8 us  [the longest x2 44.6 us: col_sum(): lax.all_to_all(parts, COL, 0, 0, tiled=True).astype(F32)]
  transfers between devices with their start and end apart: 27 -> 56, of which waited for: 23 -> 25; matrix products, arithmetic and copies ran while one was open for 22% -> 19% of each run, Pallas kernels for 0% -> 13%
where the time goes in v1:
time: 1090 us; the launch traced here: 1080 us
  waiting for transfers between devices  501 us (46%)
  starting transfers between devices  159 us (15%)
  Pallas kernels  138 us (13%)
  local copies, waits for them, and re-layouts  115 us (11%)
  other arithmetic  75.1 us (7%)
  matrix products  47.8 us (4%)
  blocking collectives  24.6 us (2%)
  between operations  17.6 us (2%)
    ppermute x12, waiting for transfers between devices, shift_chips(): return lax.ppermute(value, 'g', [(i, i ^ shift) for i in range(n_g)])  287 us
    pallas_call x2, Pallas kernels, ffn_pass(): pl.pallas_call(functools.partial(ffn_kernel, sizes), grid_spec=pltpu.Pref...  97.6 us
    ppermute x12, starting transfers between devices, shift_chips(): return lax.ppermute(value, 'g', [(i, i ^ shift) for i in range(n_g)])  80.8 us
    ppermute x23, waiting for transfers between devices, swap(): return lax.ppermute(value, axis, [(0, 1), (1, 0)])  64.7 us
    all_to_all x2, waiting for transfers between devices, col_sum(): lax.all_to_all(parts, COL, 0, 0, tiled=True).astype(F32)  44.6 us
    unnamed x173, local copies, waits for them, and re-layouts  41.8 us
    pallas_call x3, Pallas kernels, weight_grad(): pl.pallas_call(functools.partial(grad_kernel, parts, f_pad), grid_spec=pl...  40.6 us
    all_to_all x4, waiting for transfers between devices, scatter_rows(): lax.all_to_all(part, 'g', 0, 0, tiled=True).astype(F32)  33.3 us
  transfers between devices with their start and end apart: 56, of which 25 were waited for; matrix products, arithmetic and copies ran while one was open for 19% of the time, Pallas kernels for 13%

profile of v1, /device:TPU:0, one launch (start us, length us, event | category | flops | bytes accessed | tf_op | source)
XLA Modules:
  0.0 1078.4 jit_solution(14529522506021734351)
XLA Ops:
  22.6 15.2 %all-gather = f32[192,256]{1,0:T(8,128)S(1)} all-gather(f32[24,256]{1,0:T(8,128)S(1)} %pad_maximum_fusion.26), channel_id=2, replica_groups=mesh['g'=4,'k'=2,'y'=2,'x'=2] {'g','k'}, dimensions={0}, use_global_device_ids=true | all-gather | bytes 221184 | tf_op jit(solution)/shard_map/all_gather | solution.py:348
  54.3 25.7 %all-gather.7.cloned.1.call-done = bf16[2048,1536]{1,0:T(8,128)(2,1)} async-done(((bf16[256,1536]{1,0:T(8,128)(2,1)}), bf16[2048,1536]{1,0:T(8,128)(2,1)}) %all-gather.7.cloned.1.call-update) | async-done | bytes 6291472 | tf_op jit(solution)/shard_map/all_gather | solution.py:363
  99.0 11.9 %all-gather.9.cloned.1.call-done = bf16[512,2048]{1,0:T(8,128)(2,1)} async-done(((bf16[512,256]{1,0:T(8,128)(2,1)}), bf16[512,2048]{1,0:T(8,128)(2,1)}) %all-gather.9.cloned.1.call-update) | async-done | bytes 2097168 | tf_op jit(solution)/shard_map/all_gather | solution.py:366
  119.5 24.7 %all-to-all-done.2 = bf16[4,128,2048]{2,1,0:T(8,128)(2,1)S(1)} async-done(((bf16[4,128,2048]{2,1,0:T(8,128)(2,1)}), bf16[4,128,2048]{2,1,0:T(8,128)(2,1)S(1)}, u32[]{:S(2)}, u32[]{:S(2)}) %all-to-all-start.2) | async-done | bytes 2097184 | tf_op jit(solution)/shard_map/all_to_all | solution.py:283
  147.2 20.5 %all-gather.13.cloned.1.call-done = bf16[2048,512]{1,0:T(8,128)(2,1)} async-done(((bf16[512,512]{1,0:T(8,128)(2,1)}), bf16[2048,512]{1,0:T(8,128)(2,1)}) %all-gather.13.cloned.1.call-update) | async-done | bytes 2097168 | tf_op jit(solution)/shard_map/all_gather | solution.py:439
  209.0 38.4 %collective-permute-done.2.refs_3_ = bf16[3,1056,256]{2,1,0:T(8,128)(2,1)} collective-permute-done((bf16[3,1056,256]{2,1,0:T(8,128)(2,1)S(1)}, bf16[3,1056,256]{2,1,0:T(8,128)(2,1)}, u32[]{:S(2)}, u32[]{:S(2)}) %collective-permute-start.2) | collective-permute-done | bytes 1622048 | tf_op jit(solution)/shard_map/ppermute | solution.py:273
  247.4 140.5 %collective-permute-done.1.refs_2_ = bf16[3,1056,256]{2,1,0:T(8,128)(2,1)} collective-permute-done((bf16[3,1056,256]{2,1,0:T(8,128)(2,1)S(1)}, bf16[3,1056,256]{2,1,0:T(8,128)(2,1)}, u32[]{:S(2)}, u32[]{:S(2)}) %collective-permute-start.1) | collective-permute-done | bytes 1622048 | tf_op jit(solution)/shard_map/ppermute | solution.py:273
  394.0 48.7 %ffn_pass.3 = (bf16[1024,2048]{1,0:T(8,128)(2,1)}, bf16[1024,2048]{1,0:T(8,128)(2,1)}, bf16[1056,1024]{1,0:T(8,128)(2,1)}, bf16[1072,1024]{1,0:T(8,128)(2,1)}, bf16[1056,1024]{1,0:T(8,128)(2,1)}) custom-call(s32[2]{0:T(128)} %pad_add_fusion.meta, bf16[1024,2048]{1,0:T(8,128)(2,1)} %all-gather.15.cloned.1.call-done.rows_ref.refs_3_, ...), custom_call_target="tpu_custom_call" | custom-call | flops 26575110144 | bytes 36241408 | tf_op jit(solution)/shard_map/ffn_pass/pallas_call | solution.py:154
  458.4 48.9 %ffn_pass.2 = (bf16[1024,2048]{1,0:T(8,128)(2,1)}, bf16[1024,2048]{1,0:T(8,128)(2,1)}, bf16[1056,1024]{1,0:T(8,128)(2,1)}, bf16[1072,1024]{1,0:T(8,128)(2,1)}, bf16[1056,1024]{1,0:T(8,128)(2,1)}) custom-call(s32[2]{0:T(128)} %pad_add_fusion.meta, bf16[1024,2048]{1,0:T(8,128)(2,1)} %all-gather.11.cloned.1.call-done.rows_ref.refs_2_, ...), custom_call_target="tpu_custom_call" | custom-call | flops 26575110144 | bytes 36241408 | tf_op jit(solution)/shard_map/ffn_pass/pallas_call | solution.py:154
  528.5 26.5 %collective-permute-done.22 = bf16[4,64,1024]{2,1,0:T(8,128)(2,1)S(1)} collective-permute-done((bf16[4,64,1024]{2,1,0:T(8,128)(2,1)S(1)}, bf16[4,64,1024]{2,1,0:T(8,128)(2,1)S(1)}, u32[]{:S(2)}, u32[]{:S(2)}) %collective-permute-start.22) | collective-permute-done | bytes 524320 | tf_op jit(solution)/shard_map/ppermute | solution.py:267
  570.9 18.9 %collective-permute-done.14 = bf16[4,64,1024]{2,1,0:T(8,128)(2,1)S(1)} collective-permute-done((bf16[4,64,1024]{2,1,0:T(8,128)(2,1)S(1)}, bf16[4,64,1024]{2,1,0:T(8,128)(2,1)S(1)}, u32[]{:S(2)}, u32[]{:S(2)}) %collective-permute-start.14) | collective-permute-done | bytes 524320 | tf_op jit(solution)/shard_map/ppermute | solution.py:267
  627.5 8.2 collective-permute-done.10
  657.7 18.8 %all-to-all-done.5 = bf16[4,64,2048]{2,1,0:T(8,128)(2,1)} async-done(((bf16[4,64,2048]{2,1,0:T(8,128)(2,1)}), bf16[4,64,2048]{2,1,0:T(8,128)(2,1)}, u32[]{:S(2)}, u32[]{:S(2)}) %all-to-all-start.5) | async-done | bytes 1048608 | tf_op jit(solution)/shard_map/all_to_all | solution.py:479
  688.3 13.6 %weight_grad.5 = bf16[2,4,1056,256]{3,2,1,0:T(8,128)(2,1)} custom-call(s32[2]{0:T(128)S(1)} %copy-done, bf16[1056,1024]{1,0:T(8,128)(2,1)S(1)} %copy-done.2, bf16[1056,1024]{1,0:T(8,128)(2,1)S(1)} %copy-done.1, bf16[4,4,4,2,64,512]{5,4,3,2,1,0:T(8,128)(2,1)} %bitcast.14.cot_ref.refs_2_.refs_3_, bf16[4,4,4,2,64,512]{5,4,3,2,1,0:T(8,128)(2,1)} %bitcast.14.cot_ref.refs_2_.refs_3_), custom_call_target="tpu_custom_call" | custom-call | flops 8858370048 | bytes 17039360 | tf_op jit(solution)/shard_map/weight_grad/pallas_call | solution.py:237
  705.2 13.4 %weight_grad.4 = bf16[2,4,1056,256]{3,2,1,0:T(8,128)(2,1)} custom-call(s32[2]{0:T(128)S(1)} %copy-done, bf16[1056,1024]{1,0:T(8,128)(2,1)S(1)} %copy-done.4, bf16[1056,1024]{1,0:T(8,128)(2,1)S(1)} %copy-done.3, bf16[1024,2048]{1,0:T(8,128)(2,1)} %all-gather.11.cloned.1.call-done.rows_ref.refs_2_, ...), custom_call_target="tpu_custom_call" | custom-call | flops 8858370048 | bytes 17039360 | tf_op jit(solution)/shard_map/weight_grad/pallas_call | solution.py:237
  757.7 13.6 %weight_grad.3 = (bf16[2,4,1056,256]{3,2,1,0:T(8,128)(2,1)}, f32[8,2048]{1,0:T(8,128)S(1)}) custom-call(s32[2]{0:T(128)S(1)} %copy-done, bf16[1072,1024]{1,0:T(8,128)(2,1)S(1)} %copy-done.6, bf16[1072,1024]{1,0:T(8,128)(2,1)S(1)} %copy-done.5, bf16[1024,2048]{1,0:T(8,128)(2,1)} %all-gather.11.cloned.1.call-done.rows_ref.refs_2_, ...), custom_call_target="tpu_custom_call" | custom-call | flops 8992587776 | bytes 17104896 | tf_op jit(solution)/shard_map/weight_grad/pallas_call | solution.py:237
  785.5 19.3 %collective-permute-done.34 = bf16[1056,256]{1,0:T(8,128)(2,1)S(1)} collective-permute-done((bf16[1056,256]{1,0:T(8,128)(2,1)S(1)}, bf16[1056,256]{1,0:T(8,128)(2,1)S(1)}, u32[]{:S(2)}, u32[]{:S(2)}) %collective-permute-start.34) | collective-permute-done | bytes 540704 | tf_op jit(solution)/shard_map/ppermute | solution.py:273
  804.8 29.6 %collective-permute-start.28 = (bf16[1056,256]{1,0:T(8,128)(2,1)S(1)}, bf16[1056,256]{1,0:T(8,128)(2,1)S(1)}, u32[]{:S(2)}, u32[]{:S(2)}) collective-permute-start(bf16[1056,256]{1,0:T(8,128)(2,1)S(1)} %get-tuple-element.247), channel_id=1, source_target_pairs={{0,8},{8,0},{16,24},{24,16},{1,9},{9,1},{17,25},{25,17},{2,10},{10... | collective-permute-start | bytes 1622024 | tf_op jit(solution)/shard_map/ppermute | solution.py:273
  834.4 49.8 %collective-permute-done.33 = bf16[1056,256]{1,0:T(8,128)(2,1)S(1)} collective-permute-done((bf16[1056,256]{1,0:T(8,128)(2,1)S(1)}, bf16[1056,256]{1,0:T(8,128)(2,1)S(1)}, u32[]{:S(2)}, u32[]{:S(2)}) %collective-permute-start.33) | collective-permute-done | bytes 540704 | tf_op jit(solution)/shard_map/ppermute | solution.py:273
  886.1 39.2 %collective-permute-start.24 = (bf16[1056,256]{1,0:T(8,128)(2,1)S(1)}, bf16[1056,256]{1,0:T(8,128)(2,1)S(1)}, u32[]{:S(2)}, u32[]{:S(2)}) collective-permute-start(bf16[1056,256]{1,0:T(8,128)(2,1)S(1)} %get-tuple-element.255), channel_id=1, source_target_pairs={{0,8},{8,0},{16,24},{24,16},{1,9},{9,1},{17,25},{25,17},{2,10},{10... | collective-permute-start | bytes 1622024 | tf_op jit(solution)/shard_map/ppermute | solution.py:273
  925.3 16.8 %collective-permute-done.29 = bf16[1056,256]{1,0:T(8,128)(2,1)S(1)} collective-permute-done((bf16[1056,256]{1,0:T(8,128)(2,1)S(1)}, bf16[1056,256]{1,0:T(8,128)(2,1)S(1)}, u32[]{:S(2)}, u32[]{:S(2)}) %collective-permute-start.29) | collective-permute-done | bytes 540704 | tf_op jit(solution)/shard_map/ppermute | solution.py:273
  944.5 22.4 %collective-permute-done.25 = bf16[1056,256]{1,0:T(8,128)(2,1)S(1)} collective-permute-done((bf16[1056,256]{1,0:T(8,128)(2,1)S(1)}, bf16[1056,256]{1,0:T(8,128)(2,1)S(1)}, u32[]{:S(2)}, u32[]{:S(2)}) %collective-permute-start.25) | collective-permute-done | bytes 540704 | tf_op jit(solution)/shard_map/ppermute | solution.py:273
  975.0 8.0 convolution_convert_fusion.2
  993.0 19.9 %all-to-all-done.12 = bf16[4,128,2048]{2,1,0:T(8,128)(2,1)} async-done(((bf16[4,128,2048]{2,1,0:T(8,128)(2,1)}), bf16[4,128,2048]{2,1,0:T(8,128)(2,1)}, u32[]{:S(2)}, u32[]{:S(2)}) %all-to-all-start.12) | async-done | bytes 2097184 | tf_op jit(solution)/shard_map/all_to_all | solution.py:283
  (466 shorter events, 368.4 us)
Async XLA Ops:
  8.0 72.0 %all-gather.7.cloned.1.call-start = ((), (), s32[]{:S(2)}) async-start(), calls=%async_computation.18 | async-start | bytes 7077888 | tf_op jit(solution)/shard_map/all_gather | solution.py:363
  21.2 89.7 %all-gather.9.cloned.1.call-start = ((), (), s32[]{:S(2)}) async-start(), calls=%async_computation.19 | async-start | bytes 2359296 | tf_op jit(solution)/shard_map/all_gather | solution.py:366
  46.4 68.7 %all-to-all-start.3 = ((bf16[2,256,512]{2,1,0:T(8,128)(2,1)}), bf16[2,256,512]{2,1,0:T(8,128)(2,1)}, u32[]{:S(2)}, u32[]{:S(2)}) async-start(bf16[2,256,512]{2,1,0:T(8,128)(2,1)} %param.45), calls=%async_computation.3 | async-start | bytes 1048576 | tf_op jit(solution)/shard_map/all_to_all | solution.py:361
  119.3 274.8 %all-gather.15.cloned.1.call-start = ((), (), s32[]{:S(2)}) async-start(), calls=%async_computation.22 | async-start | bytes 4456448 | tf_op jit(solution)/shard_map/all_gather | solution.py:433
  173.2 220.8 %all-to-all-start.4 = ((bf16[4,2048,512]{2,1,0:T(8,128)(2,1)}), bf16[4,2048,512]{2,1,0:T(8,128)(2,1)}, u32[]{:S(2)}, u32[]{:S(2)}) async-start(bf16[4,2048,512]{2,1,0:T(8,128)(2,1)} %broadcast_in_dim.58), calls=%async_computation.4 | async-start | bytes 16777216 | tf_op jit(solution)/shard_map/all_to_all | solution.py:278
  178.9 279.4 %all-gather.11.cloned.1.call-start = ((), (), s32[]{:S(2)}) async-start(), calls=%async_computation.20 | async-start | bytes 4456448 | tf_op jit(solution)/shard_map/all_gather | solution.py:433
  206.0 181.9 %collective-permute-start.1 = (bf16[3,1056,256]{2,1,0:T(8,128)(2,1)S(1)}, bf16[3,1056,256]{2,1,0:T(8,128)(2,1)}, u32[]{:S(2)}, u32[]{:S(2)}) collective-permute-start(bf16[3,1056,256]{2,1,0:T(8,128)(2,1)S(1)} %get-tuple-element.215), channel_id=1, source_target_pairs={{0,16},{8,24},{16,0},{24,8},{1,17},{9,25},{17,1},{25,9},{2,18},{10... | collective-permute-start | bytes 4866056 | tf_op jit(solution)/shard_map/ppermute | solution.py:273
  206.3 181.6 %collective-permute-start = (bf16[3,1056,256]{2,1,0:T(8,128)(2,1)S(1)}, bf16[3,1056,256]{2,1,0:T(8,128)(2,1)}, u32[]{:S(2)}, u32[]{:S(2)}) collective-permute-start(bf16[3,1056,256]{2,1,0:T(8,128)(2,1)S(1)} %get-tuple-element.216), channel_id=1, source_target_pairs={{0,8},{8,0},{16,24},{24,16},{1,9},{9,1},{17,25},{25,17},{2,10},{10... | collective-permute-start | bytes 4866056 | tf_op jit(solution)/shard_map/ppermute | solution.py:273
  209.0 182.5 %collective-permute-start.3 = (bf16[3,1056,256]{2,1,0:T(8,128)(2,1)S(1)}, bf16[3,1056,256]{2,1,0:T(8,128)(2,1)}, u32[]{:S(2)}, u32[]{:S(2)}) collective-permute-start(bf16[3,1056,256]{2,1,0:T(8,128)(2,1)S(1)} %get-tuple-element.217.refs_0_), channel_id=1, source_target_pairs={{0,4},{4,0},{1,5},{5,1},{2,6},{6,2},{3,7},{7,3},{8,12},{12,8},{9,1... | collective-permute-start | bytes 4866056 | tf_op jit(solution)/shard_map/ppermute | solution.py:267
  247.4 144.1 %collective-permute-start.6 = (bf16[3,1056,256]{2,1,0:T(8,128)(2,1)}, bf16[3,1056,256]{2,1,0:T(8,128)(2,1)}, u32[]{:S(2)}, u32[]{:S(2)}) collective-permute-start(bf16[3,1056,256]{2,1,0:T(8,128)(2,1)} %collective-permute-done.2.refs_3_), channel_id=1, source_target_pairs={{0,4},{4,0},{1,5},{5,1},{2,6},{6,2},{3,7},{7,3},{8,12},{12,8},{9,1... | collective-permute-start | bytes 4866056 | tf_op jit(solution)/shard_map/ppermute | solution.py:267
  455.9 69.5 %collective-permute-start.13 = (bf16[4,2,64,1024]{3,2,1,0:T(8,128)(2,1)}, bf16[4,2,64,1024]{3,2,1,0:T(8,128)(2,1)}, u32[]{:S(2)}, u32[]{:S(2)}) collective-permute-start(bf16[4,2,64,1024]{3,2,1,0:T(8,128)(2,1)} %dynamic-slice_bitcast_fusion.6), channel_id=1, source_target_pairs={{0,2},{2,0},{1,3},{3,1},{4,6},{6,4},{5,7},{7,5},{8,10},{10,8},{9,1... | collective-permute-start | bytes 3145736 | tf_op jit(solution)/shard_map/ppermute | solution.py:267
  456.3 106.3 %collective-permute-start.11 = (bf16[4,2,64,1024]{3,2,0,1:T(8,128)(2,1)}, bf16[4,2,64,1024]{3,2,0,1:T(8,128)(2,1)}, u32[]{:S(2)}, u32[]{:S(2)}) collective-permute-start(bf16[4,2,64,1024]{3,2,0,1:T(8,128)(2,1)} %bitcast.308), channel_id=1, source_target_pairs={{0,1},{1,0},{2,3},{3,2},{4,5},{5,4},{6,7},{7,6},{8,9},{9,8},{10,11... | collective-permute-start | bytes 3145736 | tf_op jit(solution)/shard_map/ppermute | solution.py:267
  519.8 77.4 %collective-permute-start.15 = (bf16[4,2,64,1024]{3,2,0,1:T(8,128)(2,1)}, bf16[4,2,64,1024]{3,2,0,1:T(8,128)(2,1)}, u32[]{:S(2)}, u32[]{:S(2)}) collective-permute-start(bf16[4,2,64,1024]{3,2,0,1:T(8,128)(2,1)} %bitcast.311), channel_id=1, source_target_pairs={{0,1},{1,0},{2,3},{3,2},{4,5},{5,4},{6,7},{7,6},{8,9},{9,8},{10,11... | collective-permute-start | bytes 3145736 | tf_op jit(solution)/shard_map/ppermute | solution.py:267
  555.6 68.4 %collective-permute-start.7 = (bf16[4,2,64,1024]{3,2,0,1:T(8,128)(2,1)}, bf16[4,2,64,1024]{3,2,0,1:T(8,128)(2,1)}, u32[]{:S(2)}, u32[]{:S(2)}) collective-permute-start(bf16[4,2,64,1024]{3,2,0,1:T(8,128)(2,1)} %bitcast.309), channel_id=1, source_target_pairs={{0,1},{1,0},{2,3},{3,2},{4,5},{5,4},{6,7},{7,6},{8,9},{9,8},{10,11... | collective-permute-start | bytes 3145736 | tf_op jit(solution)/shard_map/ppermute | solution.py:267
  686.6 377.8 %reduce-scatter.5.cloned.1.call-start = ((), (), s32[]{:S(2)}) async-start(), calls=%async_computation.24 | async-start | bytes 2359296 | tf_op jit(solution)/shard_map/reduce_scatter | solution.py:534
  705.2 68.3 %collective-permute-start.31 = (bf16[4,1056,256]{2,1,0:T(8,128)(2,1)}, bf16[4,1056,256]{2,1,0:T(8,128)(2,1)}, u32[]{:S(2)}, u32[]{:S(2)}) collective-permute-start(bf16[4,1056,256]{2,1,0:T(8,128)(2,1)} %slice_bitcast_fusion), channel_id=1, source_target_pairs={{0,4},{4,0},{1,5},{5,1},{2,6},{6,2},{3,7},{7,3},{8,12},{12,8},{9,1... | collective-permute-start | bytes 6488072 | tf_op jit(solution)/shard_map/ppermute | solution.py:267
  722.9 343.6 %reduce-scatter.3.cloned.1.call-start = ((), (), s32[]{:S(2)}) async-start(), calls=%async_computation.23 | async-start | bytes 7077888 | tf_op jit(solution)/shard_map/reduce_scatter | solution.py:535
  777.9 106.3 %collective-permute-start.33 = (bf16[1056,256]{1,0:T(8,128)(2,1)S(1)}, bf16[1056,256]{1,0:T(8,128)(2,1)S(1)}, u32[]{:S(2)}, u32[]{:S(2)}) collective-permute-start(bf16[1056,256]{1,0:T(8,128)(2,1)S(1)} %get-tuple-element.238), channel_id=1, source_target_pairs={{0,16},{8,24},{16,0},{24,8},{1,17},{9,25},{17,1},{25,9},{2,18},{10... | collective-permute-start | bytes 1622024 | tf_op jit(solution)/shard_map/ppermute | solution.py:273
  777.9 107.8 %collective-permute-start.32 = (bf16[1056,256]{1,0:T(8,128)(2,1)S(1)}, bf16[1056,256]{1,0:T(8,128)(2,1)S(1)}, u32[]{:S(2)}, u32[]{:S(2)}) collective-permute-start(bf16[1056,256]{1,0:T(8,128)(2,1)S(1)} %get-tuple-element.239), channel_id=1, source_target_pairs={{0,8},{8,0},{16,24},{24,16},{1,9},{9,1},{17,25},{25,17},{2,10},{10... | collective-permute-start | bytes 1622024 | tf_op jit(solution)/shard_map/ppermute | solution.py:273
  783.2 102.9 %collective-permute-start.30 = (bf16[1056,256]{1,0:T(8,128)(2,1)S(1)}, bf16[1056,256]{1,0:T(8,128)(2,1)S(1)}, u32[]{:S(2)}, u32[]{:S(2)}) collective-permute-start(bf16[1056,256]{1,0:T(8,128)(2,1)S(1)} %get-tuple-element.245), channel_id=1, source_target_pairs={{0,24},{8,16},{16,8},{24,0},{1,25},{9,17},{17,9},{25,1},{2,26},{10... | collective-permute-start | bytes 1622024 | tf_op jit(solution)/shard_map/ppermute | solution.py:273
  784.7 157.5 %collective-permute-start.29 = (bf16[1056,256]{1,0:T(8,128)(2,1)S(1)}, bf16[1056,256]{1,0:T(8,128)(2,1)S(1)}, u32[]{:S(2)}, u32[]{:S(2)}) collective-permute-start(bf16[1056,256]{1,0:T(8,128)(2,1)S(1)} %get-tuple-element.246), channel_id=1, source_target_pairs={{0,16},{8,24},{16,0},{24,8},{1,17},{9,25},{17,1},{25,9},{2,18},{10... | collective-permute-start | bytes 1622024 | tf_op jit(solution)/shard_map/ppermute | solution.py:273
  804.8 137.3 %collective-permute-start.28 = (bf16[1056,256]{1,0:T(8,128)(2,1)S(1)}, bf16[1056,256]{1,0:T(8,128)(2,1)S(1)}, u32[]{:S(2)}, u32[]{:S(2)}) collective-permute-start(bf16[1056,256]{1,0:T(8,128)(2,1)S(1)} %get-tuple-element.247), channel_id=1, source_target_pairs={{0,8},{8,0},{16,24},{24,16},{1,9},{9,1},{17,25},{25,17},{2,10},{10... | collective-permute-start | bytes 1622024 | tf_op jit(solution)/shard_map/ppermute | solution.py:273
  885.7 81.2 %collective-permute-start.25 = (bf16[1056,256]{1,0:T(8,128)(2,1)S(1)}, bf16[1056,256]{1,0:T(8,128)(2,1)S(1)}, u32[]{:S(2)}, u32[]{:S(2)}) collective-permute-start(bf16[1056,256]{1,0:T(8,128)(2,1)S(1)} %get-tuple-element.254), channel_id=1, source_target_pairs={{0,16},{8,24},{16,0},{24,8},{1,17},{9,25},{17,1},{25,9},{2,18},{10... | collective-permute-start | bytes 1622024 | tf_op jit(solution)/shard_map/ppermute | solution.py:273
  886.1 80.7 %collective-permute-start.24 = (bf16[1056,256]{1,0:T(8,128)(2,1)S(1)}, bf16[1056,256]{1,0:T(8,128)(2,1)S(1)}, u32[]{:S(2)}, u32[]{:S(2)}) collective-permute-start(bf16[1056,256]{1,0:T(8,128)(2,1)S(1)} %get-tuple-element.255), channel_id=1, source_target_pairs={{0,8},{8,0},{16,24},{24,16},{1,9},{9,1},{17,25},{25,17},{2,10},{10... | collective-permute-start | bytes 1622024 | tf_op jit(solution)/shard_map/ppermute | solution.py:273
  (111 other events, 1994.2 us)
Sparse Core Ops, SparseCore 0:
  11.0 68.8 all-gather.6
  81.6 29.2 all-gather.8
  723.0 35.7 reduce-scatter.4
  760.9 132.0 reduce-scatter.2
Sparse Core Ops, SparseCore 1:
  120.8 46.8 all-gather.12
  170.8 184.3 all-gather.14
  358.4 83.4 all-gather.10

commit v2 on v1

--- a/solution.py
+++ b/solution.py
@@ -74,9 +74,9 @@
 
 def ffn_kernel(sizes, meta, rows_ref, cot_ref, mix_ref, logit_ref, *refs):
     n_g, f_pad, f_shared, f_routed, local_experts, d_own = sizes
-    blocks = refs[: 2 * n_g]
-    out_ref, normed_ref, act_ref, gate_ref, up_ref = refs[2 * n_g : 2 * n_g + 5]
-    w_gu, w_down, sems = refs[2 * n_g + 5 :]
+    blocks = refs[: 6 * n_g]
+    out_ref, normed_ref, act_ref, gate_ref, up_ref = refs[6 * n_g : 6 * n_g + 5]
+    w_gu, w_down, sems = refs[6 * n_g + 5 :]
     g_at, k_at = meta[0], meta[1]
 
     @pl.when((pl.program_id(0) == 0) & (pl.program_id(1) == 0))
@@ -86,13 +86,13 @@
             for shift in range(n_g):
                 column = 2 * (g_at ^ shift) + (k_at ^ half)
                 lanes = pl.ds(pl.multiple_of(column * d_own, d_own), d_own)
-                source = blocks[half * n_g + shift]
+                first = (half * n_g + shift) * 3
                 for kind, target in enumerate(
                     (w_gu.at[:f_pad, lanes], w_gu.at[f_pad : 2 * f_pad, lanes], w_down.at[:, lanes])
                 ):
                     copies.append(
                         pltpu.make_async_copy(
-                            source.at[kind], target, sems.at[(half * n_g + shift) * 3 + kind]
+                            blocks[first + kind], target, sems.at[first + kind]
                         )
                     )
         for copy in copies:
@@ -104,7 +104,7 @@
     rows = rows_ref[...]
     count = rows.shape[0]
     cot = jnp.concatenate(
-        [cot_ref[c, 0, :, 0].reshape(count, -1) for c in range(cot_ref.shape[0])], axis=1
+        [cot_ref[c, 0].reshape(count, -1) for c in range(cot_ref.shape[0])], axis=1
     )
     minor = ((1,), (1,))
     pre = dot(w_gu[...], rows, minor)
@@ -141,10 +141,10 @@
     normed_ref[...] = dot(both, w_gu[...], major).astype(BF16)
 
 
-def ffn_pass(sizes, meta, rows, cot, mix, logit, blocks, part):
+def ffn_pass(sizes, meta, rows, cot, mix, logit, blocks):
     n_g, f_pad, _, _, local_experts, d_own = sizes
     total, dim = rows.shape
-    n_c, _, _, parts, sub, cw = cot.shape
+    n_c, _, _, sub, cw = cot.shape
     take = min(TILE // sub, n_c)
     tile = take * sub
     steps = n_c // take
@@ -158,11 +158,11 @@
             grid=(n_g, steps),
             in_specs=[
                 pl.BlockSpec((tile, dim), flat),
-                pl.BlockSpec((n_c, 1, take, 1, sub, cw), lambda i, j, m: (0, i, j, part, 0, 0)),
+                pl.BlockSpec((n_c, 1, take, sub, cw), lambda i, j, m: (0, i, j, 0, 0)),
                 pl.BlockSpec((1, 8, tile), lambda i, j, m: (i * steps + j, 0, 0)),
                 pl.BlockSpec((EXTRA, dim), lambda i, j, m: (0, 0)),
             ]
-            + [any_spec] * (2 * n_g),
+            + [any_spec] * (6 * n_g),
             out_specs=[
                 pl.BlockSpec((tile, dim), flat),
                 pl.BlockSpec((tile, dim), flat),
@@ -214,15 +214,13 @@
     f_rows, part_rows = lefts[0].shape
     dim = 2 * n_g * d_own
     if cot:
-        n_c, _, _, _, sub, cw = rights[0].shape
+        n_c, _, _, sub, cw = rights[0].shape
         per = cw // d_own
         right_specs = [
             pl.BlockSpec(
-                (1, n_g, n_c, 1, sub, d_own),
-                functools.partial(lambda part, j, m: (j // per, 0, 0, part, 0, j % per), part),
+                (1, n_g, n_c, sub, d_own), lambda j, m: (j // per, 0, 0, 0, j % per)
             )
-            for part in range(parts)
-        ]
+        ] * parts
     else:
         right_specs = [pl.BlockSpec((part_rows, d_own), lambda j, m: (0, j))] * parts
     out_specs = [
@@ -253,6 +251,10 @@
         ),
         name="weight_grad",
     )(meta, *lefts, *rights)
+
+
+def tie(*values):
+    return lax.optimization_barrier(values)
 
 
 def norm_back(normed_grad, unit_rows, scale, gain):
@@ -357,16 +359,6 @@
     )
     mixing_own = mixing_own.transpose(0, 2, 1).reshape(total, local_experts)
 
-    token_part = lax.all_to_all(tokens, "k", 0, 0, tiled=True).reshape(span, -1)
-    cot_part = lax.all_to_all(cotangent, "k", 0, 0, tiled=True).reshape(span, -1)
-
-    qkv = lax.all_gather(
-        jnp.concatenate([query_weight, key_weight, value_weight], axis=1), ROW, axis=0, tiled=True
-    )
-    out_w = lax.all_gather(output_weight, ROW, axis=1, tiled=True)
-    inputs = col_gather(token_part, n_c).reshape(n_c, span, -1).transpose(1, 0, 2)
-    inputs = inputs.reshape(span, dim).astype(F32)
-
     f_shared = shared_gate.shape[1] // n_g
     f_routed = expert_gate.shape[2] // n_g
     f_all = f_shared + local_experts * f_routed
@@ -385,19 +377,28 @@
             parts.append(jnp.zeros((n_g, f_pad - f_all, d_own), BF16))
         return jnp.concatenate(parts, axis=1)
 
-    weight_slices = jnp.stack(
-        [
-            slices(shared_gate.T, expert_gate.transpose(1, 2, 0)),
-            slices(shared_up.T, expert_up.transpose(1, 2, 0)),
-            slices(shared_down, expert_down),
-        ],
-        axis=1,
-    )
+    weight_slices = [
+        slices(shared_gate.T, expert_gate.transpose(1, 2, 0)),
+        slices(shared_up.T, expert_up.transpose(1, 2, 0)),
+        slices(shared_down, expert_down),
+    ]
+    picked = [[pick(value, at_g ^ shift) for shift in range(n_g)] for value in weight_slices]
+    picked[0], tokens = tie(picked[0], tokens)
     own_blocks = [
-        shift_chips(pick(weight_slices, at_g ^ shift), shift, n_g) for shift in range(n_g)
-    ]
-    weight_blocks = own_blocks + [swap(value, "k") for value in own_blocks]
-
+        [shift_chips(value, shift, n_g) for shift, value in enumerate(values)] for values in picked
+    ]
+
+    token_part = lax.all_to_all(tokens, "k", 0, 0, tiled=True).reshape(span, -1)
+    cot_part = lax.all_to_all(cotangent, "k", 0, 0, tiled=True).reshape(span, -1)
+
+    qkv = lax.all_gather(
+        jnp.concatenate([query_weight, key_weight, value_weight], axis=1), ROW, axis=0, tiled=True
+    )
+    out_w = lax.all_gather(output_weight, ROW, axis=1, tiled=True)
+    inputs = col_gather(token_part, n_c).reshape(n_c, span, -1).transpose(1, 0, 2)
+    inputs = inputs.reshape(span, dim).astype(F32)
+
+    own_blocks[0], inputs = tie(own_blocks[0], inputs)
     first_scale = lax.rsqrt(jnp.mean(inputs * inputs, axis=-1, keepdims=True) + epsilon)
     normed_1 = (inputs * first_scale * gain_1).astype(BF16)
     projected = dot(normed_1, qkv, ((1,), (0,)))
@@ -424,6 +425,7 @@
     attention = col_sum(dot(mixed, out_w, ((1,), (0,))), n_c)
 
     own_inputs = lax.dynamic_slice_in_dim(inputs, at_c * own_rows, own_rows, 0)
+    own_blocks[1], attention = tie(own_blocks[1], attention)
     hidden = own_inputs + attention
     second_scale = lax.rsqrt(jnp.mean(hidden * hidden, axis=-1, keepdims=True) + epsilon)
     unit_2 = hidden * second_scale
@@ -437,23 +439,35 @@
     ]
 
     cot_rows = lax.all_gather(cot_part, "g", axis=0, tiled=True)
-    cot_all = col_gather(cot_rows, n_c).reshape(n_c, n_g, n_c, PARTS, sub, dim // n_c)
-    own_cot = pick(pick(cot_all, at_g, 1), at_c, 1).reshape(n_c, own_rows, -1)
-    own_cot = own_cot.transpose(1, 0, 2).reshape(own_rows, dim)
+    cot_rows = cot_rows.reshape(n_g, n_c, PARTS, sub, dim // n_c)
+    cot_all = [
+        col_gather(cot_rows[:, :, part], n_c).reshape(n_c, n_g, n_c, sub, dim // n_c)
+        for part in range(PARTS)
+    ]
+    own_cot = [
+        pick(pick(cot, at_g, 1), at_c, 1).transpose(1, 0, 2).reshape(sub, dim) for cot in cot_all
+    ]
+    own_cot = jnp.concatenate(own_cot, axis=0)
 
     logit_low = jnp.zeros((EXTRA, dim), BF16).at[:2].set(logit_w.astype(BF16)[None])
     mixing_parts = mixing_own.reshape(n_g, n_c, PARTS, sub, local_experts)
     mixing_parts = jnp.pad(mixing_parts, ((0, 0),) * 4 + ((0, 8 - local_experts),))
+    swapped = [[swap(value, "k") for value in values] for values in own_blocks]
+    weight_blocks = [
+        values[shift]
+        for half in (own_blocks, swapped)
+        for shift in range(n_g)
+        for values in half
+    ]
     passes = [
         ffn_pass(
             sizes,
             meta,
             normed_parts[part],
-            cot_all,
+            cot_all[part],
             mixing_parts[:, :, part].reshape(-1, 8),
             logit_low,
             weight_blocks,
-            part,
         )
         for part in range(PARTS)
     ]
@@ -474,19 +488,17 @@
         left, right = scatter_axis(left, "y", 1), scatter_axis(right, "x", 1)
         return jnp.concatenate([left, right], axis=-1)
 
-    def scatter_rows(partial):
-        part = scatter_cols(partial)
+    def scatter_chips(part):
         return jnp.sum(lax.all_to_all(part, "g", 0, 0, tiled=True).astype(F32), axis=0)
 
-    normed_grad_2 = jnp.concatenate([scatter_rows(parts[1]) for parts in passes], axis=0)
-    hidden_part, gain_2_sum = norm_back(normed_grad_2, unit_2, second_scale, gain_2)
-    hidden_grad = own_cot.astype(F32) + hidden_part
-    attn_grad = col_gather(hidden_grad.astype(BF16), n_c).reshape(span, dim)
-
-    def return_slices(grad):
+    def own_core(grad):
         other = swap(grad[1], "k")
-        both = (grad[0].astype(F32) + other.astype(F32)).astype(BF16)
-        moved = [shift_chips(both[shift], shift, n_g) for shift in range(n_g)]
+        return (grad[0].astype(F32) + other.astype(F32)).astype(BF16)
+
+    def send_slices(both):
+        return [shift_chips(both[shift], shift, n_g) for shift in range(n_g)]
+
+    def place_slices(moved):
         moved = jnp.stack(moved)
         moved = jnp.stack([pick(moved, at_g ^ source) for source in range(n_g)])
         shared = moved[:, :f_shared].reshape(n_g * f_shared, d_own)
@@ -494,20 +506,29 @@
         routed = routed.transpose(1, 0, 2, 3).reshape(local_experts, n_g * f_routed, d_own)
         return (shared, routed)
 
+    (down_blocks,) = weight_grad(sizes, meta, [parts[2] for parts in passes], cot_all, True)
     gate_blocks, logit_sum = weight_grad(
         sizes, meta, [parts[3] for parts in passes], normed_parts, False
     )
     (up_blocks,) = weight_grad(sizes, meta, [parts[4] for parts in passes], normed_parts, False)
-    (down_blocks,) = weight_grad(
-        sizes, meta, [parts[2] for parts in passes], [cot_all] * PARTS, True
-    )
-    gate_s, gate_e = return_slices(gate_blocks)
-    up_s, up_e = return_slices(up_blocks)
-    down_s, down_e = return_slices(down_blocks)
     logit_sum = logit_sum[0]
-
-    out_rows = jnp.concatenate([scatter_rows(parts[0]) for parts in passes], axis=0)
-    result = rows_to_features((hidden + out_rows).astype(BF16), n_c)
+    down_both = own_core(down_blocks)
+
+    normed_cols = [scatter_cols(parts[1]) for parts in passes]
+    normed_cols[1], down_both, gate_blocks = tie(normed_cols[1], down_both, gate_blocks)
+    normed_grad_2 = jnp.concatenate([scatter_chips(part) for part in normed_cols], axis=0)
+    down_moved = send_slices(down_both)
+    gate_both, up_both = own_core(gate_blocks), own_core(up_blocks)
+    normed_grad_2, down_moved, gate_both, up_both = tie(
+        normed_grad_2, down_moved, gate_both, up_both
+    )
+    hidden_part, gain_2_sum = norm_back(normed_grad_2, unit_2, second_scale, gain_2)
+    hidden_grad = own_cot.astype(F32) + hidden_part
+    gate_moved = send_slices(gate_both)
+    up_moved = send_slices(up_both)
+    attn_grad = col_gather(hidden_grad.astype(BF16), n_c).reshape(span, dim)
+    out_parts, attn_grad = tie([parts[0] for parts in passes], attn_grad)
+    down_s, down_e = place_slices(down_moved)
 
     out_grad = dot(attn_grad, mixed, ((0,), (0,)))
     mixed_grad = dot(attn_grad, out_w, ((1,), (1,))).astype(BF16).reshape(head_shape)
@@ -520,11 +541,18 @@
     qkv_grad = jnp.concatenate(
         [part.reshape(span, width) for part in (query_grad, key_grad, value_grad)], axis=1
     )
+    qkv_grad, gate_moved = tie(qkv_grad, gate_moved)
+    gate_s, gate_e = place_slices(gate_moved)
     qkv_sum = dot(normed_1, qkv_grad, ((0,), (0,)))
     normed_grad_1 = col_sum(dot(qkv_grad, qkv, ((1,), (1,))), n_c)
+    normed_grad_1, up_moved = tie(normed_grad_1, up_moved)
+    up_s, up_e = place_slices(up_moved)
     own_scale = lax.dynamic_slice_in_dim(first_scale, at_c * own_rows, own_rows, 0)
     rows_part, gain_1_sum = norm_back(normed_grad_1, own_inputs * own_scale, own_scale, gain_1)
     token_grad = rows_to_features((hidden_grad + rows_part).astype(BF16), n_c).astype(F32)
+
+    out_rows = jnp.concatenate([scatter_chips(scatter_cols(part)) for part in out_parts], axis=0)
+    result = rows_to_features((hidden + out_rows).astype(BF16), n_c)
 
     sums = jnp.stack([gain_1_sum, gain_2_sum, logit_sum]).reshape(3, n_row, d_own)
     sums = jnp.broadcast_to(sums.transpose(1, 0, 2)[:, None], (n_row, n_c, 3, d_own))

time: 1090 us -> 1070 us (0.982)
  blocking collectives: 24.6 us -> 105 us
  waiting for transfers between devices: 501 us -> 432 us
  starting transfers between devices: 159 us -> 105 us
  local copies, waits for them, and re-layouts: 115 us -> 127 us
    ppermute x12 -> x18, waiting for transfers between devices: 287 us -> 177 us  [shift_chips(): return lax.ppermute(value, 'g', [(i, i ^ shift) for i in range(n_g)])]
    all_gather x2, waiting for transfers between devices: 0.01 us -> 90.3 us  [shards(): lax.all_gather(normed_own[part * sub:(part + 1) * sub], ('g',) + COL, axi...]
    all_gather x1, blocking collectives: 15.2 us -> 94.8 us  [shards(): small_all = lax.all_gather(small, ROW, axis=0, tiled=False)]
    ppermute x12 -> x18, starting transfers between devices: 80.8 us -> 26.4 us  [shift_chips(): return lax.ppermute(value, 'g', [(i, i ^ shift) for i in range(n_g)])]
    all_to_all x2, waiting for transfers between devices: 44.6 us -> 11.5 us  [col_sum(): lax.all_to_all(parts, COL, 0, 0, tiled=True).astype(F32)]
    all_to_all x5, waiting for transfers between devices: 33.3 us -> 64.3 us  [the longest x4 64.3 us: scatter_chips(): lax.all_to_all(part, 'g', 0, 0, tiled=True).astype(F32)]
    all_gather x1, waiting for transfers between devices: 25.7 us -> 0.01 us  [shards(): lax.all_gather(jnp.concatenate([query_weight, key_weight, value_weight],...]
    all_gather x1, waiting for transfers between devices: 20.5 us -> 0.02 us  [shards(): cot_rows = lax.all_gather(cot_part, 'g', axis=0, tiled=True)]
  transfers between devices with their start and end apart: 56 -> 71, of which waited for: 25 -> 28; matrix products, arithmetic and copies ran while one was open for 19% -> 22% of each run, Pallas kernels for 13% -> 13%
where the time goes in v2:
time: 1070 us; the launch traced here: 1060 us
  waiting for transfers between devices  432 us (40%)
  Pallas kernels  137 us (13%)
  local copies, waits for them, and re-layouts  127 us (12%)
  starting transfers between devices  105 us (10%)
  blocking collectives  105 us (10%)
  other arithmetic  81.8 us (8%)
  matrix products  54.9 us (5%)
  between operations  17.7 us (2%)
    ppermute x18, waiting for transfers between devices, shift_chips(): return lax.ppermute(value, 'g', [(i, i ^ shift) for i in range(n_g)])  177 us
    pallas_call x2, Pallas kernels, ffn_pass(): pl.pallas_call(functools.partial(ffn_kernel, sizes), grid_spec=pltpu.Pref...  96.6 us
    all_gather x1, blocking collectives, shards(): small_all = lax.all_gather(small, ROW, axis=0, tiled=False)  94.8 us
    all_gather x2, waiting for transfers between devices, shards(): lax.all_gather(normed_own[part * sub:(part + 1) * sub], ('g',) + COL, axi...  90.3 us
    all_to_all x4, waiting for transfers between devices, scatter_chips(): lax.all_to_all(part, 'g', 0, 0, tiled=True).astype(F32)  64.3 us
    ppermute x31, waiting for transfers between devices, swap(): return lax.ppermute(value, axis, [(0, 1), (1, 0)])  50.9 us
    unnamed x185, local copies, waits for them, and re-layouts  44 us
    pallas_call x3, Pallas kernels, weight_grad(): pl.pallas_call(functools.partial(grad_kernel, parts, f_pad), grid_spec=pl...  40.4 us
  transfers between devices with their start and end apart: 71, of which 28 were waited for; matrix products, arithmetic and copies ran while one was open for 22% of the time, Pallas kernels for 13%

profile of v2, /device:TPU:0, one launch (start us, length us, event | category | flops | bytes accessed | tf_op | source)
XLA Modules:
  0.0 1060.5 jit_solution(18011344285291996286)
XLA Ops:
  34.3 94.8 %all-gather = f32[192,256]{1,0:T(8,128)S(1)} all-gather(f32[24,256]{1,0:T(8,128)S(1)} %pad_maximum_fusion.26), channel_id=2, replica_groups=mesh['g'=4,'k'=2,'y'=2,'x'=2] {'g','k'}, dimensions={0}, use_global_device_ids=true | all-gather | bytes 221184 | tf_op jit(solution)/shard_map/all_gather | solution.py:350
  180.2 11.5 %all-to-all-done.2 = bf16[4,128,2048]{2,1,0:T(8,128)(2,1)S(1)} async-done(((bf16[4,128,2048]{2,1,0:T(8,128)(2,1)}), bf16[4,128,2048]{2,1,0:T(8,128)(2,1)S(1)}, u32[]{:S(2)}, u32[]{:S(2)}) %all-to-all-start.2) | async-done | bytes 2097184 | tf_op jit(solution)/shard_map/all_to_all | solution.py:285
  192.1 12.2 %collective-permute-done.5.refs_10_ = bf16[1056,256]{1,0:T(8,128)(2,1)S(1)} collective-permute-done((bf16[1056,256]{1,0:T(8,128)(2,1)}, bf16[1056,256]{1,0:T(8,128)(2,1)S(1)}, u32[]{:S(2)}, u32[]{:S(2)}) %collective-permute-start.5) | collective-permute-done | bytes 540704 | tf_op jit(solution)/shard_map/ppermute | solution.py:275
  204.3 24.7 %collective-permute-done.3.refs_4_ = bf16[1056,256]{1,0:T(8,128)(2,1)} collective-permute-done((bf16[1056,256]{1,0:T(8,128)(2,1)}, bf16[1056,256]{1,0:T(8,128)(2,1)}, u32[]{:S(2)}, u32[]{:S(2)}) %collective-permute-start.3) | collective-permute-done | bytes 540704 | tf_op jit(solution)/shard_map/ppermute | solution.py:275
  229.0 30.1 %collective-permute-done.4.refs_7_ = bf16[1056,256]{1,0:T(8,128)(2,1)} collective-permute-done((bf16[1056,256]{1,0:T(8,128)(2,1)}, bf16[1056,256]{1,0:T(8,128)(2,1)}, u32[]{:S(2)}, u32[]{:S(2)}) %collective-permute-start.4) | collective-permute-done | bytes 540704 | tf_op jit(solution)/shard_map/ppermute | solution.py:275
  277.4 13.5 %collective-permute-done.8.refs_11_ = bf16[1056,256]{1,0:T(8,128)(2,1)S(1)} collective-permute-done((bf16[1056,256]{1,0:T(8,128)(2,1)S(1)}, bf16[1056,256]{1,0:T(8,128)(2,1)S(1)}, u32[]{:S(2)}, u32[]{:S(2)}) %collective-permute-start.8) | collective-permute-done | bytes 540704 | tf_op jit(solution)/shard_map/ppermute | solution.py:275
  290.9 12.9 %collective-permute-done.6.refs_5_ = bf16[1056,256]{1,0:T(8,128)(2,1)} collective-permute-done((bf16[1056,256]{1,0:T(8,128)(2,1)S(1)}, bf16[1056,256]{1,0:T(8,128)(2,1)}, u32[]{:S(2)}, u32[]{:S(2)}) %collective-permute-start.6) | collective-permute-done | bytes 540704 | tf_op jit(solution)/shard_map/ppermute | solution.py:275
  303.8 27.2 %collective-permute-done.7.refs_8_ = bf16[1056,256]{1,0:T(8,128)(2,1)} collective-permute-done((bf16[1056,256]{1,0:T(8,128)(2,1)S(1)}, bf16[1056,256]{1,0:T(8,128)(2,1)}, u32[]{:S(2)}, u32[]{:S(2)}) %collective-permute-start.7) | collective-permute-done | bytes 540704 | tf_op jit(solution)/shard_map/ppermute | solution.py:275
  346.3 57.9 %all-gather.11.cloned.1.call-done.rows_ref.refs_2_ = bf16[1024,2048]{1,0:T(8,128)(2,1)} async-done(((bf16[64,2048]{1,0:T(8,128)(2,1)}), bf16[1024,2048]{1,0:T(8,128)(2,1)}) %all-gather.11.cloned.1.call-update) | async-done | bytes 4194320 | tf_op jit(solution)/shard_map/all_gather | solution.py:435
  404.2 48.1 %ffn_pass.2 = (bf16[1024,2048]{1,0:T(8,128)(2,1)}, bf16[1024,2048]{1,0:T(8,128)(2,1)}, bf16[1056,1024]{1,0:T(8,128)(2,1)}, bf16[1072,1024]{1,0:T(8,128)(2,1)}, bf16[1056,1024]{1,0:T(8,128)(2,1)}) custom-call(s32[2]{0:T(128)} %pad_add_fusion.meta, bf16[1024,2048]{1,0:T(8,128)(2,1)} %all-gather.11.cloned.1.call-done.rows_ref.refs_2_, ...), custom_call_target="tpu_custom_call" | custom-call | flops 26575110144 | bytes 36241408 | tf_op jit(solution)/shard_map/ffn_pass/pallas_call | solution.py:154
  459.9 32.5 %all-gather.15.cloned.1.call-done.rows_ref.refs_3_ = bf16[1024,2048]{1,0:T(8,128)(2,1)} async-done(((bf16[64,2048]{1,0:T(8,128)(2,1)}), bf16[1024,2048]{1,0:T(8,128)(2,1)}) %all-gather.15.cloned.1.call-update) | async-done | bytes 4194320 | tf_op jit(solution)/shard_map/all_gather | solution.py:435
  492.3 48.5 %ffn_pass.3 = (bf16[1024,2048]{1,0:T(8,128)(2,1)}, bf16[1024,2048]{1,0:T(8,128)(2,1)}, bf16[1056,1024]{1,0:T(8,128)(2,1)}, bf16[1072,1024]{1,0:T(8,128)(2,1)}, bf16[1056,1024]{1,0:T(8,128)(2,1)}) custom-call(s32[2]{0:T(128)} %pad_add_fusion.meta, bf16[1024,2048]{1,0:T(8,128)(2,1)} %all-gather.15.cloned.1.call-done.rows_ref.refs_3_, ...), custom_call_target="tpu_custom_call" | custom-call | flops 26575110144 | bytes 36241408 | tf_op jit(solution)/shard_map/ffn_pass/pallas_call | solution.py:154
  547.9 13.4 %weight_grad.5 = bf16[2,4,1056,256]{3,2,1,0:T(8,128)(2,1)} custom-call(s32[2]{0:T(128)S(1)} %copy-done, bf16[1056,1024]{1,0:T(8,128)(2,1)S(1)} %copy-done.2, bf16[1056,1024]{1,0:T(8,128)(2,1)S(1)} %copy-done.4, bf16[1024,2048]{1,0:T(8,128)(2,1)} %all-gather.11.cloned.1.call-done.rows_ref.refs_2_, ...), custom_call_target="tpu_custom_call" | custom-call | flops 8858370048 | bytes 17039360 | tf_op jit(solution)/shard_map/weight_grad/pallas_call | solution.py:235
  564.5 13.4 %weight_grad.3 = bf16[2,4,1056,256]{3,2,1,0:T(8,128)(2,1)} custom-call(s32[2]{0:T(128)S(1)} %copy-done, bf16[1056,1024]{1,0:T(8,128)(2,1)S(1)} %copy-done.1, bf16[1056,1024]{1,0:T(8,128)(2,1)S(1)} %copy-done.3, bf16[4,4,4,64,512]{4,3,2,1,0:T(8,128)(2,1)} %all-to-all-done.4.cot_ref.refs_2_, bf16[4,4,4,64,512]{4,3,2,1,0:T(8,128)(2,1)} %all-to-all-done.5.cot_ref.refs_3_), custom_call_target="tpu_custom_call" | custom-call | flops 8858370048 | bytes 17039360 | tf_op jit(solution)/shard_map/weight_grad/pallas_call | solution.py:235
  581.2 13.6 %weight_grad.4 = (bf16[2,4,1056,256]{3,2,1,0:T(8,128)(2,1)}, f32[8,2048]{1,0:T(8,128)S(1)}) custom-call(s32[2]{0:T(128)S(1)} %copy-done, bf16[1072,1024]{1,0:T(8,128)(2,1)S(1)} %copy-done.5, bf16[1072,1024]{1,0:T(8,128)(2,1)S(1)} %copy-done.6, bf16[1024,2048]{1,0:T(8,128)(2,1)} %all-gather.11.cloned.1.call-done.rows_ref.refs_2_, ...), custom_call_target="tpu_custom_call" | custom-call | flops 8992587776 | bytes 17104896 | tf_op jit(solution)/shard_map/weight_grad/pallas_call | solution.py:235
  633.2 11.3 %all-to-all-done.6 = bf16[4,64,2048]{2,1,0:T(8,128)(2,1)} async-done(((bf16[4,64,2048]{2,1,0:T(8,128)(2,1)}), bf16[4,64,2048]{2,1,0:T(8,128)(2,1)}, u32[]{:S(2)}, u32[]{:S(2)}) %all-to-all-start.6) | async-done | bytes 1048608 | tf_op jit(solution)/shard_map/all_to_all | solution.py:492
  661.3 37.0 %all-to-all-done.7 = bf16[4,64,2048]{2,1,0:T(8,128)(2,1)} async-done(((bf16[4,64,2048]{2,1,0:T(8,128)(2,1)}), bf16[4,64,2048]{2,1,0:T(8,128)(2,1)}, u32[]{:S(2)}, u32[]{:S(2)}) %all-to-all-start.7) | async-done | bytes 1048608 | tf_op jit(solution)/shard_map/all_to_all | solution.py:492
  705.0 15.5 %collective-permute-done.31 = bf16[1056,256]{1,0:T(8,128)(2,1)} collective-permute-done((bf16[1056,256]{1,0:T(8,128)(2,1)}, bf16[1056,256]{1,0:T(8,128)(2,1)}, u32[]{:S(2)}, u32[]{:S(2)}) %collective-permute-start.31) | collective-permute-done | bytes 540704 | tf_op jit(solution)/shard_map/ppermute | solution.py:275
  728.6 24.3 %all-to-all-done.8 = bf16[4,128,2048]{2,1,0:T(8,128)(2,1)} async-done(((bf16[4,128,2048]{2,1,0:T(8,128)(2,1)}), bf16[4,128,2048]{2,1,0:T(8,128)(2,1)}, u32[]{:S(2)}, u32[]{:S(2)}) %all-to-all-start.8) | async-done | bytes 2097184 | tf_op jit(solution)/shard_map/all_to_all | solution.py:280
  802.9 23.3 %collective-permute-done.44 = bf16[1056,256]{1,0:T(8,128)(2,1)} collective-permute-done((bf16[1056,256]{1,0:T(8,128)(2,1)}, bf16[1056,256]{1,0:T(8,128)(2,1)}, u32[]{:S(2)}, u32[]{:S(2)}) %collective-permute-start.44) | collective-permute-done | bytes 540704 | tf_op jit(solution)/shard_map/ppermute | solution.py:275
  888.6 13.1 %collective-permute-done.41 = bf16[4,2,64,1024]{3,2,1,0:T(8,128)(2,1)} collective-permute-done((bf16[4,2,64,1024]{3,2,1,0:T(8,128)(2,1)}, bf16[4,2,64,1024]{3,2,1,0:T(8,128)(2,1)}, u32[]{:S(2)}, u32[]{:S(2)}) %collective-permute-start.41) | collective-permute-done | bytes 1048608 | tf_op jit(solution)/shard_map/ppermute | solution.py:269
  909.5 13.7 %collective-permute-done.37 = bf16[4,2,64,1024]{3,2,1,0:T(8,128)(2,1)} collective-permute-done((bf16[4,2,64,1024]{3,2,1,0:T(8,128)(2,1)}, bf16[4,2,64,1024]{3,2,1,0:T(8,128)(2,1)}, u32[]{:S(2)}, u32[]{:S(2)}) %collective-permute-start.37) | collective-permute-done | bytes 1048608 | tf_op jit(solution)/shard_map/ppermute | solution.py:269
  947.4 17.7 %collective-permute-done.46 = bf16[1056,256]{1,0:T(8,128)(2,1)} collective-permute-done((bf16[1056,256]{1,0:T(8,128)(2,1)}, bf16[1056,256]{1,0:T(8,128)(2,1)}, u32[]{:S(2)}, u32[]{:S(2)}) %collective-permute-start.46) | collective-permute-done | bytes 540704 | tf_op jit(solution)/shard_map/ppermute | solution.py:275
  980.2 16.0 %all-to-all-done.9 = bf16[4,64,2048]{2,1,0:T(8,128)(2,1)} async-done(((bf16[4,64,2048]{2,1,0:T(8,128)(2,1)}), bf16[4,64,2048]{2,1,0:T(8,128)(2,1)}, u32[]{:S(2)}, u32[]{:S(2)}) %all-to-all-start.9) | async-done | bytes 1048608 | tf_op jit(solution)/shard_map/all_to_all | solution.py:492
  (508 shorter events, 416.5 us)
Async XLA Ops:
  8.0 130.6 %all-gather.7.cloned.1.call-start = ((), (), s32[]{:S(2)}) async-start(), calls=%async_computation.19 | async-start | bytes 7077888 | tf_op jit(solution)/shard_map/all_gather | solution.py:394
  21.6 115.0 %collective-permute-start = (bf16[1056,256]{1,0:T(8,128)(2,1)}, bf16[1056,256]{1,0:T(8,128)(2,1)}, u32[]{:S(2)}, u32[]{:S(2)}) collective-permute-start(bf16[1056,256]{1,0:T(8,128)(2,1)} %get-tuple-element.126), channel_id=1, source_target_pairs={{0,8},{8,0},{16,24},{24,16},{1,9},{9,1},{17,25},{25,17},{2,10},{10... | collective-permute-start | bytes 1622024 | tf_op jit(solution)/shard_map/ppermute | solution.py:275
  24.7 111.9 %collective-permute-start.1 = (bf16[1056,256]{1,0:T(8,128)(2,1)}, bf16[1056,256]{1,0:T(8,128)(2,1)}, u32[]{:S(2)}, u32[]{:S(2)}) collective-permute-start(bf16[1056,256]{1,0:T(8,128)(2,1)} %get-tuple-element.127), channel_id=1, source_target_pairs={{0,16},{8,24},{16,0},{24,8},{1,17},{9,25},{17,1},{25,9},{2,18},{10... | collective-permute-start | bytes 1622024 | tf_op jit(solution)/shard_map/ppermute | solution.py:275
  27.3 109.3 %collective-permute-start.2 = (bf16[1056,256]{1,0:T(8,128)(2,1)}, bf16[1056,256]{1,0:T(8,128)(2,1)}, u32[]{:S(2)}, u32[]{:S(2)}) collective-permute-start(bf16[1056,256]{1,0:T(8,128)(2,1)} %get-tuple-element.128), channel_id=1, source_target_pairs={{0,24},{8,16},{16,8},{24,0},{1,25},{9,17},{17,9},{25,1},{2,26},{10... | collective-permute-start | bytes 1622024 | tf_op jit(solution)/shard_map/ppermute | solution.py:275
  28.8 102.1 %all-to-all-start.1 = ((bf16[4,512,512]{2,1,0:T(8,128)(2,1)}), bf16[4,512,512]{2,1,0:T(8,128)(2,1)S(1)}, u32[]{:S(2)}, u32[]{:S(2)}) async-start(bf16[4,512,512]{2,1,0:T(8,128)(2,1)} %broadcast_in_dim.57), calls=%async_computation.1 | async-start | bytes 4194304 | tf_op jit(solution)/shard_map/all_to_all | solution.py:280
  32.9 125.0 %all-gather.9.cloned.1.call-start = ((), (), s32[]{:S(2)}) async-start(), calls=%async_computation.20 | async-start | bytes 2359296 | tf_op jit(solution)/shard_map/all_gather | solution.py:397
  166.2 96.0 %all-gather.13.cloned.1.call-start = ((), (), s32[]{:S(2)}) async-start(), calls=%async_computation.22 | async-start | bytes 2621440 | tf_op jit(solution)/shard_map/all_gather | solution.py:441
  166.8 237.4 %all-gather.11.cloned.1.call-start = ((), (), s32[]{:S(2)}) async-start(), calls=%async_computation.21 | async-start | bytes 4456448 | tf_op jit(solution)/shard_map/all_gather | solution.py:435
  178.0 81.1 %collective-permute-start.4 = (bf16[1056,256]{1,0:T(8,128)(2,1)}, bf16[1056,256]{1,0:T(8,128)(2,1)}, u32[]{:S(2)}, u32[]{:S(2)}) collective-permute-start(bf16[1056,256]{1,0:T(8,128)(2,1)} %get-tuple-element.339), channel_id=1, source_target_pairs={{0,16},{8,24},{16,0},{24,8},{1,17},{9,25},{17,1},{25,9},{2,18},{10... | collective-permute-start | bytes 1622024 | tf_op jit(solution)/shard_map/ppermute | solution.py:275
  261.6 230.8 %all-gather.15.cloned.1.call-start = ((), (), s32[]{:S(2)}) async-start(), calls=%async_computation.23 | async-start | bytes 4456448 | tf_op jit(solution)/shard_map/all_gather | solution.py:435
  266.4 72.4 %all-to-all-start.4 = ((bf16[4,4,4,64,512]{4,3,2,1,0:T(8,128)(2,1)}), bf16[4,4,4,64,512]{4,3,2,1,0:T(8,128)(2,1)}, u32[]{:S(2)}, u32[]{:S(2)}) async-start(bf16[4,4,4,64,512]{4,3,2,1,0:T(8,128)(2,1)} %broadcast_in_dim.65), calls=%async_computation.4 | async-start | bytes 8388608 | tf_op jit(solution)/shard_map/all_to_all | solution.py:280
  341.4 118.5 %all-to-all-start.5 = ((bf16[4,4,4,64,512]{4,3,2,1,0:T(8,128)(2,1)}), bf16[4,4,4,64,512]{4,3,2,1,0:T(8,128)(2,1)}, u32[]{:S(2)}, u32[]{:S(2)}) async-start(bf16[4,4,4,64,512]{4,3,2,1,0:T(8,128)(2,1)} %broadcast_in_dim.67), calls=%async_computation.5 | async-start | bytes 8388608 | tf_op jit(solution)/shard_map/all_to_all | solution.py:280
  458.8 136.1 %collective-permute-start.23 = (bf16[4,2,64,1024]{3,2,1,0:T(8,128)(2,1)}, bf16[4,2,64,1024]{3,2,1,0:T(8,128)(2,1)}, u32[]{:S(2)}, u32[]{:S(2)}) collective-permute-start(bf16[4,2,64,1024]{3,2,1,0:T(8,128)(2,1)} %dynamic-slice_bitcast_fusion.3), channel_id=1, source_target_pairs={{0,2},{2,0},{1,3},{3,1},{4,6},{6,4},{5,7},{7,5},{8,10},{10,8},{9,1... | collective-permute-start | bytes 3145736 | tf_op jit(solution)/shard_map/ppermute | solution.py:269
  459.9 137.2 %collective-permute-start.21 = (bf16[4,2,64,1024]{3,2,0,1:T(8,128)(2,1)}, bf16[4,2,64,1024]{3,2,0,1:T(8,128)(2,1)}, u32[]{:S(2)}, u32[]{:S(2)}) collective-permute-start(bf16[4,2,64,1024]{3,2,0,1:T(8,128)(2,1)} %bitcast.339), channel_id=1, source_target_pairs={{0,1},{1,0},{2,3},{3,2},{4,5},{5,4},{6,7},{7,6},{8,9},{9,8},{10,11... | collective-permute-start | bytes 3145736 | tf_op jit(solution)/shard_map/ppermute | solution.py:269
  633.2 67.7 %collective-permute-start.33 = (bf16[4,1056,256]{2,1,0:T(8,128)(2,1)}, bf16[4,1056,256]{2,1,0:T(8,128)(2,1)}, u32[]{:S(2)}, u32[]{:S(2)}) collective-permute-start(bf16[4,1056,256]{2,1,0:T(8,128)(2,1)} %slice_bitcast_fusion.4), channel_id=1, source_target_pairs={{0,4},{4,0},{1,5},{5,1},{2,6},{6,2},{3,7},{7,3},{8,12},{12,8},{9,1... | collective-permute-start | bytes 6488072 | tf_op jit(solution)/shard_map/ppermute | solution.py:269
  655.7 64.8 %collective-permute-start.31 = (bf16[1056,256]{1,0:T(8,128)(2,1)}, bf16[1056,256]{1,0:T(8,128)(2,1)}, u32[]{:S(2)}, u32[]{:S(2)}) collective-permute-start(bf16[1056,256]{1,0:T(8,128)(2,1)} %get-tuple-element.325), channel_id=1, source_target_pairs={{0,16},{8,24},{16,0},{24,8},{1,17},{9,25},{17,1},{25,9},{2,18},{10... | collective-permute-start | bytes 1622024 | tf_op jit(solution)/shard_map/ppermute | solution.py:275
  655.7 64.8 %collective-permute-start.30 = (bf16[1056,256]{1,0:T(8,128)(2,1)}, bf16[1056,256]{1,0:T(8,128)(2,1)}, u32[]{:S(2)}, u32[]{:S(2)}) collective-permute-start(bf16[1056,256]{1,0:T(8,128)(2,1)} %get-tuple-element.326), channel_id=1, source_target_pairs={{0,8},{8,0},{16,24},{24,16},{1,9},{9,1},{17,25},{25,17},{2,10},{10... | collective-permute-start | bytes 1622024 | tf_op jit(solution)/shard_map/ppermute | solution.py:275
  728.4 319.1 %reduce-scatter.5.cloned.1.call-start = ((), (), s32[]{:S(2)}) async-start(), calls=%async_computation.25 | async-start | bytes 2359296 | tf_op jit(solution)/shard_map/reduce_scatter | solution.py:562
  757.2 292.3 %reduce-scatter.3.cloned.1.call-start = ((), (), s32[]{:S(2)}) async-start(), calls=%async_computation.24 | async-start | bytes 7077888 | tf_op jit(solution)/shard_map/reduce_scatter | solution.py:563
  761.0 65.2 %collective-permute-start.44 = (bf16[1056,256]{1,0:T(8,128)(2,1)}, bf16[1056,256]{1,0:T(8,128)(2,1)}, u32[]{:S(2)}, u32[]{:S(2)}) collective-permute-start(bf16[1056,256]{1,0:T(8,128)(2,1)} %get-tuple-element.321), channel_id=1, source_target_pairs={{0,16},{8,24},{16,0},{24,8},{1,17},{9,25},{17,1},{25,9},{2,18},{10... | collective-permute-start | bytes 1622024 | tf_op jit(solution)/shard_map/ppermute | solution.py:275
  761.0 65.2 %collective-permute-start.43 = (bf16[1056,256]{1,0:T(8,128)(2,1)}, bf16[1056,256]{1,0:T(8,128)(2,1)}, u32[]{:S(2)}, u32[]{:S(2)}) collective-permute-start(bf16[1056,256]{1,0:T(8,128)(2,1)} %get-tuple-element.322), channel_id=1, source_target_pairs={{0,8},{8,0},{16,24},{24,16},{1,9},{9,1},{17,25},{25,17},{2,10},{10... | collective-permute-start | bytes 1622024 | tf_op jit(solution)/shard_map/ppermute | solution.py:275
  839.5 107.9 %collective-permute-start.48 = (bf16[1056,256]{1,0:T(8,128)(2,1)}, bf16[1056,256]{1,0:T(8,128)(2,1)}, u32[]{:S(2)}, u32[]{:S(2)}) collective-permute-start(bf16[1056,256]{1,0:T(8,128)(2,1)} %get-tuple-element.316), channel_id=1, source_target_pairs={{0,24},{8,16},{16,8},{24,0},{1,25},{9,17},{17,9},{25,1},{2,26},{10... | collective-permute-start | bytes 1622024 | tf_op jit(solution)/shard_map/ppermute | solution.py:275
  842.1 105.3 %collective-permute-start.47 = (bf16[1056,256]{1,0:T(8,128)(2,1)}, bf16[1056,256]{1,0:T(8,128)(2,1)}, u32[]{:S(2)}, u32[]{:S(2)}) collective-permute-start(bf16[1056,256]{1,0:T(8,128)(2,1)} %get-tuple-element.317), channel_id=1, source_target_pairs={{0,16},{8,24},{16,0},{24,8},{1,17},{9,25},{17,1},{25,9},{2,18},{10... | collective-permute-start | bytes 1622024 | tf_op jit(solution)/shard_map/ppermute | solution.py:275
  851.6 87.0 %all-to-all-start.13 = ((bf16[4,128,2048]{2,1,0:T(8,128)(2,1)}), bf16[4,128,2048]{2,1,0:T(8,128)(2,1)S(1)}, u32[]{:S(2)}, u32[]{:S(2)}) async-start(bf16[4,128,2048]{2,1,0:T(8,128)(2,1)} %bitcast.378), calls=%async_computation.13 | async-start | bytes 4194304 | tf_op jit(solution)/shard_map/all_to_all | solution.py:285
  (131 other events, 2102.2 us)
Sparse Core Ops, SparseCore 0:
  11.0 114.0 all-gather.6
  126.7 28.7 all-gather.8
  757.3 62.1 reduce-scatter.4
  832.2 106.9 reduce-scatter.2
Sparse Core Ops, SparseCore 1:
  168.2 85.9 all-gather.12
  261.7 142.5 all-gather.10
  407.4 84.9 all-gather.14

commit v3 on v2

--- a/solution.py
+++ b/solution.py
@@ -67,7 +67,6 @@
     return lax.dot_general(left, right, (dims, ((), ())), preferred_element_type=F32)
 
 
-TILE = 256
 PARTS = 2
 EXTRA = 16
 
@@ -77,9 +76,9 @@
     blocks = refs[: 6 * n_g]
     out_ref, normed_ref, act_ref, gate_ref, up_ref = refs[6 * n_g : 6 * n_g + 5]
     w_gu, w_down, sems = refs[6 * n_g + 5 :]
-    g_at, k_at = meta[0], meta[1]
-
-    @pl.when((pl.program_id(0) == 0) & (pl.program_id(1) == 0))
+    g_at, k_at, c_at = meta[0], meta[1], meta[2]
+
+    @pl.when(pl.program_id(0) == 0)
     def _():
         copies = []
         for half in range(2):
@@ -103,8 +102,13 @@
 
     rows = rows_ref[...]
     count = rows.shape[0]
+    n_c = cot_ref.shape[0]
     cot = jnp.concatenate(
-        [cot_ref[c, 0].reshape(count, -1) for c in range(cot_ref.shape[0])], axis=1
+        [
+            jnp.concatenate([cot_ref[c ^ c_at, 0, row ^ c_at] for row in range(n_c)], axis=0)
+            for c in range(n_c)
+        ],
+        axis=1,
     )
     minor = ((1,), (1,))
     pre = dot(w_gu[...], rows, minor)
@@ -145,22 +149,20 @@
     n_g, f_pad, _, _, local_experts, d_own = sizes
     total, dim = rows.shape
     n_c, _, _, sub, cw = cot.shape
-    take = min(TILE // sub, n_c)
-    tile = take * sub
-    steps = n_c // take
-    flat = lambda i, j, m: (i * steps + j, 0)
-    wide = lambda i, j, m: (0, i * steps + j)
+    tile = n_c * sub
+    flat = lambda i, m: (i, 0)
+    wide = lambda i, m: (0, i)
     any_spec = pl.BlockSpec(memory_space=pl.ANY)
     return pl.pallas_call(
         functools.partial(ffn_kernel, sizes),
         grid_spec=pltpu.PrefetchScalarGridSpec(
             num_scalar_prefetch=1,
-            grid=(n_g, steps),
+            grid=(n_g,),
             in_specs=[
                 pl.BlockSpec((tile, dim), flat),
-                pl.BlockSpec((n_c, 1, take, sub, cw), lambda i, j, m: (0, i, j, 0, 0)),
-                pl.BlockSpec((1, 8, tile), lambda i, j, m: (i * steps + j, 0, 0)),
-                pl.BlockSpec((EXTRA, dim), lambda i, j, m: (0, 0)),
+                pl.BlockSpec((n_c, 1, n_c, sub, cw), lambda i, m: (0, i, 0, 0, 0)),
+                pl.BlockSpec((1, 8, tile), lambda i, m: (i, 0, 0)),
+                pl.BlockSpec((EXTRA, dim), lambda i, m: (0, 0)),
             ]
             + [any_spec] * (6 * n_g),
             out_specs=[
@@ -184,7 +186,7 @@
             jax.ShapeDtypeStruct((f_pad, total), BF16),
         ],
         compiler_params=pltpu.CompilerParams(
-            dimension_semantics=("arbitrary", "arbitrary"), vmem_limit_bytes=60 * 1024 * 1024
+            dimension_semantics=("arbitrary",), vmem_limit_bytes=60 * 1024 * 1024
         ),
         cost_estimate=pl.CostEstimate(
             flops=12 * total * dim * f_pad,
@@ -198,7 +200,12 @@
 def grad_kernel(parts, f_pad, meta, *refs):
     total = None
     for left, right in zip(refs[:parts], refs[parts : 2 * parts]):
-        value = right[...].reshape(left.shape[1], -1)
+        value = right[...]
+        if len(value.shape) > 2:
+            _, n_g, n_c, sub, _ = right.shape
+            value = jnp.concatenate(
+                [right[0, g, row ^ meta[2]] for g in range(n_g) for row in range(n_c)], axis=0
+            )
         term = dot(left[...], value, ((1,), (0,)))
         total = term if total is None else total + term
     refs[2 * parts][0, 0] = total[:f_pad].astype(BF16)
@@ -218,7 +225,7 @@
         per = cw // d_own
         right_specs = [
             pl.BlockSpec(
-                (1, n_g, n_c, sub, d_own), lambda j, m: (j // per, 0, 0, 0, j % per)
+                (1, n_g, n_c, sub, d_own), lambda j, m: ((j // per) ^ m[2], 0, 0, 0, j % per)
             )
         ] * parts
     else:
@@ -269,10 +276,28 @@
     return lax.ppermute(value, axis, [(0, 1), (1, 0)])
 
 
-def shift_chips(value, shift, n_g):
+def shift_by(value, axis, shift):
     if shift == 0:
         return value
-    return lax.ppermute(value, "g", [(i, i ^ shift) for i in range(n_g)])
+    return lax.ppermute(value, axis, [(i, i ^ shift) for i in range(lax.axis_size(axis))])
+
+
+def gather_joined(value, axis, at):
+    bit = lax.axis_size(axis) // 2
+    while bit:
+        shape = value.shape[:at] + (2 * value.shape[at],) + value.shape[at + 1 :]
+        value = jnp.stack([value, shift_by(value, axis, bit)], axis=at + 1).reshape(shape)
+        bit //= 2
+    return value
+
+
+def halve(value, axis, at, bit):
+    size = value.shape[at]
+    shape = value.shape[:at] + (size // 2, 2) + value.shape[at + 1 :]
+    pair = value.reshape(shape)
+    keep, send = (lax.index_in_dim(pair, i, at + 1, keepdims=False) for i in range(2))
+    other = shift_by(send, axis, bit)
+    return (keep.astype(F32) + other.astype(F32)).astype(BF16)
 
 
 def col_gather(value, count):
@@ -315,6 +340,7 @@
 ):
     n_g = lax.axis_size("g")
     n_c = lax.axis_size("y") * lax.axis_size("x")
+    n_y, n_x = lax.axis_size("y"), lax.axis_size("x")
     n_row = 2 * n_g
     at_g, at_k = lax.axis_index("g"), lax.axis_index("k")
     at_c = lax.axis_index(COL)
@@ -347,24 +373,15 @@
         ],
         axis=0,
     )
-    small_all = lax.all_gather(small, ROW, axis=0, tiled=False)
-    gain_1 = small_all[:, 16, :d_own].reshape(dim)
-    gain_2 = small_all[:, 17, :d_own].reshape(dim)
-    logit_w = small_all[:, 18, :d_own].reshape(dim)
-    groups_all = small_all[:, 19, : 2 * CONTS].reshape(n_g, 2, 2, CONTS)
-    groups = pick(pick(groups_all, at_g), at_k, 1).astype(jnp.int32)
-    mixing_all = small_all[:, : 2 * EXPERTS].reshape(n_row, 2, EXPERTS, block)
-    mixing_own = lax.dynamic_slice_in_dim(
-        pick(mixing_all, at_k, 1), at_c * local_experts, local_experts, 1
-    )
-    mixing_own = mixing_own.transpose(0, 2, 1).reshape(total, local_experts)
-
+    small_all = lax.all_to_all(
+        jnp.broadcast_to(small[None], (n_row,) + small.shape), ROW, 0, 0, tiled=True
+    )
     f_shared = shared_gate.shape[1] // n_g
     f_routed = expert_gate.shape[2] // n_g
     f_all = f_shared + local_experts * f_routed
     f_pad = -(-f_all // 16) * 16
     sizes = (n_g, f_pad, f_shared, f_routed, local_experts, d_own)
-    meta = jnp.stack([at_g, at_k]).astype(jnp.int32)
+    meta = jnp.stack([at_g, at_k, at_c]).astype(jnp.int32)
 
     def slices(shared, routed):
         parts = [
@@ -383,13 +400,34 @@
         slices(shared_down, expert_down),
     ]
     picked = [[pick(value, at_g ^ shift) for shift in range(n_g)] for value in weight_slices]
-    picked[0], tokens = tie(picked[0], tokens)
+    picked[0], small_all = tie(picked[0], small_all)
     own_blocks = [
-        [shift_chips(value, shift, n_g) for shift, value in enumerate(values)] for values in picked
+        [shift_by(value, "g", shift) for shift, value in enumerate(values)] for values in picked
     ]
+
+    gain_1 = small_all[:, 16, :d_own].reshape(dim)
+    gain_2 = small_all[:, 17, :d_own].reshape(dim)
+    logit_w = small_all[:, 18, :d_own].reshape(dim)
+    groups_all = small_all[:, 19, : 2 * CONTS].reshape(n_g, 2, 2, CONTS)
+    groups = pick(pick(groups_all, at_g), at_k, 1).astype(jnp.int32)
+    mixing_all = small_all[:, : 2 * EXPERTS].reshape(n_row, 2, EXPERTS, block)
+    mixing_own = lax.dynamic_slice_in_dim(
+        pick(mixing_all, at_k, 1), at_c * local_experts, local_experts, 1
+    )
+    mixing_own = mixing_own.transpose(0, 2, 1).reshape(total, local_experts)
 
     token_part = lax.all_to_all(tokens, "k", 0, 0, tiled=True).reshape(span, -1)
     cot_part = lax.all_to_all(cotangent, "k", 0, 0, tiled=True).reshape(span, -1)
+
+    sub = own_rows // PARTS
+    cot_rows = cot_part.reshape(1, n_c, PARTS, sub, dim // n_c)
+    cot_rows = gather_joined(cot_rows, "g", 0)
+    cot_all = []
+    for part in range(PARTS):
+        value = cot_rows[:, :, part][None, None]
+        for axis in ("x", "y") if part % 2 else ("y", "x"):
+            value = gather_joined(value, axis, ("y", "x").index(axis))
+        cot_all.append(value.reshape(n_c, n_g, n_c, sub, dim // n_c))
 
     qkv = lax.all_gather(
         jnp.concatenate([query_weight, key_weight, value_weight], axis=1), ROW, axis=0, tiled=True
@@ -422,35 +460,39 @@
     probabilities = exp_scores / jnp.sum(exp_scores, axis=-1, keepdims=True)
     prob_low = probabilities.astype(BF16)
     mixed = einsum("bhqk,bkhd->bqhd", prob_low, value_low).astype(BF16).reshape(span, width)
+    own_blocks[1], mixed = tie(own_blocks[1], mixed)
     attention = col_sum(dot(mixed, out_w, ((1,), (0,))), n_c)
 
     own_inputs = lax.dynamic_slice_in_dim(inputs, at_c * own_rows, own_rows, 0)
-    own_blocks[1], attention = tie(own_blocks[1], attention)
+    cot_all, attention = tie(cot_all, attention)
     hidden = own_inputs + attention
     second_scale = lax.rsqrt(jnp.mean(hidden * hidden, axis=-1, keepdims=True) + epsilon)
     unit_2 = hidden * second_scale
     normed_own = (unit_2 * gain_2).astype(BF16)
-    sub = own_rows // PARTS
-    normed_parts = [
-        lax.all_gather(
-            normed_own[part * sub : (part + 1) * sub], ("g",) + COL, axis=0, tiled=True
-        )
-        for part in range(PARTS)
+    own_blocks[2], normed_own = tie(own_blocks[2], normed_own)
+
+    def gather_rows(rows):
+        value = gather_joined(rows[None], "g", 0)[:, None, None]
+        sides = []
+        for side, order in enumerate((("y", "x"), ("x", "y"))):
+            half = value[..., side * (dim // 2) : (side + 1) * (dim // 2)]
+            for axis in order:
+                half = gather_joined(half, axis, 1 + ("y", "x").index(axis))
+            sides.append(half)
+        return jnp.concatenate(sides, axis=-1).reshape(-1, dim)
+
+    normed_parts = [gather_rows(normed_own[part * sub : (part + 1) * sub]) for part in range(PARTS)]
+    own_cot = [
+        lax.dynamic_index_in_dim(cot[:, 0], at_c, 1, keepdims=False) for cot in cot_all
     ]
-
-    cot_rows = lax.all_gather(cot_part, "g", axis=0, tiled=True)
-    cot_rows = cot_rows.reshape(n_g, n_c, PARTS, sub, dim // n_c)
-    cot_all = [
-        col_gather(cot_rows[:, :, part], n_c).reshape(n_c, n_g, n_c, sub, dim // n_c)
-        for part in range(PARTS)
-    ]
-    own_cot = [
-        pick(pick(cot, at_g, 1), at_c, 1).transpose(1, 0, 2).reshape(sub, dim) for cot in cot_all
-    ]
-    own_cot = jnp.concatenate(own_cot, axis=0)
+    own_cot = jnp.concatenate(own_cot, axis=1)
+    own_cot = jnp.stack([pick(own_cot, at_c ^ c) for c in range(n_c)], axis=1)
+    own_cot = own_cot.reshape(own_rows, dim)
 
     logit_low = jnp.zeros((EXTRA, dim), BF16).at[:2].set(logit_w.astype(BF16)[None])
     mixing_parts = mixing_own.reshape(n_g, n_c, PARTS, sub, local_experts)
+    mixing_parts = jnp.stack([pick(mixing_parts, at_g ^ shift) for shift in range(n_g)])
+    mixing_parts = jnp.stack([pick(mixing_parts, at_c ^ c, 1) for c in range(n_c)], axis=1)
     mixing_parts = jnp.pad(mixing_parts, ((0, 0),) * 4 + ((0, 8 - local_experts),))
     swapped = [[swap(value, "k") for value in values] for values in own_blocks]
     weight_blocks = [
@@ -472,31 +514,41 @@
         for part in range(PARTS)
     ]
 
+    def split_sides(partial):
+        part = partial.reshape(n_g, n_y, n_x, sub, dim)
+        return [part[..., : dim // 2], part[..., dim // 2 :]]
+
     def scatter_axis(value, axis, at):
-        size = lax.axis_size(axis)
-        index = lax.axis_index(axis)
-        if size == 2:
-            other = swap(pick(value, 1 - index, at), axis)
-            return (pick(value, index, at).astype(F32) + other.astype(F32)).astype(BF16)
-        moved = lax.all_to_all(value, axis, at, at, tiled=True)
-        return jnp.sum(moved.astype(F32), axis=at).astype(BF16)
-
-    def scatter_cols(partial):
-        part = partial.reshape(n_g, lax.axis_size("y"), 2, sub, dim)
-        left, right = part[..., : dim // 2], part[..., dim // 2 :]
-        left, right = scatter_axis(left, "x", 2), scatter_axis(right, "y", 1)
-        left, right = scatter_axis(left, "y", 1), scatter_axis(right, "x", 1)
-        return jnp.concatenate([left, right], axis=-1)
-
-    def scatter_chips(part):
-        return jnp.sum(lax.all_to_all(part, "g", 0, 0, tiled=True).astype(F32), axis=0)
+        bit = 1
+        while bit < lax.axis_size(axis):
+            value = halve(value, axis, at, bit)
+            bit *= 2
+        return lax.index_in_dim(value, 0, at, keepdims=False)
+
+    def cols_first(sides):
+        return [scatter_axis(sides[0], "x", 2), scatter_axis(sides[1], "y", 1)]
+
+    def cols_second(sides):
+        sides = [scatter_axis(sides[0], "y", 1), scatter_axis(sides[1], "x", 1)]
+        return jnp.concatenate(sides, axis=-1)
+
+    def chips_steps(value):
+        bit = 1
+        while 2 * bit < n_g:
+            value = halve(value, "g", 0, bit)
+            bit *= 2
+        return value
+
+    def chips_last(value):
+        other = shift_by(value[1], "g", n_g // 2)
+        return value[0].astype(F32) + other.astype(F32)
 
     def own_core(grad):
         other = swap(grad[1], "k")
         return (grad[0].astype(F32) + other.astype(F32)).astype(BF16)
 
     def send_slices(both):
-        return [shift_chips(both[shift], shift, n_g) for shift in range(n_g)]
+        return [shift_by(both[shift], "g", shift) for shift in range(n_g)]
 
     def place_slices(moved):
         moved = jnp.stack(moved)
@@ -506,32 +558,43 @@
         routed = routed.transpose(1, 0, 2, 3).reshape(local_experts, n_g * f_routed, d_own)
         return (shared, routed)
 
-    (down_blocks,) = weight_grad(sizes, meta, [parts[2] for parts in passes], cot_all, True)
-    gate_blocks, logit_sum = weight_grad(
-        sizes, meta, [parts[3] for parts in passes], normed_parts, False
-    )
-    (up_blocks,) = weight_grad(sizes, meta, [parts[4] for parts in passes], normed_parts, False)
+    acts, gates, ups = ([parts[i] for parts in passes] for i in (2, 3, 4))
+    first = cols_first(split_sides(passes[0][1]))
+    first, acts = tie(first, acts)
+    (down_blocks,) = weight_grad(sizes, meta, acts, cot_all, True)
+    first = cols_second(first)
+    second = cols_first(split_sides(passes[1][1]))
+    first, second, gates, down_blocks = tie(first, second, gates, down_blocks)
+    gate_blocks, logit_sum = weight_grad(sizes, meta, gates, normed_parts, False)
     logit_sum = logit_sum[0]
+    first = chips_steps(first)
+    second = cols_second(second)
     down_both = own_core(down_blocks)
-
-    normed_cols = [scatter_cols(parts[1]) for parts in passes]
-    normed_cols[1], down_both, gate_blocks = tie(normed_cols[1], down_both, gate_blocks)
-    normed_grad_2 = jnp.concatenate([scatter_chips(part) for part in normed_cols], axis=0)
+    first, second, down_both, ups, gate_blocks = tie(first, second, down_both, ups, gate_blocks)
     down_moved = send_slices(down_both)
-    gate_both, up_both = own_core(gate_blocks), own_core(up_blocks)
-    normed_grad_2, down_moved, gate_both, up_both = tie(
-        normed_grad_2, down_moved, gate_both, up_both
-    )
+    (up_blocks,) = weight_grad(sizes, meta, ups, normed_parts, False)
+    first = chips_last(first)
+    second = chips_steps(second)
+    gate_both = own_core(gate_blocks)
+    first, second, gate_both, up_blocks = tie(first, second, gate_both, up_blocks)
+    second = chips_last(second)
+    up_both = own_core(up_blocks)
+    out_sides = [cols_first(split_sides(parts[0])) for parts in passes]
+    normed_grad_2 = jnp.concatenate([first, second], axis=0)
+    normed_grad_2, up_both = tie(normed_grad_2, up_both)
     hidden_part, gain_2_sum = norm_back(normed_grad_2, unit_2, second_scale, gain_2)
     hidden_grad = own_cot.astype(F32) + hidden_part
     gate_moved = send_slices(gate_both)
     up_moved = send_slices(up_both)
     attn_grad = col_gather(hidden_grad.astype(BF16), n_c).reshape(span, dim)
-    out_parts, attn_grad = tie([parts[0] for parts in passes], attn_grad)
+    out_sides, attn_grad, down_moved = tie(out_sides, attn_grad, down_moved)
+    out_parts = [cols_second(sides) for sides in out_sides]
     down_s, down_e = place_slices(down_moved)
 
     out_grad = dot(attn_grad, mixed, ((0,), (0,)))
     mixed_grad = dot(attn_grad, out_w, ((1,), (1,))).astype(BF16).reshape(head_shape)
+    out_parts, mixed_grad = tie(out_parts, mixed_grad)
+    out_parts = [chips_steps(part) for part in out_parts]
     prob_grad = einsum("bqhd,bkhd->bhqk", mixed_grad, value_low)
     value_grad = einsum("bhqk,bqhd->bkhd", prob_low, mixed_grad).astype(BF16)
     center = jnp.sum(prob_grad * probabilities, axis=-1, keepdims=True)
@@ -541,7 +604,8 @@
     qkv_grad = jnp.concatenate(
         [part.reshape(span, width) for part in (query_grad, key_grad, value_grad)], axis=1
     )
-    qkv_grad, gate_moved = tie(qkv_grad, gate_moved)
+    qkv_grad, gate_moved, out_parts = tie(qkv_grad, gate_moved, out_parts)
+    out_rows = jnp.concatenate([chips_last(part) for part in out_parts], axis=0)
     gate_s, gate_e = place_slices(gate_moved)
     qkv_sum = dot(normed_1, qkv_grad, ((0,), (0,)))
     normed_grad_1 = col_sum(dot(qkv_grad, qkv, ((1,), (1,))), n_c)
@@ -551,7 +615,6 @@
     rows_part, gain_1_sum = norm_back(normed_grad_1, own_inputs * own_scale, own_scale, gain_1)
     token_grad = rows_to_features((hidden_grad + rows_part).astype(BF16), n_c).astype(F32)
 
-    out_rows = jnp.concatenate([scatter_chips(scatter_cols(part)) for part in out_parts], axis=0)
     result = rows_to_features((hidden + out_rows).astype(BF16), n_c)
 
     sums = jnp.stack([gain_1_sum, gain_2_sum, logit_sum]).reshape(3, n_row, d_own)

time: 1070 us -> 1030 us (0.963)
  blocking collectives: 105 us -> 13.9 us
  starting transfers between devices: 105 us -> 167 us
  other arithmetic: 81.8 us -> 115 us
  waiting for transfers between devices: 432 us -> 400 us
    ppermute x18 -> x60, waiting for transfers between devices: 177 us -> 366 us  [shift_by(): lax.ppermute(value, axis, [(i, i ^ shift) for i in range(lax.axis_size(ax...]
    ppermute x18 -> x60, starting transfers between devices: 26.4 us -> 128 us  [shift_by(): lax.ppermute(value, axis, [(i, i ^ shift) for i in range(lax.axis_size(ax...]
    all_gather x1 -> x0, blocking collectives: 94.8 us -> none  [shards(): small_all = lax.all_gather(small, ROW, axis=0, tiled=False)]
    all_gather x3 -> x0, waiting for transfers between devices: 90.4 us -> none  [the longest x2 90.3 us: shards(): lax.all_gather(normed_own[part * sub:(part + 1) * sub], ('g',) + COL, axi...]
    all_to_all x5 -> x1, waiting for transfers between devices: 64.3 us -> 5.61 us  [shards(): lax.all_to_all(jnp.broadcast_to(small[None], (n_row,) + small.shape), ROW...]
    ppermute x31 -> x15, waiting for transfers between devices: 50.9 us -> 0.04 us  [swap(): return lax.ppermute(value, axis, [(0, 1), (1, 0)])]
    squeeze x0 -> x16, other arithmetic: none -> 25.1 us  [scatter_axis(): return lax.index_in_dim(value, 0, at, keepdims=False)]
    all_to_all x4 -> x2, waiting for transfers between devices: 24.3 us -> 0.01 us  [col_gather(): return lax.all_to_all(spread, COL, 0, 0, tiled=True)]
  transfers between devices with their start and end apart: 71 -> 88, of which waited for: 28 -> 29; matrix products, arithmetic and copies ran while one was open for 22% -> 27% of each run, Pallas kernels for 13% -> 13%
where the time goes in v3:
time: 1030 us
  waiting for transfers between devices  400 us (39%)
  starting transfers between devices  167 us (16%)
  Pallas kernels  137 us (13%)
  local copies, waits for them, and re-layouts  124 us (12%)
  other arithmetic  115 us (11%)
  matrix products  54.1 us (5%)
  between operations  16.3 us (2%)
  blocking collectives  13.9 us (1%)
    ppermute x60, waiting for transfers between devices, shift_by(): lax.ppermute(value, axis, [(i, i ^ shift) for i in range(lax.axis_size(ax...  366 us
    ppermute x60, starting transfers between devices, shift_by(): lax.ppermute(value, axis, [(i, i ^ shift) for i in range(lax.axis_size(ax...  128 us
    pallas_call x2, Pallas kernels, ffn_pass(): pl.pallas_call(functools.partial(ffn_kernel, sizes), grid_spec=pltpu.Pref...  96.9 us
    pallas_call x3, Pallas kernels, weight_grad(): pl.pallas_call(functools.partial(grad_kernel, parts, f_pad), grid_spec=pl...  40.6 us
    unnamed x247, local copies, waits for them, and re-layouts  37 us
    dot_general x6, matrix products, dot(): lax.dot_general(left, right, (dims, ((), ())), preferred_element_type=F32)  32.6 us
    squeeze x16, other arithmetic, scatter_axis(): return lax.index_in_dim(value, 0, at, keepdims=False)  25.1 us
    all_to_all x2, waiting for transfers between devices, col_sum(): lax.all_to_all(parts, COL, 0, 0, tiled=True).astype(F32)  23.6 us
  transfers between devices with their start and end apart: 88, of which 29 were waited for; matrix products, arithmetic and copies ran while one was open for 27% of the time, Pallas kernels for 13%

profile of v3, /device:TPU:0, one launch (start us, length us, event | category | flops | bytes accessed | tf_op | source)
XLA Modules:
  0.0 1026.8 jit_solution(16961617947298321251)
XLA Ops:
  45.5 30.2 %collective-permute-done.3 = bf16[1,4,2,64,512]{4,3,2,1,0:T(8,128)(2,1)} collective-permute-done((bf16[1,4,2,64,512]{4,3,2,1,0:T(8,128)(2,1)}, bf16[1,4,2,64,512]{4,3,2,1,0:T(8,128)(2,1)}, u32[]{:S(2)}, u32[]{:S(2)}) %collective-permute-start.3) | collective-permute-done | bytes 524320 | tf_op jit(solution)/shard_map/ppermute | solution.py:282
  96.1 42.3 %collective-permute-done.4 = bf16[2,4,2,64,512]{4,3,2,1,0:T(8,128)(2,1)} collective-permute-done((bf16[2,4,2,64,512]{4,3,2,1,0:T(8,128)(2,1)}, bf16[2,4,2,64,512]{4,3,2,1,0:T(8,128)(2,1)}, u32[]{:S(2)}, u32[]{:S(2)}) %collective-permute-start.4) | collective-permute-done | bytes 1048608 | tf_op jit(solution)/shard_map/ppermute | solution.py:282
  148.0 20.6 %collective-permute-done.refs_3_ = bf16[1056,256]{1,0:T(8,128)(2,1)} collective-permute-done((bf16[1056,256]{1,0:T(8,128)(2,1)}, bf16[1056,256]{1,0:T(8,128)(2,1)}, u32[]{:S(2)}, u32[]{:S(2)}) %collective-permute-start) | collective-permute-done | bytes 540704 | tf_op jit(solution)/shard_map/ppermute | solution.py:282
  218.6 10.1 collective-permute-start.12
  240.3 9.3 all-to-all-done.4
  254.3 14.0 %collective-permute-done.13.refs_8_ = bf16[1056,256]{1,0:T(8,128)(2,1)} collective-permute-done((bf16[1056,256]{1,0:T(8,128)(2,1)}, bf16[1056,256]{1,0:T(8,128)(2,1)}, u32[]{:S(2)}, u32[]{:S(2)}) %collective-permute-start.13) | collective-permute-done | bytes 540704 | tf_op jit(solution)/shard_map/ppermute | solution.py:282
  268.4 13.3 %collective-permute-start.15 = (bf16[1,64,2048]{2,1,0:T(8,128)(2,1)S(1)}, bf16[1,64,2048]{2,1,0:T(8,128)(2,1)S(1)}, u32[]{:S(2)}, u32[]{:S(2)}) collective-permute-start(bf16[1,64,2048]{2,1,0:T(8,128)(2,1)S(1)} %get-tuple-element.440), channel_id=1, source_target_pairs={{0,16},{8,24},{16,0},{24,8},{1,17},{9,25},{17,1},{25,9},{2,18},{10... | collective-permute-start | bytes 786440 | tf_op jit(solution)/shard_map/ppermute | solution.py:282
  282.5 15.8 %collective-permute-done.15 = bf16[1,64,2048]{2,1,0:T(8,128)(2,1)S(1)} collective-permute-done((bf16[1,64,2048]{2,1,0:T(8,128)(2,1)S(1)}, bf16[1,64,2048]{2,1,0:T(8,128)(2,1)S(1)}, u32[]{:S(2)}, u32[]{:S(2)}) %collective-permute-start.15) | collective-permute-done | bytes 262176 | tf_op jit(solution)/shard_map/ppermute | solution.py:282
  303.9 11.1 %collective-permute-done.16 = bf16[2,64,2048]{2,1,0:T(8,128)(2,1)S(1)} collective-permute-done((bf16[2,64,2048]{2,1,0:T(8,128)(2,1)S(1)}, bf16[2,64,2048]{2,1,0:T(8,128)(2,1)S(1)}, u32[]{:S(2)}, u32[]{:S(2)}) %collective-permute-start.16) | collective-permute-done | bytes 524320 | tf_op jit(solution)/shard_map/ppermute | solution.py:282
  317.5 8.6 collective-permute-done.36
  330.2 9.7 collective-permute-done.19
  390.0 48.6 %ffn_pass.2 = (bf16[1024,2048]{1,0:T(8,128)(2,1)}, bf16[1024,2048]{1,0:T(8,128)(2,1)}, bf16[1056,1024]{1,0:T(8,128)(2,1)}, bf16[1072,1024]{1,0:T(8,128)(2,1)}, bf16[1056,1024]{1,0:T(8,128)(2,1)}) custom-call(s32[3]{0:T(128)} %pad_add_fusion.meta, bf16[1024,2048]{1,0:T(8,128)(2,1)} %pad_maximum_fusion.2.rows_ref.refs_2_, ...), custom_call_target="tpu_custom_call" | custom-call | flops 26575110144 | bytes 36241408 | tf_op jit(solution)/shard_map/ffn_pass/pallas_call | solution.py:156
  451.6 48.3 %ffn_pass.3 = (bf16[1024,2048]{1,0:T(8,128)(2,1)}, bf16[1024,2048]{1,0:T(8,128)(2,1)}, bf16[1056,1024]{1,0:T(8,128)(2,1)}, bf16[1072,1024]{1,0:T(8,128)(2,1)}, bf16[1056,1024]{1,0:T(8,128)(2,1)}) custom-call(s32[3]{0:T(128)} %pad_add_fusion.meta, bf16[1024,2048]{1,0:T(8,128)(2,1)} %pad_maximum_fusion.3.rows_ref.refs_3_, ...), custom_call_target="tpu_custom_call" | custom-call | flops 26575110144 | bytes 36241408 | tf_op jit(solution)/shard_map/ffn_pass/pallas_call | solution.py:156
  525.4 13.8 %weight_grad.3 = bf16[2,4,1056,256]{3,2,1,0:T(8,128)(2,1)} custom-call(s32[3]{0:T(128)S(1)} %copy-done, bf16[1056,1024]{1,0:T(8,128)(2,1)S(1)} %copy-done.3, bf16[1056,1024]{1,0:T(8,128)(2,1)S(1)} %copy-done.4, bf16[4,4,4,64,512]{4,3,2,1,0:T(8,128)(2,1)} %bitcast.601, bf16[4,4,4,64,512]{4,3,2,1,0:T(8,128)(2,1)} %bitcast.604), custom_call_target="tpu_custom_call" | custom-call | flops 8858370048 | bytes 17039360 | tf_op jit(solution)/shard_map/weight_grad/pallas_call | solution.py:242
  543.8 18.4 %collective-permute-done.45 = bf16[4,1,64,1024]{3,2,0,1:T(8,128)(2,1)S(1)} collective-permute-done((bf16[4,1,64,1024]{3,2,0,1:T(8,128)(2,1)}, bf16[4,1,64,1024]{3,2,0,1:T(8,128)(2,1)S(1)}, u32[]{:S(2)}, u32[]{:S(2)}) %collective-permute-start.45) | collective-permute-done | bytes 524320 | tf_op jit(solution)/shard_map/ppermute | solution.py:282
  571.2 13.4 %weight_grad.4 = (bf16[2,4,1056,256]{3,2,1,0:T(8,128)(2,1)}, f32[8,2048]{1,0:T(8,128)S(1)}) custom-call(s32[3]{0:T(128)S(1)} %copy-done, bf16[1072,1024]{1,0:T(8,128)(2,1)S(1)} %copy-done.5, bf16[1072,1024]{1,0:T(8,128)(2,1)S(1)} %copy-done.6, bf16[1024,2048]{1,0:T(8,128)(2,1)} %pad_maximum_fusion.2.rows_ref.refs_2_, ...), custom_call_target="tpu_custom_call" | custom-call | flops 8992587776 | bytes 17104896 | tf_op jit(solution)/shard_map/weight_grad/pallas_call | solution.py:242
  587.5 11.0 %collective-permute-done.49 = bf16[2,64,2048]{2,1,0:T(8,128)(2,1)S(1)} collective-permute-done((bf16[2,64,2048]{2,1,0:T(8,128)(2,1)S(1)}, bf16[2,64,2048]{2,1,0:T(8,128)(2,1)S(1)}, u32[]{:S(2)}, u32[]{:S(2)}) %collective-permute-start.49) | collective-permute-done | bytes 524320 | tf_op jit(solution)/shard_map/ppermute | solution.py:282
  605.5 13.4 %weight_grad.5 = bf16[2,4,1056,256]{3,2,1,0:T(8,128)(2,1)} custom-call(s32[3]{0:T(128)S(1)} %copy-done, bf16[1056,1024]{1,0:T(8,128)(2,1)S(1)} %copy-done.1, bf16[1056,1024]{1,0:T(8,128)(2,1)S(1)} %copy-done.2, bf16[1024,2048]{1,0:T(8,128)(2,1)} %pad_maximum_fusion.2.rows_ref.refs_2_, bf16[1024,2048]{1,0:T(8,128)(2,1)} %pad_maximum_fusion.3.rows_ref.refs_3_), custom_call_target="tpu_custom_call" | custom-call | flops 8858370048 | bytes 17039360 | tf_op jit(solution)/shard_map/weight_grad/pallas_call | solution.py:242
  638.9 10.0 collective-permute-done.56
  673.7 18.5 %collective-permute-done.58 = bf16[1056,256]{1,0:T(8,128)(2,1)} collective-permute-done((bf16[1056,256]{1,0:T(8,128)(2,1)S(1)}, bf16[1056,256]{1,0:T(8,128)(2,1)}, u32[]{:S(2)}, u32[]{:S(2)}) %collective-permute-start.58) | collective-permute-done | bytes 540704 | tf_op jit(solution)/shard_map/ppermute | solution.py:282
  693.6 11.5 %collective-permute-done.59 = bf16[1056,256]{1,0:T(8,128)(2,1)} collective-permute-done((bf16[1056,256]{1,0:T(8,128)(2,1)S(1)}, bf16[1056,256]{1,0:T(8,128)(2,1)}, u32[]{:S(2)}, u32[]{:S(2)}) %collective-permute-start.59) | collective-permute-done | bytes 540704 | tf_op jit(solution)/shard_map/ppermute | solution.py:282
  738.4 36.5 %collective-permute-start.69 = (bf16[2,64,2048]{2,1,0:T(8,128)(2,1)}, bf16[2,64,2048]{2,1,0:T(8,128)(2,1)}, u32[]{:S(2)}, u32[]{:S(2)}) collective-permute-start(bf16[2,64,2048]{2,1,0:T(8,128)(2,1)} %slice_bitcast_fusion.35), channel_id=1, source_target_pairs={{0,8},{8,0},{16,24},{24,16},{1,9},{9,1},{17,25},{25,17},{2,10},{10... | collective-permute-start | bytes 1572872 | tf_op jit(solution)/shard_map/ppermute | solution.py:282
  827.7 97.3 %collective-permute-done.70 = bf16[64,2048]{1,0:T(8,128)(2,1)S(1)} collective-permute-done((bf16[64,2048]{1,0:T(8,128)(2,1)S(1)}, bf16[64,2048]{1,0:T(8,128)(2,1)S(1)}, u32[]{:S(2)}, u32[]{:S(2)}) %collective-permute-start.70) | collective-permute-done | bytes 262176 | tf_op jit(solution)/shard_map/ppermute | solution.py:282
  967.5 14.4 %all-to-all-done.8 = bf16[4,128,2048]{2,1,0:T(8,128)(2,1)} async-done(((bf16[4,128,2048]{2,1,0:T(8,128)(2,1)}), bf16[4,128,2048]{2,1,0:T(8,128)(2,1)}, u32[]{:S(2)}, u32[]{:S(2)}) %all-to-all-start.8) | async-done | bytes 2097184 | tf_op jit(solution)/shard_map/all_to_all | solution.py:310
  (655 shorter events, 470.5 us)
Async XLA Ops:
  7.2 174.8 %all-gather.3.cloned.1.call-start = ((), (), s32[]{:S(2)}) async-start(), calls=%async_computation.14 | async-start | bytes 7077888 | tf_op jit(solution)/shard_map/all_gather | solution.py:432
  17.8 189.3 %all-gather.5.cloned.1.call-start = ((), (), s32[]{:S(2)}) async-start(), calls=%async_computation.15 | async-start | bytes 2359296 | tf_op jit(solution)/shard_map/all_gather | solution.py:435
  85.3 61.5 %all-to-all-start.2 = ((bf16[4,512,512]{2,1,0:T(8,128)(2,1)}), bf16[4,512,512]{2,1,0:T(8,128)(2,1)S(1)}, u32[]{:S(2)}, u32[]{:S(2)}) async-start(bf16[4,512,512]{2,1,0:T(8,128)(2,1)} %broadcast_in_dim.54), calls=%async_computation.2 | async-start | bytes 4194304 | tf_op jit(solution)/shard_map/all_to_all | solution.py:305
  89.8 78.8 %collective-permute-start = (bf16[1056,256]{1,0:T(8,128)(2,1)}, bf16[1056,256]{1,0:T(8,128)(2,1)}, u32[]{:S(2)}, u32[]{:S(2)}) collective-permute-start(bf16[1056,256]{1,0:T(8,128)(2,1)} %get-tuple-element.157), channel_id=1, source_target_pairs={{0,8},{8,0},{16,24},{24,16},{1,9},{9,1},{17,25},{25,17},{2,10},{10... | collective-permute-start | bytes 1622024 | tf_op jit(solution)/shard_map/ppermute | solution.py:282
  89.9 79.4 %collective-permute-start.1 = (bf16[1056,256]{1,0:T(8,128)(2,1)}, bf16[1056,256]{1,0:T(8,128)(2,1)}, u32[]{:S(2)}, u32[]{:S(2)}) collective-permute-start(bf16[1056,256]{1,0:T(8,128)(2,1)} %get-tuple-element.158), channel_id=1, source_target_pairs={{0,16},{8,24},{16,0},{24,8},{1,17},{9,25},{17,1},{25,9},{2,18},{10... | collective-permute-start | bytes 1622024 | tf_op jit(solution)/shard_map/ppermute | solution.py:282
  93.0 78.3 %collective-permute-start.2 = (bf16[1056,256]{1,0:T(8,128)(2,1)}, bf16[1056,256]{1,0:T(8,128)(2,1)}, u32[]{:S(2)}, u32[]{:S(2)}) collective-permute-start(bf16[1056,256]{1,0:T(8,128)(2,1)} %get-tuple-element.159), channel_id=1, source_target_pairs={{0,24},{8,16},{16,8},{24,0},{1,25},{9,17},{17,9},{25,1},{2,26},{10... | collective-permute-start | bytes 1622024 | tf_op jit(solution)/shard_map/ppermute | solution.py:282
  175.3 61.4 %collective-permute-start.8 = (bf16[1,2,4,4,64,512]{5,4,3,2,1,0:T(8,128)(2,1)}, bf16[1,2,4,4,64,512]{5,4,3,2,1,0:T(8,128)(2,1)}, u32[]{:S(2)}, u32[]{:S(2)}) collective-permute-start(bf16[1,2,4,4,64,512]{5,4,3,2,1,0:T(8,128)(2,1)} %maximum_bitcast_fusion), channel_id=1, source_target_pairs={{0,2},{2,0},{1,3},{3,1},{4,6},{6,4},{5,7},{7,5},{8,10},{10,8},{9,1... | collective-permute-start | bytes 6291464 | tf_op jit(solution)/shard_map/ppermute | solution.py:282
  385.0 60.7 %collective-permute-start.38 = (bf16[4,2,1,64,1024]{4,3,0,1,2:T(8,128)(2,1)}, bf16[4,2,1,64,1024]{4,3,0,1,2:T(8,128)(2,1)}, u32[]{:S(2)}, u32[]{:S(2)}) collective-permute-start(bf16[4,2,1,64,1024]{4,3,0,1,2:T(8,128)(2,1)} %get-tuple-element.413), channel_id=1, source_target_pairs={{0,1},{1,0},{2,3},{3,2},{4,5},{5,4},{6,7},{7,6},{8,9},{9,8},{10,11... | collective-permute-start | bytes 3145736 | tf_op jit(solution)/shard_map/ppermute | solution.py:282
  386.4 61.0 %collective-permute-start.40 = (bf16[4,1,2,64,1024]{4,3,0,2,1:T(8,128)(2,1)}, bf16[4,1,2,64,1024]{4,3,0,2,1:T(8,128)(2,1)}, u32[]{:S(2)}, u32[]{:S(2)}) collective-permute-start(bf16[4,1,2,64,1024]{4,3,0,2,1:T(8,128)(2,1)} %maximum_bitcast_fusion.2), channel_id=1, source_target_pairs={{0,2},{2,0},{1,3},{3,1},{4,6},{6,4},{5,7},{7,5},{8,10},{10,8},{9,1... | collective-permute-start | bytes 3145736 | tf_op jit(solution)/shard_map/ppermute | solution.py:282
  442.6 74.6 %collective-permute-start.44 = (bf16[4,1,2,64,1024]{4,3,0,2,1:T(8,128)(2,1)}, bf16[4,1,2,64,1024]{4,3,0,2,1:T(8,128)(2,1)S(1)}, u32[]{:S(2)}, u32[]{:S(2)}) collective-permute-start(bf16[4,1,2,64,1024]{4,3,0,2,1:T(8,128)(2,1)} %slice_bitcast_fusion.7), channel_id=1, source_target_pairs={{0,2},{2,0},{1,3},{3,1},{4,6},{6,4},{5,7},{7,5},{8,10},{10,8},{9,1... | collective-permute-start | bytes 3145736 | tf_op jit(solution)/shard_map/ppermute | solution.py:282
  444.9 75.9 %collective-permute-start.43 = (bf16[4,2,1,64,1024]{4,3,0,1,2:T(8,128)(2,1)}, bf16[4,2,1,64,1024]{4,3,0,1,2:T(8,128)(2,1)}, u32[]{:S(2)}, u32[]{:S(2)}) collective-permute-start(bf16[4,2,1,64,1024]{4,3,0,1,2:T(8,128)(2,1)} %slice_bitcast_fusion.9), channel_id=1, source_target_pairs={{0,1},{1,0},{2,3},{3,2},{4,5},{5,4},{6,7},{7,6},{8,9},{9,8},{10,11... | collective-permute-start | bytes 3145736 | tf_op jit(solution)/shard_map/ppermute | solution.py:282
  510.7 121.5 %collective-permute-start.42 = (bf16[4,1,2,64,1024]{4,3,0,2,1:T(8,128)(2,1)}, bf16[4,1,2,64,1024]{4,3,0,2,1:T(8,128)(2,1)}, u32[]{:S(2)}, u32[]{:S(2)}) collective-permute-start(bf16[4,1,2,64,1024]{4,3,0,2,1:T(8,128)(2,1)} %slice_bitcast_fusion.11), channel_id=1, source_target_pairs={{0,2},{2,0},{1,3},{3,1},{4,6},{6,4},{5,7},{7,5},{8,10},{10,8},{9,1... | collective-permute-start | bytes 3145736 | tf_op jit(solution)/shard_map/ppermute | solution.py:282
  518.2 118.0 %collective-permute-start.41 = (bf16[4,2,1,64,1024]{4,3,0,1,2:T(8,128)(2,1)}, bf16[4,2,1,64,1024]{4,3,0,1,2:T(8,128)(2,1)}, u32[]{:S(2)}, u32[]{:S(2)}) collective-permute-start(bf16[4,2,1,64,1024]{4,3,0,1,2:T(8,128)(2,1)} %slice_bitcast_fusion.13), channel_id=1, source_target_pairs={{0,1},{1,0},{2,3},{3,2},{4,5},{5,4},{6,7},{7,6},{8,9},{9,8},{10,11... | collective-permute-start | bytes 3145736 | tf_op jit(solution)/shard_map/ppermute | solution.py:282
  658.8 356.1 %reduce-scatter.5.cloned.1.call-start = ((), (), s32[]{:S(2)}) async-start(), calls=%async_computation.17 | async-start | bytes 2359296 | tf_op jit(solution)/shard_map/reduce_scatter | solution.py:625
  671.4 138.2 %collective-permute-start.65 = (bf16[1056,256]{1,0:T(8,128)(2,1)}, bf16[1056,256]{1,0:T(8,128)(2,1)}, u32[]{:S(2)}, u32[]{:S(2)}) collective-permute-start(bf16[1056,256]{1,0:T(8,128)(2,1)} %get-tuple-element.384), channel_id=1, source_target_pairs={{0,8},{8,0},{16,24},{24,16},{1,9},{9,1},{17,25},{25,17},{2,10},{10... | collective-permute-start | bytes 1622024 | tf_op jit(solution)/shard_map/ppermute | solution.py:282
  671.4 138.2 %collective-permute-start.66 = (bf16[1056,256]{1,0:T(8,128)(2,1)}, bf16[1056,256]{1,0:T(8,128)(2,1)}, u32[]{:S(2)}, u32[]{:S(2)}) collective-permute-start(bf16[1056,256]{1,0:T(8,128)(2,1)} %get-tuple-element.383), channel_id=1, source_target_pairs={{0,16},{8,24},{16,0},{24,8},{1,17},{9,25},{17,1},{25,9},{2,18},{10... | collective-permute-start | bytes 1622024 | tf_op jit(solution)/shard_map/ppermute | solution.py:282
  692.2 117.5 %collective-permute-start.67 = (bf16[1056,256]{1,0:T(8,128)(2,1)}, bf16[1056,256]{1,0:T(8,128)(2,1)}, u32[]{:S(2)}, u32[]{:S(2)}) collective-permute-start(bf16[1056,256]{1,0:T(8,128)(2,1)} %get-tuple-element.382), channel_id=1, source_target_pairs={{0,24},{8,16},{16,8},{24,0},{1,25},{9,17},{17,9},{25,1},{2,26},{10... | collective-permute-start | bytes 1622024 | tf_op jit(solution)/shard_map/ppermute | solution.py:282
  724.1 292.9 %reduce-scatter.3.cloned.1.call-start = ((), (), s32[]{:S(2)}) async-start(), calls=%async_computation.16 | async-start | bytes 7077888 | tf_op jit(solution)/shard_map/reduce_scatter | solution.py:626
  738.4 66.8 %collective-permute-start.69 = (bf16[2,64,2048]{2,1,0:T(8,128)(2,1)}, bf16[2,64,2048]{2,1,0:T(8,128)(2,1)}, u32[]{:S(2)}, u32[]{:S(2)}) collective-permute-start(bf16[2,64,2048]{2,1,0:T(8,128)(2,1)} %slice_bitcast_fusion.35), channel_id=1, source_target_pairs={{0,8},{8,0},{16,24},{24,16},{1,9},{9,1},{17,25},{25,17},{2,10},{10... | collective-permute-start | bytes 1572872 | tf_op jit(solution)/shard_map/ppermute | solution.py:282
  816.8 167.1 %collective-permute-start.72 = (bf16[1056,256]{1,0:T(8,128)(2,1)}, bf16[1056,256]{1,0:T(8,128)(2,1)}, u32[]{:S(2)}, u32[]{:S(2)}) collective-permute-start(bf16[1056,256]{1,0:T(8,128)(2,1)} %get-tuple-element.380), channel_id=1, source_target_pairs={{0,8},{8,0},{16,24},{24,16},{1,9},{9,1},{17,25},{25,17},{2,10},{10... | collective-permute-start | bytes 1622024 | tf_op jit(solution)/shard_map/ppermute | solution.py:282
  818.6 165.3 %collective-permute-start.73 = (bf16[1056,256]{1,0:T(8,128)(2,1)}, bf16[1056,256]{1,0:T(8,128)(2,1)}, u32[]{:S(2)}, u32[]{:S(2)}) collective-permute-start(bf16[1056,256]{1,0:T(8,128)(2,1)} %get-tuple-element.379), channel_id=1, source_target_pairs={{0,16},{8,24},{16,0},{24,8},{1,17},{9,25},{17,1},{25,9},{2,18},{10... | collective-permute-start | bytes 1622024 | tf_op jit(solution)/shard_map/ppermute | solution.py:282
  819.2 164.8 %collective-permute-start.74 = (bf16[1056,256]{1,0:T(8,128)(2,1)}, bf16[1056,256]{1,0:T(8,128)(2,1)}, u32[]{:S(2)}, u32[]{:S(2)}) collective-permute-start(bf16[1056,256]{1,0:T(8,128)(2,1)} %get-tuple-element.378), channel_id=1, source_target_pairs={{0,24},{8,16},{16,8},{24,0},{1,25},{9,17},{17,9},{25,1},{2,26},{10... | collective-permute-start | bytes 1622024 | tf_op jit(solution)/shard_map/ppermute | solution.py:282
  824.6 100.4 %collective-permute-start.70 = (bf16[64,2048]{1,0:T(8,128)(2,1)S(1)}, bf16[64,2048]{1,0:T(8,128)(2,1)S(1)}, u32[]{:S(2)}, u32[]{:S(2)}) collective-permute-start(bf16[64,2048]{1,0:T(8,128)(2,1)S(1)} %slice_bitcast_fusion.60), channel_id=1, source_target_pairs={{0,16},{8,24},{16,0},{24,8},{1,17},{9,25},{17,1},{25,9},{2,18},{10... | collective-permute-start | bytes 786440 | tf_op jit(solution)/shard_map/ppermute | solution.py:282
  825.2 107.5 %collective-permute-start.71 = (bf16[64,2048]{1,0:T(8,128)(2,1)S(1)}, bf16[64,2048]{1,0:T(8,128)(2,1)S(1)}, u32[]{:S(2)}, u32[]{:S(2)}) collective-permute-start(bf16[64,2048]{1,0:T(8,128)(2,1)S(1)} %slice_bitcast_fusion.59), channel_id=1, source_target_pairs={{0,16},{8,24},{16,0},{24,8},{1,17},{9,25},{17,1},{25,9},{2,18},{10... | collective-permute-start | bytes 786440 | tf_op jit(solution)/shard_map/ppermute | solution.py:282
  (177 other events, 2811.4 us)
Sparse Core Ops, SparseCore 0:
  10.2 96.6 all-gather.2
  108.5 48.3 all-gather.4
  724.2 75.4 reduce-scatter.4
  815.4 123.6 reduce-scatter.2

commit v4 on v3

--- a/solution.py
+++ b/solution.py
@@ -71,32 +71,34 @@
 EXTRA = 16
 
 
-def ffn_kernel(sizes, meta, rows_ref, cot_ref, mix_ref, logit_ref, *refs):
-    n_g, f_pad, f_shared, f_routed, local_experts, d_own = sizes
-    blocks = refs[: 6 * n_g]
-    out_ref, normed_ref, act_ref, gate_ref, up_ref = refs[6 * n_g : 6 * n_g + 5]
-    w_gu, w_down, sems = refs[6 * n_g + 5 :]
+def ffn_kernel(sizes, groups, meta, rows_ref, cot_ref, side_ref, *refs):
+    n_g, f_pad, f_one, d_own = sizes
+    blocks = refs[: groups * 2 * n_g]
+    sums = refs[groups * 2 * n_g : -8]
+    out_ref, normed_ref, act_ref, gate_ref, up_ref, w_gu, w_down, sems = refs[-8:]
     g_at, k_at, c_at = meta[0], meta[1], meta[2]
+    shared = groups == 1
 
     @pl.when(pl.program_id(0) == 0)
     def _():
         copies = []
         for half in range(2):
             for shift in range(n_g):
+                at = half * n_g + shift
                 column = 2 * (g_at ^ shift) + (k_at ^ half)
                 lanes = pl.ds(pl.multiple_of(column * d_own, d_own), d_own)
-                first = (half * n_g + shift) * 3
-                for kind, target in enumerate(
-                    (w_gu.at[:f_pad, lanes], w_gu.at[f_pad : 2 * f_pad, lanes], w_down.at[:, lanes])
-                ):
-                    copies.append(
-                        pltpu.make_async_copy(
-                            blocks[first + kind], target, sems.at[first + kind]
-                        )
-                    )
+                if shared:
+                    both, down = blocks[at].at[: 2 * f_pad], blocks[at].at[2 * f_pad :]
+                else:
+                    both, down = blocks[at], blocks[2 * n_g + at]
+                copies.append(
+                    pltpu.make_async_copy(both, w_gu.at[: 2 * f_pad, lanes], sems.at[2 * at])
+                )
+                copies.append(pltpu.make_async_copy(down, w_down.at[:, lanes], sems.at[2 * at + 1]))
         for copy in copies:
             copy.start()
-        w_gu[2 * f_pad :, :] = logit_ref[...]
+        if shared:
+            w_gu[2 * f_pad :, :] = side_ref[...]
         for copy in copies:
             copy.wait()
 
@@ -114,75 +116,89 @@
     pre = dot(w_gu[...], rows, minor)
     down_back = dot(w_down[...], cot, minor)
     gate_pre, up_pre = pre[:f_pad], pre[f_pad : 2 * f_pad]
-    prob = jax.nn.sigmoid(pre[2 * f_pad : 2 * f_pad + 1])
-    pieces = [jnp.broadcast_to(prob, (f_shared, count))]
-    for e in range(local_experts):
-        pieces.append(jnp.broadcast_to(mix_ref[0, e : e + 1, :], (f_routed, count)))
-    rest = f_pad - f_shared - local_experts * f_routed
-    if rest:
-        pieces.append(jnp.zeros((rest, count), F32))
-    scale = jnp.concatenate(pieces, axis=0)
+    if shared:
+        prob = jax.nn.sigmoid(pre[2 * f_pad : 2 * f_pad + 1])
+        scale = jnp.broadcast_to(prob, (f_pad, count))
+    else:
+        full = f_pad // f_one
+        pieces = [jnp.broadcast_to(side_ref[0, e : e + 1, :], (f_one, count)) for e in range(full)]
+        if f_pad > full * f_one:
+            pieces.append(jnp.zeros((f_pad - full * f_one, count), F32))
+        scale = jnp.concatenate(pieces, axis=0)
     sigma = jax.nn.sigmoid(gate_pre)
     silu = gate_pre * sigma
     act = silu * up_pre
-    prob_part = jnp.sum(act[:f_shared] * down_back[:f_shared], axis=0, keepdims=True)
     act_grad = down_back * scale
     act_low = (act * scale).astype(BF16)
     gate_low = (act_grad * up_pre * sigma * (1.0 + gate_pre * (1.0 - sigma))).astype(BF16)
     up_low = (act_grad * silu).astype(BF16)
-    logit_part = prob_part * prob * (1.0 - prob)
-    logit_high = logit_part.astype(BF16).astype(F32)
-    logit_rows = jnp.concatenate(
-        [logit_high, logit_part - logit_high, jnp.zeros((EXTRA - 2, count), F32)], axis=0
-    ).astype(BF16)
     act_ref[...] = act_low
     gate_ref[:f_pad, :] = gate_low
-    gate_ref[f_pad:, :] = logit_rows
     up_ref[...] = up_low
+    both = [gate_low, up_low]
+    if shared:
+        prob_part = jnp.sum(act * down_back, axis=0, keepdims=True)
+        logit_part = prob_part * prob * (1.0 - prob)
+        logit_high = logit_part.astype(BF16).astype(F32)
+        logit_rows = jnp.concatenate(
+            [logit_high, logit_part - logit_high, jnp.zeros((EXTRA - 2, count), F32)], axis=0
+        ).astype(BF16)
+        gate_ref[f_pad:, :] = logit_rows
+        both.append(logit_rows)
     major = ((0,), (0,))
-    out_ref[...] = dot(act_low, w_down[...], major).astype(BF16)
-    both = jnp.concatenate([gate_low, up_low, logit_rows], axis=0)
-    normed_ref[...] = dot(both, w_gu[...], major).astype(BF16)
-
-
-def ffn_pass(sizes, meta, rows, cot, mix, logit, blocks):
-    n_g, f_pad, _, _, local_experts, d_own = sizes
+    out = dot(act_low, w_down[...], major)
+    normed = dot(jnp.concatenate(both, axis=0), w_gu[...], major)
+    if sums:
+        out = out + sums[0][...].astype(F32)
+        normed = normed + sums[1][...].astype(F32)
+    out_ref[...] = out.astype(BF16)
+    normed_ref[...] = normed.astype(BF16)
+
+
+def ffn_pass(sizes, meta, rows, cot, side, blocks, sums):
+    n_g, f_pad, _, d_own = sizes
     total, dim = rows.shape
     n_c, _, _, sub, cw = cot.shape
     tile = n_c * sub
+    groups = len(blocks) // (2 * n_g)
+    extra = EXTRA if groups == 1 else 0
     flat = lambda i, m: (i, 0)
     wide = lambda i, m: (0, i)
-    any_spec = pl.BlockSpec(memory_space=pl.ANY)
+    if groups == 1:
+        side_spec = pl.BlockSpec((EXTRA, dim), lambda i, m: (0, 0))
+    else:
+        side = side.reshape(-1, tile, 8).transpose(0, 2, 1)
+        side_spec = pl.BlockSpec((1, 8, tile), lambda i, m: (i, 0, 0))
     return pl.pallas_call(
-        functools.partial(ffn_kernel, sizes),
+        functools.partial(ffn_kernel, sizes, groups),
         grid_spec=pltpu.PrefetchScalarGridSpec(
             num_scalar_prefetch=1,
             grid=(n_g,),
             in_specs=[
                 pl.BlockSpec((tile, dim), flat),
                 pl.BlockSpec((n_c, 1, n_c, sub, cw), lambda i, m: (0, i, 0, 0, 0)),
-                pl.BlockSpec((1, 8, tile), lambda i, m: (i, 0, 0)),
-                pl.BlockSpec((EXTRA, dim), lambda i, m: (0, 0)),
+                side_spec,
             ]
-            + [any_spec] * (6 * n_g),
+            + [pl.BlockSpec(memory_space=pl.ANY)] * len(blocks)
+            + [pl.BlockSpec((tile, dim), flat)] * len(sums),
             out_specs=[
                 pl.BlockSpec((tile, dim), flat),
                 pl.BlockSpec((tile, dim), flat),
                 pl.BlockSpec((f_pad, tile), wide),
-                pl.BlockSpec((f_pad + EXTRA, tile), wide),
+                pl.BlockSpec((f_pad + extra, tile), wide),
                 pl.BlockSpec((f_pad, tile), wide),
             ],
             scratch_shapes=[
-                pltpu.VMEM((2 * f_pad + EXTRA, dim), BF16),
+                pltpu.VMEM((2 * f_pad + extra, dim), BF16),
                 pltpu.VMEM((f_pad, dim), BF16),
-                pltpu.SemaphoreType.DMA((6 * n_g,)),
+                pltpu.SemaphoreType.DMA((4 * n_g,)),
             ],
         ),
         out_shape=[
             jax.ShapeDtypeStruct((total, dim), BF16),
             jax.ShapeDtypeStruct((total, dim), BF16),
             jax.ShapeDtypeStruct((f_pad, total), BF16),
-            jax.ShapeDtypeStruct((f_pad + EXTRA, total), BF16),
+            jax.ShapeDtypeStruct((f_pad + extra, total), BF16),
             jax.ShapeDtypeStruct((f_pad, total), BF16),
         ],
         compiler_params=pltpu.CompilerParams(
@@ -190,74 +206,84 @@
         ),
         cost_estimate=pl.CostEstimate(
             flops=12 * total * dim * f_pad,
-            bytes_accessed=8 * total * dim + 6 * total * f_pad + 6 * f_pad * dim,
+            bytes_accessed=(8 + 4 * len(sums)) * total * dim + 6 * total * f_pad + 6 * f_pad * dim,
             transcendentals=total * f_pad,
         ),
         name="ffn_pass",
-    )(meta, rows, cot, mix.reshape(-1, tile, 8).transpose(0, 2, 1), logit, *blocks)
-
-
-def grad_kernel(parts, f_pad, meta, *refs):
-    total = None
-    for left, right in zip(refs[:parts], refs[parts : 2 * parts]):
-        value = right[...]
-        if len(value.shape) > 2:
-            _, n_g, n_c, sub, _ = right.shape
-            value = jnp.concatenate(
-                [right[0, g, row ^ meta[2]] for g in range(n_g) for row in range(n_c)], axis=0
+    )(meta, rows, cot, side, *blocks, *sums)
+
+
+def grad_kernel(parts, kinds, f_pad, meta, *refs):
+    lefts, refs = refs[: parts * len(kinds)], refs[parts * len(kinds) :]
+    values = {}
+    for cot in sorted(set(kinds)):
+        rights, refs = refs[:parts], refs[parts:]
+        if cot:
+            _, n_g, n_c, _, _ = rights[0].shape
+            order = [(g, c) for g in range(n_g) for c in range(n_c)]
+            values[cot] = [
+                jnp.concatenate([right[0, g, c ^ meta[2]] for g, c in order], axis=0)
+                for right in rights
+            ]
+        else:
+            values[cot] = [right[...] for right in rights]
+    for i, cot in enumerate(kinds):
+        total = None
+        for left, value in zip(lefts[i * parts : (i + 1) * parts], values[cot]):
+            term = dot(left[...], value, ((1,), (0,)))
+            total = term if total is None else total + term
+        refs[0][0, 0, i * f_pad : (i + 1) * f_pad] = total[:f_pad].astype(BF16)
+        if total.shape[0] > f_pad:
+            refs[1][...] = jnp.broadcast_to(
+                total[f_pad : f_pad + 1] + total[f_pad + 1 : f_pad + 2], refs[1].shape
             )
-        term = dot(left[...], value, ((1,), (0,)))
-        total = term if total is None else total + term
-    refs[2 * parts][0, 0] = total[:f_pad].astype(BF16)
-    if len(refs) > 2 * parts + 1:
-        refs[2 * parts + 1][...] = jnp.broadcast_to(
-            total[f_pad : f_pad + 1] + total[f_pad + 1 : f_pad + 2], refs[2 * parts + 1].shape
-        )
-
-
-def weight_grad(sizes, meta, lefts, rights, cot):
-    n_g, f_pad, _, _, _, d_own = sizes
-    parts = len(lefts)
-    f_rows, part_rows = lefts[0].shape
-    dim = 2 * n_g * d_own
-    if cot:
-        n_c, _, _, sub, cw = rights[0].shape
-        per = cw // d_own
-        right_specs = [
+
+
+def weight_grad(sizes, meta, kinds, lefts, normed, cots):
+    n_g, f_pad, _, d_own = sizes
+    parts = len(normed)
+    part_rows, dim = normed[0].shape
+    extra = max(value[0].shape[0] for value in lefts) > f_pad
+    n_c, _, _, sub, cw = cots[0].shape
+    per = cw // d_own
+    arrays, specs = [], []
+    for values in lefts:
+        arrays += values
+        specs += [pl.BlockSpec(values[0].shape, lambda j, m: (0, 0))] * parts
+    if False in kinds:
+        arrays += normed
+        specs += [pl.BlockSpec((part_rows, d_own), lambda j, m: (0, j))] * parts
+    if True in kinds:
+        arrays += cots
+        specs += [
             pl.BlockSpec(
                 (1, n_g, n_c, sub, d_own), lambda j, m: ((j // per) ^ m[2], 0, 0, 0, j % per)
             )
         ] * parts
-    else:
-        right_specs = [pl.BlockSpec((part_rows, d_own), lambda j, m: (0, j))] * parts
+    f_out = len(kinds) * f_pad
     out_specs = [
-        pl.BlockSpec(
-            (1, 1, f_pad, d_own), lambda j, m: ((j % 2) ^ m[1], (j // 2) ^ m[0], 0, 0)
-        )
+        pl.BlockSpec((1, 1, f_out, d_own), lambda j, m: ((j % 2) ^ m[1], (j // 2) ^ m[0], 0, 0))
     ]
-    out_shape = [jax.ShapeDtypeStruct((2, n_g, f_pad, d_own), BF16)]
-    if f_rows > f_pad:
+    out_shape = [jax.ShapeDtypeStruct((2, n_g, f_out, d_own), BF16)]
+    if extra:
         out_specs.append(pl.BlockSpec((8, d_own), lambda j, m: (0, j)))
         out_shape.append(jax.ShapeDtypeStruct((8, dim), F32))
     return pl.pallas_call(
-        functools.partial(grad_kernel, parts, f_pad),
+        functools.partial(grad_kernel, parts, kinds, f_pad),
         grid_spec=pltpu.PrefetchScalarGridSpec(
-            num_scalar_prefetch=1,
-            grid=(2 * n_g,),
-            in_specs=[pl.BlockSpec((f_rows, part_rows), lambda j, m: (0, 0))] * parts + right_specs,
-            out_specs=out_specs,
+            num_scalar_prefetch=1, grid=(2 * n_g,), in_specs=specs, out_specs=out_specs
         ),
         out_shape=out_shape,
         compiler_params=pltpu.CompilerParams(
-            dimension_semantics=("arbitrary",), vmem_limit_bytes=48 * 1024 * 1024
+            dimension_semantics=("arbitrary",), vmem_limit_bytes=56 * 1024 * 1024
         ),
         cost_estimate=pl.CostEstimate(
-            flops=2 * parts * part_rows * dim * f_rows,
-            bytes_accessed=2 * parts * part_rows * (dim + f_rows) + 2 * f_pad * dim,
+            flops=2 * parts * part_rows * dim * f_out,
+            bytes_accessed=2 * parts * part_rows * (dim + f_out) + 2 * f_out * dim,
             transcendentals=0,
         ),
         name="weight_grad",
-    )(meta, *lefts, *rights)
+    )(meta, *arrays)
 
 
 def tie(*values):
@@ -378,26 +404,26 @@
     )
     f_shared = shared_gate.shape[1] // n_g
     f_routed = expert_gate.shape[2] // n_g
-    f_all = f_shared + local_experts * f_routed
-    f_pad = -(-f_all // 16) * 16
-    sizes = (n_g, f_pad, f_shared, f_routed, local_experts, d_own)
+    f_experts = local_experts * f_routed
+    f_one, f_two = -(-f_shared // 16) * 16, -(-f_experts // 16) * 16
+    sizes_s = (n_g, f_one, f_shared, d_own)
+    sizes_e = (n_g, f_two, f_routed, d_own)
     meta = jnp.stack([at_g, at_k, at_c]).astype(jnp.int32)
 
-    def slices(shared, routed):
-        parts = [
-            shared.reshape(n_g, f_shared, d_own),
-            routed.reshape(local_experts, n_g, f_routed, d_own)
-            .transpose(1, 0, 2, 3)
-            .reshape(n_g, -1, d_own),
-        ]
-        if f_pad > f_all:
-            parts.append(jnp.zeros((n_g, f_pad - f_all, d_own), BF16))
-        return jnp.concatenate(parts, axis=1)
+    def fill(value, size):
+        return jnp.pad(value, ((0, 0), (0, size - value.shape[1]), (0, 0)))
+
+    def slices_s(value):
+        return fill(value.reshape(n_g, f_shared, d_own), f_one)
+
+    def slices_e(value):
+        value = value.reshape(local_experts, n_g, f_routed, d_own).transpose(1, 0, 2, 3)
+        return fill(value.reshape(n_g, f_experts, d_own), f_two)
 
     weight_slices = [
-        slices(shared_gate.T, expert_gate.transpose(1, 2, 0)),
-        slices(shared_up.T, expert_up.transpose(1, 2, 0)),
-        slices(shared_down, expert_down),
+        jnp.concatenate([slices_s(w) for w in (shared_gate.T, shared_up.T, shared_down)], axis=1),
+        jnp.concatenate([slices_e(w.transpose(1, 2, 0)) for w in (expert_gate, expert_up)], axis=1),
+        slices_e(expert_down),
     ]
     picked = [[pick(value, at_g ^ shift) for shift in range(n_g)] for value in weight_slices]
     picked[0], small_all = tie(picked[0], small_all)
@@ -460,7 +486,6 @@
     probabilities = exp_scores / jnp.sum(exp_scores, axis=-1, keepdims=True)
     prob_low = probabilities.astype(BF16)
     mixed = einsum("bhqk,bkhd->bqhd", prob_low, value_low).astype(BF16).reshape(span, width)
-    own_blocks[1], mixed = tie(own_blocks[1], mixed)
     attention = col_sum(dot(mixed, out_w, ((1,), (0,))), n_c)
 
     own_inputs = lax.dynamic_slice_in_dim(inputs, at_c * own_rows, own_rows, 0)
@@ -469,10 +494,8 @@
     second_scale = lax.rsqrt(jnp.mean(hidden * hidden, axis=-1, keepdims=True) + epsilon)
     unit_2 = hidden * second_scale
     normed_own = (unit_2 * gain_2).astype(BF16)
-    own_blocks[2], normed_own = tie(own_blocks[2], normed_own)
-
-    def gather_rows(rows):
-        value = gather_joined(rows[None], "g", 0)[:, None, None]
+
+    def gather_cols(value):
         sides = []
         for side, order in enumerate((("y", "x"), ("x", "y"))):
             half = value[..., side * (dim // 2) : (side + 1) * (dim // 2)]
@@ -481,7 +504,18 @@
             sides.append(half)
         return jnp.concatenate(sides, axis=-1).reshape(-1, dim)
 
-    normed_parts = [gather_rows(normed_own[part * sub : (part + 1) * sub]) for part in range(PARTS)]
+    routed_gu, routed_d = own_blocks[1:]
+    routed_gu[1], normed_own = tie(routed_gu[1], normed_own)
+    halves = [normed_own[part * sub : (part + 1) * sub][None] for part in range(PARTS)]
+    halves[0] = gather_joined(halves[0], "g", 0)
+    halves[0], halves[1], routed_gu[2:3] = tie(halves[0], halves[1], routed_gu[2:3])
+    halves[1] = gather_joined(halves[1], "g", 0)
+    normed_parts = [gather_cols(halves[0][:, None, None])]
+    normed_parts[0], halves[1], routed_gu[3:], routed_d[1] = tie(
+        normed_parts[0], halves[1], routed_gu[3:], routed_d[1]
+    )
+    normed_parts.append(gather_cols(halves[1][:, None, None]))
+    normed_parts[1], routed_d[2:3] = tie(normed_parts[1], routed_d[2:3])
     own_cot = [
         lax.dynamic_index_in_dim(cot[:, 0], at_c, 1, keepdims=False) for cot in cot_all
     ]
@@ -489,30 +523,66 @@
     own_cot = jnp.stack([pick(own_cot, at_c ^ c) for c in range(n_c)], axis=1)
     own_cot = own_cot.reshape(own_rows, dim)
 
+    def own_core(grad):
+        other = swap(grad[1], "k")
+        return (grad[0].astype(F32) + other.astype(F32)).astype(BF16)
+
+    def send_slices(both):
+        return [shift_by(both[shift], "g", shift) for shift in range(n_g)]
+
+    def place_slices(moved, kinds):
+        moved = jnp.stack(moved)
+        moved = jnp.stack([pick(moved, at_g ^ source) for source in range(n_g)])
+        return [
+            moved[:, i * (moved.shape[1] // kinds) :][:, : moved.shape[1] // kinds]
+            for i in range(kinds)
+        ]
+
+    def place_s(value):
+        return value[:, :f_shared].reshape(n_g * f_shared, d_own)
+
+    def place_e(value):
+        value = value[:, :f_experts].reshape(n_g, local_experts, f_routed, d_own)
+        return value.transpose(1, 0, 2, 3).reshape(local_experts, n_g * f_routed, d_own)
+
     logit_low = jnp.zeros((EXTRA, dim), BF16).at[:2].set(logit_w.astype(BF16)[None])
     mixing_parts = mixing_own.reshape(n_g, n_c, PARTS, sub, local_experts)
     mixing_parts = jnp.stack([pick(mixing_parts, at_g ^ shift) for shift in range(n_g)])
     mixing_parts = jnp.stack([pick(mixing_parts, at_c ^ c, 1) for c in range(n_c)], axis=1)
     mixing_parts = jnp.pad(mixing_parts, ((0, 0),) * 4 + ((0, 8 - local_experts),))
-    swapped = [[swap(value, "k") for value in values] for values in own_blocks]
-    weight_blocks = [
-        values[shift]
-        for half in (own_blocks, swapped)
-        for shift in range(n_g)
-        for values in half
-    ]
-    passes = [
-        ffn_pass(
-            sizes,
-            meta,
-            normed_parts[part],
-            cot_all[part],
-            mixing_parts[:, :, part].reshape(-1, 8),
-            logit_low,
-            weight_blocks,
-        )
+    def blocks_of(values):
+        return values + [swap(value, "k") for value in values]
+
+    blocks_s = blocks_of(own_blocks[0])
+    passes_s = [
+        ffn_pass(sizes_s, meta, normed_parts[part], cot_all[part], logit_low, blocks_s, [])
         for part in range(PARTS)
     ]
+    kinds = (False, False, True)
+    grad_s, logit_sum = weight_grad(
+        sizes_s, meta, kinds, [[p[i] for p in passes_s] for i in (3, 4, 2)], normed_parts, cot_all
+    )
+    logit_sum = logit_sum[0]
+    sums = [[passes_s[part][0], passes_s[part][1]] for part in range(PARTS)]
+    sums[0], grad_s = tie(sums[0], grad_s)
+    blocks_e = blocks_of(own_blocks[1]) + blocks_of(own_blocks[2])
+    passes = []
+    for part in range(PARTS):
+        if part == 1:
+            both_s = own_core(grad_s)
+            sums[1], both_s = tie(sums[1], both_s)
+        passes.append(
+            ffn_pass(
+                sizes_e,
+                meta,
+                normed_parts[part],
+                cot_all[part],
+                mixing_parts[:, :, part].reshape(-1, 8),
+                blocks_e,
+                sums[part],
+            )
+        )
+    moved_s = send_slices(both_s)
 
     def split_sides(partial):
         part = partial.reshape(n_g, n_y, n_x, sub, dim)
@@ -543,53 +613,34 @@
         other = shift_by(value[1], "g", n_g // 2)
         return value[0].astype(F32) + other.astype(F32)
 
-    def own_core(grad):
-        other = swap(grad[1], "k")
-        return (grad[0].astype(F32) + other.astype(F32)).astype(BF16)
-
-    def send_slices(both):
-        return [shift_by(both[shift], "g", shift) for shift in range(n_g)]
-
-    def place_slices(moved):
-        moved = jnp.stack(moved)
-        moved = jnp.stack([pick(moved, at_g ^ source) for source in range(n_g)])
-        shared = moved[:, :f_shared].reshape(n_g * f_shared, d_own)
-        routed = moved[:, f_shared:f_all].reshape(n_g, local_experts, f_routed, d_own)
-        routed = routed.transpose(1, 0, 2, 3).reshape(local_experts, n_g * f_routed, d_own)
-        return (shared, routed)
-
     acts, gates, ups = ([parts[i] for parts in passes] for i in (2, 3, 4))
     first = cols_first(split_sides(passes[0][1]))
     first, acts = tie(first, acts)
-    (down_blocks,) = weight_grad(sizes, meta, acts, cot_all, True)
+    (grad_d,) = weight_grad(sizes_e, meta, (True,), [acts], normed_parts, cot_all)
     first = cols_second(first)
     second = cols_first(split_sides(passes[1][1]))
-    first, second, gates, down_blocks = tie(first, second, gates, down_blocks)
-    gate_blocks, logit_sum = weight_grad(sizes, meta, gates, normed_parts, False)
-    logit_sum = logit_sum[0]
+    first, second, gates, grad_d = tie(first, second, gates, grad_d)
+    (grad_gu,) = weight_grad(sizes_e, meta, (False, False), [gates, ups], normed_parts, cot_all)
     first = chips_steps(first)
     second = cols_second(second)
-    down_both = own_core(down_blocks)
-    first, second, down_both, ups, gate_blocks = tie(first, second, down_both, ups, gate_blocks)
-    down_moved = send_slices(down_both)
-    (up_blocks,) = weight_grad(sizes, meta, ups, normed_parts, False)
+    both_d = own_core(grad_d)
+    first, second, both_d, moved_s, grad_gu = tie(first, second, both_d, moved_s, grad_gu)
+    moved_d = send_slices(both_d)
     first = chips_last(first)
     second = chips_steps(second)
-    gate_both = own_core(gate_blocks)
-    first, second, gate_both, up_blocks = tie(first, second, gate_both, up_blocks)
+    both_gu = own_core(grad_gu)
+    first, second, both_gu = tie(first, second, both_gu)
     second = chips_last(second)
-    up_both = own_core(up_blocks)
     out_sides = [cols_first(split_sides(parts[0])) for parts in passes]
     normed_grad_2 = jnp.concatenate([first, second], axis=0)
-    normed_grad_2, up_both = tie(normed_grad_2, up_both)
     hidden_part, gain_2_sum = norm_back(normed_grad_2, unit_2, second_scale, gain_2)
     hidden_grad = own_cot.astype(F32) + hidden_part
-    gate_moved = send_slices(gate_both)
-    up_moved = send_slices(up_both)
+    moved_gu = send_slices(both_gu)
     attn_grad = col_gather(hidden_grad.astype(BF16), n_c).reshape(span, dim)
-    out_sides, attn_grad, down_moved = tie(out_sides, attn_grad, down_moved)
+    out_sides, attn_grad, moved_d = tie(out_sides, attn_grad, moved_d)
     out_parts = [cols_second(sides) for sides in out_sides]
-    down_s, down_e = place_slices(down_moved)
+    gate_s, up_s, down_s = (place_s(value) for value in place_slices(moved_s, 3))
+    down_e = place_e(place_slices(moved_d, 1)[0])
 
     out_grad = dot(attn_grad, mixed, ((0,), (0,)))
     mixed_grad = dot(attn_grad, out_w, ((1,), (1,))).astype(BF16).reshape(head_shape)
@@ -604,13 +655,12 @@
     qkv_grad = jnp.concatenate(
         [part.reshape(span, width) for part in (query_grad, key_grad, value_grad)], axis=1
     )
-    qkv_grad, gate_moved, out_parts = tie(qkv_grad, gate_moved, out_parts)
+    qkv_grad, out_parts = tie(qkv_grad, out_parts)
     out_rows = jnp.concatenate([chips_last(part) for part in out_parts], axis=0)
-    gate_s, gate_e = place_slices(gate_moved)
     qkv_sum = dot(normed_1, qkv_grad, ((0,), (0,)))
     normed_grad_1 = col_sum(dot(qkv_grad, qkv, ((1,), (1,))), n_c)
-    normed_grad_1, up_moved = tie(normed_grad_1, up_moved)
-    up_s, up_e = place_slices(up_moved)
+    normed_grad_1, moved_gu, out_rows = tie(normed_grad_1, moved_gu, out_rows)
+    gate_e, up_e = (place_e(value) for value in place_slices(moved_gu, 2))
     own_scale = lax.dynamic_slice_in_dim(first_scale, at_c * own_rows, own_rows, 0)
     rows_part, gain_1_sum = norm_back(normed_grad_1, own_inputs * own_scale, own_scale, gain_1)
     token_grad = rows_to_features((hidden_grad + rows_part).astype(BF16), n_c).astype(F32)

time: 1030 us -> 1060 us (1.029)
  waiting for transfers between devices: 400 us -> 444 us
  Pallas kernels: 137 us -> 159 us
  starting transfers between devices: 167 us -> 153 us
    ppermute x60, waiting for transfers between devices: 366 us -> 421 us  [shift_by(): lax.ppermute(value, axis, [(i, i ^ shift) for i in range(lax.axis_size(ax...]
    ppermute x60, starting transfers between devices: 128 us -> 105 us  [shift_by(): lax.ppermute(value, axis, [(i, i ^ shift) for i in range(lax.axis_size(ax...]
    pallas_call x5 -> x7, Pallas kernels: 137 us -> 159 us  [the longest x4 112 us: ffn_pass(): pl.pallas_call(functools.partial(ffn_kernel, sizes, groups), grid_spec=pl...]
    all_to_all x2, waiting for transfers between devices: 23.6 us -> 12.6 us  [col_sum(): lax.all_to_all(parts, COL, 0, 0, tiled=True).astype(F32)]
    unnamed x247 -> x206, local copies, waits for them, and re-layouts: 37 us -> 32.3 us
  transfers between devices with their start and end apart: 88 -> 90, of which waited for: 29 -> 33; matrix products, arithmetic and copies ran while one was open for 27% -> 24% of each run, Pallas kernels for 13% -> 12%
where the time goes in v4:
time: 1060 us
  waiting for transfers between devices  444 us (42%)
  Pallas kernels  159 us (15%)
  starting transfers between devices  153 us (14%)
  local copies, waits for them, and re-layouts  123 us (12%)
  other arithmetic  110 us (10%)
  matrix products  47.2 us (4%)
  between operations  16.5 us (2%)
    ppermute x60, waiting for transfers between devices, shift_by(): lax.ppermute(value, axis, [(i, i ^ shift) for i in range(lax.axis_size(ax...  421 us
    pallas_call x4, Pallas kernels, ffn_pass(): pl.pallas_call(functools.partial(ffn_kernel, sizes, groups), grid_spec=pl...  112 us
    ppermute x60, starting transfers between devices, shift_by(): lax.ppermute(value, axis, [(i, i ^ shift) for i in range(lax.axis_size(ax...  105 us
    pallas_call x3, Pallas kernels, weight_grad(): pl.pallas_call(functools.partial(grad_kernel, parts, kinds, f_pad), grid_...  47.3 us
    unnamed x206, local copies, waits for them, and re-layouts  32.3 us
    dot_general x6, matrix products, dot(): lax.dot_general(left, right, (dims, ((), ())), preferred_element_type=F32)  29.7 us
    squeeze x16, other arithmetic, scatter_axis(): return lax.index_in_dim(value, 0, at, keepdims=False)  25.1 us
    another operation x15, other arithmetic, gather_joined(): jnp.stack([value, shift_by(value, axis, bit)], axis=at + 1).reshape(shape)  22.8 us
  transfers between devices with their start and end apart: 90, of which 33 were waited for; matrix products, arithmetic and copies ran while one was open for 24% of the time, Pallas kernels for 12%

profile of v4, /device:TPU:0, one launch (start us, length us, event | category | flops | bytes accessed | tf_op | source)
XLA Modules:
  0.0 1056.3 jit_solution(3456489285558428127)
XLA Ops:
  31.7 43.4 %collective-permute-done.3 = bf16[1,4,2,64,512]{4,3,2,1,0:T(8,128)(2,1)} collective-permute-done((bf16[1,4,2,64,512]{4,3,2,1,0:T(8,128)(2,1)S(1)}, bf16[1,4,2,64,512]{4,3,2,1,0:T(8,128)(2,1)}, u32[]{:S(2)}, u32[]{:S(2)}) %collective-permute-start.3) | collective-permute-done | bytes 524320 | tf_op jit(solution)/shard_map/ppermute | solution.py:308
  96.7 41.1 %collective-permute-done.4 = bf16[2,4,2,64,512]{4,3,2,1,0:T(8,128)(2,1)} collective-permute-done((bf16[2,4,2,64,512]{4,3,2,1,0:T(8,128)(2,1)}, bf16[2,4,2,64,512]{4,3,2,1,0:T(8,128)(2,1)}, u32[]{:S(2)}, u32[]{:S(2)}) %collective-permute-start.4) | collective-permute-done | bytes 1048608 | tf_op jit(solution)/shard_map/ppermute | solution.py:308
  156.3 12.5 %collective-permute-done.2.refs_3_ = bf16[1056,256]{1,0:T(8,128)(2,1)} collective-permute-done((bf16[1056,256]{1,0:T(8,128)(2,1)}, bf16[1056,256]{1,0:T(8,128)(2,1)}, u32[]{:S(2)}, u32[]{:S(2)}) %collective-permute-start.2) | collective-permute-done | bytes 540704 | tf_op jit(solution)/shard_map/ppermute | solution.py:308
  234.2 12.6 %all-to-all-done.4 = bf16[4,128,2048]{2,1,0:T(8,128)(2,1)} async-done(((bf16[4,128,2048]{2,1,0:T(8,128)(2,1)}), bf16[4,128,2048]{2,1,0:T(8,128)(2,1)}, u32[]{:S(2)}, u32[]{:S(2)}) %all-to-all-start.4) | async-done | bytes 2097184 | tf_op jit(solution)/shard_map/all_to_all | solution.py:336
  269.4 19.6 %collective-permute-done.11 = bf16[2,64,2048]{2,1,0:T(8,128)(2,1)S(1)} collective-permute-done((bf16[2,64,2048]{2,1,0:T(8,128)(2,1)S(1)}, bf16[2,64,2048]{2,1,0:T(8,128)(2,1)S(1)}, u32[]{:S(2)}, u32[]{:S(2)}) %collective-permute-start.11) | collective-permute-done | bytes 524320 | tf_op jit(solution)/shard_map/ppermute | solution.py:308
  289.1 11.7 %collective-permute-done.12.refs_2_ = bf16[1408,256]{1,0:T(8,128)(2,1)S(1)} collective-permute-done((bf16[1408,256]{1,0:T(8,128)(2,1)S(1)}, bf16[1408,256]{1,0:T(8,128)(2,1)S(1)}, u32[]{:S(2)}, u32[]{:S(2)}) %collective-permute-start.12) | collective-permute-done | bytes 720928 | tf_op jit(solution)/shard_map/ppermute | solution.py:308
  302.4 11.5 %collective-permute-done.15 = bf16[4,1,1,64,1024]{4,3,0,2,1:T(8,128)(2,1)S(1)} collective-permute-done((bf16[4,1,1,64,1024]{4,3,0,2,1:T(8,128)(2,1)S(1)}, bf16[4,1,1,64,1024]{4,3,0,2,1:T(8,128)(2,1)S(1)}, u32[]{:S(2)}, u32[]{:S(2)}) %collective-permute-start.15) | collective-permute-done | bytes 524320 | tf_op jit(solution)/shard_map/ppermute | solution.py:308
  323.7 24.7 %collective-permute-done.18 = bf16[2,64,2048]{2,1,0:T(8,128)(2,1)} collective-permute-done((bf16[2,64,2048]{2,1,0:T(8,128)(2,1)}, bf16[2,64,2048]{2,1,0:T(8,128)(2,1)}, u32[]{:S(2)}, u32[]{:S(2)}) %collective-permute-start.18) | collective-permute-done | bytes 524320 | tf_op jit(solution)/shard_map/ppermute | solution.py:308
  376.7 21.2 %ffn_pass.4 = (bf16[1024,2048]{1,0:T(8,128)(2,1)}, bf16[1024,2048]{1,0:T(8,128)(2,1)}, bf16[352,1024]{1,0:T(8,128)(2,1)}, bf16[368,1024]{1,0:T(8,128)(2,1)}, bf16[352,1024]{1,0:T(8,128)(2,1)}) custom-call(s32[3]{0:T(128)} %pad_add_fusion.meta, bf16[1024,2048]{1,0:T(8,128)(2,1)} %pad_maximum_fusion.2.rows_ref.refs_6_.refs_4_, ...), custom_call_target="tpu_custom_call" | custom-call | flops 8858370048 | bytes 23265280 | tf_op jit(solution)/shard_map/ffn_pass/pallas_call | solution.py:172
  404.7 21.0 %ffn_pass.5 = (bf16[1024,2048]{1,0:T(8,128)(2,1)}, bf16[1024,2048]{1,0:T(8,128)(2,1)}, bf16[352,1024]{1,0:T(8,128)(2,1)}, bf16[368,1024]{1,0:T(8,128)(2,1)}, bf16[352,1024]{1,0:T(8,128)(2,1)}) custom-call(s32[3]{0:T(128)} %pad_add_fusion.meta, bf16[1024,2048]{1,0:T(8,128)(2,1)} %pad_maximum_fusion.3.rows_ref.refs_7_.refs_5_, ...), custom_call_target="tpu_custom_call" | custom-call | flops 8858370048 | bytes 23265280 | tf_op jit(solution)/shard_map/ffn_pass/pallas_call | solution.py:172
  426.0 16.6 %weight_grad.3 = (bf16[2,4,1056,256]{3,2,1,0:T(8,128)(2,1)}, f32[8,2048]{1,0:T(8,128)}) custom-call(s32[3]{0:T(128)} %pad_add_fusion.meta, bf16[368,1024]{1,0:T(8,128)(2,1)} %get-tuple-element.193.refs_0_, bf16[368,1024]{1,0:T(8,128)(2,1)} %get-tuple-element.196.refs_1_, bf16[352,1024]{1,0:T(8,128)(2,1)} %get-tuple-element.197.refs_2_, ...), custom_call_target="tpu_custom_call" | custom-call | flops 8858370048 | bytes 17039360 | tf_op jit(solution)/shard_map/weight_grad/pallas_call | solution.py:271
  447.9 35.0 %ffn_pass.6 = (bf16[1024,2048]{1,0:T(8,128)(2,1)}, bf16[1024,2048]{1,0:T(8,128)(2,1)}, bf16[704,1024]{1,0:T(8,128)(2,1)}, bf16[704,1024]{1,0:T(8,128)(2,1)}, bf16[704,1024]{1,0:T(8,128)(2,1)}) custom-call(s32[3]{0:T(128)} %pad_add_fusion.meta, bf16[1024,2048]{1,0:T(8,128)(2,1)} %pad_maximum_fusion.2.rows_ref.refs_6_.refs_4_, ...), custom_call_target="tpu_custom_call" | custom-call | flops 17716740096 | bytes 46530560 | tf_op jit(solution)/shard_map/ffn_pass/pallas_call | solution.py:172
  498.5 14.1 %collective-permute-done.45 = bf16[4,1,2,64,1024]{4,3,0,2,1:T(8,128)(2,1)} collective-permute-done((bf16[4,1,2,64,1024]{4,3,0,2,1:T(8,128)(2,1)}, bf16[4,1,2,64,1024]{4,3,0,2,1:T(8,128)(2,1)}, u32[]{:S(2)}, u32[]{:S(2)}) %collective-permute-start.45) | collective-permute-done | bytes 1048608 | tf_op jit(solution)/shard_map/ppermute | solution.py:308
  520.5 34.7 %ffn_pass.7 = (bf16[1024,2048]{1,0:T(8,128)(2,1)}, bf16[1024,2048]{1,0:T(8,128)(2,1)}, bf16[704,1024]{1,0:T(8,128)(2,1)}, bf16[704,1024]{1,0:T(8,128)(2,1)}, bf16[704,1024]{1,0:T(8,128)(2,1)}) custom-call(s32[3]{0:T(128)} %pad_add_fusion.meta, bf16[1024,2048]{1,0:T(8,128)(2,1)} %pad_maximum_fusion.3.rows_ref.refs_7_.refs_5_, ...), custom_call_target="tpu_custom_call" | custom-call | flops 17716740096 | bytes 46530560 | tf_op jit(solution)/shard_map/ffn_pass/pallas_call | solution.py:172
  567.6 10.9 %collective-permute-start.54 = (bf16[1056,256]{1,0:T(8,128)(2,1)}, bf16[1056,256]{1,0:T(8,128)(2,1)}, u32[]{:S(2)}, u32[]{:S(2)}) collective-permute-start(bf16[1056,256]{1,0:T(8,128)(2,1)} %get-tuple-element.415), channel_id=1, source_target_pairs={{0,8},{8,0},{16,24},{24,16},{1,9},{9,1},{17,25},{25,17},{2,10},{10... | collective-permute-start | bytes 1622024 | tf_op jit(solution)/shard_map/ppermute | solution.py:308
  578.5 12.6 %weight_grad.4 = bf16[2,4,704,256]{3,2,1,0:T(8,128)(2,1)} custom-call(s32[3]{0:T(128)} %pad_add_fusion.meta, bf16[704,1024]{1,0:T(8,128)(2,1)} %get-tuple-element.219.refs_0_, bf16[704,1024]{1,0:T(8,128)(2,1)} %get-tuple-element.220.refs_1_, bf16[4,4,4,64,512]{4,3,2,1,0:T(8,128)(2,1)} %bitcast.604, bf16[4,4,4,64,512]{4,3,2,1,0:T(8,128)(2,1)} %bitcast.609), custom_call_target="tpu_custom_call" | custom-call | flops 5905580032 | bytes 14155776 | tf_op jit(solution)/shard_map/weight_grad/pallas_call | solution.py:271
  595.1 11.0 %collective-permute-start.55 = (bf16[1056,256]{1,0:T(8,128)(2,1)}, bf16[1056,256]{1,0:T(8,128)(2,1)}, u32[]{:S(2)}, u32[]{:S(2)}) collective-permute-start(bf16[1056,256]{1,0:T(8,128)(2,1)} %get-tuple-element.414), channel_id=1, source_target_pairs={{0,16},{8,24},{16,0},{24,8},{1,17},{9,25},{17,1},{25,9},{2,18},{10... | collective-permute-start | bytes 1622024 | tf_op jit(solution)/shard_map/ppermute | solution.py:308
  615.3 18.1 %weight_grad.5 = bf16[2,4,1408,256]{3,2,1,0:T(8,128)(2,1)} custom-call(s32[3]{0:T(128)} %pad_add_fusion.meta, bf16[704,1024]{1,0:T(8,128)(2,1)} %get-tuple-element.226.refs_0_, bf16[704,1024]{1,0:T(8,128)(2,1)} %get-tuple-element.227.refs_1_, bf16[704,1024]{1,0:T(8,128)(2,1)} %get-tuple-element.228.refs_2_, bf16[704,1024]{1,0:T(8,128)(2,1)} %get-tuple-element.229.refs_3_, ...), custom_call_target="tpu_custom_call" | custom-call | flops 11811160064 | bytes 19922944 | tf_op jit(solution)/shard_map/weight_grad/pallas_call | solution.py:271
  636.9 10.6 %collective-permute-done.50 = bf16[2,64,2048]{2,1,0:T(8,128)(2,1)S(1)} collective-permute-done((bf16[2,64,2048]{2,1,0:T(8,128)(2,1)S(1)}, bf16[2,64,2048]{2,1,0:T(8,128)(2,1)S(1)}, u32[]{:S(2)}, u32[]{:S(2)}) %collective-permute-start.50) | collective-permute-done | bytes 524320 | tf_op jit(solution)/shard_map/ppermute | solution.py:308
  649.3 10.2 collective-permute-done.56
  674.3 11.0 %collective-permute-done.57 = bf16[64,2048]{1,0:T(8,128)(2,1)S(1)} collective-permute-done((bf16[64,2048]{1,0:T(8,128)(2,1)S(1)}, bf16[64,2048]{1,0:T(8,128)(2,1)S(1)}, u32[]{:S(2)}, u32[]{:S(2)}) %collective-permute-start.57) | collective-permute-done | bytes 262176 | tf_op jit(solution)/shard_map/ppermute | solution.py:308
  732.6 23.4 %collective-permute-done.42 = bf16[4,2,1,64,1024]{4,3,0,1,2:T(8,128)(2,1)S(1)} collective-permute-done((bf16[4,2,1,64,1024]{4,3,0,1,2:T(8,128)(2,1)S(1)}, bf16[4,2,1,64,1024]{4,3,0,1,2:T(8,128)(2,1)S(1)}, u32[]{:S(2)}, u32[]{:S(2)}) %collective-permute-start.42) | collective-permute-done | bytes 1048608 | tf_op jit(solution)/shard_map/ppermute | solution.py:308
  817.8 12.5 %collective-permute-done.68 = bf16[2,64,2048]{2,1,0:T(8,128)(2,1)} collective-permute-done((bf16[2,64,2048]{2,1,0:T(8,128)(2,1)}, bf16[2,64,2048]{2,1,0:T(8,128)(2,1)}, u32[]{:S(2)}, u32[]{:S(2)}) %collective-permute-start.68) | collective-permute-done | bytes 524320 | tf_op jit(solution)/shard_map/ppermute | solution.py:308
  872.4 107.2 %collective-permute-done.73 = bf16[64,2048]{1,0:T(8,128)(2,1)S(1)} collective-permute-done((bf16[64,2048]{1,0:T(8,128)(2,1)S(1)}, bf16[64,2048]{1,0:T(8,128)(2,1)S(1)}, u32[]{:S(2)}, u32[]{:S(2)}) %collective-permute-start.73) | collective-permute-done | bytes 262176 | tf_op jit(solution)/shard_map/ppermute | solution.py:308
  (617 shorter events, 492.6 us)
Async XLA Ops:
  7.2 171.5 %all-gather.3.cloned.1.call-start = ((), (), s32[]{:S(2)}) async-start(), calls=%async_computation.14 | async-start | bytes 7077888 | tf_op jit(solution)/shard_map/all_gather | solution.py:458
  17.4 182.0 %all-gather.5.cloned.1.call-start = ((), (), s32[]{:S(2)}) async-start(), calls=%async_computation.15 | async-start | bytes 2359296 | tf_op jit(solution)/shard_map/all_gather | solution.py:461
  17.4 57.6 %collective-permute-start.3 = (bf16[1,4,2,64,512]{4,3,2,1,0:T(8,128)(2,1)S(1)}, bf16[1,4,2,64,512]{4,3,2,1,0:T(8,128)(2,1)}, u32[]{:S(2)}, u32[]{:S(2)}) collective-permute-start(bf16[1,4,2,64,512]{4,3,2,1,0:T(8,128)(2,1)S(1)} %bitcast.660), channel_id=1, source_target_pairs={{0,16},{8,24},{16,0},{24,8},{1,17},{9,25},{17,1},{25,9},{2,18},{10... | collective-permute-start | bytes 1572872 | tf_op jit(solution)/shard_map/ppermute | solution.py:308
  28.3 54.9 %all-to-all-start = ((f32[8,24,256]{2,1,0:T(8,128)}), f32[8,24,256]{2,1,0:T(8,128)S(1)}, u32[]{:S(2)}, u32[]{:S(2)}) async-start(f32[8,24,256]{2,1,0:T(8,128)} %broadcast_in_dim.56), calls=%async_computation | async-start | bytes 393216 | tf_op jit(solution)/shard_map/all_to_all | solution.py:402
  77.2 60.6 %collective-permute-start.4 = (bf16[2,4,2,64,512]{4,3,2,1,0:T(8,128)(2,1)}, bf16[2,4,2,64,512]{4,3,2,1,0:T(8,128)(2,1)}, u32[]{:S(2)}, u32[]{:S(2)}) collective-permute-start(bf16[2,4,2,64,512]{4,3,2,1,0:T(8,128)(2,1)} %get-tuple-element.460), channel_id=1, source_target_pairs={{0,8},{8,0},{16,24},{24,16},{1,9},{9,1},{17,25},{25,17},{2,10},{10... | collective-permute-start | bytes 3145736 | tf_op jit(solution)/shard_map/ppermute | solution.py:308
  84.7 60.7 %all-to-all-start.2 = ((bf16[4,512,512]{2,1,0:T(8,128)(2,1)}), bf16[4,512,512]{2,1,0:T(8,128)(2,1)S(1)}, u32[]{:S(2)}, u32[]{:S(2)}) async-start(bf16[4,512,512]{2,1,0:T(8,128)(2,1)} %broadcast_in_dim.62), calls=%async_computation.2 | async-start | bytes 4194304 | tf_op jit(solution)/shard_map/all_to_all | solution.py:331
  89.0 67.3 %collective-permute-start = (bf16[1056,256]{1,0:T(8,128)(2,1)}, bf16[1056,256]{1,0:T(8,128)(2,1)}, u32[]{:S(2)}, u32[]{:S(2)}) collective-permute-start(bf16[1056,256]{1,0:T(8,128)(2,1)} %get-tuple-element.170), channel_id=1, source_target_pairs={{0,8},{8,0},{16,24},{24,16},{1,9},{9,1},{17,25},{25,17},{2,10},{10... | collective-permute-start | bytes 1622024 | tf_op jit(solution)/shard_map/ppermute | solution.py:308
  89.6 66.7 %collective-permute-start.1 = (bf16[1056,256]{1,0:T(8,128)(2,1)}, bf16[1056,256]{1,0:T(8,128)(2,1)}, u32[]{:S(2)}, u32[]{:S(2)}) collective-permute-start(bf16[1056,256]{1,0:T(8,128)(2,1)} %get-tuple-element.171), channel_id=1, source_target_pairs={{0,16},{8,24},{16,0},{24,8},{1,17},{9,25},{17,1},{25,9},{2,18},{10... | collective-permute-start | bytes 1622024 | tf_op jit(solution)/shard_map/ppermute | solution.py:308
  93.1 75.6 %collective-permute-start.2 = (bf16[1056,256]{1,0:T(8,128)(2,1)}, bf16[1056,256]{1,0:T(8,128)(2,1)}, u32[]{:S(2)}, u32[]{:S(2)}) collective-permute-start(bf16[1056,256]{1,0:T(8,128)(2,1)} %get-tuple-element.172), channel_id=1, source_target_pairs={{0,24},{8,16},{16,8},{24,0},{1,25},{9,17},{17,9},{25,1},{2,26},{10... | collective-permute-start | bytes 1622024 | tf_op jit(solution)/shard_map/ppermute | solution.py:308
  172.0 58.6 %collective-permute-start.8 = (bf16[1,2,4,4,64,512]{5,4,3,2,1,0:T(8,128)(2,1)}, bf16[1,2,4,4,64,512]{5,4,3,2,1,0:T(8,128)(2,1)}, u32[]{:S(2)}, u32[]{:S(2)}) collective-permute-start(bf16[1,2,4,4,64,512]{5,4,3,2,1,0:T(8,128)(2,1)} %maximum_bitcast_fusion), channel_id=1, source_target_pairs={{0,2},{2,0},{1,3},{3,1},{4,6},{6,4},{5,7},{7,5},{8,10},{10,8},{9,1... | collective-permute-start | bytes 6291464 | tf_op jit(solution)/shard_map/ppermute | solution.py:308
  374.1 68.5 %collective-permute-start.21 = (bf16[1408,256]{1,0:T(8,128)(2,1)S(1)}, bf16[1408,256]{1,0:T(8,128)(2,1)}, u32[]{:S(2)}, u32[]{:S(2)}) collective-permute-start(bf16[1408,256]{1,0:T(8,128)(2,1)S(1)} %copy-done.48), channel_id=1, source_target_pairs={{0,4},{4,0},{1,5},{5,1},{2,6},{6,2},{3,7},{7,3},{8,12},{12,8},{9,1... | collective-permute-start | bytes 2162696 | tf_op jit(solution)/shard_map/ppermute | solution.py:302
  446.3 71.5 %collective-permute-start.41 = (bf16[4,1056,256]{2,1,0:T(8,128)(2,1)}, bf16[4,1056,256]{2,1,0:T(8,128)(2,1)}, u32[]{:S(2)}, u32[]{:S(2)}) collective-permute-start(bf16[4,1056,256]{2,1,0:T(8,128)(2,1)} %slice_bitcast_fusion.1), channel_id=1, source_target_pairs={{0,4},{4,0},{1,5},{5,1},{2,6},{6,2},{3,7},{7,3},{8,12},{12,8},{9,1... | collective-permute-start | bytes 6488072 | tf_op jit(solution)/shard_map/ppermute | solution.py:302
  567.6 81.7 %collective-permute-start.54 = (bf16[1056,256]{1,0:T(8,128)(2,1)}, bf16[1056,256]{1,0:T(8,128)(2,1)}, u32[]{:S(2)}, u32[]{:S(2)}) collective-permute-start(bf16[1056,256]{1,0:T(8,128)(2,1)} %get-tuple-element.415), channel_id=1, source_target_pairs={{0,8},{8,0},{16,24},{24,16},{1,9},{9,1},{17,25},{25,17},{2,10},{10... | collective-permute-start | bytes 1622024 | tf_op jit(solution)/shard_map/ppermute | solution.py:308
  595.1 54.2 %collective-permute-start.55 = (bf16[1056,256]{1,0:T(8,128)(2,1)}, bf16[1056,256]{1,0:T(8,128)(2,1)}, u32[]{:S(2)}, u32[]{:S(2)}) collective-permute-start(bf16[1056,256]{1,0:T(8,128)(2,1)} %get-tuple-element.414), channel_id=1, source_target_pairs={{0,16},{8,24},{16,0},{24,8},{1,17},{9,25},{17,1},{25,9},{2,18},{10... | collective-permute-start | bytes 1622024 | tf_op jit(solution)/shard_map/ppermute | solution.py:308
  663.7 50.1 %collective-permute-start.40 = (bf16[4,1,2,64,1024]{4,3,0,2,1:T(8,128)(2,1)}, bf16[4,1,2,64,1024]{4,3,0,2,1:T(8,128)(2,1)}, u32[]{:S(2)}, u32[]{:S(2)}) collective-permute-start(bf16[4,1,2,64,1024]{4,3,0,2,1:T(8,128)(2,1)} %slice_bitcast_fusion.15), channel_id=1, source_target_pairs={{0,2},{2,0},{1,3},{3,1},{4,6},{6,4},{5,7},{7,5},{8,10},{10,8},{9,1... | collective-permute-start | bytes 3145736 | tf_op jit(solution)/shard_map/ppermute | solution.py:308
  705.8 51.6 %all-to-all-start.5 = ((bf16[4,128,2048]{2,1,0:T(8,128)(2,1)}), bf16[4,128,2048]{2,1,0:T(8,128)(2,1)}, u32[]{:S(2)}, u32[]{:S(2)}) async-start(bf16[4,128,2048]{2,1,0:T(8,128)(2,1)} %broadcast_in_dim.71), calls=%async_computation.5 | async-start | bytes 4194304 | tf_op jit(solution)/shard_map/all_to_all | solution.py:331
  710.3 333.9 %reduce-scatter.5.cloned.1.call-start = ((), (), s32[]{:S(2)}) async-start(), calls=%async_computation.17 | async-start | bytes 2359296 | tf_op jit(solution)/shard_map/reduce_scatter | solution.py:675
  777.1 269.1 %reduce-scatter.3.cloned.1.call-start = ((), (), s32[]{:S(2)}) async-start(), calls=%async_computation.16 | async-start | bytes 7077888 | tf_op jit(solution)/shard_map/reduce_scatter | solution.py:676
  851.7 138.9 %collective-permute-start.70 = (bf16[1408,256]{1,0:T(8,128)(2,1)}, bf16[1408,256]{1,0:T(8,128)(2,1)}, u32[]{:S(2)}, u32[]{:S(2)}) collective-permute-start(bf16[1408,256]{1,0:T(8,128)(2,1)} %get-tuple-element.396), channel_id=1, source_target_pairs={{0,8},{8,0},{16,24},{24,16},{1,9},{9,1},{17,25},{25,17},{2,10},{10... | collective-permute-start | bytes 2162696 | tf_op jit(solution)/shard_map/ppermute | solution.py:308
  852.0 138.5 %collective-permute-start.71 = (bf16[1408,256]{1,0:T(8,128)(2,1)}, bf16[1408,256]{1,0:T(8,128)(2,1)}, u32[]{:S(2)}, u32[]{:S(2)}) collective-permute-start(bf16[1408,256]{1,0:T(8,128)(2,1)} %get-tuple-element.395), channel_id=1, source_target_pairs={{0,16},{8,24},{16,0},{24,8},{1,17},{9,25},{17,1},{25,9},{2,18},{10... | collective-permute-start | bytes 2162696 | tf_op jit(solution)/shard_map/ppermute | solution.py:308
  855.5 135.0 %collective-permute-start.72 = (bf16[1408,256]{1,0:T(8,128)(2,1)}, bf16[1408,256]{1,0:T(8,128)(2,1)}, u32[]{:S(2)}, u32[]{:S(2)}) collective-permute-start(bf16[1408,256]{1,0:T(8,128)(2,1)} %get-tuple-element.394), channel_id=1, source_target_pairs={{0,24},{8,16},{16,8},{24,0},{1,25},{9,17},{17,9},{25,1},{2,26},{10... | collective-permute-start | bytes 2162696 | tf_op jit(solution)/shard_map/ppermute | solution.py:308
  860.0 119.6 %collective-permute-start.73 = (bf16[64,2048]{1,0:T(8,128)(2,1)S(1)}, bf16[64,2048]{1,0:T(8,128)(2,1)S(1)}, u32[]{:S(2)}, u32[]{:S(2)}) collective-permute-start(bf16[64,2048]{1,0:T(8,128)(2,1)S(1)} %slice_bitcast_fusion.60), channel_id=1, source_target_pairs={{0,16},{8,24},{16,0},{24,8},{1,17},{9,25},{17,1},{25,9},{2,18},{10... | collective-permute-start | bytes 786440 | tf_op jit(solution)/shard_map/ppermute | solution.py:308
  866.8 121.7 %all-to-all-start.6 = ((bf16[4,128,2048]{2,1,0:T(8,128)(2,1)}), bf16[4,128,2048]{2,1,0:T(8,128)(2,1)}, u32[]{:S(2)}, u32[]{:S(2)}) async-start(bf16[4,128,2048]{2,1,0:T(8,128)(2,1)} %bitcast.655), calls=%async_computation.6 | async-start | bytes 4194304 | tf_op jit(solution)/shard_map/all_to_all | solution.py:336
  871.4 116.0 %collective-permute-start.74 = (bf16[64,2048]{1,0:T(8,128)(2,1)S(1)}, bf16[64,2048]{1,0:T(8,128)(2,1)S(1)}, u32[]{:S(2)}, u32[]{:S(2)}) collective-permute-start(bf16[64,2048]{1,0:T(8,128)(2,1)S(1)} %slice_bitcast_fusion.59), channel_id=1, source_target_pairs={{0,16},{8,24},{16,0},{24,8},{1,17},{9,25},{17,1},{25,9},{2,18},{10... | collective-permute-start | bytes 786440 | tf_op jit(solution)/shard_map/ppermute | solution.py:308
  (159 other events, 2675.8 us)
Sparse Core Ops, SparseCore 0:
  10.2 95.3 all-gather.2
  107.2 49.4 all-gather.4
  777.2 48.1 reduce-scatter.4
  838.3 125.9 reduce-scatter.2

commit v5 on v4

--- a/solution.py
+++ b/solution.py
@@ -399,9 +399,6 @@
         ],
         axis=0,
     )
-    small_all = lax.all_to_all(
-        jnp.broadcast_to(small[None], (n_row,) + small.shape), ROW, 0, 0, tiled=True
-    )
     f_shared = shared_gate.shape[1] // n_g
     f_routed = expert_gate.shape[2] // n_g
     f_experts = local_experts * f_routed
@@ -426,11 +423,28 @@
         slices_e(expert_down),
     ]
     picked = [[pick(value, at_g ^ shift) for shift in range(n_g)] for value in weight_slices]
-    picked[0], small_all = tie(picked[0], small_all)
+    picked[0], tokens, cotangent = tie(picked[0], tokens, cotangent)
     own_blocks = [
         [shift_by(value, "g", shift) for shift, value in enumerate(values)] for values in picked
     ]
 
+    token_part = lax.all_to_all(tokens, "k", 0, 0, tiled=True).reshape(span, -1)
+    cot_part = lax.all_to_all(cotangent, "k", 0, 0, tiled=True).reshape(span, -1)
+
+    sub = own_rows // PARTS
+    cot_rows = cot_part.reshape(1, n_c, PARTS, sub, dim // n_c)
+    cot_rows = gather_joined(cot_rows, "g", 0)
+    qkv = lax.all_gather(
+        jnp.concatenate([query_weight, key_weight, value_weight], axis=1), ROW, axis=0, tiled=True
+    )
+    out_w = lax.all_gather(output_weight, ROW, axis=1, tiled=True)
+    inputs = col_gather(token_part, n_c).reshape(n_c, span, -1).transpose(1, 0, 2)
+    inputs = inputs.reshape(span, dim).astype(F32)
+
+    small, inputs = tie(small, inputs)
+    small_all = lax.all_to_all(
+        jnp.broadcast_to(small[None], (n_row,) + small.shape), ROW, 0, 0, tiled=True
+    )
     gain_1 = small_all[:, 16, :d_own].reshape(dim)
     gain_2 = small_all[:, 17, :d_own].reshape(dim)
     logit_w = small_all[:, 18, :d_own].reshape(dim)
@@ -442,12 +456,7 @@
     )
     mixing_own = mixing_own.transpose(0, 2, 1).reshape(total, local_experts)
 
-    token_part = lax.all_to_all(tokens, "k", 0, 0, tiled=True).reshape(span, -1)
-    cot_part = lax.all_to_all(cotangent, "k", 0, 0, tiled=True).reshape(span, -1)
-
-    sub = own_rows // PARTS
-    cot_rows = cot_part.reshape(1, n_c, PARTS, sub, dim // n_c)
-    cot_rows = gather_joined(cot_rows, "g", 0)
+    own_blocks[0][1:], inputs, cot_rows = tie(own_blocks[0][1:], inputs, cot_rows)
     cot_all = []
     for part in range(PARTS):
         value = cot_rows[:, :, part][None, None]
@@ -455,14 +464,6 @@
             value = gather_joined(value, axis, ("y", "x").index(axis))
         cot_all.append(value.reshape(n_c, n_g, n_c, sub, dim // n_c))
 
-    qkv = lax.all_gather(
-        jnp.concatenate([query_weight, key_weight, value_weight], axis=1), ROW, axis=0, tiled=True
-    )
-    out_w = lax.all_gather(output_weight, ROW, axis=1, tiled=True)
-    inputs = col_gather(token_part, n_c).reshape(n_c, span, -1).transpose(1, 0, 2)
-    inputs = inputs.reshape(span, dim).astype(F32)
-
-    own_blocks[0], inputs = tie(own_blocks[0], inputs)
     first_scale = lax.rsqrt(jnp.mean(inputs * inputs, axis=-1, keepdims=True) + epsilon)
     normed_1 = (inputs * first_scale * gain_1).astype(BF16)
     projected = dot(normed_1, qkv, ((1,), (0,)))
@@ -615,7 +616,7 @@
 
     acts, gates, ups = ([parts[i] for parts in passes] for i in (2, 3, 4))
     first = cols_first(split_sides(passes[0][1]))
-    first, acts = tie(first, acts)
+    first, acts, moved_s[1:3] = tie(first, acts, moved_s[1:3])
     (grad_d,) = weight_grad(sizes_e, meta, (True,), [acts], normed_parts, cot_all)
     first = cols_second(first)
     second = cols_first(split_sides(passes[1][1]))
@@ -624,7 +625,7 @@
     first = chips_steps(first)
     second = cols_second(second)
     both_d = own_core(grad_d)
-    first, second, both_d, moved_s, grad_gu = tie(first, second, both_d, moved_s, grad_gu)
+    first, second, both_d, moved_s[3:], grad_gu = tie(first, second, both_d, moved_s[3:], grad_gu)
     moved_d = send_slices(both_d)
     first = chips_last(first)
     second = chips_steps(second)
@@ -632,34 +633,36 @@
     first, second, both_gu = tie(first, second, both_gu)
     second = chips_last(second)
     out_sides = [cols_first(split_sides(parts[0])) for parts in passes]
+    moved_gu = send_slices(both_gu)
     normed_grad_2 = jnp.concatenate([first, second], axis=0)
+    normed_grad_2, moved_d[1:] = tie(normed_grad_2, moved_d[1:])
     hidden_part, gain_2_sum = norm_back(normed_grad_2, unit_2, second_scale, gain_2)
     hidden_grad = own_cot.astype(F32) + hidden_part
-    moved_gu = send_slices(both_gu)
     attn_grad = col_gather(hidden_grad.astype(BF16), n_c).reshape(span, dim)
-    out_sides, attn_grad, moved_d = tie(out_sides, attn_grad, moved_d)
+    out_sides, attn_grad, moved_gu[1] = tie(out_sides, attn_grad, moved_gu[1])
     out_parts = [cols_second(sides) for sides in out_sides]
     gate_s, up_s, down_s = (place_s(value) for value in place_slices(moved_s, 3))
     down_e = place_e(place_slices(moved_d, 1)[0])
 
     out_grad = dot(attn_grad, mixed, ((0,), (0,)))
     mixed_grad = dot(attn_grad, out_w, ((1,), (1,))).astype(BF16).reshape(head_shape)
-    out_parts, mixed_grad = tie(out_parts, mixed_grad)
+    out_parts, mixed_grad, moved_gu[2:3] = tie(out_parts, mixed_grad, moved_gu[2:3])
     out_parts = [chips_steps(part) for part in out_parts]
     prob_grad = einsum("bqhd,bkhd->bhqk", mixed_grad, value_low)
     value_grad = einsum("bhqk,bqhd->bkhd", prob_low, mixed_grad).astype(BF16)
     center = jnp.sum(prob_grad * probabilities, axis=-1, keepdims=True)
     score_grad = (probabilities * (prob_grad - center) * (1.0 / math.sqrt(HEAD_DIM))).astype(BF16)
+    out_parts, score_grad = tie(out_parts, score_grad)
+    out_rows = [chips_last(part) for part in out_parts]
     query_grad = rotate(einsum("bhqk,bkhd->bqhd", score_grad, key_rot), cosine, -sine).astype(BF16)
     key_grad = rotate(einsum("bhqk,bqhd->bkhd", score_grad, query_rot), cosine, -sine).astype(BF16)
     qkv_grad = jnp.concatenate(
         [part.reshape(span, width) for part in (query_grad, key_grad, value_grad)], axis=1
     )
-    qkv_grad, out_parts = tie(qkv_grad, out_parts)
-    out_rows = jnp.concatenate([chips_last(part) for part in out_parts], axis=0)
+    qkv_grad, out_rows, moved_gu[3:] = tie(qkv_grad, out_rows, moved_gu[3:])
+    out_rows = jnp.concatenate(out_rows, axis=0)
     qkv_sum = dot(normed_1, qkv_grad, ((0,), (0,)))
     normed_grad_1 = col_sum(dot(qkv_grad, qkv, ((1,), (1,))), n_c)
-    normed_grad_1, moved_gu, out_rows = tie(normed_grad_1, moved_gu, out_rows)
     gate_e, up_e = (place_e(value) for value in place_slices(moved_gu, 2))
     own_scale = lax.dynamic_slice_in_dim(first_scale, at_c * own_rows, own_rows, 0)
     rows_part, gain_1_sum = norm_back(normed_grad_1, own_inputs * own_scale, own_scale, gain_1)

time: 1060 us -> 1050 us (level)
  waiting for transfers between devices: 444 us -> 423 us
    ppermute x60, waiting for transfers between devices: 421 us -> 382 us  [shift_by(): lax.ppermute(value, axis, [(i, i ^ shift) for i in range(lax.axis_size(ax...]
    all_to_all x2, waiting for transfers between devices: 12.6 us -> 30.8 us  [col_sum(): lax.all_to_all(parts, COL, 0, 0, tiled=True).astype(F32)]
    unnamed x206 -> x238, local copies, waits for them, and re-layouts: 32.3 us -> 35.8 us
  transfers between devices with their start and end apart: 90 -> 88, of which waited for: 33 -> 34; matrix products, arithmetic and copies ran while one was open for 24% -> 25% of each run, Pallas kernels for 12% -> 15%
where the time goes in v5:
time: 1050 us; the launch traced here: 1040 us
  waiting for transfers between devices  423 us (40%)
  Pallas kernels  159 us (15%)
  starting transfers between devices  145 us (14%)
  local copies, waits for them, and re-layouts  133 us (13%)
  other arithmetic  105 us (10%)
  matrix products  43.2 us (4%)
  between operations  16.5 us (2%)
  blocking collectives  12.4 us (1%)
    ppermute x60, waiting for transfers between devices, shift_by(): lax.ppermute(value, axis, [(i, i ^ shift) for i in range(lax.axis_size(ax...  382 us
    pallas_call x4, Pallas kernels, ffn_pass(): pl.pallas_call(functools.partial(ffn_kernel, sizes, groups), grid_spec=pl...  112 us
    ppermute x60, starting transfers between devices, shift_by(): lax.ppermute(value, axis, [(i, i ^ shift) for i in range(lax.axis_size(ax...  105 us
    pallas_call x3, Pallas kernels, weight_grad(): pl.pallas_call(functools.partial(grad_kernel, parts, kinds, f_pad), grid_...  47.3 us
    unnamed x238, local copies, waits for them, and re-layouts  35.8 us
    dot_general x6, matrix products, dot(): lax.dot_general(left, right, (dims, ((), ())), preferred_element_type=F32)  33.4 us
    all_to_all x2, waiting for transfers between devices, col_sum(): lax.all_to_all(parts, COL, 0, 0, tiled=True).astype(F32)  30.8 us
    another operation x15, other arithmetic, gather_joined(): jnp.stack([value, shift_by(value, axis, bit)], axis=at + 1).reshape(shape)  22.5 us
  transfers between devices with their start and end apart: 88, of which 34 were waited for; matrix products, arithmetic and copies ran while one was open for 25% of the time, Pallas kernels for 15%

profile of v5, /device:TPU:0, one launch (start us, length us, event | category | flops | bytes accessed | tf_op | source)
XLA Modules:
  0.0 1037.1 jit_solution(8123842990773290345)
XLA Ops:
  34.5 31.5 %collective-permute-done.3 = bf16[1,4,2,64,512]{4,3,2,1,0:T(8,128)(2,1)S(1)} collective-permute-done((bf16[1,4,2,64,512]{4,3,2,1,0:T(8,128)(2,1)S(1)}, bf16[1,4,2,64,512]{4,3,2,1,0:T(8,128)(2,1)S(1)}, u32[]{:S(2)}, u32[]{:S(2)}) %collective-permute-start.3) | collective-permute-done | bytes 524320 | tf_op jit(solution)/shard_map/ppermute | solution.py:308
  74.2 66.9 %collective-permute-done.4 = bf16[2,4,2,64,512]{4,3,2,1,0:T(8,128)(2,1)} collective-permute-done((bf16[2,4,2,64,512]{4,3,2,1,0:T(8,128)(2,1)}, bf16[2,4,2,64,512]{4,3,2,1,0:T(8,128)(2,1)}, u32[]{:S(2)}, u32[]{:S(2)}) %collective-permute-start.4) | collective-permute-done | bytes 1048608 | tf_op jit(solution)/shard_map/ppermute | solution.py:308
  170.4 12.1 %collective-permute-done.7 = bf16[1,1,4,4,64,512]{5,4,3,2,1,0:T(8,128)(2,1)S(1)} collective-permute-done((bf16[1,1,4,4,64,512]{5,4,3,2,1,0:T(8,128)(2,1)}, bf16[1,1,4,4,64,512]{5,4,3,2,1,0:T(8,128)(2,1)S(1)}, u32[]{:S(2)}, u32[]{:S(2)}) %collective-permute-start.7) | collective-permute-done | bytes 1048608 | tf_op jit(solution)/shard_map/ppermute | solution.py:308
  244.7 13.0 %all-to-all-done.4 = bf16[4,128,2048]{2,1,0:T(8,128)(2,1)} async-done(((bf16[4,128,2048]{2,1,0:T(8,128)(2,1)}), bf16[4,128,2048]{2,1,0:T(8,128)(2,1)}, u32[]{:S(2)}, u32[]{:S(2)}) %all-to-all-start.4) | async-done | bytes 2097184 | tf_op jit(solution)/shard_map/all_to_all | solution.py:336
  263.8 11.2 %collective-permute-done.10 = bf16[1,64,2048]{2,1,0:T(8,128)(2,1)S(1)} collective-permute-done((bf16[1,64,2048]{2,1,0:T(8,128)(2,1)S(1)}, bf16[1,64,2048]{2,1,0:T(8,128)(2,1)S(1)}, u32[]{:S(2)}, u32[]{:S(2)}) %collective-permute-start.10) | collective-permute-done | bytes 262176 | tf_op jit(solution)/shard_map/ppermute | solution.py:308
  278.2 21.6 %collective-permute-done.11 = bf16[2,64,2048]{2,1,0:T(8,128)(2,1)S(1)} collective-permute-done((bf16[2,64,2048]{2,1,0:T(8,128)(2,1)S(1)}, bf16[2,64,2048]{2,1,0:T(8,128)(2,1)S(1)}, u32[]{:S(2)}, u32[]{:S(2)}) %collective-permute-start.11) | collective-permute-done | bytes 524320 | tf_op jit(solution)/shard_map/ppermute | solution.py:308
  327.9 27.2 %collective-permute-done.17 = bf16[1,64,2048]{2,1,0:T(8,128)(2,1)S(1)} collective-permute-done((bf16[1,64,2048]{2,1,0:T(8,128)(2,1)S(1)}, bf16[1,64,2048]{2,1,0:T(8,128)(2,1)S(1)}, u32[]{:S(2)}, u32[]{:S(2)}) %collective-permute-start.17) | collective-permute-done | bytes 262176 | tf_op jit(solution)/shard_map/ppermute | solution.py:308
  360.5 10.6 %collective-permute-done.18 = bf16[2,64,2048]{2,1,0:T(8,128)(2,1)} collective-permute-done((bf16[2,64,2048]{2,1,0:T(8,128)(2,1)}, bf16[2,64,2048]{2,1,0:T(8,128)(2,1)}, u32[]{:S(2)}, u32[]{:S(2)}) %collective-permute-start.18) | collective-permute-done | bytes 524320 | tf_op jit(solution)/shard_map/ppermute | solution.py:308
  381.6 12.6 %collective-permute-done.27 = bf16[4,1,1,64,1024]{4,3,0,2,1:T(8,128)(2,1)S(1)} collective-permute-done((bf16[4,1,1,64,1024]{4,3,0,2,1:T(8,128)(2,1)S(1)}, bf16[4,1,1,64,1024]{4,3,0,2,1:T(8,128)(2,1)S(1)}, u32[]{:S(2)}, u32[]{:S(2)}) %collective-permute-start.27) | collective-permute-done | bytes 524320 | tf_op jit(solution)/shard_map/ppermute | solution.py:308
  405.9 21.2 %ffn_pass.4 = (bf16[1024,2048]{1,0:T(8,128)(2,1)}, bf16[1024,2048]{1,0:T(8,128)(2,1)}, bf16[352,1024]{1,0:T(8,128)(2,1)}, bf16[368,1024]{1,0:T(8,128)(2,1)}, bf16[352,1024]{1,0:T(8,128)(2,1)}) custom-call(s32[3]{0:T(128)} %pad_add_fusion.meta, bf16[1024,2048]{1,0:T(8,128)(2,1)} %pad_maximum_fusion.2.rows_ref.refs_6_.refs_4_, ...), custom_call_target="tpu_custom_call" | custom-call | flops 8858370048 | bytes 23265280 | tf_op jit(solution)/shard_map/ffn_pass/pallas_call | solution.py:172
  433.9 21.0 %ffn_pass.5 = (bf16[1024,2048]{1,0:T(8,128)(2,1)}, bf16[1024,2048]{1,0:T(8,128)(2,1)}, bf16[352,1024]{1,0:T(8,128)(2,1)}, bf16[368,1024]{1,0:T(8,128)(2,1)}, bf16[352,1024]{1,0:T(8,128)(2,1)}) custom-call(s32[3]{0:T(128)} %pad_add_fusion.meta, bf16[1024,2048]{1,0:T(8,128)(2,1)} %pad_maximum_fusion.3.rows_ref.refs_7_.refs_5_, ...), custom_call_target="tpu_custom_call" | custom-call | flops 8858370048 | bytes 23265280 | tf_op jit(solution)/shard_map/ffn_pass/pallas_call | solution.py:172
  455.1 16.6 %weight_grad.3 = (bf16[2,4,1056,256]{3,2,1,0:T(8,128)(2,1)}, f32[8,2048]{1,0:T(8,128)}) custom-call(s32[3]{0:T(128)} %pad_add_fusion.meta, bf16[368,1024]{1,0:T(8,128)(2,1)} %get-tuple-element.198.refs_0_, bf16[368,1024]{1,0:T(8,128)(2,1)} %get-tuple-element.201.refs_1_, bf16[352,1024]{1,0:T(8,128)(2,1)} %get-tuple-element.202.refs_2_, ...), custom_call_target="tpu_custom_call" | custom-call | flops 8858370048 | bytes 17039360 | tf_op jit(solution)/shard_map/weight_grad/pallas_call | solution.py:271
  477.1 35.1 %ffn_pass.6 = (bf16[1024,2048]{1,0:T(8,128)(2,1)}, bf16[1024,2048]{1,0:T(8,128)(2,1)}, bf16[704,1024]{1,0:T(8,128)(2,1)}, bf16[704,1024]{1,0:T(8,128)(2,1)}, bf16[704,1024]{1,0:T(8,128)(2,1)}) custom-call(s32[3]{0:T(128)} %pad_add_fusion.meta, bf16[1024,2048]{1,0:T(8,128)(2,1)} %pad_maximum_fusion.2.rows_ref.refs_6_.refs_4_, ...), custom_call_target="tpu_custom_call" | custom-call | flops 17716740096 | bytes 46530560 | tf_op jit(solution)/shard_map/ffn_pass/pallas_call | solution.py:172
  523.1 18.3 %collective-permute-done.45 = bf16[4,1,2,64,1024]{4,3,0,2,1:T(8,128)(2,1)S(1)} collective-permute-done((bf16[4,1,2,64,1024]{4,3,0,2,1:T(8,128)(2,1)S(1)}, bf16[4,1,2,64,1024]{4,3,0,2,1:T(8,128)(2,1)S(1)}, u32[]{:S(2)}, u32[]{:S(2)}) %collective-permute-start.45) | collective-permute-done | bytes 1048608 | tf_op jit(solution)/shard_map/ppermute | solution.py:308
  546.8 10.9 %collective-permute-start.46 = (bf16[1056,256]{1,0:T(8,128)(2,1)}, bf16[1056,256]{1,0:T(8,128)(2,1)S(1)}, u32[]{:S(2)}, u32[]{:S(2)}) collective-permute-start(bf16[1056,256]{1,0:T(8,128)(2,1)} %get-tuple-element.420), channel_id=1, source_target_pairs={{0,8},{8,0},{16,24},{24,16},{1,9},{9,1},{17,25},{25,17},{2,10},{10... | collective-permute-start | bytes 1622024 | tf_op jit(solution)/shard_map/ppermute | solution.py:308
  558.0 34.6 %ffn_pass.7 = (bf16[1024,2048]{1,0:T(8,128)(2,1)}, bf16[1024,2048]{1,0:T(8,128)(2,1)}, bf16[704,1024]{1,0:T(8,128)(2,1)}, bf16[704,1024]{1,0:T(8,128)(2,1)}, bf16[704,1024]{1,0:T(8,128)(2,1)}) custom-call(s32[3]{0:T(128)} %pad_add_fusion.meta, bf16[1024,2048]{1,0:T(8,128)(2,1)} %pad_maximum_fusion.3.rows_ref.refs_7_.refs_5_, ...), custom_call_target="tpu_custom_call" | custom-call | flops 17716740096 | bytes 46530560 | tf_op jit(solution)/shard_map/ffn_pass/pallas_call | solution.py:172
  605.4 12.6 %weight_grad.4 = bf16[2,4,704,256]{3,2,1,0:T(8,128)(2,1)} custom-call(s32[3]{0:T(128)} %pad_add_fusion.meta, bf16[704,1024]{1,0:T(8,128)(2,1)} %get-tuple-element.225.refs_0_, bf16[704,1024]{1,0:T(8,128)(2,1)} %get-tuple-element.226.refs_1_, bf16[4,4,4,64,512]{4,3,2,1,0:T(8,128)(2,1)} %bitcast.597, bf16[4,4,4,64,512]{4,3,2,1,0:T(8,128)(2,1)} %bitcast.602), custom_call_target="tpu_custom_call" | custom-call | flops 5905580032 | bytes 14155776 | tf_op jit(solution)/shard_map/weight_grad/pallas_call | solution.py:271
  638.8 18.1 %weight_grad.5 = bf16[2,4,1408,256]{3,2,1,0:T(8,128)(2,1)} custom-call(s32[3]{0:T(128)} %pad_add_fusion.meta, bf16[704,1024]{1,0:T(8,128)(2,1)} %get-tuple-element.231.refs_0_, bf16[704,1024]{1,0:T(8,128)(2,1)} %get-tuple-element.232.refs_1_, bf16[704,1024]{1,0:T(8,128)(2,1)} %get-tuple-element.233.refs_2_, bf16[704,1024]{1,0:T(8,128)(2,1)} %get-tuple-element.234.refs_3_, ...), custom_call_target="tpu_custom_call" | custom-call | flops 11811160064 | bytes 19922944 | tf_op jit(solution)/shard_map/weight_grad/pallas_call | solution.py:271
  659.2 11.6 %collective-permute-done.52 = bf16[2,64,2048]{2,1,0:T(8,128)(2,1)S(1)} collective-permute-done((bf16[2,64,2048]{2,1,0:T(8,128)(2,1)S(1)}, bf16[2,64,2048]{2,1,0:T(8,128)(2,1)S(1)}, u32[]{:S(2)}, u32[]{:S(2)}) %collective-permute-start.52) | collective-permute-done | bytes 524320 | tf_op jit(solution)/shard_map/ppermute | solution.py:308
  693.4 15.2 %collective-permute-done.57 = bf16[64,2048]{1,0:T(8,128)(2,1)S(1)} collective-permute-done((bf16[64,2048]{1,0:T(8,128)(2,1)S(1)}, bf16[64,2048]{1,0:T(8,128)(2,1)S(1)}, u32[]{:S(2)}, u32[]{:S(2)}) %collective-permute-start.57) | collective-permute-done | bytes 262176 | tf_op jit(solution)/shard_map/ppermute | solution.py:308
  738.2 14.5 %collective-permute-done.62 = bf16[704,256]{1,0:T(8,128)(2,1)S(1)} collective-permute-done((bf16[704,256]{1,0:T(8,128)(2,1)S(1)}, bf16[704,256]{1,0:T(8,128)(2,1)S(1)}, u32[]{:S(2)}, u32[]{:S(2)}) %collective-permute-start.62) | collective-permute-done | bytes 360480 | tf_op jit(solution)/shard_map/ppermute | solution.py:308
  779.6 26.5 %collective-permute-done.42 = bf16[4,2,1,64,1024]{4,3,0,1,2:T(8,128)(2,1)S(1)} collective-permute-done((bf16[4,2,1,64,1024]{4,3,0,1,2:T(8,128)(2,1)S(1)}, bf16[4,2,1,64,1024]{4,3,0,1,2:T(8,128)(2,1)S(1)}, u32[]{:S(2)}, u32[]{:S(2)}) %collective-permute-start.42) | collective-permute-done | bytes 1048608 | tf_op jit(solution)/shard_map/ppermute | solution.py:308
  846.6 34.3 %collective-permute-done.69 = bf16[1408,256]{1,0:T(8,128)(2,1)} collective-permute-done((bf16[1408,256]{1,0:T(8,128)(2,1)}, bf16[1408,256]{1,0:T(8,128)(2,1)}, u32[]{:S(2)}, u32[]{:S(2)}) %collective-permute-start.69) | collective-permute-done | bytes 720928 | tf_op jit(solution)/shard_map/ppermute | solution.py:308
  966.0 17.8 %all-to-all-done.8 = bf16[4,128,2048]{2,1,0:T(8,128)(2,1)} async-done(((bf16[4,128,2048]{2,1,0:T(8,128)(2,1)}), bf16[4,128,2048]{2,1,0:T(8,128)(2,1)}, u32[]{:S(2)}, u32[]{:S(2)}) %all-to-all-start.8) | async-done | bytes 2097184 | tf_op jit(solution)/shard_map/all_to_all | solution.py:336
  (649 shorter events, 505.6 us)
Async XLA Ops:
  7.2 182.2 %all-gather.3.cloned.1.call-start = ((), (), s32[]{:S(2)}) async-start(), calls=%async_computation.14 | async-start | bytes 7077888 | tf_op jit(solution)/shard_map/all_gather | solution.py:437
  16.3 49.8 %collective-permute-start.3 = (bf16[1,4,2,64,512]{4,3,2,1,0:T(8,128)(2,1)S(1)}, bf16[1,4,2,64,512]{4,3,2,1,0:T(8,128)(2,1)S(1)}, u32[]{:S(2)}, u32[]{:S(2)}) collective-permute-start(bf16[1,4,2,64,512]{4,3,2,1,0:T(8,128)(2,1)S(1)} %bitcast.660), channel_id=1, source_target_pairs={{0,16},{8,24},{16,0},{24,8},{1,17},{9,25},{17,1},{25,9},{2,18},{10... | collective-permute-start | bytes 1572872 | tf_op jit(solution)/shard_map/ppermute | solution.py:308
  26.0 118.0 %all-to-all-start.1 = ((bf16[4,512,512]{2,1,0:T(8,128)(2,1)}), bf16[4,512,512]{2,1,0:T(8,128)(2,1)S(1)}, u32[]{:S(2)}, u32[]{:S(2)}) async-start(bf16[4,512,512]{2,1,0:T(8,128)(2,1)} %broadcast_in_dim.61), calls=%async_computation.1 | async-start | bytes 4194304 | tf_op jit(solution)/shard_map/all_to_all | solution.py:331
  29.9 181.6 %all-gather.5.cloned.1.call-start = ((), (), s32[]{:S(2)}) async-start(), calls=%async_computation.15 | async-start | bytes 2359296 | tf_op jit(solution)/shard_map/all_gather | solution.py:440
  29.9 117.3 %collective-permute-start = (bf16[1056,256]{1,0:T(8,128)(2,1)}, bf16[1056,256]{1,0:T(8,128)(2,1)}, u32[]{:S(2)}, u32[]{:S(2)}) collective-permute-start(bf16[1056,256]{1,0:T(8,128)(2,1)} %get-tuple-element.171), channel_id=1, source_target_pairs={{0,8},{8,0},{16,24},{24,16},{1,9},{9,1},{17,25},{25,17},{2,10},{10... | collective-permute-start | bytes 1622024 | tf_op jit(solution)/shard_map/ppermute | solution.py:308
  31.5 115.7 %collective-permute-start.1 = (bf16[1056,256]{1,0:T(8,128)(2,1)}, bf16[1056,256]{1,0:T(8,128)(2,1)}, u32[]{:S(2)}, u32[]{:S(2)}) collective-permute-start(bf16[1056,256]{1,0:T(8,128)(2,1)} %get-tuple-element.172), channel_id=1, source_target_pairs={{0,16},{8,24},{16,0},{24,8},{1,17},{9,25},{17,1},{25,9},{2,18},{10... | collective-permute-start | bytes 1622024 | tf_op jit(solution)/shard_map/ppermute | solution.py:308
  32.3 114.9 %collective-permute-start.2 = (bf16[1056,256]{1,0:T(8,128)(2,1)}, bf16[1056,256]{1,0:T(8,128)(2,1)}, u32[]{:S(2)}, u32[]{:S(2)}) collective-permute-start(bf16[1056,256]{1,0:T(8,128)(2,1)} %get-tuple-element.173), channel_id=1, source_target_pairs={{0,24},{8,16},{16,8},{24,0},{1,25},{9,17},{17,9},{25,1},{2,26},{10... | collective-permute-start | bytes 1622024 | tf_op jit(solution)/shard_map/ppermute | solution.py:308
  69.2 71.9 %collective-permute-start.4 = (bf16[2,4,2,64,512]{4,3,2,1,0:T(8,128)(2,1)}, bf16[2,4,2,64,512]{4,3,2,1,0:T(8,128)(2,1)}, u32[]{:S(2)}, u32[]{:S(2)}) collective-permute-start(bf16[2,4,2,64,512]{4,3,2,1,0:T(8,128)(2,1)} %get-tuple-element.464), channel_id=1, source_target_pairs={{0,8},{8,0},{16,24},{24,16},{1,9},{9,1},{17,25},{25,17},{2,10},{10... | collective-permute-start | bytes 3145736 | tf_op jit(solution)/shard_map/ppermute | solution.py:308
  184.2 57.1 %collective-permute-start.8 = (bf16[1,2,4,4,64,512]{5,4,3,2,1,0:T(8,128)(2,1)}, bf16[1,2,4,4,64,512]{5,4,3,2,1,0:T(8,128)(2,1)}, u32[]{:S(2)}, u32[]{:S(2)}) collective-permute-start(bf16[1,2,4,4,64,512]{5,4,3,2,1,0:T(8,128)(2,1)} %maximum_bitcast_fusion), channel_id=1, source_target_pairs={{0,2},{2,0},{1,3},{3,1},{4,6},{6,4},{5,7},{7,5},{8,10},{10,8},{9,1... | collective-permute-start | bytes 6291464 | tf_op jit(solution)/shard_map/ppermute | solution.py:308
  312.8 65.9 %collective-permute-start.19 = (bf16[1408,256]{1,0:T(8,128)(2,1)S(1)}, bf16[1408,256]{1,0:T(8,128)(2,1)}, u32[]{:S(2)}, u32[]{:S(2)}) collective-permute-start(bf16[1408,256]{1,0:T(8,128)(2,1)S(1)} %copy-done.60), channel_id=1, source_target_pairs={{0,24},{8,16},{16,8},{24,0},{1,25},{9,17},{17,9},{25,1},{2,26},{10... | collective-permute-start | bytes 2162696 | tf_op jit(solution)/shard_map/ppermute | solution.py:308
  324.0 50.4 %collective-permute-start.14 = (bf16[4,2,1,64,1024]{4,3,0,1,2:T(8,128)(2,1)}, bf16[4,2,1,64,1024]{4,3,0,1,2:T(8,128)(2,1)}, u32[]{:S(2)}, u32[]{:S(2)}) collective-permute-start(bf16[4,2,1,64,1024]{4,3,0,1,2:T(8,128)(2,1)} %get-tuple-element.454), channel_id=1, source_target_pairs={{0,1},{1,0},{2,3},{3,2},{4,5},{5,4},{6,7},{7,6},{8,9},{9,8},{10,11... | collective-permute-start | bytes 3145736 | tf_op jit(solution)/shard_map/ppermute | solution.py:308
  403.4 68.3 %collective-permute-start.21 = (bf16[1408,256]{1,0:T(8,128)(2,1)S(1)}, bf16[1408,256]{1,0:T(8,128)(2,1)}, u32[]{:S(2)}, u32[]{:S(2)}) collective-permute-start(bf16[1408,256]{1,0:T(8,128)(2,1)S(1)} %copy-done.59), channel_id=1, source_target_pairs={{0,4},{4,0},{1,5},{5,1},{2,6},{6,2},{3,7},{7,3},{8,12},{12,8},{9,1... | collective-permute-start | bytes 2162696 | tf_op jit(solution)/shard_map/ppermute | solution.py:302
  475.4 67.8 %collective-permute-start.41 = (bf16[4,1056,256]{2,1,0:T(8,128)(2,1)}, bf16[4,1056,256]{2,1,0:T(8,128)(2,1)}, u32[]{:S(2)}, u32[]{:S(2)}) collective-permute-start(bf16[4,1056,256]{2,1,0:T(8,128)(2,1)} %slice_bitcast_fusion.1), channel_id=1, source_target_pairs={{0,4},{4,0},{1,5},{5,1},{2,6},{6,2},{3,7},{7,3},{8,12},{12,8},{9,1... | collective-permute-start | bytes 6488072 | tf_op jit(solution)/shard_map/ppermute | solution.py:302
  522.4 164.2 %collective-permute-start.40 = (bf16[4,1,2,64,1024]{4,3,0,2,1:T(8,128)(2,1)}, bf16[4,1,2,64,1024]{4,3,0,2,1:T(8,128)(2,1)}, u32[]{:S(2)}, u32[]{:S(2)}) collective-permute-start(bf16[4,1,2,64,1024]{4,3,0,2,1:T(8,128)(2,1)} %slice_bitcast_fusion.15), channel_id=1, source_target_pairs={{0,2},{2,0},{1,3},{3,1},{4,6},{6,4},{5,7},{7,5},{8,10},{10,8},{9,1... | collective-permute-start | bytes 3145736 | tf_op jit(solution)/shard_map/ppermute | solution.py:308
  546.8 54.1 %collective-permute-start.46 = (bf16[1056,256]{1,0:T(8,128)(2,1)}, bf16[1056,256]{1,0:T(8,128)(2,1)S(1)}, u32[]{:S(2)}, u32[]{:S(2)}) collective-permute-start(bf16[1056,256]{1,0:T(8,128)(2,1)} %get-tuple-element.420), channel_id=1, source_target_pairs={{0,8},{8,0},{16,24},{24,16},{1,9},{9,1},{17,25},{25,17},{2,10},{10... | collective-permute-start | bytes 1622024 | tf_op jit(solution)/shard_map/ppermute | solution.py:308
  600.9 72.5 %collective-permute-start.56 = (bf16[1056,256]{1,0:T(8,128)(2,1)}, bf16[1056,256]{1,0:T(8,128)(2,1)}, u32[]{:S(2)}, u32[]{:S(2)}) collective-permute-start(bf16[1056,256]{1,0:T(8,128)(2,1)} %get-tuple-element.418), channel_id=1, source_target_pairs={{0,24},{8,16},{16,8},{24,0},{1,25},{9,17},{17,9},{25,1},{2,26},{10... | collective-permute-start | bytes 1622024 | tf_op jit(solution)/shard_map/ppermute | solution.py:308
  686.1 88.1 %collective-permute-start.39 = (bf16[4,2,1,64,1024]{4,3,0,1,2:T(8,128)(2,1)}, bf16[4,2,1,64,1024]{4,3,0,1,2:T(8,128)(2,1)}, u32[]{:S(2)}, u32[]{:S(2)}) collective-permute-start(bf16[4,2,1,64,1024]{4,3,0,1,2:T(8,128)(2,1)} %slice_bitcast_fusion.17), channel_id=1, source_target_pairs={{0,1},{1,0},{2,3},{3,2},{4,5},{5,4},{6,7},{7,6},{8,9},{9,8},{10,11... | collective-permute-start | bytes 3145736 | tf_op jit(solution)/shard_map/ppermute | solution.py:308
  717.6 59.2 %collective-permute-start.43 = (bf16[4,1,2,64,1024]{4,3,0,2,1:T(8,128)(2,1)}, bf16[4,1,2,64,1024]{4,3,0,2,1:T(8,128)(2,1)}, u32[]{:S(2)}, u32[]{:S(2)}) collective-permute-start(bf16[4,1,2,64,1024]{4,3,0,2,1:T(8,128)(2,1)} %slice_bitcast_fusion.11), channel_id=1, source_target_pairs={{0,2},{2,0},{1,3},{3,1},{4,6},{6,4},{5,7},{7,5},{8,10},{10,8},{9,1... | collective-permute-start | bytes 3145736 | tf_op jit(solution)/shard_map/ppermute | solution.py:308
  756.6 61.3 %all-to-all-start.5 = ((bf16[4,128,2048]{2,1,0:T(8,128)(2,1)}), bf16[4,128,2048]{2,1,0:T(8,128)(2,1)}, u32[]{:S(2)}, u32[]{:S(2)}) async-start(bf16[4,128,2048]{2,1,0:T(8,128)(2,1)} %broadcast_in_dim.71), calls=%async_computation.5 | async-start | bytes 4194304 | tf_op jit(solution)/shard_map/all_to_all | solution.py:331
  761.1 263.9 %reduce-scatter.5.cloned.1.call-start = ((), (), s32[]{:S(2)}) async-start(), calls=%async_computation.17 | async-start | bytes 2359296 | tf_op jit(solution)/shard_map/reduce_scatter | solution.py:678
  767.7 50.3 %collective-permute-start.64 = (bf16[1408,256]{1,0:T(8,128)(2,1)S(1)}, bf16[1408,256]{1,0:T(8,128)(2,1)}, u32[]{:S(2)}, u32[]{:S(2)}) collective-permute-start(bf16[1408,256]{1,0:T(8,128)(2,1)S(1)} %get-tuple-element.401), channel_id=1, source_target_pairs={{0,8},{8,0},{16,24},{24,16},{1,9},{9,1},{17,25},{25,17},{2,10},{10... | collective-permute-start | bytes 2162696 | tf_op jit(solution)/shard_map/ppermute | solution.py:308
  807.4 73.5 %collective-permute-start.69 = (bf16[1408,256]{1,0:T(8,128)(2,1)}, bf16[1408,256]{1,0:T(8,128)(2,1)}, u32[]{:S(2)}, u32[]{:S(2)}) collective-permute-start(bf16[1408,256]{1,0:T(8,128)(2,1)} %get-tuple-element.400), channel_id=1, source_target_pairs={{0,16},{8,24},{16,0},{24,8},{1,17},{9,25},{17,1},{25,9},{2,18},{10... | collective-permute-start | bytes 2162696 | tf_op jit(solution)/shard_map/ppermute | solution.py:308
  816.3 109.5 %collective-permute-start.74 = (bf16[1408,256]{1,0:T(8,128)(2,1)}, bf16[1408,256]{1,0:T(8,128)(2,1)}, u32[]{:S(2)}, u32[]{:S(2)}) collective-permute-start(bf16[1408,256]{1,0:T(8,128)(2,1)} %get-tuple-element.399), channel_id=1, source_target_pairs={{0,24},{8,16},{16,8},{24,0},{1,25},{9,17},{17,9},{25,1},{2,26},{10... | collective-permute-start | bytes 2162696 | tf_op jit(solution)/shard_map/ppermute | solution.py:308
  834.2 192.8 %reduce-scatter.3.cloned.1.call-start = ((), (), s32[]{:S(2)}) async-start(), calls=%async_computation.16 | async-start | bytes 7077888 | tf_op jit(solution)/shard_map/reduce_scatter | solution.py:679
  (173 other events, 2915.0 us)
Sparse Core Ops, SparseCore 0:
  9.6 124.6 all-gather.2
  135.9 34.9 all-gather.4
  834.3 46.8 reduce-scatter.4
  931.5 68.1 reduce-scatter.2

commit v6 on v5

--- a/solution.py
+++ b/solution.py
@@ -317,12 +317,14 @@
     return value
 
 
-def halve(value, axis, at, bit):
+def halve(value, axis, at, bit, after=None):
     size = value.shape[at]
     shape = value.shape[:at] + (size // 2, 2) + value.shape[at + 1 :]
     pair = value.reshape(shape)
     keep, send = (lax.index_in_dim(pair, i, at + 1, keepdims=False) for i in range(2))
     other = shift_by(send, axis, bit)
+    if after is not None:
+        keep, _ = tie(keep, after)
     return (keep.astype(F32) + other.astype(F32)).astype(BF16)
 
 
@@ -399,6 +401,9 @@
         ],
         axis=0,
     )
+    small_all = lax.all_to_all(
+        jnp.broadcast_to(small[None], (n_row,) + small.shape), ROW, 0, 0, tiled=True
+    )
     f_shared = shared_gate.shape[1] // n_g
     f_routed = expert_gate.shape[2] // n_g
     f_experts = local_experts * f_routed
@@ -423,7 +428,11 @@
         slices_e(expert_down),
     ]
     picked = [[pick(value, at_g ^ shift) for shift in range(n_g)] for value in weight_slices]
-    picked[0], tokens, cotangent = tie(picked[0], tokens, cotangent)
+    qkv = lax.all_gather(
+        jnp.concatenate([query_weight, key_weight, value_weight], axis=1), ROW, axis=0, tiled=True
+    )
+    out_w = lax.all_gather(output_weight, ROW, axis=1, tiled=True)
+    picked[0], qkv, small_all = tie(picked[0], qkv, small_all)
     own_blocks = [
         [shift_by(value, "g", shift) for shift, value in enumerate(values)] for values in picked
     ]
@@ -433,18 +442,11 @@
 
     sub = own_rows // PARTS
     cot_rows = cot_part.reshape(1, n_c, PARTS, sub, dim // n_c)
+    cot_rows, qkv = tie(cot_rows, qkv)
     cot_rows = gather_joined(cot_rows, "g", 0)
-    qkv = lax.all_gather(
-        jnp.concatenate([query_weight, key_weight, value_weight], axis=1), ROW, axis=0, tiled=True
-    )
-    out_w = lax.all_gather(output_weight, ROW, axis=1, tiled=True)
     inputs = col_gather(token_part, n_c).reshape(n_c, span, -1).transpose(1, 0, 2)
     inputs = inputs.reshape(span, dim).astype(F32)
 
-    small, inputs = tie(small, inputs)
-    small_all = lax.all_to_all(
-        jnp.broadcast_to(small[None], (n_row,) + small.shape), ROW, 0, 0, tiled=True
-    )
     gain_1 = small_all[:, 16, :d_own].reshape(dim)
     gain_2 = small_all[:, 17, :d_own].reshape(dim)
     logit_w = small_all[:, 18, :d_own].reshape(dim)
@@ -455,14 +457,6 @@
         pick(mixing_all, at_k, 1), at_c * local_experts, local_experts, 1
     )
     mixing_own = mixing_own.transpose(0, 2, 1).reshape(total, local_experts)
-
-    own_blocks[0][1:], inputs, cot_rows = tie(own_blocks[0][1:], inputs, cot_rows)
-    cot_all = []
-    for part in range(PARTS):
-        value = cot_rows[:, :, part][None, None]
-        for axis in ("x", "y") if part % 2 else ("y", "x"):
-            value = gather_joined(value, axis, ("y", "x").index(axis))
-        cot_all.append(value.reshape(n_c, n_g, n_c, sub, dim // n_c))
 
     first_scale = lax.rsqrt(jnp.mean(inputs * inputs, axis=-1, keepdims=True) + epsilon)
     normed_1 = (inputs * first_scale * gain_1).astype(BF16)
@@ -487,10 +481,17 @@
     probabilities = exp_scores / jnp.sum(exp_scores, axis=-1, keepdims=True)
     prob_low = probabilities.astype(BF16)
     mixed = einsum("bhqk,bkhd->bqhd", prob_low, value_low).astype(BF16).reshape(span, width)
+    cot_rows, mixed, own_blocks[0][1] = tie(cot_rows, mixed, own_blocks[0][1])
+    cot_all = []
+    for part in range(PARTS):
+        value = cot_rows[:, :, part][None, None]
+        for axis in ("x", "y") if part % 2 else ("y", "x"):
+            value = gather_joined(value, axis, ("y", "x").index(axis))
+        cot_all.append(value.reshape(n_c, n_g, n_c, sub, dim // n_c))
     attention = col_sum(dot(mixed, out_w, ((1,), (0,))), n_c)
 
     own_inputs = lax.dynamic_slice_in_dim(inputs, at_c * own_rows, own_rows, 0)
-    cot_all, attention = tie(cot_all, attention)
+    own_blocks[0][2:], attention = tie(own_blocks[0][2:], attention)
     hidden = own_inputs + attention
     second_scale = lax.rsqrt(jnp.mean(hidden * hidden, axis=-1, keepdims=True) + epsilon)
     unit_2 = hidden * second_scale
@@ -506,17 +507,18 @@
         return jnp.concatenate(sides, axis=-1).reshape(-1, dim)
 
     routed_gu, routed_d = own_blocks[1:]
-    routed_gu[1], normed_own = tie(routed_gu[1], normed_own)
     halves = [normed_own[part * sub : (part + 1) * sub][None] for part in range(PARTS)]
     halves[0] = gather_joined(halves[0], "g", 0)
-    halves[0], halves[1], routed_gu[2:3] = tie(halves[0], halves[1], routed_gu[2:3])
+    halves[0], halves[1], routed_gu[1] = tie(halves[0], halves[1], routed_gu[1])
     halves[1] = gather_joined(halves[1], "g", 0)
     normed_parts = [gather_cols(halves[0][:, None, None])]
-    normed_parts[0], halves[1], routed_gu[3:], routed_d[1] = tie(
-        normed_parts[0], halves[1], routed_gu[3:], routed_d[1]
+    normed_parts[0], halves[1], routed_gu[2:3], cot_all = tie(
+        normed_parts[0], halves[1], routed_gu[2:3], cot_all
     )
     normed_parts.append(gather_cols(halves[1][:, None, None]))
-    normed_parts[1], routed_d[2:3] = tie(normed_parts[1], routed_d[2:3])
+    normed_parts[1], routed_gu[3:], routed_d[1] = tie(
+        normed_parts[1], routed_gu[3:], routed_d[1]
+    )
     own_cot = [
         lax.dynamic_index_in_dim(cot[:, 0], at_c, 1, keepdims=False) for cot in cot_all
     ]
@@ -524,9 +526,12 @@
     own_cot = jnp.stack([pick(own_cot, at_c ^ c) for c in range(n_c)], axis=1)
     own_cot = own_cot.reshape(own_rows, dim)
 
-    def own_core(grad):
+    def own_core(grad, after=None):
         other = swap(grad[1], "k")
-        return (grad[0].astype(F32) + other.astype(F32)).astype(BF16)
+        grad = grad[0]
+        if after is not None:
+            grad, _ = tie(grad, after)
+        return (grad.astype(F32) + other.astype(F32)).astype(BF16)
 
     def send_slices(both):
         return [shift_by(both[shift], "g", shift) for shift in range(n_g)]
@@ -570,7 +575,7 @@
     passes = []
     for part in range(PARTS):
         if part == 1:
-            both_s = own_core(grad_s)
+            both_s = own_core(grad_s, passes[0][2][:16, :128])
             sums[1], both_s = tie(sums[1], both_s)
         passes.append(
             ffn_pass(
@@ -589,15 +594,15 @@
         part = partial.reshape(n_g, n_y, n_x, sub, dim)
         return [part[..., : dim // 2], part[..., dim // 2 :]]
 
-    def scatter_axis(value, axis, at):
+    def scatter_axis(value, axis, at, after=None):
         bit = 1
         while bit < lax.axis_size(axis):
-            value = halve(value, axis, at, bit)
+            value = halve(value, axis, at, bit, after)
             bit *= 2
         return lax.index_in_dim(value, 0, at, keepdims=False)
 
-    def cols_first(sides):
-        return [scatter_axis(sides[0], "x", 2), scatter_axis(sides[1], "y", 1)]
+    def cols_first(sides, after=None):
+        return [scatter_axis(sides[0], "x", 2, after), scatter_axis(sides[1], "y", 1, after)]
 
     def cols_second(sides):
         sides = [scatter_axis(sides[0], "y", 1), scatter_axis(sides[1], "x", 1)]
@@ -615,7 +620,7 @@
         return value[0].astype(F32) + other.astype(F32)
 
     acts, gates, ups = ([parts[i] for parts in passes] for i in (2, 3, 4))
-    first = cols_first(split_sides(passes[0][1]))
+    first = cols_first(split_sides(passes[0][1]), passes[1][2][:16, :128])
     first, acts, moved_s[1:3] = tie(first, acts, moved_s[1:3])
     (grad_d,) = weight_grad(sizes_e, meta, (True,), [acts], normed_parts, cot_all)
     first = cols_second(first)
@@ -635,34 +640,34 @@
     out_sides = [cols_first(split_sides(parts[0])) for parts in passes]
     moved_gu = send_slices(both_gu)
     normed_grad_2 = jnp.concatenate([first, second], axis=0)
-    normed_grad_2, moved_d[1:] = tie(normed_grad_2, moved_d[1:])
+    normed_grad_2, moved_d[1] = tie(normed_grad_2, moved_d[1])
     hidden_part, gain_2_sum = norm_back(normed_grad_2, unit_2, second_scale, gain_2)
     hidden_grad = own_cot.astype(F32) + hidden_part
     attn_grad = col_gather(hidden_grad.astype(BF16), n_c).reshape(span, dim)
-    out_sides, attn_grad, moved_gu[1] = tie(out_sides, attn_grad, moved_gu[1])
-    out_parts = [cols_second(sides) for sides in out_sides]
+    attn_grad, moved_d[2:], moved_gu[1] = tie(attn_grad, moved_d[2:], moved_gu[1])
     gate_s, up_s, down_s = (place_s(value) for value in place_slices(moved_s, 3))
     down_e = place_e(place_slices(moved_d, 1)[0])
 
     out_grad = dot(attn_grad, mixed, ((0,), (0,)))
     mixed_grad = dot(attn_grad, out_w, ((1,), (1,))).astype(BF16).reshape(head_shape)
-    out_parts, mixed_grad, moved_gu[2:3] = tie(out_parts, mixed_grad, moved_gu[2:3])
-    out_parts = [chips_steps(part) for part in out_parts]
+    out_sides, mixed_grad = tie(out_sides, mixed_grad)
+    out_parts = [cols_second(sides) for sides in out_sides]
     prob_grad = einsum("bqhd,bkhd->bhqk", mixed_grad, value_low)
     value_grad = einsum("bhqk,bqhd->bkhd", prob_low, mixed_grad).astype(BF16)
     center = jnp.sum(prob_grad * probabilities, axis=-1, keepdims=True)
     score_grad = (probabilities * (prob_grad - center) * (1.0 / math.sqrt(HEAD_DIM))).astype(BF16)
-    out_parts, score_grad = tie(out_parts, score_grad)
-    out_rows = [chips_last(part) for part in out_parts]
+    out_parts, score_grad, moved_gu[2:3] = tie(out_parts, score_grad, moved_gu[2:3])
+    out_parts = [chips_steps(part) for part in out_parts]
     query_grad = rotate(einsum("bhqk,bkhd->bqhd", score_grad, key_rot), cosine, -sine).astype(BF16)
     key_grad = rotate(einsum("bhqk,bqhd->bkhd", score_grad, query_rot), cosine, -sine).astype(BF16)
     qkv_grad = jnp.concatenate(
         [part.reshape(span, width) for part in (query_grad, key_grad, value_grad)], axis=1
     )
-    qkv_grad, out_rows, moved_gu[3:] = tie(qkv_grad, out_rows, moved_gu[3:])
-    out_rows = jnp.concatenate(out_rows, axis=0)
+    qkv_grad, out_parts = tie(qkv_grad, out_parts)
+    out_rows = jnp.concatenate([chips_last(part) for part in out_parts], axis=0)
     qkv_sum = dot(normed_1, qkv_grad, ((0,), (0,)))
     normed_grad_1 = col_sum(dot(qkv_grad, qkv, ((1,), (1,))), n_c)
+    normed_grad_1, out_rows, moved_gu[3:] = tie(normed_grad_1, out_rows, moved_gu[3:])
     gate_e, up_e = (place_e(value) for value in place_slices(moved_gu, 2))
     own_scale = lax.dynamic_slice_in_dim(first_scale, at_c * own_rows, own_rows, 0)
     rows_part, gain_1_sum = norm_back(normed_grad_1, own_inputs * own_scale, own_scale, gain_1)

time: 1050 us -> 1040 us (level)
  starting transfers between devices: 145 us -> 132 us
    all_to_all x2, waiting for transfers between devices: 30.8 us -> 4.13 us  [col_sum(): lax.all_to_all(parts, COL, 0, 0, tiled=True).astype(F32)]
    ppermute x60, starting transfers between devices: 105 us -> 86.7 us  [shift_by(): lax.ppermute(value, axis, [(i, i ^ shift) for i in range(lax.axis_size(ax...]
    all_to_all x2, waiting for transfers between devices: 0.01 us -> 12.5 us  [col_gather(): return lax.all_to_all(spread, COL, 0, 0, tiled=True)]
    all_gather x1, waiting for transfers between devices: 0.01 us -> 11.3 us  [shards(): lax.all_gather(jnp.concatenate([query_weight, key_weight, value_weight],...]
    unnamed x238 -> x233, local copies, waits for them, and re-layouts: 35.8 us -> 42.8 us
  transfers between devices with their start and end apart: 88 -> 89, of which waited for: 34 -> 34; matrix products, arithmetic and copies ran while one was open for 25% -> 26% of each run, Pallas kernels for 15% -> 15%
where the time goes in v6:
time: 1040 us; the launch traced here: 1030 us
  waiting for transfers between devices  424 us (41%)
  Pallas kernels  160 us (15%)
  local copies, waits for them, and re-layouts  141 us (14%)
  starting transfers between devices  132 us (13%)
  other arithmetic  112 us (11%)
  matrix products  39.5 us (4%)
  between operations  16.2 us (2%)
    ppermute x60, waiting for transfers between devices, shift_by(): lax.ppermute(value, axis, [(i, i ^ shift) for i in range(lax.axis_size(ax...  377 us
    pallas_call x4, Pallas kernels, ffn_pass(): pl.pallas_call(functools.partial(ffn_kernel, sizes, groups), grid_spec=pl...  112 us
    ppermute x60, starting transfers between devices, shift_by(): lax.ppermute(value, axis, [(i, i ^ shift) for i in range(lax.axis_size(ax...  86.7 us
    pallas_call x3, Pallas kernels, weight_grad(): pl.pallas_call(functools.partial(grad_kernel, parts, kinds, f_pad), grid_...  47.4 us
    unnamed x233, local copies, waits for them, and re-layouts  42.8 us
    dot_general x6, matrix products, dot(): lax.dot_general(left, right, (dims, ((), ())), preferred_element_type=F32)  29 us
    another operation x15, other arithmetic, gather_joined(): jnp.stack([value, shift_by(value, axis, bit)], axis=at + 1).reshape(shape)  25.1 us
    squeeze x16, other arithmetic, scatter_axis(): return lax.index_in_dim(value, 0, at, keepdims=False)  22.3 us
  transfers between devices with their start and end apart: 89, of which 34 were waited for; matrix products, arithmetic and copies ran while one was open for 26% of the time, Pallas kernels for 15%

profile of v6, /device:TPU:0, one launch (start us, length us, event | category | flops | bytes accessed | tf_op | source)
XLA Modules:
  0.0 1033.0 jit_solution(8750591107633315193)
XLA Ops:
  33.0 12.5 %all-to-all-done.1 = bf16[4,512,512]{2,1,0:T(8,128)(2,1)S(1)} async-done(((bf16[4,512,512]{2,1,0:T(8,128)(2,1)}), bf16[4,512,512]{2,1,0:T(8,128)(2,1)S(1)}, u32[]{:S(2)}, u32[]{:S(2)}) %all-to-all-start.1) | async-done | bytes 2097184 | tf_op jit(solution)/shard_map/all_to_all | solution.py:333
  55.0 11.0 %all-to-all-done.2 = f32[8,24,256]{2,1,0:T(8,128)S(1)} async-done(((f32[8,24,256]{2,1,0:T(8,128)}), f32[8,24,256]{2,1,0:T(8,128)S(1)}, u32[]{:S(2)}, u32[]{:S(2)}) %all-to-all-start.2) | async-done | bytes 196640 | tf_op jit(solution)/shard_map/all_to_all | solution.py:404
  70.5 11.3 %all-gather.3.cloned.1.call-done = bf16[2048,1536]{1,0:T(8,128)(2,1)} async-done(((bf16[256,1536]{1,0:T(8,128)(2,1)}), bf16[2048,1536]{1,0:T(8,128)(2,1)}) %all-gather.3.cloned.1.call-update) | async-done | bytes 6291472 | tf_op jit(solution)/shard_map/all_gather | solution.py:431
  97.0 21.8 %collective-permute-done.2 = bf16[1,4,2,64,512]{4,3,2,1,0:T(8,128)(2,1)} collective-permute-done((bf16[1,4,2,64,512]{4,3,2,1,0:T(8,128)(2,1)}, bf16[1,4,2,64,512]{4,3,2,1,0:T(8,128)(2,1)}, u32[]{:S(2)}, u32[]{:S(2)}) %collective-permute-start.2) | collective-permute-done | bytes 524320 | tf_op jit(solution)/shard_map/ppermute | solution.py:308
  128.3 28.1 %collective-permute-done.3 = bf16[2,4,2,64,512]{4,3,2,1,0:T(8,128)(2,1)} collective-permute-done((bf16[2,4,2,64,512]{4,3,2,1,0:T(8,128)(2,1)}, bf16[2,4,2,64,512]{4,3,2,1,0:T(8,128)(2,1)}, u32[]{:S(2)}, u32[]{:S(2)}) %collective-permute-start.3) | collective-permute-done | bytes 1048608 | tf_op jit(solution)/shard_map/ppermute | solution.py:308
  208.3 12.4 %collective-permute-start.5 = (bf16[1,64,2048]{2,1,0:T(8,128)(2,1)S(1)}, bf16[1,64,2048]{2,1,0:T(8,128)(2,1)S(1)}, u32[]{:S(2)}, u32[]{:S(2)}) collective-permute-start(bf16[1,64,2048]{2,1,0:T(8,128)(2,1)S(1)} %get-tuple-element.481), channel_id=1, source_target_pairs={{0,16},{8,24},{16,0},{24,8},{1,17},{9,25},{17,1},{25,9},{2,18},{10... | collective-permute-start | bytes 786440 | tf_op jit(solution)/shard_map/ppermute | solution.py:308
  242.7 12.0 %collective-permute-done.6 = bf16[2,64,2048]{2,1,0:T(8,128)(2,1)S(1)} collective-permute-done((bf16[2,64,2048]{2,1,0:T(8,128)(2,1)S(1)}, bf16[2,64,2048]{2,1,0:T(8,128)(2,1)S(1)}, u32[]{:S(2)}, u32[]{:S(2)}) %collective-permute-start.6) | collective-permute-done | bytes 524320 | tf_op jit(solution)/shard_map/ppermute | solution.py:308
  266.8 28.4 %collective-permute-done.10 = bf16[4,1,1,64,1024]{4,3,0,2,1:T(8,128)(2,1)} collective-permute-done((bf16[4,1,1,64,1024]{4,3,0,2,1:T(8,128)(2,1)}, bf16[4,1,1,64,1024]{4,3,0,2,1:T(8,128)(2,1)}, u32[]{:S(2)}, u32[]{:S(2)}) %collective-permute-start.10) | collective-permute-done | bytes 524320 | tf_op jit(solution)/shard_map/ppermute | solution.py:308
  315.2 11.6 %collective-permute-done.13 = bf16[2,64,2048]{2,1,0:T(8,128)(2,1)} collective-permute-done((bf16[2,64,2048]{2,1,0:T(8,128)(2,1)}, bf16[2,64,2048]{2,1,0:T(8,128)(2,1)}, u32[]{:S(2)}, u32[]{:S(2)}) %collective-permute-start.13) | collective-permute-done | bytes 524320 | tf_op jit(solution)/shard_map/ppermute | solution.py:308
  362.5 21.2 %ffn_pass.4 = (bf16[1024,2048]{1,0:T(8,128)(2,1)}, bf16[1024,2048]{1,0:T(8,128)(2,1)}, bf16[352,1024]{1,0:T(8,128)(2,1)}, bf16[368,1024]{1,0:T(8,128)(2,1)}, bf16[352,1024]{1,0:T(8,128)(2,1)}) custom-call(s32[3]{0:T(128)} %pad_add_fusion.meta, bf16[1024,2048]{1,0:T(8,128)(2,1)} %pad_maximum_fusion.rows_ref.refs_6_.refs_4_, ...), custom_call_target="tpu_custom_call" | custom-call | flops 8858370048 | bytes 23265280 | tf_op jit(solution)/shard_map/ffn_pass/pallas_call | solution.py:172
  394.6 21.3 %collective-permute-done.29.refs_10_ = bf16[704,256]{1,0:T(8,128)(2,1)S(1)} collective-permute-done((bf16[704,256]{1,0:T(8,128)(2,1)}, bf16[704,256]{1,0:T(8,128)(2,1)S(1)}, u32[]{:S(2)}, u32[]{:S(2)}) %collective-permute-start.29) | collective-permute-done | bytes 360480 | tf_op jit(solution)/shard_map/ppermute | solution.py:308
  416.5 21.0 %ffn_pass.5 = (bf16[1024,2048]{1,0:T(8,128)(2,1)}, bf16[1024,2048]{1,0:T(8,128)(2,1)}, bf16[352,1024]{1,0:T(8,128)(2,1)}, bf16[368,1024]{1,0:T(8,128)(2,1)}, bf16[352,1024]{1,0:T(8,128)(2,1)}) custom-call(s32[3]{0:T(128)} %pad_add_fusion.meta, bf16[1024,2048]{1,0:T(8,128)(2,1)} %pad_maximum_fusion.3.rows_ref.refs_7_.refs_5_, ...), custom_call_target="tpu_custom_call" | custom-call | flops 8858370048 | bytes 23265280 | tf_op jit(solution)/shard_map/ffn_pass/pallas_call | solution.py:172
  437.6 16.7 %weight_grad.3 = (bf16[2,4,1056,256]{3,2,1,0:T(8,128)(2,1)}, f32[8,2048]{1,0:T(8,128)}) custom-call(s32[3]{0:T(128)} %pad_add_fusion.meta, bf16[368,1024]{1,0:T(8,128)(2,1)} %get-tuple-element.196.refs_0_, bf16[368,1024]{1,0:T(8,128)(2,1)} %get-tuple-element.199.refs_1_, bf16[352,1024]{1,0:T(8,128)(2,1)} %get-tuple-element.200.refs_2_, ...), custom_call_target="tpu_custom_call" | custom-call | flops 8858370048 | bytes 17039360 | tf_op jit(solution)/shard_map/weight_grad/pallas_call | solution.py:271
  461.7 34.9 %ffn_pass.6 = (bf16[1024,2048]{1,0:T(8,128)(2,1)}, bf16[1024,2048]{1,0:T(8,128)(2,1)}, bf16[704,1024]{1,0:T(8,128)(2,1)}, bf16[704,1024]{1,0:T(8,128)(2,1)}, bf16[704,1024]{1,0:T(8,128)(2,1)}) custom-call(s32[3]{0:T(128)} %pad_add_fusion.meta, bf16[1024,2048]{1,0:T(8,128)(2,1)} %pad_maximum_fusion.rows_ref.refs_6_.refs_4_, ...), custom_call_target="tpu_custom_call" | custom-call | flops 17716740096 | bytes 46530560 | tf_op jit(solution)/shard_map/ffn_pass/pallas_call | solution.py:172
  512.5 35.1 %ffn_pass.7 = (bf16[1024,2048]{1,0:T(8,128)(2,1)}, bf16[1024,2048]{1,0:T(8,128)(2,1)}, bf16[704,1024]{1,0:T(8,128)(2,1)}, bf16[704,1024]{1,0:T(8,128)(2,1)}, bf16[704,1024]{1,0:T(8,128)(2,1)}) custom-call(s32[3]{0:T(128)} %pad_add_fusion.meta, bf16[1024,2048]{1,0:T(8,128)(2,1)} %pad_maximum_fusion.3.rows_ref.refs_7_.refs_5_, ...), custom_call_target="tpu_custom_call" | custom-call | flops 17716740096 | bytes 46530560 | tf_op jit(solution)/shard_map/ffn_pass/pallas_call | solution.py:172
  564.8 14.0 %collective-permute-done.46 = bf16[1056,256]{1,0:T(8,128)(2,1)} collective-permute-done((bf16[1056,256]{1,0:T(8,128)(2,1)S(1)}, bf16[1056,256]{1,0:T(8,128)(2,1)}, u32[]{:S(2)}, u32[]{:S(2)}) %collective-permute-start.46) | collective-permute-done | bytes 540704 | tf_op jit(solution)/shard_map/ppermute | solution.py:308
  580.9 13.7 %collective-permute-done.47 = bf16[1056,256]{1,0:T(8,128)(2,1)} collective-permute-done((bf16[1056,256]{1,0:T(8,128)(2,1)S(1)}, bf16[1056,256]{1,0:T(8,128)(2,1)}, u32[]{:S(2)}, u32[]{:S(2)}) %collective-permute-start.47) | collective-permute-done | bytes 540704 | tf_op jit(solution)/shard_map/ppermute | solution.py:308
  597.3 12.4 %weight_grad.4 = bf16[2,4,704,256]{3,2,1,0:T(8,128)(2,1)} custom-call(s32[3]{0:T(128)} %pad_add_fusion.meta, bf16[704,1024]{1,0:T(8,128)(2,1)} %get-tuple-element.225.refs_0_, bf16[704,1024]{1,0:T(8,128)(2,1)} %get-tuple-element.226.refs_1_, bf16[4,4,4,64,512]{4,3,2,1,0:T(8,128)(2,1)} %bitcast.587, bf16[4,4,4,64,512]{4,3,2,1,0:T(8,128)(2,1)} %bitcast.592), custom_call_target="tpu_custom_call" | custom-call | flops 5905580032 | bytes 14155776 | tf_op jit(solution)/shard_map/weight_grad/pallas_call | solution.py:271
  623.0 18.3 %weight_grad.5 = bf16[2,4,1408,256]{3,2,1,0:T(8,128)(2,1)} custom-call(s32[3]{0:T(128)} %pad_add_fusion.meta, bf16[704,1024]{1,0:T(8,128)(2,1)} %get-tuple-element.231.refs_0_, bf16[704,1024]{1,0:T(8,128)(2,1)} %get-tuple-element.232.refs_1_, bf16[704,1024]{1,0:T(8,128)(2,1)} %get-tuple-element.233.refs_2_, bf16[704,1024]{1,0:T(8,128)(2,1)} %get-tuple-element.234.refs_3_, ...), custom_call_target="tpu_custom_call" | custom-call | flops 11811160064 | bytes 19922944 | tf_op jit(solution)/shard_map/weight_grad/pallas_call | solution.py:271
  641.9 13.9 %collective-permute-done.52 = bf16[2,64,2048]{2,1,0:T(8,128)(2,1)S(1)} collective-permute-done((bf16[2,64,2048]{2,1,0:T(8,128)(2,1)S(1)}, bf16[2,64,2048]{2,1,0:T(8,128)(2,1)S(1)}, u32[]{:S(2)}, u32[]{:S(2)}) %collective-permute-start.52) | collective-permute-done | bytes 524320 | tf_op jit(solution)/shard_map/ppermute | solution.py:308
  672.3 13.1 %collective-permute-done.57 = bf16[64,2048]{1,0:T(8,128)(2,1)S(1)} collective-permute-done((bf16[64,2048]{1,0:T(8,128)(2,1)S(1)}, bf16[64,2048]{1,0:T(8,128)(2,1)S(1)}, u32[]{:S(2)}, u32[]{:S(2)}) %collective-permute-start.57) | collective-permute-done | bytes 262176 | tf_op jit(solution)/shard_map/ppermute | solution.py:308
  739.4 31.5 %collective-permute-done.43 = bf16[4,1,2,64,1024]{4,3,0,2,1:T(8,128)(2,1)S(1)} collective-permute-done((bf16[4,1,2,64,1024]{4,3,0,2,1:T(8,128)(2,1)S(1)}, bf16[4,1,2,64,1024]{4,3,0,2,1:T(8,128)(2,1)S(1)}, u32[]{:S(2)}, u32[]{:S(2)}) %collective-permute-start.43) | collective-permute-done | bytes 1048608 | tf_op jit(solution)/shard_map/ppermute | solution.py:308
  821.7 19.5 %collective-permute-done.70 = bf16[2,64,2048]{2,1,0:T(8,128)(2,1)S(1)} collective-permute-done((bf16[2,64,2048]{2,1,0:T(8,128)(2,1)S(1)}, bf16[2,64,2048]{2,1,0:T(8,128)(2,1)S(1)}, u32[]{:S(2)}, u32[]{:S(2)}) %collective-permute-start.70) | collective-permute-done | bytes 524320 | tf_op jit(solution)/shard_map/ppermute | solution.py:308
  889.1 64.9 %collective-permute-done.73 = bf16[64,2048]{1,0:T(8,128)(2,1)S(1)} collective-permute-done((bf16[64,2048]{1,0:T(8,128)(2,1)S(1)}, bf16[64,2048]{1,0:T(8,128)(2,1)S(1)}, u32[]{:S(2)}, u32[]{:S(2)}) %collective-permute-start.73) | collective-permute-done | bytes 262176 | tf_op jit(solution)/shard_map/ppermute | solution.py:308
  (646 shorter events, 515.9 us)
Async XLA Ops:
  7.2 74.6 %all-gather.3.cloned.1.call-start = ((), (), s32[]{:S(2)}) async-start(), calls=%async_computation.14 | async-start | bytes 7077888 | tf_op jit(solution)/shard_map/all_gather | solution.py:431
  20.4 137.7 %all-gather.5.cloned.1.call-start = ((), (), s32[]{:S(2)}) async-start(), calls=%async_computation.15 | async-start | bytes 2359296 | tf_op jit(solution)/shard_map/all_gather | solution.py:434
  94.0 64.0 %collective-permute-start.4 = (bf16[1056,256]{1,0:T(8,128)(2,1)}, bf16[1056,256]{1,0:T(8,128)(2,1)}, u32[]{:S(2)}, u32[]{:S(2)}) collective-permute-start(bf16[1056,256]{1,0:T(8,128)(2,1)} %get-tuple-element.177), channel_id=1, source_target_pairs={{0,8},{8,0},{16,24},{24,16},{1,9},{9,1},{17,25},{25,17},{2,10},{10... | collective-permute-start | bytes 1622024 | tf_op jit(solution)/shard_map/ppermute | solution.py:308
  188.7 49.8 %collective-permute-start.17 = (bf16[1,1,4,4,64,512]{5,4,3,2,1,0:T(8,128)(2,1)}, bf16[1,1,4,4,64,512]{5,4,3,2,1,0:T(8,128)(2,1)}, u32[]{:S(2)}, u32[]{:S(2)}) collective-permute-start(bf16[1,1,4,4,64,512]{5,4,3,2,1,0:T(8,128)(2,1)} %get-tuple-element.433), channel_id=1, source_target_pairs={{0,1},{1,0},{2,3},{3,2},{4,5},{5,4},{6,7},{7,6},{8,9},{9,8},{10,11... | collective-permute-start | bytes 3145736 | tf_op jit(solution)/shard_map/ppermute | solution.py:308
  236.8 69.1 %collective-permute-start.16 = (bf16[2,1,4,4,64,512]{5,4,3,2,0,1:T(8,128)(2,1)}, bf16[2,1,4,4,64,512]{5,4,3,2,0,1:T(8,128)(2,1)}, u32[]{:S(2)}, u32[]{:S(2)}) collective-permute-start(bf16[2,1,4,4,64,512]{5,4,3,2,0,1:T(8,128)(2,1)} %get-tuple-element.436), channel_id=1, source_target_pairs={{0,1},{1,0},{2,3},{3,2},{4,5},{5,4},{6,7},{7,6},{8,9},{9,8},{10,11... | collective-permute-start | bytes 6291464 | tf_op jit(solution)/shard_map/ppermute | solution.py:308
  241.2 70.2 %collective-permute-start.18 = (bf16[1,2,4,4,64,512]{5,4,3,2,1,0:T(8,128)(2,1)}, bf16[1,2,4,4,64,512]{5,4,3,2,1,0:T(8,128)(2,1)}, u32[]{:S(2)}, u32[]{:S(2)}) collective-permute-start(bf16[1,2,4,4,64,512]{5,4,3,2,1,0:T(8,128)(2,1)} %maximum_bitcast_fusion), channel_id=1, source_target_pairs={{0,2},{2,0},{1,3},{3,1},{4,6},{6,4},{5,7},{7,5},{8,10},{10,8},{9,1... | collective-permute-start | bytes 6291464 | tf_op jit(solution)/shard_map/ppermute | solution.py:308
  359.3 57.2 %collective-permute-start.23 = (bf16[1408,256]{1,0:T(8,128)(2,1)}, bf16[1408,256]{1,0:T(8,128)(2,1)}, u32[]{:S(2)}, u32[]{:S(2)}) collective-permute-start(bf16[1408,256]{1,0:T(8,128)(2,1)} %get-tuple-element.404), channel_id=1, source_target_pairs={{0,24},{8,16},{16,8},{24,0},{1,25},{9,17},{17,9},{25,1},{2,26},{10... | collective-permute-start | bytes 2162696 | tf_op jit(solution)/shard_map/ppermute | solution.py:308
  361.4 93.4 %collective-permute-start.25 = (bf16[1408,256]{1,0:T(8,128)(2,1)S(1)}, bf16[1408,256]{1,0:T(8,128)(2,1)}, u32[]{:S(2)}, u32[]{:S(2)}) collective-permute-start(bf16[1408,256]{1,0:T(8,128)(2,1)S(1)} %copy-done.55), channel_id=1, source_target_pairs={{0,4},{4,0},{1,5},{5,1},{2,6},{6,2},{3,7},{7,3},{8,12},{12,8},{9,1... | collective-permute-start | bytes 2162696 | tf_op jit(solution)/shard_map/ppermute | solution.py:302
  394.6 59.7 %collective-permute-start.31 = (bf16[704,256]{1,0:T(8,128)(2,1)S(1)}, bf16[704,256]{1,0:T(8,128)(2,1)}, u32[]{:S(2)}, u32[]{:S(2)}) collective-permute-start(bf16[704,256]{1,0:T(8,128)(2,1)S(1)} %copy-done.69), channel_id=1, source_target_pairs={{0,4},{4,0},{1,5},{5,1},{2,6},{6,2},{3,7},{7,3},{8,12},{12,8},{9,1... | collective-permute-start | bytes 1081352 | tf_op jit(solution)/shard_map/ppermute | solution.py:302
  460.0 50.4 %collective-permute-start.41 = (bf16[4,1056,256]{2,1,0:T(8,128)(2,1)S(1)}, bf16[4,1056,256]{2,1,0:T(8,128)(2,1)}, u32[]{:S(2)}, u32[]{:S(2)}) collective-permute-start(bf16[4,1056,256]{2,1,0:T(8,128)(2,1)S(1)} %get-tuple-element.383), channel_id=1, source_target_pairs={{0,4},{4,0},{1,5},{5,1},{2,6},{6,2},{3,7},{7,3},{8,12},{12,8},{9,1... | collective-permute-start | bytes 6488072 | tf_op jit(solution)/shard_map/ppermute | solution.py:302
  503.4 163.9 %collective-permute-start.39 = (bf16[4,2,1,64,1024]{4,3,0,1,2:T(8,128)(2,1)}, bf16[4,2,1,64,1024]{4,3,0,1,2:T(8,128)(2,1)}, u32[]{:S(2)}, u32[]{:S(2)}) collective-permute-start(bf16[4,2,1,64,1024]{4,3,0,1,2:T(8,128)(2,1)} %slice_bitcast_fusion.18), channel_id=1, source_target_pairs={{0,1},{1,0},{2,3},{3,2},{4,5},{5,4},{6,7},{7,6},{8,9},{9,8},{10,11... | collective-permute-start | bytes 3145736 | tf_op jit(solution)/shard_map/ppermute | solution.py:308
  506.3 52.4 %collective-permute-start.44 = (bf16[4,2,1,64,1024]{4,3,0,1,2:T(8,128)(2,1)}, bf16[4,2,1,64,1024]{4,3,0,1,2:T(8,128)(2,1)}, u32[]{:S(2)}, u32[]{:S(2)}) collective-permute-start(bf16[4,2,1,64,1024]{4,3,0,1,2:T(8,128)(2,1)} %get-tuple-element.430), channel_id=1, source_target_pairs={{0,1},{1,0},{2,3},{3,2},{4,5},{5,4},{6,7},{7,6},{8,9},{9,8},{10,11... | collective-permute-start | bytes 3145736 | tf_op jit(solution)/shard_map/ppermute | solution.py:308
  509.2 53.0 %collective-permute-start.45 = (bf16[4,1,2,64,1024]{4,3,0,2,1:T(8,128)(2,1)}, bf16[4,1,2,64,1024]{4,3,0,2,1:T(8,128)(2,1)}, u32[]{:S(2)}, u32[]{:S(2)}) collective-permute-start(bf16[4,1,2,64,1024]{4,3,0,2,1:T(8,128)(2,1)} %get-tuple-element.428), channel_id=1, source_target_pairs={{0,2},{2,0},{1,3},{3,1},{4,6},{6,4},{5,7},{7,5},{8,10},{10,8},{9,1... | collective-permute-start | bytes 3145736 | tf_op jit(solution)/shard_map/ppermute | solution.py:308
  558.7 51.1 %collective-permute-start.50 = (bf16[4,2,1,64,1024]{4,3,0,1,2:T(8,128)(2,1)}, bf16[4,2,1,64,1024]{4,3,0,1,2:T(8,128)(2,1)}, u32[]{:S(2)}, u32[]{:S(2)}) collective-permute-start(bf16[4,2,1,64,1024]{4,3,0,1,2:T(8,128)(2,1)} %slice_bitcast_fusion.6), channel_id=1, source_target_pairs={{0,1},{1,0},{2,3},{3,2},{4,5},{5,4},{6,7},{7,6},{8,9},{9,8},{10,11... | collective-permute-start | bytes 3145736 | tf_op jit(solution)/shard_map/ppermute | solution.py:308
  562.2 50.4 %collective-permute-start.51 = (bf16[4,1,2,64,1024]{4,3,0,2,1:T(8,128)(2,1)}, bf16[4,1,2,64,1024]{4,3,0,2,1:T(8,128)(2,1)}, u32[]{:S(2)}, u32[]{:S(2)}) collective-permute-start(bf16[4,1,2,64,1024]{4,3,0,2,1:T(8,128)(2,1)} %slice_bitcast_fusion.4), channel_id=1, source_target_pairs={{0,2},{2,0},{1,3},{3,1},{4,6},{6,4},{5,7},{7,5},{8,10},{10,8},{9,1... | collective-permute-start | bytes 3145736 | tf_op jit(solution)/shard_map/ppermute | solution.py:308
  578.8 79.5 %collective-permute-start.56 = (bf16[1056,256]{1,0:T(8,128)(2,1)}, bf16[1056,256]{1,0:T(8,128)(2,1)S(1)}, u32[]{:S(2)}, u32[]{:S(2)}) collective-permute-start(bf16[1056,256]{1,0:T(8,128)(2,1)} %get-tuple-element.420), channel_id=1, source_target_pairs={{0,24},{8,16},{16,8},{24,0},{1,25},{9,17},{17,9},{25,1},{2,26},{10... | collective-permute-start | bytes 1622024 | tf_op jit(solution)/shard_map/ppermute | solution.py:308
  666.4 64.4 %collective-permute-start.40 = (bf16[4,1,2,64,1024]{4,3,0,2,1:T(8,128)(2,1)}, bf16[4,1,2,64,1024]{4,3,0,2,1:T(8,128)(2,1)}, u32[]{:S(2)}, u32[]{:S(2)}) collective-permute-start(bf16[4,1,2,64,1024]{4,3,0,2,1:T(8,128)(2,1)} %slice_bitcast_fusion.16), channel_id=1, source_target_pairs={{0,2},{2,0},{1,3},{3,1},{4,6},{6,4},{5,7},{7,5},{8,10},{10,8},{9,1... | collective-permute-start | bytes 3145736 | tf_op jit(solution)/shard_map/ppermute | solution.py:308
  719.8 52.6 %all-to-all-start.5 = ((bf16[4,128,2048]{2,1,0:T(8,128)(2,1)}), bf16[4,128,2048]{2,1,0:T(8,128)(2,1)}, u32[]{:S(2)}, u32[]{:S(2)}) async-start(bf16[4,128,2048]{2,1,0:T(8,128)(2,1)} %broadcast_in_dim.71), calls=%async_computation.5 | async-start | bytes 4194304 | tf_op jit(solution)/shard_map/all_to_all | solution.py:333
  724.2 296.8 %reduce-scatter.5.cloned.1.call-start = ((), (), s32[]{:S(2)}) async-start(), calls=%async_computation.17 | async-start | bytes 2359296 | tf_op jit(solution)/shard_map/reduce_scatter | solution.py:683
  798.9 224.2 %reduce-scatter.3.cloned.1.call-start = ((), (), s32[]{:S(2)}) async-start(), calls=%async_computation.16 | async-start | bytes 7077888 | tf_op jit(solution)/shard_map/reduce_scatter | solution.py:684
  867.6 98.9 %collective-permute-start.74 = (bf16[1408,256]{1,0:T(8,128)(2,1)}, bf16[1408,256]{1,0:T(8,128)(2,1)}, u32[]{:S(2)}, u32[]{:S(2)}) collective-permute-start(bf16[1408,256]{1,0:T(8,128)(2,1)} %get-tuple-element.401), channel_id=1, source_target_pairs={{0,24},{8,16},{16,8},{24,0},{1,25},{9,17},{17,9},{25,1},{2,26},{10... | collective-permute-start | bytes 2162696 | tf_op jit(solution)/shard_map/ppermute | solution.py:308
  881.1 83.2 %all-to-all-start.6 = ((bf16[4,128,2048]{2,1,0:T(8,128)(2,1)}), bf16[4,128,2048]{2,1,0:T(8,128)(2,1)}, u32[]{:S(2)}, u32[]{:S(2)}) async-start(bf16[4,128,2048]{2,1,0:T(8,128)(2,1)} %bitcast.639), calls=%async_computation.6 | async-start | bytes 4194304 | tf_op jit(solution)/shard_map/all_to_all | solution.py:338
  886.0 68.0 %collective-permute-start.73 = (bf16[64,2048]{1,0:T(8,128)(2,1)S(1)}, bf16[64,2048]{1,0:T(8,128)(2,1)S(1)}, u32[]{:S(2)}, u32[]{:S(2)}) collective-permute-start(bf16[64,2048]{1,0:T(8,128)(2,1)S(1)} %slice_bitcast_fusion.58), channel_id=1, source_target_pairs={{0,16},{8,24},{16,0},{24,8},{1,17},{9,25},{17,1},{25,9},{2,18},{10... | collective-permute-start | bytes 786440 | tf_op jit(solution)/shard_map/ppermute | solution.py:308
  886.1 78.1 %collective-permute-start.72 = (bf16[64,2048]{1,0:T(8,128)(2,1)S(1)}, bf16[64,2048]{1,0:T(8,128)(2,1)S(1)}, u32[]{:S(2)}, u32[]{:S(2)}) collective-permute-start(bf16[64,2048]{1,0:T(8,128)(2,1)S(1)} %slice_bitcast_fusion.59), channel_id=1, source_target_pairs={{0,16},{8,24},{16,0},{24,8},{1,17},{9,25},{17,1},{25,9},{2,18},{10... | collective-permute-start | bytes 786440 | tf_op jit(solution)/shard_map/ppermute | solution.py:308
  (171 other events, 2722.2 us)
Sparse Core Ops, SparseCore 0:
  10.2 71.5 all-gather.2
  83.4 52.2 all-gather.4
  799.0 40.8 reduce-scatter.4
  857.8 115.3 reduce-scatter.2

commit v7 on v6

--- a/solution.py
+++ b/solution.py
@@ -442,8 +442,8 @@
 
     sub = own_rows // PARTS
     cot_rows = cot_part.reshape(1, n_c, PARTS, sub, dim // n_c)
+    cot_rows = gather_joined(cot_rows, "g", 0)
     cot_rows, qkv = tie(cot_rows, qkv)
-    cot_rows = gather_joined(cot_rows, "g", 0)
     inputs = col_gather(token_part, n_c).reshape(n_c, span, -1).transpose(1, 0, 2)
     inputs = inputs.reshape(span, dim).astype(F32)
 
@@ -481,13 +481,16 @@
     probabilities = exp_scores / jnp.sum(exp_scores, axis=-1, keepdims=True)
     prob_low = probabilities.astype(BF16)
     mixed = einsum("bhqk,bkhd->bqhd", prob_low, value_low).astype(BF16).reshape(span, width)
-    cot_rows, mixed, own_blocks[0][1] = tie(cot_rows, mixed, own_blocks[0][1])
     cot_all = []
     for part in range(PARTS):
         value = cot_rows[:, :, part][None, None]
-        for axis in ("x", "y") if part % 2 else ("y", "x"):
-            value = gather_joined(value, axis, ("y", "x").index(axis))
-        cot_all.append(value.reshape(n_c, n_g, n_c, sub, dim // n_c))
+        axis = ("x", "y")[1 - part % 2]
+        cot_all.append(gather_joined(value, axis, ("y", "x").index(axis)))
+    cot_all, mixed, own_blocks[0][1] = tie(cot_all, mixed, own_blocks[0][1])
+    for part in range(PARTS):
+        axis = ("x", "y")[part % 2]
+        value = gather_joined(cot_all[part], axis, ("y", "x").index(axis))
+        cot_all[part] = value.reshape(n_c, n_g, n_c, sub, dim // n_c)
     attention = col_sum(dot(mixed, out_w, ((1,), (0,))), n_c)
 
     own_inputs = lax.dynamic_slice_in_dim(inputs, at_c * own_rows, own_rows, 0)
@@ -507,14 +510,13 @@
         return jnp.concatenate(sides, axis=-1).reshape(-1, dim)
 
     routed_gu, routed_d = own_blocks[1:]
+    normed_own, cot_all = tie(normed_own, cot_all)
     halves = [normed_own[part * sub : (part + 1) * sub][None] for part in range(PARTS)]
     halves[0] = gather_joined(halves[0], "g", 0)
     halves[0], halves[1], routed_gu[1] = tie(halves[0], halves[1], routed_gu[1])
     halves[1] = gather_joined(halves[1], "g", 0)
     normed_parts = [gather_cols(halves[0][:, None, None])]
-    normed_parts[0], halves[1], routed_gu[2:3], cot_all = tie(
-        normed_parts[0], halves[1], routed_gu[2:3], cot_all
-    )
+    normed_parts[0], halves[1], routed_gu[2:3] = tie(normed_parts[0], halves[1], routed_gu[2:3])
     normed_parts.append(gather_cols(halves[1][:, None, None]))
     normed_parts[1], routed_gu[3:], routed_d[1] = tie(
         normed_parts[1], routed_gu[3:], routed_d[1]
@@ -621,7 +623,7 @@
 
     acts, gates, ups = ([parts[i] for parts in passes] for i in (2, 3, 4))
     first = cols_first(split_sides(passes[0][1]), passes[1][2][:16, :128])
-    first, acts, moved_s[1:3] = tie(first, acts, moved_s[1:3])
+    first, acts = tie(first, acts)
     (grad_d,) = weight_grad(sizes_e, meta, (True,), [acts], normed_parts, cot_all)
     first = cols_second(first)
     second = cols_first(split_sides(passes[1][1]))
@@ -630,44 +632,45 @@
     first = chips_steps(first)
     second = cols_second(second)
     both_d = own_core(grad_d)
-    first, second, both_d, moved_s[3:], grad_gu = tie(first, second, both_d, moved_s[3:], grad_gu)
+    first, second, both_d, moved_s[1:3], grad_gu = tie(first, second, both_d, moved_s[1:3], grad_gu)
     moved_d = send_slices(both_d)
     first = chips_last(first)
     second = chips_steps(second)
     both_gu = own_core(grad_gu)
-    first, second, both_gu = tie(first, second, both_gu)
+    out_sides = [cols_first(split_sides(parts[0])) for parts in passes]
+    first, second, both_gu, out_sides[0] = tie(first, second, both_gu, out_sides[0])
     second = chips_last(second)
-    out_sides = [cols_first(split_sides(parts[0])) for parts in passes]
     moved_gu = send_slices(both_gu)
     normed_grad_2 = jnp.concatenate([first, second], axis=0)
-    normed_grad_2, moved_d[1] = tie(normed_grad_2, moved_d[1])
+    normed_grad_2, moved_s[3:], out_sides[1] = tie(normed_grad_2, moved_s[3:], out_sides[1])
     hidden_part, gain_2_sum = norm_back(normed_grad_2, unit_2, second_scale, gain_2)
     hidden_grad = own_cot.astype(F32) + hidden_part
     attn_grad = col_gather(hidden_grad.astype(BF16), n_c).reshape(span, dim)
-    attn_grad, moved_d[2:], moved_gu[1] = tie(attn_grad, moved_d[2:], moved_gu[1])
+    attn_grad, moved_d[1:] = tie(attn_grad, moved_d[1:])
+    out_parts = [cols_second(sides) for sides in out_sides]
     gate_s, up_s, down_s = (place_s(value) for value in place_slices(moved_s, 3))
     down_e = place_e(place_slices(moved_d, 1)[0])
 
     out_grad = dot(attn_grad, mixed, ((0,), (0,)))
     mixed_grad = dot(attn_grad, out_w, ((1,), (1,))).astype(BF16).reshape(head_shape)
-    out_sides, mixed_grad = tie(out_sides, mixed_grad)
-    out_parts = [cols_second(sides) for sides in out_sides]
+    out_parts, mixed_grad, moved_gu[1] = tie(out_parts, mixed_grad, moved_gu[1])
+    out_parts = [chips_steps(part) for part in out_parts]
     prob_grad = einsum("bqhd,bkhd->bhqk", mixed_grad, value_low)
     value_grad = einsum("bhqk,bqhd->bkhd", prob_low, mixed_grad).astype(BF16)
     center = jnp.sum(prob_grad * probabilities, axis=-1, keepdims=True)
     score_grad = (probabilities * (prob_grad - center) * (1.0 / math.sqrt(HEAD_DIM))).astype(BF16)
-    out_parts, score_grad, moved_gu[2:3] = tie(out_parts, score_grad, moved_gu[2:3])
-    out_parts = [chips_steps(part) for part in out_parts]
+    out_parts, score_grad = tie(out_parts, score_grad)
+    out_rows = [chips_last(part) for part in out_parts]
     query_grad = rotate(einsum("bhqk,bkhd->bqhd", score_grad, key_rot), cosine, -sine).astype(BF16)
     key_grad = rotate(einsum("bhqk,bqhd->bkhd", score_grad, query_rot), cosine, -sine).astype(BF16)
     qkv_grad = jnp.concatenate(
         [part.reshape(span, width) for part in (query_grad, key_grad, value_grad)], axis=1
     )
-    qkv_grad, out_parts = tie(qkv_grad, out_parts)
-    out_rows = jnp.concatenate([chips_last(part) for part in out_parts], axis=0)
+    qkv_grad, out_rows, moved_gu[2:3] = tie(qkv_grad, out_rows, moved_gu[2:3])
+    out_rows = jnp.concatenate(out_rows, axis=0)
     qkv_sum = dot(normed_1, qkv_grad, ((0,), (0,)))
     normed_grad_1 = col_sum(dot(qkv_grad, qkv, ((1,), (1,))), n_c)
-    normed_grad_1, out_rows, moved_gu[3:] = tie(normed_grad_1, out_rows, moved_gu[3:])
+    normed_grad_1, moved_gu[3:] = tie(normed_grad_1, moved_gu[3:])
     gate_e, up_e = (place_e(value) for value in place_slices(moved_gu, 2))
     own_scale = lax.dynamic_slice_in_dim(first_scale, at_c * own_rows, own_rows, 0)
     rows_part, gain_1_sum = norm_back(normed_grad_1, own_inputs * own_scale, own_scale, gain_1)

time: 1040 us -> 1110 us (1.067)
  waiting for transfers between devices: 424 us -> 525 us
  other arithmetic: 112 us -> 96.9 us
  starting transfers between devices: 132 us -> 118 us
    ppermute x60, waiting for transfers between devices: 377 us -> 473 us  [shift_by(): lax.ppermute(value, axis, [(i, i ^ shift) for i in range(lax.axis_size(ax...]
    all_to_all x2, waiting for transfers between devices: 4.13 us -> 37.9 us  [col_sum(): lax.all_to_all(parts, COL, 0, 0, tiled=True).astype(F32)]
    all_to_all x2, waiting for transfers between devices: 12.5 us -> 0.01 us  [col_gather(): return lax.all_to_all(spread, COL, 0, 0, tiled=True)]
    all_gather x1, waiting for transfers between devices: 11.3 us -> 0.01 us  [shards(): lax.all_gather(jnp.concatenate([query_weight, key_weight, value_weight],...]
    unnamed x233 -> x229, local copies, waits for them, and re-layouts: 42.8 us -> 35.3 us
    another operation x15 -> x14, other arithmetic: 25.1 us -> 23 us  [gather_joined(): jnp.stack([value, shift_by(value, axis, bit)], axis=at + 1).reshape(shape)]
  transfers between devices with their start and end apart: 89 -> 87, of which waited for: 34 -> 34; matrix products, arithmetic and copies ran while one was open for 26% -> 22% of each run, Pallas kernels for 15% -> 14%
where the time goes in v7:
time: 1110 us
  waiting for transfers between devices  525 us (47%)
  Pallas kernels  160 us (14%)
  local copies, waits for them, and re-layouts  130 us (12%)
  starting transfers between devices  118 us (11%)
  other arithmetic  96.9 us (9%)
  matrix products  41.6 us (4%)
  blocking collectives  17.5 us (2%)
  between operations  16.2 us (1%)
    ppermute x60, waiting for transfers between devices, shift_by(): lax.ppermute(value, axis, [(i, i ^ shift) for i in range(lax.axis_size(ax...  473 us
    pallas_call x4, Pallas kernels, ffn_pass(): pl.pallas_call(functools.partial(ffn_kernel, sizes, groups), grid_spec=pl...  112 us
    ppermute x60, starting transfers between devices, shift_by(): lax.ppermute(value, axis, [(i, i ^ shift) for i in range(lax.axis_size(ax...  76.3 us
    pallas_call x3, Pallas kernels, weight_grad(): pl.pallas_call(functools.partial(grad_kernel, parts, kinds, f_pad), grid_...  47.6 us
    all_to_all x2, waiting for transfers between devices, col_sum(): lax.all_to_all(parts, COL, 0, 0, tiled=True).astype(F32)  37.9 us
    unnamed x229, local copies, waits for them, and re-layouts  35.3 us
    dot_general x6, matrix products, dot(): lax.dot_general(left, right, (dims, ((), ())), preferred_element_type=F32)  32.9 us
    another operation x14, other arithmetic, gather_joined(): jnp.stack([value, shift_by(value, axis, bit)], axis=at + 1).reshape(shape)  23 us
  transfers between devices with their start and end apart: 87, of which 34 were waited for; matrix products, arithmetic and copies ran while one was open for 22% of the time, Pallas kernels for 14%

profile of v7, /device:TPU:0, one launch (start us, length us, event | category | flops | bytes accessed | tf_op | source)
XLA Modules:
  0.0 1105.9 jit_solution(8908370652651394313)
XLA Ops:
  29.3 39.3 %collective-permute-done.2 = bf16[1,4,2,64,512]{4,3,2,1,0:T(8,128)(2,1)S(1)} collective-permute-done((bf16[1,4,2,64,512]{4,3,2,1,0:T(8,128)(2,1)S(1)}, bf16[1,4,2,64,512]{4,3,2,1,0:T(8,128)(2,1)S(1)}, u32[]{:S(2)}, u32[]{:S(2)}) %collective-permute-start.2) | collective-permute-done | bytes 524320 | tf_op jit(solution)/shard_map/ppermute | solution.py:308
  84.1 23.8 %collective-permute-done.3 = bf16[2,4,2,64,512]{4,3,2,1,0:T(8,128)(2,1)} collective-permute-done((bf16[2,4,2,64,512]{4,3,2,1,0:T(8,128)(2,1)}, bf16[2,4,2,64,512]{4,3,2,1,0:T(8,128)(2,1)}, u32[]{:S(2)}, u32[]{:S(2)}) %collective-permute-start.3) | collective-permute-done | bytes 1048608 | tf_op jit(solution)/shard_map/ppermute | solution.py:308
  157.5 15.4 %collective-permute-done.5 = bf16[1,1,4,4,64,512]{5,4,3,2,1,0:T(8,128)(2,1)} collective-permute-done((bf16[1,1,4,4,64,512]{5,4,3,2,1,0:T(8,128)(2,1)}, bf16[1,1,4,4,64,512]{5,4,3,2,1,0:T(8,128)(2,1)}, u32[]{:S(2)}, u32[]{:S(2)}) %collective-permute-start.5) | collective-permute-done | bytes 1048608 | tf_op jit(solution)/shard_map/ppermute | solution.py:308
  191.1 21.6 %all-to-all-done.4 = bf16[4,128,2048]{2,1,0:T(8,128)(2,1)S(1)} async-done(((bf16[4,128,2048]{2,1,0:T(8,128)(2,1)}), bf16[4,128,2048]{2,1,0:T(8,128)(2,1)S(1)}, u32[]{:S(2)}, u32[]{:S(2)}) %all-to-all-start.4) | async-done | bytes 2097184 | tf_op jit(solution)/shard_map/all_to_all | solution.py:338
  227.7 28.4 %collective-permute-done.7 = bf16[2,1,4,4,64,512]{5,4,3,2,0,1:T(8,128)(2,1)} collective-permute-done((bf16[2,1,4,4,64,512]{5,4,3,2,0,1:T(8,128)(2,1)}, bf16[2,1,4,4,64,512]{5,4,3,2,0,1:T(8,128)(2,1)}, u32[]{:S(2)}, u32[]{:S(2)}) %collective-permute-start.7) | collective-permute-done | bytes 2097184 | tf_op jit(solution)/shard_map/ppermute | solution.py:308
  327.2 27.9 %collective-permute-done.16 = bf16[1,64,2048]{2,1,0:T(8,128)(2,1)S(1)} collective-permute-done((bf16[1,64,2048]{2,1,0:T(8,128)(2,1)S(1)}, bf16[1,64,2048]{2,1,0:T(8,128)(2,1)S(1)}, u32[]{:S(2)}, u32[]{:S(2)}) %collective-permute-start.16) | collective-permute-done | bytes 262176 | tf_op jit(solution)/shard_map/ppermute | solution.py:308
  402.3 21.4 %ffn_pass.4 = (bf16[1024,2048]{1,0:T(8,128)(2,1)}, bf16[1024,2048]{1,0:T(8,128)(2,1)}, bf16[352,1024]{1,0:T(8,128)(2,1)}, bf16[368,1024]{1,0:T(8,128)(2,1)}, bf16[352,1024]{1,0:T(8,128)(2,1)}) custom-call(s32[3]{0:T(128)} %pad_add_fusion.meta, bf16[1024,2048]{1,0:T(8,128)(2,1)} %pad_maximum_fusion.2.rows_ref.refs_6_.refs_4_, ...), custom_call_target="tpu_custom_call" | custom-call | flops 8858370048 | bytes 23265280 | tf_op jit(solution)/shard_map/ffn_pass/pallas_call | solution.py:172
  434.0 24.9 %collective-permute-done.29.refs_10_ = bf16[704,256]{1,0:T(8,128)(2,1)} collective-permute-done((bf16[704,256]{1,0:T(8,128)(2,1)S(1)}, bf16[704,256]{1,0:T(8,128)(2,1)}, u32[]{:S(2)}, u32[]{:S(2)}) %collective-permute-start.29) | collective-permute-done | bytes 360480 | tf_op jit(solution)/shard_map/ppermute | solution.py:308
  459.4 21.0 %ffn_pass.5 = (bf16[1024,2048]{1,0:T(8,128)(2,1)}, bf16[1024,2048]{1,0:T(8,128)(2,1)}, bf16[352,1024]{1,0:T(8,128)(2,1)}, bf16[368,1024]{1,0:T(8,128)(2,1)}, bf16[352,1024]{1,0:T(8,128)(2,1)}) custom-call(s32[3]{0:T(128)} %pad_add_fusion.meta, bf16[1024,2048]{1,0:T(8,128)(2,1)} %pad_maximum_fusion.3.rows_ref.refs_7_.refs_5_, ...), custom_call_target="tpu_custom_call" | custom-call | flops 8858370048 | bytes 23265280 | tf_op jit(solution)/shard_map/ffn_pass/pallas_call | solution.py:172
  480.5 16.6 %weight_grad.3 = (bf16[2,4,1056,256]{3,2,1,0:T(8,128)(2,1)}, f32[8,2048]{1,0:T(8,128)}) custom-call(s32[3]{0:T(128)} %pad_add_fusion.meta, bf16[368,1024]{1,0:T(8,128)(2,1)} %get-tuple-element.201.refs_0_, bf16[368,1024]{1,0:T(8,128)(2,1)} %get-tuple-element.204.refs_1_, bf16[352,1024]{1,0:T(8,128)(2,1)} %get-tuple-element.205.refs_2_, ...), custom_call_target="tpu_custom_call" | custom-call | flops 8858370048 | bytes 17039360 | tf_op jit(solution)/shard_map/weight_grad/pallas_call | solution.py:271
  504.6 35.1 %ffn_pass.6 = (bf16[1024,2048]{1,0:T(8,128)(2,1)}, bf16[1024,2048]{1,0:T(8,128)(2,1)}, bf16[704,1024]{1,0:T(8,128)(2,1)}, bf16[704,1024]{1,0:T(8,128)(2,1)}, bf16[704,1024]{1,0:T(8,128)(2,1)}) custom-call(s32[3]{0:T(128)} %pad_add_fusion.meta, bf16[1024,2048]{1,0:T(8,128)(2,1)} %pad_maximum_fusion.2.rows_ref.refs_6_.refs_4_, ...), custom_call_target="tpu_custom_call" | custom-call | flops 17716740096 | bytes 46530560 | tf_op jit(solution)/shard_map/ffn_pass/pallas_call | solution.py:172
  553.6 15.3 %collective-permute-done.56 = bf16[4,1,2,64,1024]{4,3,0,2,1:T(8,128)(2,1)S(1)} collective-permute-done((bf16[4,1,2,64,1024]{4,3,0,2,1:T(8,128)(2,1)S(1)}, bf16[4,1,2,64,1024]{4,3,0,2,1:T(8,128)(2,1)S(1)}, u32[]{:S(2)}, u32[]{:S(2)}) %collective-permute-start.56) | collective-permute-done | bytes 1048608 | tf_op jit(solution)/shard_map/ppermute | solution.py:308
  571.4 34.8 %ffn_pass.7 = (bf16[1024,2048]{1,0:T(8,128)(2,1)}, bf16[1024,2048]{1,0:T(8,128)(2,1)}, bf16[704,1024]{1,0:T(8,128)(2,1)}, bf16[704,1024]{1,0:T(8,128)(2,1)}, bf16[704,1024]{1,0:T(8,128)(2,1)}) custom-call(s32[3]{0:T(128)} %pad_add_fusion.meta, bf16[1024,2048]{1,0:T(8,128)(2,1)} %pad_maximum_fusion.3.rows_ref.refs_7_.refs_5_, ...), custom_call_target="tpu_custom_call" | custom-call | flops 17716740096 | bytes 46530560 | tf_op jit(solution)/shard_map/ffn_pass/pallas_call | solution.py:172
  640.8 27.8 %collective-permute-done.42 = bf16[4,1,64,1024]{3,2,0,1:T(8,128)(2,1)} collective-permute-done((bf16[4,1,64,1024]{3,2,0,1:T(8,128)(2,1)}, bf16[4,1,64,1024]{3,2,0,1:T(8,128)(2,1)}, u32[]{:S(2)}, u32[]{:S(2)}) %collective-permute-start.42) | collective-permute-done | bytes 524320 | tf_op jit(solution)/shard_map/ppermute | solution.py:308
  674.9 17.0 %collective-permute-done.44 = bf16[4,2,1,64,1024]{4,3,0,1,2:T(8,128)(2,1)S(1)} collective-permute-done((bf16[4,2,1,64,1024]{4,3,0,1,2:T(8,128)(2,1)S(1)}, bf16[4,2,1,64,1024]{4,3,0,1,2:T(8,128)(2,1)S(1)}, u32[]{:S(2)}, u32[]{:S(2)}) %collective-permute-start.44) | collective-permute-done | bytes 1048608 | tf_op jit(solution)/shard_map/ppermute | solution.py:308
  697.5 18.5 %weight_grad.5 = bf16[2,4,1408,256]{3,2,1,0:T(8,128)(2,1)} custom-call(s32[3]{0:T(128)} %pad_add_fusion.meta, bf16[704,1024]{1,0:T(8,128)(2,1)} %get-tuple-element.234.refs_0_, bf16[704,1024]{1,0:T(8,128)(2,1)} %get-tuple-element.235.refs_1_, bf16[704,1024]{1,0:T(8,128)(2,1)} %get-tuple-element.236.refs_2_, bf16[704,1024]{1,0:T(8,128)(2,1)} %get-tuple-element.237.refs_3_, ...), custom_call_target="tpu_custom_call" | custom-call | flops 11811160064 | bytes 19922944 | tf_op jit(solution)/shard_map/weight_grad/pallas_call | solution.py:271
  741.0 15.2 %collective-permute-done.50 = bf16[1056,256]{1,0:T(8,128)(2,1)S(1)} collective-permute-done((bf16[1056,256]{1,0:T(8,128)(2,1)S(1)}, bf16[1056,256]{1,0:T(8,128)(2,1)S(1)}, u32[]{:S(2)}, u32[]{:S(2)}) %collective-permute-start.50) | collective-permute-done | bytes 540704 | tf_op jit(solution)/shard_map/ppermute | solution.py:308
  773.1 26.1 %collective-permute-done.52 = bf16[64,2048]{1,0:T(8,128)(2,1)S(1)} collective-permute-done((bf16[64,2048]{1,0:T(8,128)(2,1)S(1)}, bf16[64,2048]{1,0:T(8,128)(2,1)S(1)}, u32[]{:S(2)}, u32[]{:S(2)}) %collective-permute-start.52) | collective-permute-done | bytes 262176 | tf_op jit(solution)/shard_map/ppermute | solution.py:308
  808.3 36.4 %collective-permute-done.59 = bf16[64,2048]{1,0:T(8,128)(2,1)S(1)} collective-permute-done((bf16[64,2048]{1,0:T(8,128)(2,1)S(1)}, bf16[64,2048]{1,0:T(8,128)(2,1)S(1)}, u32[]{:S(2)}, u32[]{:S(2)}) %collective-permute-start.59) | collective-permute-done | bytes 262176 | tf_op jit(solution)/shard_map/ppermute | solution.py:308
  871.2 20.0 %collective-permute-done.63 = bf16[4,1,64,1024]{3,2,0,1:T(8,128)(2,1)S(1)} collective-permute-done((bf16[4,1,64,1024]{3,2,0,1:T(8,128)(2,1)S(1)}, bf16[4,1,64,1024]{3,2,0,1:T(8,128)(2,1)S(1)}, u32[]{:S(2)}, u32[]{:S(2)}) %collective-permute-start.63) | collective-permute-done | bytes 524320 | tf_op jit(solution)/shard_map/ppermute | solution.py:308
  901.9 20.9 %collective-permute-done.68 = bf16[1408,256]{1,0:T(8,128)(2,1)} collective-permute-done((bf16[1408,256]{1,0:T(8,128)(2,1)}, bf16[1408,256]{1,0:T(8,128)(2,1)}, u32[]{:S(2)}, u32[]{:S(2)}) %collective-permute-start.68) | collective-permute-done | bytes 720928 | tf_op jit(solution)/shard_map/ppermute | solution.py:308
  944.2 15.4 %collective-permute-done.69 = bf16[2,64,2048]{2,1,0:T(8,128)(2,1)} collective-permute-done((bf16[2,64,2048]{2,1,0:T(8,128)(2,1)}, bf16[2,64,2048]{2,1,0:T(8,128)(2,1)}, u32[]{:S(2)}, u32[]{:S(2)}) %collective-permute-start.69) | collective-permute-done | bytes 524320 | tf_op jit(solution)/shard_map/ppermute | solution.py:308
  968.2 18.1 %collective-permute-done.72 = bf16[64,2048]{1,0:T(8,128)(2,1)S(1)} collective-permute-done((bf16[64,2048]{1,0:T(8,128)(2,1)S(1)}, bf16[64,2048]{1,0:T(8,128)(2,1)S(1)}, u32[]{:S(2)}, u32[]{:S(2)}) %collective-permute-start.72) | collective-permute-done | bytes 262176 | tf_op jit(solution)/shard_map/ppermute | solution.py:308
  1036.3 16.3 %all-to-all-done.8 = bf16[4,128,2048]{2,1,0:T(8,128)(2,1)S(1)} async-done(((bf16[4,128,2048]{2,1,0:T(8,128)(2,1)}), bf16[4,128,2048]{2,1,0:T(8,128)(2,1)S(1)}, u32[]{:S(2)}, u32[]{:S(2)}) %all-to-all-start.8) | async-done | bytes 2097184 | tf_op jit(solution)/shard_map/all_to_all | solution.py:338
  (637 shorter events, 532.3 us)
Async XLA Ops:
  7.2 125.7 %all-gather.3.cloned.1.call-start = ((), (), s32[]{:S(2)}) async-start(), calls=%async_computation.14 | async-start | bytes 7077888 | tf_op jit(solution)/shard_map/all_gather | solution.py:431
  13.6 55.1 %collective-permute-start.2 = (bf16[1,4,2,64,512]{4,3,2,1,0:T(8,128)(2,1)S(1)}, bf16[1,4,2,64,512]{4,3,2,1,0:T(8,128)(2,1)S(1)}, u32[]{:S(2)}, u32[]{:S(2)}) collective-permute-start(bf16[1,4,2,64,512]{4,3,2,1,0:T(8,128)(2,1)S(1)} %bitcast.647), channel_id=1, source_target_pairs={{0,16},{8,24},{16,0},{24,8},{1,17},{9,25},{17,1},{25,9},{2,18},{10... | collective-permute-start | bytes 1572872 | tf_op jit(solution)/shard_map/ppermute | solution.py:308
  23.3 87.7 %all-to-all-start.1 = ((bf16[4,512,512]{2,1,0:T(8,128)(2,1)}), bf16[4,512,512]{2,1,0:T(8,128)(2,1)S(1)}, u32[]{:S(2)}, u32[]{:S(2)}) async-start(bf16[4,512,512]{2,1,0:T(8,128)(2,1)} %broadcast_in_dim.55), calls=%async_computation.1 | async-start | bytes 4194304 | tf_op jit(solution)/shard_map/all_to_all | solution.py:333
  27.1 151.3 %all-gather.5.cloned.1.call-start = ((), (), s32[]{:S(2)}) async-start(), calls=%async_computation.15 | async-start | bytes 2359296 | tf_op jit(solution)/shard_map/all_gather | solution.py:434
  186.5 69.6 %collective-permute-start.7 = (bf16[2,1,4,4,64,512]{5,4,3,2,0,1:T(8,128)(2,1)}, bf16[2,1,4,4,64,512]{5,4,3,2,0,1:T(8,128)(2,1)}, u32[]{:S(2)}, u32[]{:S(2)}) collective-permute-start(bf16[2,1,4,4,64,512]{5,4,3,2,0,1:T(8,128)(2,1)} %maximum_bitcast_fusion), channel_id=1, source_target_pairs={{0,1},{1,0},{2,3},{3,2},{4,5},{5,4},{6,7},{7,6},{8,9},{9,8},{10,11... | collective-permute-start | bytes 6291464 | tf_op jit(solution)/shard_map/ppermute | solution.py:308
  188.6 72.1 %collective-permute-start.8 = (bf16[1,2,4,4,64,512]{5,4,3,2,1,0:T(8,128)(2,1)}, bf16[1,2,4,4,64,512]{5,4,3,2,1,0:T(8,128)(2,1)}, u32[]{:S(2)}, u32[]{:S(2)}) collective-permute-start(bf16[1,2,4,4,64,512]{5,4,3,2,1,0:T(8,128)(2,1)} %maximum_bitcast_fusion.1), channel_id=1, source_target_pairs={{0,2},{2,0},{1,3},{3,1},{4,6},{6,4},{5,7},{7,5},{8,10},{10,8},{9,1... | collective-permute-start | bytes 6291464 | tf_op jit(solution)/shard_map/ppermute | solution.py:308
  310.7 66.4 %collective-permute-start.18 = (bf16[1408,256]{1,0:T(8,128)(2,1)}, bf16[1408,256]{1,0:T(8,128)(2,1)}, u32[]{:S(2)}, u32[]{:S(2)}) collective-permute-start(bf16[1408,256]{1,0:T(8,128)(2,1)} %get-tuple-element.412), channel_id=1, source_target_pairs={{0,16},{8,24},{16,0},{24,8},{1,17},{9,25},{17,1},{25,9},{2,18},{10... | collective-permute-start | bytes 2162696 | tf_op jit(solution)/shard_map/ppermute | solution.py:308
  314.8 81.0 %collective-permute-start.35 = (bf16[1056,256]{1,0:T(8,128)(2,1)}, bf16[1056,256]{1,0:T(8,128)(2,1)}, u32[]{:S(2)}, u32[]{:S(2)}) collective-permute-start(bf16[1056,256]{1,0:T(8,128)(2,1)} %get-tuple-element.195.refs_0_), channel_id=1, source_target_pairs={{0,4},{4,0},{1,5},{5,1},{2,6},{6,2},{3,7},{7,3},{8,12},{12,8},{9,1... | collective-permute-start | bytes 1622024 | tf_op jit(solution)/shard_map/ppermute | solution.py:302
  400.9 58.5 %collective-permute-start.23 = (bf16[1408,256]{1,0:T(8,128)(2,1)}, bf16[1408,256]{1,0:T(8,128)(2,1)}, u32[]{:S(2)}, u32[]{:S(2)}) collective-permute-start(bf16[1408,256]{1,0:T(8,128)(2,1)} %get-tuple-element.410), channel_id=1, source_target_pairs={{0,24},{8,16},{16,8},{24,0},{1,25},{9,17},{17,9},{25,1},{2,26},{10... | collective-permute-start | bytes 2162696 | tf_op jit(solution)/shard_map/ppermute | solution.py:308
  402.3 95.3 %collective-permute-start.25 = (bf16[1408,256]{1,0:T(8,128)(2,1)S(1)}, bf16[1408,256]{1,0:T(8,128)(2,1)}, u32[]{:S(2)}, u32[]{:S(2)}) collective-permute-start(bf16[1408,256]{1,0:T(8,128)(2,1)S(1)} %copy-done.53), channel_id=1, source_target_pairs={{0,4},{4,0},{1,5},{5,1},{2,6},{6,2},{3,7},{7,3},{8,12},{12,8},{9,1... | collective-permute-start | bytes 2162696 | tf_op jit(solution)/shard_map/ppermute | solution.py:302
  434.0 63.1 %collective-permute-start.31 = (bf16[704,256]{1,0:T(8,128)(2,1)S(1)}, bf16[704,256]{1,0:T(8,128)(2,1)S(1)}, u32[]{:S(2)}, u32[]{:S(2)}) collective-permute-start(bf16[704,256]{1,0:T(8,128)(2,1)S(1)} %copy-done.71), channel_id=1, source_target_pairs={{0,4},{4,0},{1,5},{5,1},{2,6},{6,2},{3,7},{7,3},{8,12},{12,8},{9,1... | collective-permute-start | bytes 1081352 | tf_op jit(solution)/shard_map/ppermute | solution.py:302
  502.9 66.4 %collective-permute-start.39 = (bf16[4,1056,256]{2,1,0:T(8,128)(2,1)S(1)}, bf16[4,1056,256]{2,1,0:T(8,128)(2,1)}, u32[]{:S(2)}, u32[]{:S(2)}) collective-permute-start(bf16[4,1056,256]{2,1,0:T(8,128)(2,1)S(1)} %get-tuple-element.389), channel_id=1, source_target_pairs={{0,4},{4,0},{1,5},{5,1},{2,6},{6,2},{3,7},{7,3},{8,12},{12,8},{9,1... | collective-permute-start | bytes 6488072 | tf_op jit(solution)/shard_map/ppermute | solution.py:302
  546.9 214.8 %collective-permute-start.55 = (bf16[4,2,1,64,1024]{4,3,0,1,2:T(8,128)(2,1)}, bf16[4,2,1,64,1024]{4,3,0,1,2:T(8,128)(2,1)}, u32[]{:S(2)}, u32[]{:S(2)}) collective-permute-start(bf16[4,2,1,64,1024]{4,3,0,1,2:T(8,128)(2,1)} %slice_bitcast_fusion.10), channel_id=1, source_target_pairs={{0,1},{1,0},{2,3},{3,2},{4,5},{5,4},{6,7},{7,6},{8,9},{9,8},{10,11... | collective-permute-start | bytes 3145736 | tf_op jit(solution)/shard_map/ppermute | solution.py:308
  550.1 62.0 %collective-permute-start.41 = (bf16[4,1,2,64,1024]{4,3,0,2,1:T(8,128)(2,1)}, bf16[4,1,2,64,1024]{4,3,0,2,1:T(8,128)(2,1)}, u32[]{:S(2)}, u32[]{:S(2)}) collective-permute-start(bf16[4,1,2,64,1024]{4,3,0,2,1:T(8,128)(2,1)} %get-tuple-element.434), channel_id=1, source_target_pairs={{0,2},{2,0},{1,3},{3,1},{4,6},{6,4},{5,7},{7,5},{8,10},{10,8},{9,1... | collective-permute-start | bytes 3145736 | tf_op jit(solution)/shard_map/ppermute | solution.py:308
  552.5 62.5 %collective-permute-start.40 = (bf16[4,2,1,64,1024]{4,3,0,1,2:T(8,128)(2,1)}, bf16[4,2,1,64,1024]{4,3,0,1,2:T(8,128)(2,1)}, u32[]{:S(2)}, u32[]{:S(2)}) collective-permute-start(bf16[4,2,1,64,1024]{4,3,0,1,2:T(8,128)(2,1)} %get-tuple-element.436), channel_id=1, source_target_pairs={{0,1},{1,0},{2,3},{3,2},{4,5},{5,4},{6,7},{7,6},{8,9},{9,8},{10,11... | collective-permute-start | bytes 3145736 | tf_op jit(solution)/shard_map/ppermute | solution.py:308
  610.4 154.2 %collective-permute-start.62 = (bf16[4,1,2,64,1024]{4,3,0,2,1:T(8,128)(2,1)}, bf16[4,1,2,64,1024]{4,3,0,2,1:T(8,128)(2,1)}, u32[]{:S(2)}, u32[]{:S(2)}) collective-permute-start(bf16[4,1,2,64,1024]{4,3,0,2,1:T(8,128)(2,1)} %slice_bitcast_fusion.4), channel_id=1, source_target_pairs={{0,2},{2,0},{1,3},{3,1},{4,6},{6,4},{5,7},{7,5},{8,10},{10,8},{9,1... | collective-permute-start | bytes 3145736 | tf_op jit(solution)/shard_map/ppermute | solution.py:308
  618.9 54.3 %collective-permute-start.45 = (bf16[4,1,2,64,1024]{4,3,0,2,1:T(8,128)(2,1)}, bf16[4,1,2,64,1024]{4,3,0,2,1:T(8,128)(2,1)}, u32[]{:S(2)}, u32[]{:S(2)}) collective-permute-start(bf16[4,1,2,64,1024]{4,3,0,2,1:T(8,128)(2,1)} %slice_bitcast_fusion.12), channel_id=1, source_target_pairs={{0,2},{2,0},{1,3},{3,1},{4,6},{6,4},{5,7},{7,5},{8,10},{10,8},{9,1... | collective-permute-start | bytes 3145736 | tf_op jit(solution)/shard_map/ppermute | solution.py:308
  763.3 82.0 %collective-permute-start.60 = (bf16[1056,256]{1,0:T(8,128)(2,1)S(1)}, bf16[1056,256]{1,0:T(8,128)(2,1)S(1)}, u32[]{:S(2)}, u32[]{:S(2)}) collective-permute-start(bf16[1056,256]{1,0:T(8,128)(2,1)S(1)} %get-tuple-element.426), channel_id=1, source_target_pairs={{0,24},{8,16},{16,8},{24,0},{1,25},{9,17},{17,9},{25,1},{2,26},{10... | collective-permute-start | bytes 1622024 | tf_op jit(solution)/shard_map/ppermute | solution.py:308
  773.1 123.1 %collective-permute-start.65 = (bf16[704,256]{1,0:T(8,128)(2,1)}, bf16[704,256]{1,0:T(8,128)(2,1)S(1)}, u32[]{:S(2)}, u32[]{:S(2)}) collective-permute-start(bf16[704,256]{1,0:T(8,128)(2,1)} %get-tuple-element.448), channel_id=1, source_target_pairs={{0,8},{8,0},{16,24},{24,16},{1,9},{9,1},{17,25},{25,17},{2,10},{10... | collective-permute-start | bytes 1081352 | tf_op jit(solution)/shard_map/ppermute | solution.py:308
  799.2 97.0 %collective-permute-start.66 = (bf16[704,256]{1,0:T(8,128)(2,1)}, bf16[704,256]{1,0:T(8,128)(2,1)}, u32[]{:S(2)}, u32[]{:S(2)}) collective-permute-start(bf16[704,256]{1,0:T(8,128)(2,1)} %get-tuple-element.447), channel_id=1, source_target_pairs={{0,16},{8,24},{16,0},{24,8},{1,17},{9,25},{17,1},{25,9},{2,18},{10... | collective-permute-start | bytes 1081352 | tf_op jit(solution)/shard_map/ppermute | solution.py:308
  799.3 97.0 %collective-permute-start.67 = (bf16[704,256]{1,0:T(8,128)(2,1)}, bf16[704,256]{1,0:T(8,128)(2,1)}, u32[]{:S(2)}, u32[]{:S(2)}) collective-permute-start(bf16[704,256]{1,0:T(8,128)(2,1)} %get-tuple-element.446), channel_id=1, source_target_pairs={{0,24},{8,16},{16,8},{24,0},{1,25},{9,17},{17,9},{25,1},{2,26},{10... | collective-permute-start | bytes 1081352 | tf_op jit(solution)/shard_map/ppermute | solution.py:308
  854.7 239.3 %reduce-scatter.5.cloned.1.call-start = ((), (), s32[]{:S(2)}) async-start(), calls=%async_computation.17 | async-start | bytes 2359296 | tf_op jit(solution)/shard_map/reduce_scatter | solution.py:686
  891.7 99.7 %collective-permute-start.73 = (bf16[1408,256]{1,0:T(8,128)(2,1)}, bf16[1408,256]{1,0:T(8,128)(2,1)}, u32[]{:S(2)}, u32[]{:S(2)}) collective-permute-start(bf16[1408,256]{1,0:T(8,128)(2,1)} %get-tuple-element.408), channel_id=1, source_target_pairs={{0,16},{8,24},{16,0},{24,8},{1,17},{9,25},{17,1},{25,9},{2,18},{10... | collective-permute-start | bytes 2162696 | tf_op jit(solution)/shard_map/ppermute | solution.py:308
  940.1 155.9 %reduce-scatter.3.cloned.1.call-start = ((), (), s32[]{:S(2)}) async-start(), calls=%async_computation.16 | async-start | bytes 7077888 | tf_op jit(solution)/shard_map/reduce_scatter | solution.py:687
  (167 other events, 2941.6 us)
Sparse Core Ops, SparseCore 0:
  10.2 85.1 all-gather.2
  97.1 39.5 all-gather.4
  940.2 42.3 reduce-scatter.4
  997.1 87.8 reduce-scatter.2

commit v8 on v6

--- a/solution.py
+++ b/solution.py
@@ -442,8 +442,14 @@
 
     sub = own_rows // PARTS
     cot_rows = cot_part.reshape(1, n_c, PARTS, sub, dim // n_c)
-    cot_rows, qkv = tie(cot_rows, qkv)
-    cot_rows = gather_joined(cot_rows, "g", 0)
+    far = shift_by(cot_rows, "g", n_g // 2)
+    cot_rows, far, qkv = tie(cot_rows, far, qkv)
+    cot_rows = jnp.concatenate([cot_rows, far], axis=0)
+    bit = n_g // 4
+    while bit:
+        far = shift_by(cot_rows, "g", bit)
+        cot_rows = jnp.stack([cot_rows, far], axis=1).reshape((-1,) + cot_rows.shape[1:])
+        bit //= 2
     inputs = col_gather(token_part, n_c).reshape(n_c, span, -1).transpose(1, 0, 2)
     inputs = inputs.reshape(span, dim).astype(F32)
 
@@ -482,13 +488,17 @@
     prob_low = probabilities.astype(BF16)
     mixed = einsum("bhqk,bkhd->bqhd", prob_low, value_low).astype(BF16).reshape(span, width)
     cot_rows, mixed, own_blocks[0][1] = tie(cot_rows, mixed, own_blocks[0][1])
+    attention = col_sum(dot(mixed, out_w, ((1,), (0,))), n_c)
     cot_all = []
     for part in range(PARTS):
         value = cot_rows[:, :, part][None, None]
-        for axis in ("x", "y") if part % 2 else ("y", "x"):
-            value = gather_joined(value, axis, ("y", "x").index(axis))
-        cot_all.append(value.reshape(n_c, n_g, n_c, sub, dim // n_c))
-    attention = col_sum(dot(mixed, out_w, ((1,), (0,))), n_c)
+        axis = ("x", "y")[1 - part % 2]
+        cot_all.append(gather_joined(value, axis, ("y", "x").index(axis)))
+    cot_all, attention = tie(cot_all, attention)
+    for part in range(PARTS):
+        axis = ("x", "y")[part % 2]
+        value = gather_joined(cot_all[part], axis, ("y", "x").index(axis))
+        cot_all[part] = value.reshape(n_c, n_g, n_c, sub, dim // n_c)
 
     own_inputs = lax.dynamic_slice_in_dim(inputs, at_c * own_rows, own_rows, 0)
     own_blocks[0][2:], attention = tie(own_blocks[0][2:], attention)
@@ -571,6 +581,7 @@
     logit_sum = logit_sum[0]
     sums = [[passes_s[part][0], passes_s[part][1]] for part in range(PARTS)]
     sums[0], grad_s = tie(sums[0], grad_s)
+    own_blocks[2], sums[1] = tie(own_blocks[2], sums[1])
     blocks_e = blocks_of(own_blocks[1]) + blocks_of(own_blocks[2])
     passes = []
     for part in range(PARTS):
@@ -615,13 +626,16 @@
             bit *= 2
         return value
 
-    def chips_last(value):
+    def chips_last(value, after=None):
         other = shift_by(value[1], "g", n_g // 2)
-        return value[0].astype(F32) + other.astype(F32)
+        keep = value[0]
+        if after is not None:
+            keep, _ = tie(keep, after)
+        return keep.astype(F32) + other.astype(F32)
 
     acts, gates, ups = ([parts[i] for parts in passes] for i in (2, 3, 4))
     first = cols_first(split_sides(passes[0][1]), passes[1][2][:16, :128])
-    first, acts, moved_s[1:3] = tie(first, acts, moved_s[1:3])
+    first, acts = tie(first, acts)
     (grad_d,) = weight_grad(sizes_e, meta, (True,), [acts], normed_parts, cot_all)
     first = cols_second(first)
     second = cols_first(split_sides(passes[1][1]))
@@ -630,7 +644,7 @@
     first = chips_steps(first)
     second = cols_second(second)
     both_d = own_core(grad_d)
-    first, second, both_d, moved_s[3:], grad_gu = tie(first, second, both_d, moved_s[3:], grad_gu)
+    first, second, both_d, moved_s[1:3], grad_gu = tie(first, second, both_d, moved_s[1:3], grad_gu)
     moved_d = send_slices(both_d)
     first = chips_last(first)
     second = chips_steps(second)
@@ -640,11 +654,11 @@
     out_sides = [cols_first(split_sides(parts[0])) for parts in passes]
     moved_gu = send_slices(both_gu)
     normed_grad_2 = jnp.concatenate([first, second], axis=0)
-    normed_grad_2, moved_d[1] = tie(normed_grad_2, moved_d[1])
+    normed_grad_2, moved_s[3:] = tie(normed_grad_2, moved_s[3:])
     hidden_part, gain_2_sum = norm_back(normed_grad_2, unit_2, second_scale, gain_2)
     hidden_grad = own_cot.astype(F32) + hidden_part
     attn_grad = col_gather(hidden_grad.astype(BF16), n_c).reshape(span, dim)
-    attn_grad, moved_d[2:], moved_gu[1] = tie(attn_grad, moved_d[2:], moved_gu[1])
+    attn_grad, moved_d[1:] = tie(attn_grad, moved_d[1:])
     gate_s, up_s, down_s = (place_s(value) for value in place_slices(moved_s, 3))
     down_e = place_e(place_slices(moved_d, 1)[0])
 
@@ -656,23 +670,25 @@
     value_grad = einsum("bhqk,bqhd->bkhd", prob_low, mixed_grad).astype(BF16)
     center = jnp.sum(prob_grad * probabilities, axis=-1, keepdims=True)
     score_grad = (probabilities * (prob_grad - center) * (1.0 / math.sqrt(HEAD_DIM))).astype(BF16)
-    out_parts, score_grad, moved_gu[2:3] = tie(out_parts, score_grad, moved_gu[2:3])
+    out_parts, score_grad, moved_gu[1] = tie(out_parts, score_grad, moved_gu[1])
     out_parts = [chips_steps(part) for part in out_parts]
     query_grad = rotate(einsum("bhqk,bkhd->bqhd", score_grad, key_rot), cosine, -sine).astype(BF16)
     key_grad = rotate(einsum("bhqk,bqhd->bkhd", score_grad, query_rot), cosine, -sine).astype(BF16)
     qkv_grad = jnp.concatenate(
         [part.reshape(span, width) for part in (query_grad, key_grad, value_grad)], axis=1
     )
-    qkv_grad, out_parts = tie(qkv_grad, out_parts)
-    out_rows = jnp.concatenate([chips_last(part) for part in out_parts], axis=0)
+    qkv_grad, out_parts, moved_gu[2:3] = tie(qkv_grad, out_parts, moved_gu[2:3])
     qkv_sum = dot(normed_1, qkv_grad, ((0,), (0,)))
     normed_grad_1 = col_sum(dot(qkv_grad, qkv, ((1,), (1,))), n_c)
-    normed_grad_1, out_rows, moved_gu[3:] = tie(normed_grad_1, out_rows, moved_gu[3:])
+    normed_grad_1, moved_gu[3:] = tie(normed_grad_1, moved_gu[3:])
     gate_e, up_e = (place_e(value) for value in place_slices(moved_gu, 2))
     own_scale = lax.dynamic_slice_in_dim(first_scale, at_c * own_rows, own_rows, 0)
     rows_part, gain_1_sum = norm_back(normed_grad_1, own_inputs * own_scale, own_scale, gain_1)
-    token_grad = rows_to_features((hidden_grad + rows_part).astype(BF16), n_c).astype(F32)
-
+    token_rows = (hidden_grad + rows_part).astype(BF16)
+    token_grad = rows_to_features(token_rows, n_c).astype(F32)
+
+    out_rows = [chips_last(part, token_rows[:16, :128]) for part in out_parts]
+    out_rows = jnp.concatenate(out_rows, axis=0)
     result = rows_to_features((hidden + out_rows).astype(BF16), n_c)
 
     sums = jnp.stack([gain_1_sum, gain_2_sum, logit_sum]).reshape(3, n_row, d_own)

time: 1040 us -> 1000 us (0.962)
  waiting for transfers between devices: 424 us -> 375 us
  starting transfers between devices: 132 us -> 154 us
  local copies, waits for them, and re-layouts: 141 us -> 128 us
    ppermute x60, waiting for transfers between devices: 377 us -> 301 us  [shift_by(): lax.ppermute(value, axis, [(i, i ^ shift) for i in range(lax.axis_size(ax...]
    ppermute x60, starting transfers between devices: 86.7 us -> 113 us  [shift_by(): lax.ppermute(value, axis, [(i, i ^ shift) for i in range(lax.axis_size(ax...]
    all_to_all x2, waiting for transfers between devices: 4.13 us -> 15.1 us  [col_sum(): lax.all_to_all(parts, COL, 0, 0, tiled=True).astype(F32)]
    unnamed x233 -> x228, local copies, waits for them, and re-layouts: 42.8 us -> 36.7 us
    another operation x15 -> x12, other arithmetic: 25.1 us -> 20.2 us  [gather_joined(): jnp.stack([value, shift_by(value, axis, bit)], axis=at + 1).reshape(shape)]
  transfers between devices with their start and end apart: 89 -> 88, of which waited for: 34 -> 34; matrix products, arithmetic and copies ran while one was open for 26% -> 25% of each run, Pallas kernels for 15% -> 16%
where the time goes in v8:
time: 1000 us; the launch traced here: 997 us
  waiting for transfers between devices  375 us (38%)
  Pallas kernels  160 us (16%)
  starting transfers between devices  154 us (15%)
  local copies, waits for them, and re-layouts  128 us (13%)
  other arithmetic  108 us (11%)
  matrix products  42.1 us (4%)
  between operations  16.3 us (2%)
  blocking collectives  13.4 us (1%)
    ppermute x60, waiting for transfers between devices, shift_by(): lax.ppermute(value, axis, [(i, i ^ shift) for i in range(lax.axis_size(ax...  301 us
    ppermute x60, starting transfers between devices, shift_by(): lax.ppermute(value, axis, [(i, i ^ shift) for i in range(lax.axis_size(ax...  113 us
    pallas_call x4, Pallas kernels, ffn_pass(): pl.pallas_call(functools.partial(ffn_kernel, sizes, groups), grid_spec=pl...  112 us
    pallas_call x3, Pallas kernels, weight_grad(): pl.pallas_call(functools.partial(grad_kernel, parts, kinds, f_pad), grid_...  47.3 us
    unnamed x228, local copies, waits for them, and re-layouts  36.7 us
    dot_general x6, matrix products, dot(): lax.dot_general(left, right, (dims, ((), ())), preferred_element_type=F32)  31.9 us
    squeeze x16, other arithmetic, scatter_axis(): return lax.index_in_dim(value, 0, at, keepdims=False)  23.9 us
    all_gather x1, waiting for transfers between devices, shards(): lax.all_gather(jnp.concatenate([query_weight, key_weight, value_weight],...  20.5 us
  transfers between devices with their start and end apart: 88, of which 34 were waited for; matrix products, arithmetic and copies ran while one was open for 25% of the time, Pallas kernels for 16%

profile of v8, /device:TPU:0, one launch (start us, length us, event | category | flops | bytes accessed | tf_op | source)
XLA Modules:
  0.0 997.0 jit_solution(8118364944925773526)
XLA Ops:
  40.7 12.8 %all-to-all-done.1 = bf16[4,512,512]{2,1,0:T(8,128)(2,1)S(1)} async-done(((bf16[4,512,512]{2,1,0:T(8,128)(2,1)}), bf16[4,512,512]{2,1,0:T(8,128)(2,1)S(1)}, u32[]{:S(2)}, u32[]{:S(2)}) %all-to-all-start.1) | async-done | bytes 2097184 | tf_op jit(solution)/shard_map/all_to_all | solution.py:333
  61.5 16.4 %all-to-all-done.2 = f32[8,24,256]{2,1,0:T(8,128)S(1)} async-done(((f32[8,24,256]{2,1,0:T(8,128)}), f32[8,24,256]{2,1,0:T(8,128)S(1)}, u32[]{:S(2)}, u32[]{:S(2)}) %all-to-all-start.2) | async-done | bytes 196640 | tf_op jit(solution)/shard_map/all_to_all | solution.py:404
  78.0 20.5 %all-gather.3.cloned.1.call-done = bf16[2048,1536]{1,0:T(8,128)(2,1)} async-done(((bf16[256,1536]{1,0:T(8,128)(2,1)}), bf16[2048,1536]{1,0:T(8,128)(2,1)}) %all-gather.3.cloned.1.call-update) | async-done | bytes 6291472 | tf_op jit(solution)/shard_map/all_gather | solution.py:431
  123.6 21.7 %collective-permute-done.3 = bf16[2,4,2,64,512]{4,3,2,1,0:T(8,128)(2,1)} collective-permute-done((bf16[2,4,2,64,512]{4,3,2,1,0:T(8,128)(2,1)}, bf16[2,4,2,64,512]{4,3,2,1,0:T(8,128)(2,1)}, u32[]{:S(2)}, u32[]{:S(2)}) %collective-permute-start.3) | collective-permute-done | bytes 1048608 | tf_op jit(solution)/shard_map/ppermute | solution.py:308
  174.3 38.2 %collective-permute-done.5 = bf16[1,1,4,4,64,512]{5,4,3,2,1,0:T(8,128)(2,1)S(1)} collective-permute-done((bf16[1,1,4,4,64,512]{5,4,3,2,1,0:T(8,128)(2,1)}, bf16[1,1,4,4,64,512]{5,4,3,2,1,0:T(8,128)(2,1)S(1)}, u32[]{:S(2)}, u32[]{:S(2)}) %collective-permute-start.5) | collective-permute-done | bytes 1048608 | tf_op jit(solution)/shard_map/ppermute | solution.py:308
  254.0 13.7 %collective-permute-done.9.refs_1_ = bf16[1408,256]{1,0:T(8,128)(2,1)S(1)} collective-permute-done((bf16[1408,256]{1,0:T(8,128)(2,1)S(1)}, bf16[1408,256]{1,0:T(8,128)(2,1)S(1)}, u32[]{:S(2)}, u32[]{:S(2)}) %collective-permute-start.9) | collective-permute-done | bytes 720928 | tf_op jit(solution)/shard_map/ppermute | solution.py:308
  286.1 14.1 %collective-permute-done.12 = bf16[4,1,1,64,1024]{4,3,0,2,1:T(8,128)(2,1)} collective-permute-done((bf16[4,1,1,64,1024]{4,3,0,2,1:T(8,128)(2,1)}, bf16[4,1,1,64,1024]{4,3,0,2,1:T(8,128)(2,1)}, u32[]{:S(2)}, u32[]{:S(2)}) %collective-permute-start.12) | collective-permute-done | bytes 524320 | tf_op jit(solution)/shard_map/ppermute | solution.py:308
  364.5 21.2 %ffn_pass.5 = (bf16[1024,2048]{1,0:T(8,128)(2,1)}, bf16[1024,2048]{1,0:T(8,128)(2,1)}, bf16[352,1024]{1,0:T(8,128)(2,1)}, bf16[368,1024]{1,0:T(8,128)(2,1)}, bf16[352,1024]{1,0:T(8,128)(2,1)}) custom-call(s32[3]{0:T(128)} %pad_add_fusion.meta, bf16[1024,2048]{1,0:T(8,128)(2,1)} %pad_maximum_fusion.rows_ref.refs_6_.refs_4_, ...), custom_call_target="tpu_custom_call" | custom-call | flops 8858370048 | bytes 23265280 | tf_op jit(solution)/shard_map/ffn_pass/pallas_call | solution.py:172
  400.4 21.0 %ffn_pass.4 = (bf16[1024,2048]{1,0:T(8,128)(2,1)}, bf16[1024,2048]{1,0:T(8,128)(2,1)}, bf16[352,1024]{1,0:T(8,128)(2,1)}, bf16[368,1024]{1,0:T(8,128)(2,1)}, bf16[352,1024]{1,0:T(8,128)(2,1)}) custom-call(s32[3]{0:T(128)} %pad_add_fusion.meta, bf16[1024,2048]{1,0:T(8,128)(2,1)} %pad_maximum_fusion.3.rows_ref.refs_7_.refs_5_, ...), custom_call_target="tpu_custom_call" | custom-call | flops 8858370048 | bytes 23265280 | tf_op jit(solution)/shard_map/ffn_pass/pallas_call | solution.py:172
  422.0 16.6 %weight_grad.3 = (bf16[2,4,1056,256]{3,2,1,0:T(8,128)(2,1)}, f32[8,2048]{1,0:T(8,128)}) custom-call(s32[3]{0:T(128)} %pad_add_fusion.meta, bf16[368,1024]{1,0:T(8,128)(2,1)} %get-tuple-element.219.refs_0_, bf16[368,1024]{1,0:T(8,128)(2,1)} %get-tuple-element.220.refs_1_, bf16[352,1024]{1,0:T(8,128)(2,1)} %get-tuple-element.221.refs_2_, ...), custom_call_target="tpu_custom_call" | custom-call | flops 8858370048 | bytes 17039360 | tf_op jit(solution)/shard_map/weight_grad/pallas_call | solution.py:271
  444.9 34.9 %ffn_pass.6 = (bf16[1024,2048]{1,0:T(8,128)(2,1)}, bf16[1024,2048]{1,0:T(8,128)(2,1)}, bf16[704,1024]{1,0:T(8,128)(2,1)}, bf16[704,1024]{1,0:T(8,128)(2,1)}, bf16[704,1024]{1,0:T(8,128)(2,1)}) custom-call(s32[3]{0:T(128)} %pad_add_fusion.meta, bf16[1024,2048]{1,0:T(8,128)(2,1)} %pad_maximum_fusion.rows_ref.refs_6_.refs_4_, ...), custom_call_target="tpu_custom_call" | custom-call | flops 17716740096 | bytes 46530560 | tf_op jit(solution)/shard_map/ffn_pass/pallas_call | solution.py:172
  495.7 35.1 %ffn_pass.7 = (bf16[1024,2048]{1,0:T(8,128)(2,1)}, bf16[1024,2048]{1,0:T(8,128)(2,1)}, bf16[704,1024]{1,0:T(8,128)(2,1)}, bf16[704,1024]{1,0:T(8,128)(2,1)}, bf16[704,1024]{1,0:T(8,128)(2,1)}) custom-call(s32[3]{0:T(128)} %pad_add_fusion.meta, bf16[1024,2048]{1,0:T(8,128)(2,1)} %pad_maximum_fusion.3.rows_ref.refs_7_.refs_5_, ...), custom_call_target="tpu_custom_call" | custom-call | flops 17716740096 | bytes 46530560 | tf_op jit(solution)/shard_map/ffn_pass/pallas_call | solution.py:172
  544.9 12.4 %weight_grad.4 = bf16[2,4,704,256]{3,2,1,0:T(8,128)(2,1)} custom-call(s32[3]{0:T(128)} %pad_add_fusion.meta, bf16[704,1024]{1,0:T(8,128)(2,1)} %get-tuple-element.245.refs_0_, bf16[704,1024]{1,0:T(8,128)(2,1)} %get-tuple-element.246.refs_1_, bf16[4,4,4,64,512]{4,3,2,1,0:T(8,128)(2,1)} %bitcast.586, bf16[4,4,4,64,512]{4,3,2,1,0:T(8,128)(2,1)} %bitcast.581), custom_call_target="tpu_custom_call" | custom-call | flops 5905580032 | bytes 14155776 | tf_op jit(solution)/shard_map/weight_grad/pallas_call | solution.py:271
  558.7 9.9 collective-permute-start.54
  578.2 18.3 %weight_grad.5 = bf16[2,4,1408,256]{3,2,1,0:T(8,128)(2,1)} custom-call(s32[3]{0:T(128)} %pad_add_fusion.meta, bf16[704,1024]{1,0:T(8,128)(2,1)} %get-tuple-element.252.refs_0_, bf16[704,1024]{1,0:T(8,128)(2,1)} %get-tuple-element.253.refs_1_, bf16[704,1024]{1,0:T(8,128)(2,1)} %get-tuple-element.254.refs_2_, bf16[704,1024]{1,0:T(8,128)(2,1)} %get-tuple-element.255.refs_3_, ...), custom_call_target="tpu_custom_call" | custom-call | flops 11811160064 | bytes 19922944 | tf_op jit(solution)/shard_map/weight_grad/pallas_call | solution.py:271
  596.5 10.5 %collective-permute-start.50 = (bf16[2,64,2048]{2,1,0:T(8,128)(2,1)S(1)}, bf16[2,64,2048]{2,1,0:T(8,128)(2,1)S(1)}, u32[]{:S(2)}, u32[]{:S(2)}) collective-permute-start(bf16[2,64,2048]{2,1,0:T(8,128)(2,1)S(1)} %slice_bitcast_fusion.48), channel_id=1, source_target_pairs={{0,8},{8,0},{16,24},{24,16},{1,9},{9,1},{17,25},{25,17},{2,10},{10... | collective-permute-start | bytes 1572872 | tf_op jit(solution)/shard_map/ppermute | solution.py:308
  607.5 21.1 %collective-permute-done.50 = bf16[2,64,2048]{2,1,0:T(8,128)(2,1)S(1)} collective-permute-done((bf16[2,64,2048]{2,1,0:T(8,128)(2,1)S(1)}, bf16[2,64,2048]{2,1,0:T(8,128)(2,1)S(1)}, u32[]{:S(2)}, u32[]{:S(2)}) %collective-permute-start.50) | collective-permute-done | bytes 524320 | tf_op jit(solution)/shard_map/ppermute | solution.py:308
  668.0 21.8 %collective-permute-done.59 = bf16[64,2048]{1,0:T(8,128)(2,1)S(1)} collective-permute-done((bf16[64,2048]{1,0:T(8,128)(2,1)S(1)}, bf16[64,2048]{1,0:T(8,128)(2,1)S(1)}, u32[]{:S(2)}, u32[]{:S(2)}) %collective-permute-start.59) | collective-permute-done | bytes 262176 | tf_op jit(solution)/shard_map/ppermute | solution.py:308
  708.0 11.4 %collective-permute-start.61 = (bf16[704,256]{1,0:T(8,128)(2,1)S(1)}, bf16[704,256]{1,0:T(8,128)(2,1)}, u32[]{:S(2)}, u32[]{:S(2)}) collective-permute-start(bf16[704,256]{1,0:T(8,128)(2,1)S(1)} %get-tuple-element.464), channel_id=1, source_target_pairs={{0,8},{8,0},{16,24},{24,16},{1,9},{9,1},{17,25},{25,17},{2,10},{10... | collective-permute-start | bytes 1081352 | tf_op jit(solution)/shard_map/ppermute | solution.py:308
  725.4 9.8 collective-permute-done.61
  735.1 12.0 %collective-permute-done.62 = bf16[704,256]{1,0:T(8,128)(2,1)} collective-permute-done((bf16[704,256]{1,0:T(8,128)(2,1)S(1)}, bf16[704,256]{1,0:T(8,128)(2,1)}, u32[]{:S(2)}, u32[]{:S(2)}) %collective-permute-start.62) | collective-permute-done | bytes 360480 | tf_op jit(solution)/shard_map/ppermute | solution.py:308
  798.2 22.0 %collective-permute-done.69 = bf16[2,64,2048]{2,1,0:T(8,128)(2,1)S(1)} collective-permute-done((bf16[2,64,2048]{2,1,0:T(8,128)(2,1)S(1)}, bf16[2,64,2048]{2,1,0:T(8,128)(2,1)S(1)}, u32[]{:S(2)}, u32[]{:S(2)}) %collective-permute-start.69) | collective-permute-done | bytes 524320 | tf_op jit(solution)/shard_map/ppermute | solution.py:308
  868.8 15.1 %all-to-all-done.6 = bf16[4,128,2048]{2,1,0:T(8,128)(2,1)S(1)} async-done(((bf16[4,128,2048]{2,1,0:T(8,128)(2,1)}), bf16[4,128,2048]{2,1,0:T(8,128)(2,1)S(1)}, u32[]{:S(2)}, u32[]{:S(2)}) %all-to-all-start.6) | async-done | bytes 2097184 | tf_op jit(solution)/shard_map/all_to_all | solution.py:338
  888.4 33.5 %collective-permute-done.74 = bf16[64,2048]{1,0:T(8,128)(2,1)} collective-permute-done((bf16[64,2048]{1,0:T(8,128)(2,1)}, bf16[64,2048]{1,0:T(8,128)(2,1)}, u32[]{:S(2)}, u32[]{:S(2)}) %collective-permute-start.74) | collective-permute-done | bytes 262176 | tf_op jit(solution)/shard_map/ppermute | solution.py:308
  (637 shorter events, 516.8 us)
Async XLA Ops:
  7.2 91.2 %all-gather.3.cloned.1.call-start = ((), (), s32[]{:S(2)}) async-start(), calls=%async_computation.14 | async-start | bytes 7077888 | tf_op jit(solution)/shard_map/all_gather | solution.py:431
  14.3 84.2 %collective-permute-start.2 = (bf16[1,4,2,64,512]{4,3,2,1,0:T(8,128)(2,1)}, bf16[1,4,2,64,512]{4,3,2,1,0:T(8,128)(2,1)}, u32[]{:S(2)}, u32[]{:S(2)}) collective-permute-start(bf16[1,4,2,64,512]{4,3,2,1,0:T(8,128)(2,1)} %bitcast.14), channel_id=1, source_target_pairs={{0,16},{8,24},{16,0},{24,8},{1,17},{9,25},{17,1},{25,9},{2,18},{10... | collective-permute-start | bytes 1572872 | tf_op jit(solution)/shard_map/ppermute | solution.py:308
  28.0 128.2 %all-gather.5.cloned.1.call-start = ((), (), s32[]{:S(2)}) async-start(), calls=%async_computation.15 | async-start | bytes 2359296 | tf_op jit(solution)/shard_map/all_gather | solution.py:434
  160.4 57.5 %all-to-all-start.4 = ((bf16[4,128,2048]{2,1,0:T(8,128)(2,1)}), bf16[4,128,2048]{2,1,0:T(8,128)(2,1)}, u32[]{:S(2)}, u32[]{:S(2)}) async-start(bf16[4,128,2048]{2,1,0:T(8,128)(2,1)} %bitcast.630), calls=%async_computation.4 | async-start | bytes 4194304 | tf_op jit(solution)/shard_map/all_to_all | solution.py:338
  169.3 45.9 %collective-permute-start.6 = (bf16[1,1,4,4,64,512]{5,4,3,2,1,0:T(8,128)(2,1)}, bf16[1,1,4,4,64,512]{5,4,3,2,1,0:T(8,128)(2,1)}, u32[]{:S(2)}, u32[]{:S(2)}) collective-permute-start(bf16[1,1,4,4,64,512]{5,4,3,2,1,0:T(8,128)(2,1)} %get-tuple-element.455), channel_id=1, source_target_pairs={{0,1},{1,0},{2,3},{3,2},{4,5},{5,4},{6,7},{7,6},{8,9},{9,8},{10,11... | collective-permute-start | bytes 3145736 | tf_op jit(solution)/shard_map/ppermute | solution.py:308
  170.8 49.3 %collective-permute-start = (bf16[1056,256]{1,0:T(8,128)(2,1)}, bf16[1056,256]{1,0:T(8,128)(2,1)}, u32[]{:S(2)}, u32[]{:S(2)}) collective-permute-start(bf16[1056,256]{1,0:T(8,128)(2,1)} %get-tuple-element.182), channel_id=1, source_target_pairs={{0,16},{8,24},{16,0},{24,8},{1,17},{9,25},{17,1},{25,9},{2,18},{10... | collective-permute-start | bytes 1622024 | tf_op jit(solution)/shard_map/ppermute | solution.py:308
  173.1 46.9 %collective-permute-start.1 = (bf16[1056,256]{1,0:T(8,128)(2,1)}, bf16[1056,256]{1,0:T(8,128)(2,1)}, u32[]{:S(2)}, u32[]{:S(2)}) collective-permute-start(bf16[1056,256]{1,0:T(8,128)(2,1)} %get-tuple-element.183), channel_id=1, source_target_pairs={{0,24},{8,16},{16,8},{24,0},{1,25},{9,17},{17,9},{25,1},{2,26},{10... | collective-permute-start | bytes 1622024 | tf_op jit(solution)/shard_map/ppermute | solution.py:308
  242.6 66.7 %collective-permute-start.17 = (bf16[2,1,4,4,64,512]{5,4,3,2,0,1:T(8,128)(2,1)S(1)}, bf16[2,1,4,4,64,512]{5,4,3,2,0,1:T(8,128)(2,1)}, u32[]{:S(2)}, u32[]{:S(2)}) collective-permute-start(bf16[2,1,4,4,64,512]{5,4,3,2,0,1:T(8,128)(2,1)S(1)} %maximum_bitcast_fusion), channel_id=1, source_target_pairs={{0,1},{1,0},{2,3},{3,2},{4,5},{5,4},{6,7},{7,6},{8,9},{9,8},{10,11... | collective-permute-start | bytes 6291464 | tf_op jit(solution)/shard_map/ppermute | solution.py:308
  243.6 67.7 %collective-permute-start.18 = (bf16[1,2,4,4,64,512]{5,4,3,2,1,0:T(8,128)(2,1)}, bf16[1,2,4,4,64,512]{5,4,3,2,1,0:T(8,128)(2,1)}, u32[]{:S(2)}, u32[]{:S(2)}) collective-permute-start(bf16[1,2,4,4,64,512]{5,4,3,2,1,0:T(8,128)(2,1)} %maximum_bitcast_fusion.1), channel_id=1, source_target_pairs={{0,2},{2,0},{1,3},{3,1},{4,6},{6,4},{5,7},{7,5},{8,10},{10,8},{9,1... | collective-permute-start | bytes 6291464 | tf_op jit(solution)/shard_map/ppermute | solution.py:308
  363.0 75.7 %collective-permute-start.25 = (bf16[1408,256]{1,0:T(8,128)(2,1)}, bf16[1408,256]{1,0:T(8,128)(2,1)}, u32[]{:S(2)}, u32[]{:S(2)}) collective-permute-start(bf16[1408,256]{1,0:T(8,128)(2,1)} %get-tuple-element.429.refs_0_), channel_id=1, source_target_pairs={{0,4},{4,0},{1,5},{5,1},{2,6},{6,2},{3,7},{7,3},{8,12},{12,8},{9,1... | collective-permute-start | bytes 2162696 | tf_op jit(solution)/shard_map/ppermute | solution.py:302
  444.0 49.2 %collective-permute-start.41 = (bf16[4,1056,256]{2,1,0:T(8,128)(2,1)S(1)}, bf16[4,1056,256]{2,1,0:T(8,128)(2,1)}, u32[]{:S(2)}, u32[]{:S(2)}) collective-permute-start(bf16[4,1056,256]{2,1,0:T(8,128)(2,1)S(1)} %get-tuple-element.405), channel_id=1, source_target_pairs={{0,4},{4,0},{1,5},{5,1},{2,6},{6,2},{3,7},{7,3},{8,12},{12,8},{9,1... | collective-permute-start | bytes 6488072 | tf_op jit(solution)/shard_map/ppermute | solution.py:302
  484.0 154.1 %collective-permute-start.39 = (bf16[4,2,1,64,1024]{4,3,0,1,2:T(8,128)(2,1)}, bf16[4,2,1,64,1024]{4,3,0,1,2:T(8,128)(2,1)}, u32[]{:S(2)}, u32[]{:S(2)}) collective-permute-start(bf16[4,2,1,64,1024]{4,3,0,1,2:T(8,128)(2,1)} %slice_bitcast_fusion.18), channel_id=1, source_target_pairs={{0,1},{1,0},{2,3},{3,2},{4,5},{5,4},{6,7},{7,6},{8,9},{9,8},{10,11... | collective-permute-start | bytes 3145736 | tf_op jit(solution)/shard_map/ppermute | solution.py:308
  558.7 71.7 %collective-permute-start.54 = (bf16[1056,256]{1,0:T(8,128)(2,1)}, bf16[1056,256]{1,0:T(8,128)(2,1)}, u32[]{:S(2)}, u32[]{:S(2)}) collective-permute-start(bf16[1056,256]{1,0:T(8,128)(2,1)} %get-tuple-element.444), channel_id=1, source_target_pairs={{0,8},{8,0},{16,24},{24,16},{1,9},{9,1},{17,25},{25,17},{2,10},{10... | collective-permute-start | bytes 1622024 | tf_op jit(solution)/shard_map/ppermute | solution.py:308
  578.1 50.8 %collective-permute-start.53 = (bf16[4,704,256]{2,1,0:T(8,128)(2,1)S(1)}, bf16[4,704,256]{2,1,0:T(8,128)(2,1)S(1)}, u32[]{:S(2)}, u32[]{:S(2)}) collective-permute-start(bf16[4,704,256]{2,1,0:T(8,128)(2,1)S(1)} %slice_bitcast_fusion.3), channel_id=1, source_target_pairs={{0,4},{4,0},{1,5},{5,1},{2,6},{6,2},{3,7},{7,3},{8,12},{12,8},{9,1... | collective-permute-start | bytes 4325384 | tf_op jit(solution)/shard_map/ppermute | solution.py:302
  636.4 62.5 %collective-permute-start.40 = (bf16[4,1,2,64,1024]{4,3,0,2,1:T(8,128)(2,1)}, bf16[4,1,2,64,1024]{4,3,0,2,1:T(8,128)(2,1)}, u32[]{:S(2)}, u32[]{:S(2)}) collective-permute-start(bf16[4,1,2,64,1024]{4,3,0,2,1:T(8,128)(2,1)} %slice_bitcast_fusion.16), channel_id=1, source_target_pairs={{0,2},{2,0},{1,3},{3,1},{4,6},{6,4},{5,7},{7,5},{8,10},{10,8},{9,1... | collective-permute-start | bytes 3145736 | tf_op jit(solution)/shard_map/ppermute | solution.py:308
  644.3 57.4 %collective-permute-start.42 = (bf16[4,2,1,64,1024]{4,3,0,1,2:T(8,128)(2,1)}, bf16[4,2,1,64,1024]{4,3,0,1,2:T(8,128)(2,1)}, u32[]{:S(2)}, u32[]{:S(2)}) collective-permute-start(bf16[4,2,1,64,1024]{4,3,0,1,2:T(8,128)(2,1)} %slice_bitcast_fusion.14), channel_id=1, source_target_pairs={{0,1},{1,0},{2,3},{3,2},{4,5},{5,4},{6,7},{7,6},{8,9},{9,8},{10,11... | collective-permute-start | bytes 3145736 | tf_op jit(solution)/shard_map/ppermute | solution.py:308
  694.4 52.8 %all-to-all-start.5 = ((bf16[4,128,2048]{2,1,0:T(8,128)(2,1)}), bf16[4,128,2048]{2,1,0:T(8,128)(2,1)}, u32[]{:S(2)}, u32[]{:S(2)}) async-start(bf16[4,128,2048]{2,1,0:T(8,128)(2,1)} %broadcast_in_dim.71), calls=%async_computation.5 | async-start | bytes 4194304 | tf_op jit(solution)/shard_map/all_to_all | solution.py:333
  698.8 286.3 %reduce-scatter.5.cloned.1.call-start = ((), (), s32[]{:S(2)}) async-start(), calls=%async_computation.17 | async-start | bytes 2359296 | tf_op jit(solution)/shard_map/reduce_scatter | solution.py:699
  723.3 60.4 %collective-permute-start.68 = (bf16[1408,256]{1,0:T(8,128)(2,1)}, bf16[1408,256]{1,0:T(8,128)(2,1)}, u32[]{:S(2)}, u32[]{:S(2)}) collective-permute-start(bf16[1408,256]{1,0:T(8,128)(2,1)} %get-tuple-element.425), channel_id=1, source_target_pairs={{0,8},{8,0},{16,24},{24,16},{1,9},{9,1},{17,25},{25,17},{2,10},{10... | collective-permute-start | bytes 2162696 | tf_op jit(solution)/shard_map/ppermute | solution.py:308
  724.5 106.1 %collective-permute-start.71 = (bf16[1408,256]{1,0:T(8,128)(2,1)}, bf16[1408,256]{1,0:T(8,128)(2,1)}, u32[]{:S(2)}, u32[]{:S(2)}) collective-permute-start(bf16[1408,256]{1,0:T(8,128)(2,1)} %get-tuple-element.424), channel_id=1, source_target_pairs={{0,16},{8,24},{16,0},{24,8},{1,17},{9,25},{17,1},{25,9},{2,18},{10... | collective-permute-start | bytes 2162696 | tf_op jit(solution)/shard_map/ppermute | solution.py:308
  772.7 214.4 %reduce-scatter.3.cloned.1.call-start = ((), (), s32[]{:S(2)}) async-start(), calls=%async_computation.16 | async-start | bytes 7077888 | tf_op jit(solution)/shard_map/reduce_scatter | solution.py:700
  837.3 47.0 %collective-permute-start.72 = (bf16[1408,256]{1,0:T(8,128)(2,1)}, bf16[1408,256]{1,0:T(8,128)(2,1)}, u32[]{:S(2)}, u32[]{:S(2)}) collective-permute-start(bf16[1408,256]{1,0:T(8,128)(2,1)} %get-tuple-element.423), channel_id=1, source_target_pairs={{0,24},{8,16},{16,8},{24,0},{1,25},{9,17},{17,9},{25,1},{2,26},{10... | collective-permute-start | bytes 2162696 | tf_op jit(solution)/shard_map/ppermute | solution.py:308
  865.0 56.8 %collective-permute-start.74 = (bf16[64,2048]{1,0:T(8,128)(2,1)}, bf16[64,2048]{1,0:T(8,128)(2,1)}, u32[]{:S(2)}, u32[]{:S(2)}) collective-permute-start(bf16[64,2048]{1,0:T(8,128)(2,1)} %get-tuple-element.495), channel_id=1, source_target_pairs={{0,16},{8,24},{16,0},{24,8},{1,17},{9,25},{17,1},{25,9},{2,18},{10... | collective-permute-start | bytes 786440 | tf_op jit(solution)/shard_map/ppermute | solution.py:308
  865.9 64.6 %collective-permute-start.73 = (bf16[64,2048]{1,0:T(8,128)(2,1)}, bf16[64,2048]{1,0:T(8,128)(2,1)}, u32[]{:S(2)}, u32[]{:S(2)}) collective-permute-start(bf16[64,2048]{1,0:T(8,128)(2,1)} %get-tuple-element.493), channel_id=1, source_target_pairs={{0,16},{8,24},{16,0},{24,8},{1,17},{9,25},{17,1},{25,9},{2,18},{10... | collective-permute-start | bytes 786440 | tf_op jit(solution)/shard_map/ppermute | solution.py:308
  (167 other events, 2478.9 us)
Sparse Core Ops, SparseCore 0:
  10.2 88.1 all-gather.2
  100.0 43.8 all-gather.4
  772.9 48.3 reduce-scatter.4
  836.4 108.6 reduce-scatter.2

commit v9 on v8

--- a/solution.py
+++ b/solution.py
@@ -494,12 +494,6 @@
         value = cot_rows[:, :, part][None, None]
         axis = ("x", "y")[1 - part % 2]
         cot_all.append(gather_joined(value, axis, ("y", "x").index(axis)))
-    cot_all, attention = tie(cot_all, attention)
-    for part in range(PARTS):
-        axis = ("x", "y")[part % 2]
-        value = gather_joined(cot_all[part], axis, ("y", "x").index(axis))
-        cot_all[part] = value.reshape(n_c, n_g, n_c, sub, dim // n_c)
-
     own_inputs = lax.dynamic_slice_in_dim(inputs, at_c * own_rows, own_rows, 0)
     own_blocks[0][2:], attention = tie(own_blocks[0][2:], attention)
     hidden = own_inputs + attention
@@ -519,7 +513,13 @@
     routed_gu, routed_d = own_blocks[1:]
     halves = [normed_own[part * sub : (part + 1) * sub][None] for part in range(PARTS)]
     halves[0] = gather_joined(halves[0], "g", 0)
-    halves[0], halves[1], routed_gu[1] = tie(halves[0], halves[1], routed_gu[1])
+    halves[0], halves[1], routed_gu[1], cot_all = tie(
+        halves[0], halves[1], routed_gu[1], cot_all
+    )
+    for part in range(PARTS):
+        axis = ("x", "y")[part % 2]
+        value = gather_joined(cot_all[part], axis, ("y", "x").index(axis))
+        cot_all[part] = value.reshape(n_c, n_g, n_c, sub, dim // n_c)
     halves[1] = gather_joined(halves[1], "g", 0)
     normed_parts = [gather_cols(halves[0][:, None, None])]
     normed_parts[0], halves[1], routed_gu[2:3], cot_all = tie(
@@ -677,24 +677,25 @@
     qkv_grad = jnp.concatenate(
         [part.reshape(span, width) for part in (query_grad, key_grad, value_grad)], axis=1
     )
-    qkv_grad, out_parts, moved_gu[2:3] = tie(qkv_grad, out_parts, moved_gu[2:3])
+    qkv_grad, moved_gu[2:3] = tie(qkv_grad, moved_gu[2:3])
     qkv_sum = dot(normed_1, qkv_grad, ((0,), (0,)))
     normed_grad_1 = col_sum(dot(qkv_grad, qkv, ((1,), (1,))), n_c)
-    normed_grad_1, moved_gu[3:] = tie(normed_grad_1, moved_gu[3:])
+    normed_grad_1, moved_gu[3:], out_parts = tie(normed_grad_1, moved_gu[3:], out_parts)
     gate_e, up_e = (place_e(value) for value in place_slices(moved_gu, 2))
     own_scale = lax.dynamic_slice_in_dim(first_scale, at_c * own_rows, own_rows, 0)
     rows_part, gain_1_sum = norm_back(normed_grad_1, own_inputs * own_scale, own_scale, gain_1)
     token_rows = (hidden_grad + rows_part).astype(BF16)
-    token_grad = rows_to_features(token_rows, n_c).astype(F32)
-
-    out_rows = [chips_last(part, token_rows[:16, :128]) for part in out_parts]
-    out_rows = jnp.concatenate(out_rows, axis=0)
-    result = rows_to_features((hidden + out_rows).astype(BF16), n_c)
+    token_moved = rows_to_features(token_rows, n_c)
+    token_grad = token_moved.astype(F32)
 
     sums = jnp.stack([gain_1_sum, gain_2_sum, logit_sum]).reshape(3, n_row, d_own)
     sums = jnp.broadcast_to(sums.transpose(1, 0, 2)[:, None], (n_row, n_c, 3, d_own))
     sums = lax.all_to_all(sums.reshape(n_row * n_c, 3, d_own), ALL, 0, 0, tiled=True)
     sums = jnp.sum(sums, axis=0)
+
+    out_rows = [chips_last(part, (token_moved[:, :16, :128], sums[:, :128])) for part in out_parts]
+    out_rows = jnp.concatenate(out_rows, axis=0)
+    result = rows_to_features((hidden + out_rows).astype(BF16), n_c)
 
     out_w_grad = lax.psum_scatter(out_grad.astype(BF16), ROW, scatter_dimension=0, tiled=True)
     qkv_own = lax.psum_scatter(qkv_sum.astype(BF16), ROW, scatter_dimension=0, tiled=True)

time: 1000 us -> 1010 us (1.010)
    ppermute x60, waiting for transfers between devices: 301 us -> 273 us  [shift_by(): lax.ppermute(value, axis, [(i, i ^ shift) for i in range(lax.axis_size(ax...]
    all_to_all x1, waiting for transfers between devices: 7.21 us -> 22.2 us  [shards(): lax.all_to_all(sums.reshape(n_row * n_c, 3, d_own), ALL, 0, 0, tiled=True)]
    unnamed x228 -> x232, local copies, waits for them, and re-layouts: 36.7 us -> 34.7 us
  transfers between devices with their start and end apart: 88 -> 87, of which waited for: 34 -> 31; matrix products, arithmetic and copies ran while one was open for 25% -> 26% of each run, Pallas kernels for 16% -> 16%
where the time goes in v9:
time: 1010 us; the launch traced here: 1000 us
  waiting for transfers between devices  368 us (36%)
  Pallas kernels  160 us (16%)
  starting transfers between devices  158 us (16%)
  local copies, waits for them, and re-layouts  130 us (13%)
  other arithmetic  111 us (11%)
  matrix products  42.3 us (4%)
  blocking collectives  17.6 us (2%)
  between operations  16.2 us (2%)
    ppermute x60, waiting for transfers between devices, shift_by(): lax.ppermute(value, axis, [(i, i ^ shift) for i in range(lax.axis_size(ax...  273 us
    ppermute x60, starting transfers between devices, shift_by(): lax.ppermute(value, axis, [(i, i ^ shift) for i in range(lax.axis_size(ax...  123 us
    pallas_call x4, Pallas kernels, ffn_pass(): pl.pallas_call(functools.partial(ffn_kernel, sizes, groups), grid_spec=pl...  112 us
    pallas_call x3, Pallas kernels, weight_grad(): pl.pallas_call(functools.partial(grad_kernel, parts, kinds, f_pad), grid_...  47.3 us
    unnamed x232, local copies, waits for them, and re-layouts  34.7 us
    dot_general x6, matrix products, dot(): lax.dot_general(left, right, (dims, ((), ())), preferred_element_type=F32)  31.9 us
    squeeze x16, other arithmetic, scatter_axis(): return lax.index_in_dim(value, 0, at, keepdims=False)  22.7 us
    all_to_all x1, waiting for transfers between devices, shards(): lax.all_to_all(sums.reshape(n_row * n_c, 3, d_own), ALL, 0, 0, tiled=True)  22.2 us
  transfers between devices with their start and end apart: 87, of which 31 were waited for; matrix products, arithmetic and copies ran while one was open for 26% of the time, Pallas kernels for 16%

profile of v9, /device:TPU:0, one launch (start us, length us, event | category | flops | bytes accessed | tf_op | source)
XLA Modules:
  0.0 1002.1 jit_solution(15267746668434677232)
XLA Ops:
  40.8 12.7 %all-to-all-done.1 = bf16[4,512,512]{2,1,0:T(8,128)(2,1)S(1)} async-done(((bf16[4,512,512]{2,1,0:T(8,128)(2,1)}), bf16[4,512,512]{2,1,0:T(8,128)(2,1)S(1)}, u32[]{:S(2)}, u32[]{:S(2)}) %all-to-all-start.1) | async-done | bytes 2097184 | tf_op jit(solution)/shard_map/all_to_all | solution.py:333
  61.6 16.4 %all-to-all-done.2 = f32[8,24,256]{2,1,0:T(8,128)S(1)} async-done(((f32[8,24,256]{2,1,0:T(8,128)}), f32[8,24,256]{2,1,0:T(8,128)S(1)}, u32[]{:S(2)}, u32[]{:S(2)}) %all-to-all-start.2) | async-done | bytes 196640 | tf_op jit(solution)/shard_map/all_to_all | solution.py:404
  78.0 20.5 %all-gather.3.cloned.1.call-done = bf16[2048,1536]{1,0:T(8,128)(2,1)} async-done(((bf16[256,1536]{1,0:T(8,128)(2,1)}), bf16[2048,1536]{1,0:T(8,128)(2,1)}) %all-gather.3.cloned.1.call-update) | async-done | bytes 6291472 | tf_op jit(solution)/shard_map/all_gather | solution.py:431
  123.6 21.7 %collective-permute-done.3 = bf16[2,4,2,64,512]{4,3,2,1,0:T(8,128)(2,1)} collective-permute-done((bf16[2,4,2,64,512]{4,3,2,1,0:T(8,128)(2,1)}, bf16[2,4,2,64,512]{4,3,2,1,0:T(8,128)(2,1)}, u32[]{:S(2)}, u32[]{:S(2)}) %collective-permute-start.3) | collective-permute-done | bytes 1048608 | tf_op jit(solution)/shard_map/ppermute | solution.py:308
  173.5 17.7 %all-to-all-done.4 = bf16[4,128,2048]{2,1,0:T(8,128)(2,1)} async-done(((bf16[4,128,2048]{2,1,0:T(8,128)(2,1)}), bf16[4,128,2048]{2,1,0:T(8,128)(2,1)}, u32[]{:S(2)}, u32[]{:S(2)}) %all-to-all-start.4) | async-done | bytes 2097184 | tf_op jit(solution)/shard_map/all_to_all | solution.py:338
  207.8 13.2 %collective-permute-start.5 = (bf16[1,64,2048]{2,1,0:T(8,128)(2,1)S(1)}, bf16[1,64,2048]{2,1,0:T(8,128)(2,1)}, u32[]{:S(2)}, u32[]{:S(2)}) collective-permute-start(bf16[1,64,2048]{2,1,0:T(8,128)(2,1)S(1)} %get-tuple-element.501), channel_id=1, source_target_pairs={{0,16},{8,24},{16,0},{24,8},{1,17},{9,25},{17,1},{25,9},{2,18},{10... | collective-permute-start | bytes 786440 | tf_op jit(solution)/shard_map/ppermute | solution.py:308
  249.2 14.3 %collective-permute-done.7.refs_1_ = bf16[1408,256]{1,0:T(8,128)(2,1)S(1)} collective-permute-done((bf16[1408,256]{1,0:T(8,128)(2,1)S(1)}, bf16[1408,256]{1,0:T(8,128)(2,1)S(1)}, u32[]{:S(2)}, u32[]{:S(2)}) %collective-permute-start.7) | collective-permute-done | bytes 720928 | tf_op jit(solution)/shard_map/ppermute | solution.py:308
  301.2 46.0 %collective-permute-done.13 = bf16[4,1,2,64,1024]{4,3,0,2,1:T(8,128)(2,1)} collective-permute-done((bf16[4,1,2,64,1024]{4,3,0,2,1:T(8,128)(2,1)}, bf16[4,1,2,64,1024]{4,3,0,2,1:T(8,128)(2,1)}, u32[]{:S(2)}, u32[]{:S(2)}) %collective-permute-start.13) | collective-permute-done | bytes 1048608 | tf_op jit(solution)/shard_map/ppermute | solution.py:308
  383.1 21.2 %ffn_pass.5 = (bf16[1024,2048]{1,0:T(8,128)(2,1)}, bf16[1024,2048]{1,0:T(8,128)(2,1)}, bf16[352,1024]{1,0:T(8,128)(2,1)}, bf16[368,1024]{1,0:T(8,128)(2,1)}, bf16[352,1024]{1,0:T(8,128)(2,1)}) custom-call(s32[3]{0:T(128)} %pad_add_fusion.meta, bf16[1024,2048]{1,0:T(8,128)(2,1)} %pad_maximum_fusion.rows_ref.refs_6_.refs_4_, ...), custom_call_target="tpu_custom_call" | custom-call | flops 8858370048 | bytes 23265280 | tf_op jit(solution)/shard_map/ffn_pass/pallas_call | solution.py:172
  418.2 21.0 %ffn_pass.4 = (bf16[1024,2048]{1,0:T(8,128)(2,1)}, bf16[1024,2048]{1,0:T(8,128)(2,1)}, bf16[352,1024]{1,0:T(8,128)(2,1)}, bf16[368,1024]{1,0:T(8,128)(2,1)}, bf16[352,1024]{1,0:T(8,128)(2,1)}) custom-call(s32[3]{0:T(128)} %pad_add_fusion.meta, bf16[1024,2048]{1,0:T(8,128)(2,1)} %pad_maximum_fusion.3.rows_ref.refs_7_.refs_5_, ...), custom_call_target="tpu_custom_call" | custom-call | flops 8858370048 | bytes 23265280 | tf_op jit(solution)/shard_map/ffn_pass/pallas_call | solution.py:172
  440.3 16.6 %weight_grad.3 = (bf16[2,4,1056,256]{3,2,1,0:T(8,128)(2,1)}, f32[8,2048]{1,0:T(8,128)}) custom-call(s32[3]{0:T(128)} %pad_add_fusion.meta, bf16[368,1024]{1,0:T(8,128)(2,1)} %get-tuple-element.217.refs_0_, bf16[368,1024]{1,0:T(8,128)(2,1)} %get-tuple-element.218.refs_1_, bf16[352,1024]{1,0:T(8,128)(2,1)} %get-tuple-element.219.refs_2_, ...), custom_call_target="tpu_custom_call" | custom-call | flops 8858370048 | bytes 17039360 | tf_op jit(solution)/shard_map/weight_grad/pallas_call | solution.py:271
  463.2 34.9 %ffn_pass.6 = (bf16[1024,2048]{1,0:T(8,128)(2,1)}, bf16[1024,2048]{1,0:T(8,128)(2,1)}, bf16[704,1024]{1,0:T(8,128)(2,1)}, bf16[704,1024]{1,0:T(8,128)(2,1)}, bf16[704,1024]{1,0:T(8,128)(2,1)}) custom-call(s32[3]{0:T(128)} %pad_add_fusion.meta, bf16[1024,2048]{1,0:T(8,128)(2,1)} %pad_maximum_fusion.rows_ref.refs_6_.refs_4_, ...), custom_call_target="tpu_custom_call" | custom-call | flops 17716740096 | bytes 46530560 | tf_op jit(solution)/shard_map/ffn_pass/pallas_call | solution.py:172
  514.0 35.1 %ffn_pass.7 = (bf16[1024,2048]{1,0:T(8,128)(2,1)}, bf16[1024,2048]{1,0:T(8,128)(2,1)}, bf16[704,1024]{1,0:T(8,128)(2,1)}, bf16[704,1024]{1,0:T(8,128)(2,1)}, bf16[704,1024]{1,0:T(8,128)(2,1)}) custom-call(s32[3]{0:T(128)} %pad_add_fusion.meta, bf16[1024,2048]{1,0:T(8,128)(2,1)} %pad_maximum_fusion.3.rows_ref.refs_7_.refs_5_, ...), custom_call_target="tpu_custom_call" | custom-call | flops 17716740096 | bytes 46530560 | tf_op jit(solution)/shard_map/ffn_pass/pallas_call | solution.py:172
  563.1 12.4 %weight_grad.4 = bf16[2,4,704,256]{3,2,1,0:T(8,128)(2,1)} custom-call(s32[3]{0:T(128)} %pad_add_fusion.meta, bf16[704,1024]{1,0:T(8,128)(2,1)} %get-tuple-element.243.refs_0_, bf16[704,1024]{1,0:T(8,128)(2,1)} %get-tuple-element.244.refs_1_, bf16[4,4,4,64,512]{4,3,2,1,0:T(8,128)(2,1)} %bitcast.581, bf16[4,4,4,64,512]{4,3,2,1,0:T(8,128)(2,1)} %bitcast.586), custom_call_target="tpu_custom_call" | custom-call | flops 5905580032 | bytes 14155776 | tf_op jit(solution)/shard_map/weight_grad/pallas_call | solution.py:271
  577.0 14.1 %collective-permute-start.54 = (bf16[1056,256]{1,0:T(8,128)(2,1)}, bf16[1056,256]{1,0:T(8,128)(2,1)}, u32[]{:S(2)}, u32[]{:S(2)}) collective-permute-start(bf16[1056,256]{1,0:T(8,128)(2,1)} %get-tuple-element.442), channel_id=1, source_target_pairs={{0,8},{8,0},{16,24},{24,16},{1,9},{9,1},{17,25},{25,17},{2,10},{10... | collective-permute-start | bytes 1622024 | tf_op jit(solution)/shard_map/ppermute | solution.py:308
  598.1 18.3 %weight_grad.5 = bf16[2,4,1408,256]{3,2,1,0:T(8,128)(2,1)} custom-call(s32[3]{0:T(128)} %pad_add_fusion.meta, bf16[704,1024]{1,0:T(8,128)(2,1)} %get-tuple-element.250.refs_0_, bf16[704,1024]{1,0:T(8,128)(2,1)} %get-tuple-element.251.refs_1_, bf16[704,1024]{1,0:T(8,128)(2,1)} %get-tuple-element.252.refs_2_, bf16[704,1024]{1,0:T(8,128)(2,1)} %get-tuple-element.253.refs_3_, ...), custom_call_target="tpu_custom_call" | custom-call | flops 11811160064 | bytes 19922944 | tf_op jit(solution)/shard_map/weight_grad/pallas_call | solution.py:271
  616.5 13.2 %collective-permute-start.50 = (bf16[2,64,2048]{2,1,0:T(8,128)(2,1)S(1)}, bf16[2,64,2048]{2,1,0:T(8,128)(2,1)S(1)}, u32[]{:S(2)}, u32[]{:S(2)}) collective-permute-start(bf16[2,64,2048]{2,1,0:T(8,128)(2,1)S(1)} %slice_bitcast_fusion.48), channel_id=1, source_target_pairs={{0,8},{8,0},{16,24},{24,16},{1,9},{9,1},{17,25},{25,17},{2,10},{10... | collective-permute-start | bytes 1572872 | tf_op jit(solution)/shard_map/ppermute | solution.py:308
  630.2 21.0 %collective-permute-done.50 = bf16[2,64,2048]{2,1,0:T(8,128)(2,1)S(1)} collective-permute-done((bf16[2,64,2048]{2,1,0:T(8,128)(2,1)S(1)}, bf16[2,64,2048]{2,1,0:T(8,128)(2,1)S(1)}, u32[]{:S(2)}, u32[]{:S(2)}) %collective-permute-start.50) | collective-permute-done | bytes 524320 | tf_op jit(solution)/shard_map/ppermute | solution.py:308
  690.0 21.5 %collective-permute-done.59 = bf16[64,2048]{1,0:T(8,128)(2,1)S(1)} collective-permute-done((bf16[64,2048]{1,0:T(8,128)(2,1)S(1)}, bf16[64,2048]{1,0:T(8,128)(2,1)S(1)}, u32[]{:S(2)}, u32[]{:S(2)}) %collective-permute-start.59) | collective-permute-done | bytes 262176 | tf_op jit(solution)/shard_map/ppermute | solution.py:308
  729.7 11.4 %collective-permute-start.61 = (bf16[704,256]{1,0:T(8,128)(2,1)S(1)}, bf16[704,256]{1,0:T(8,128)(2,1)}, u32[]{:S(2)}, u32[]{:S(2)}) collective-permute-start(bf16[704,256]{1,0:T(8,128)(2,1)S(1)} %get-tuple-element.462), channel_id=1, source_target_pairs={{0,8},{8,0},{16,24},{24,16},{1,9},{9,1},{17,25},{25,17},{2,10},{10... | collective-permute-start | bytes 1081352 | tf_op jit(solution)/shard_map/ppermute | solution.py:308
  756.9 12.0 %collective-permute-done.62 = bf16[704,256]{1,0:T(8,128)(2,1)} collective-permute-done((bf16[704,256]{1,0:T(8,128)(2,1)S(1)}, bf16[704,256]{1,0:T(8,128)(2,1)}, u32[]{:S(2)}, u32[]{:S(2)}) %collective-permute-start.62) | collective-permute-done | bytes 360480 | tf_op jit(solution)/shard_map/ppermute | solution.py:308
  865.2 20.9 %collective-permute-done.71 = bf16[2,64,2048]{2,1,0:T(8,128)(2,1)S(1)} collective-permute-done((bf16[2,64,2048]{2,1,0:T(8,128)(2,1)S(1)}, bf16[2,64,2048]{2,1,0:T(8,128)(2,1)S(1)}, u32[]{:S(2)}, u32[]{:S(2)}) %collective-permute-start.71) | collective-permute-done | bytes 524320 | tf_op jit(solution)/shard_map/ppermute | solution.py:308
  887.0 20.2 %collective-permute-done.72 = bf16[2,64,2048]{2,1,0:T(8,128)(2,1)S(1)} collective-permute-done((bf16[2,64,2048]{2,1,0:T(8,128)(2,1)S(1)}, bf16[2,64,2048]{2,1,0:T(8,128)(2,1)S(1)}, u32[]{:S(2)}, u32[]{:S(2)}) %collective-permute-start.72) | collective-permute-done | bytes 524320 | tf_op jit(solution)/shard_map/ppermute | solution.py:308
  926.1 22.2 %all-to-all-done.9 = f32[32,3,256]{2,1,0:T(4,128)S(1)} async-done(((f32[32,3,256]{2,1,0:T(4,128)}), f32[32,3,256]{2,1,0:T(4,128)S(1)}, u32[]{:S(2)}, u32[]{:S(2)}) %all-to-all-start.9) | async-done | bytes 98336 | tf_op jit(solution)/shard_map/all_to_all | solution.py:693
  (640 shorter events, 507.1 us)
Async XLA Ops:
  7.2 91.2 %all-gather.3.cloned.1.call-start = ((), (), s32[]{:S(2)}) async-start(), calls=%async_computation.14 | async-start | bytes 7077888 | tf_op jit(solution)/shard_map/all_gather | solution.py:431
  14.3 84.1 %collective-permute-start.2 = (bf16[1,4,2,64,512]{4,3,2,1,0:T(8,128)(2,1)}, bf16[1,4,2,64,512]{4,3,2,1,0:T(8,128)(2,1)}, u32[]{:S(2)}, u32[]{:S(2)}) collective-permute-start(bf16[1,4,2,64,512]{4,3,2,1,0:T(8,128)(2,1)} %bitcast.14), channel_id=1, source_target_pairs={{0,16},{8,24},{16,0},{24,8},{1,17},{9,25},{17,1},{25,9},{2,18},{10... | collective-permute-start | bytes 1572872 | tf_op jit(solution)/shard_map/ppermute | solution.py:308
  28.1 128.1 %all-gather.5.cloned.1.call-start = ((), (), s32[]{:S(2)}) async-start(), calls=%async_computation.15 | async-start | bytes 2359296 | tf_op jit(solution)/shard_map/all_gather | solution.py:434
  171.5 66.2 %collective-permute-start.8 = (bf16[1,1,4,4,64,512]{5,4,3,2,1,0:T(8,128)(2,1)}, bf16[1,1,4,4,64,512]{5,4,3,2,1,0:T(8,128)(2,1)}, u32[]{:S(2)}, u32[]{:S(2)}) collective-permute-start(bf16[1,1,4,4,64,512]{5,4,3,2,1,0:T(8,128)(2,1)} %get-tuple-element.452), channel_id=1, source_target_pairs={{0,2},{2,0},{1,3},{3,1},{4,6},{6,4},{5,7},{7,5},{8,10},{10,8},{9,1... | collective-permute-start | bytes 3145736 | tf_op jit(solution)/shard_map/ppermute | solution.py:308
  269.8 83.2 %collective-permute-start.17 = (bf16[2,1,4,4,64,512]{5,4,3,2,0,1:T(8,128)(2,1)S(1)}, bf16[2,1,4,4,64,512]{5,4,3,2,0,1:T(8,128)(2,1)}, u32[]{:S(2)}, u32[]{:S(2)}) collective-permute-start(bf16[2,1,4,4,64,512]{5,4,3,2,0,1:T(8,128)(2,1)S(1)} %maximum_bitcast_fusion), channel_id=1, source_target_pairs={{0,1},{1,0},{2,3},{3,2},{4,5},{5,4},{6,7},{7,6},{8,9},{9,8},{10,11... | collective-permute-start | bytes 6291464 | tf_op jit(solution)/shard_map/ppermute | solution.py:308
  271.5 85.9 %collective-permute-start.18 = (bf16[1,2,4,4,64,512]{5,4,3,2,1,0:T(8,128)(2,1)}, bf16[1,2,4,4,64,512]{5,4,3,2,1,0:T(8,128)(2,1)}, u32[]{:S(2)}, u32[]{:S(2)}) collective-permute-start(bf16[1,2,4,4,64,512]{5,4,3,2,1,0:T(8,128)(2,1)} %maximum_bitcast_fusion.1), channel_id=1, source_target_pairs={{0,2},{2,0},{1,3},{3,1},{4,6},{6,4},{5,7},{7,5},{8,10},{10,8},{9,1... | collective-permute-start | bytes 6291464 | tf_op jit(solution)/shard_map/ppermute | solution.py:308
  282.3 64.9 %collective-permute-start.13 = (bf16[4,1,2,64,1024]{4,3,0,2,1:T(8,128)(2,1)}, bf16[4,1,2,64,1024]{4,3,0,2,1:T(8,128)(2,1)}, u32[]{:S(2)}, u32[]{:S(2)}) collective-permute-start(bf16[4,1,2,64,1024]{4,3,0,2,1:T(8,128)(2,1)} %maximum_bitcast_fusion.2), channel_id=1, source_target_pairs={{0,2},{2,0},{1,3},{3,1},{4,6},{6,4},{5,7},{7,5},{8,10},{10,8},{9,1... | collective-permute-start | bytes 3145736 | tf_op jit(solution)/shard_map/ppermute | solution.py:308
  286.2 62.7 %collective-permute-start.11 = (bf16[4,2,1,64,1024]{4,3,0,1,2:T(8,128)(2,1)}, bf16[4,2,1,64,1024]{4,3,0,1,2:T(8,128)(2,1)}, u32[]{:S(2)}, u32[]{:S(2)}) collective-permute-start(bf16[4,2,1,64,1024]{4,3,0,1,2:T(8,128)(2,1)} %get-tuple-element.478), channel_id=1, source_target_pairs={{0,1},{1,0},{2,3},{3,2},{4,5},{5,4},{6,7},{7,6},{8,9},{9,8},{10,11... | collective-permute-start | bytes 3145736 | tf_op jit(solution)/shard_map/ppermute | solution.py:308
  299.7 62.4 %collective-permute-start.16 = (bf16[1408,256]{1,0:T(8,128)(2,1)}, bf16[1408,256]{1,0:T(8,128)(2,1)S(1)}, u32[]{:S(2)}, u32[]{:S(2)}) collective-permute-start(bf16[1408,256]{1,0:T(8,128)(2,1)} %get-tuple-element.426), channel_id=1, source_target_pairs={{0,16},{8,24},{16,0},{24,8},{1,17},{9,25},{17,1},{25,9},{2,18},{10... | collective-permute-start | bytes 2162696 | tf_op jit(solution)/shard_map/ppermute | solution.py:308
  382.5 74.4 %collective-permute-start.25 = (bf16[1408,256]{1,0:T(8,128)(2,1)}, bf16[1408,256]{1,0:T(8,128)(2,1)}, u32[]{:S(2)}, u32[]{:S(2)}) collective-permute-start(bf16[1408,256]{1,0:T(8,128)(2,1)} %get-tuple-element.427.refs_0_), channel_id=1, source_target_pairs={{0,4},{4,0},{1,5},{5,1},{2,6},{6,2},{3,7},{7,3},{8,12},{12,8},{9,1... | collective-permute-start | bytes 2162696 | tf_op jit(solution)/shard_map/ppermute | solution.py:302
  462.2 49.3 %collective-permute-start.41 = (bf16[4,1056,256]{2,1,0:T(8,128)(2,1)S(1)}, bf16[4,1056,256]{2,1,0:T(8,128)(2,1)}, u32[]{:S(2)}, u32[]{:S(2)}) collective-permute-start(bf16[4,1056,256]{2,1,0:T(8,128)(2,1)S(1)} %get-tuple-element.403), channel_id=1, source_target_pairs={{0,4},{4,0},{1,5},{5,1},{2,6},{6,2},{3,7},{7,3},{8,12},{12,8},{9,1... | collective-permute-start | bytes 6488072 | tf_op jit(solution)/shard_map/ppermute | solution.py:302
  502.2 157.8 %collective-permute-start.39 = (bf16[4,2,1,64,1024]{4,3,0,1,2:T(8,128)(2,1)}, bf16[4,2,1,64,1024]{4,3,0,1,2:T(8,128)(2,1)}, u32[]{:S(2)}, u32[]{:S(2)}) collective-permute-start(bf16[4,2,1,64,1024]{4,3,0,1,2:T(8,128)(2,1)} %slice_bitcast_fusion.18), channel_id=1, source_target_pairs={{0,1},{1,0},{2,3},{3,2},{4,5},{5,4},{6,7},{7,6},{8,9},{9,8},{10,11... | collective-permute-start | bytes 3145736 | tf_op jit(solution)/shard_map/ppermute | solution.py:308
  577.0 76.0 %collective-permute-start.54 = (bf16[1056,256]{1,0:T(8,128)(2,1)}, bf16[1056,256]{1,0:T(8,128)(2,1)}, u32[]{:S(2)}, u32[]{:S(2)}) collective-permute-start(bf16[1056,256]{1,0:T(8,128)(2,1)} %get-tuple-element.442), channel_id=1, source_target_pairs={{0,8},{8,0},{16,24},{24,16},{1,9},{9,1},{17,25},{25,17},{2,10},{10... | collective-permute-start | bytes 1622024 | tf_op jit(solution)/shard_map/ppermute | solution.py:308
  598.1 53.4 %collective-permute-start.53 = (bf16[4,704,256]{2,1,0:T(8,128)(2,1)S(1)}, bf16[4,704,256]{2,1,0:T(8,128)(2,1)S(1)}, u32[]{:S(2)}, u32[]{:S(2)}) collective-permute-start(bf16[4,704,256]{2,1,0:T(8,128)(2,1)S(1)} %slice_bitcast_fusion.3), channel_id=1, source_target_pairs={{0,4},{4,0},{1,5},{5,1},{2,6},{6,2},{3,7},{7,3},{8,12},{12,8},{9,1... | collective-permute-start | bytes 4325384 | tf_op jit(solution)/shard_map/ppermute | solution.py:302
  658.6 62.0 %collective-permute-start.40 = (bf16[4,1,2,64,1024]{4,3,0,2,1:T(8,128)(2,1)}, bf16[4,1,2,64,1024]{4,3,0,2,1:T(8,128)(2,1)}, u32[]{:S(2)}, u32[]{:S(2)}) collective-permute-start(bf16[4,1,2,64,1024]{4,3,0,2,1:T(8,128)(2,1)} %slice_bitcast_fusion.16), channel_id=1, source_target_pairs={{0,2},{2,0},{1,3},{3,1},{4,6},{6,4},{5,7},{7,5},{8,10},{10,8},{9,1... | collective-permute-start | bytes 3145736 | tf_op jit(solution)/shard_map/ppermute | solution.py:308
  666.0 57.4 %collective-permute-start.42 = (bf16[4,2,1,64,1024]{4,3,0,1,2:T(8,128)(2,1)}, bf16[4,2,1,64,1024]{4,3,0,1,2:T(8,128)(2,1)}, u32[]{:S(2)}, u32[]{:S(2)}) collective-permute-start(bf16[4,2,1,64,1024]{4,3,0,1,2:T(8,128)(2,1)} %slice_bitcast_fusion.14), channel_id=1, source_target_pairs={{0,1},{1,0},{2,3},{3,2},{4,5},{5,4},{6,7},{7,6},{8,9},{9,8},{10,11... | collective-permute-start | bytes 3145736 | tf_op jit(solution)/shard_map/ppermute | solution.py:308
  716.1 52.8 %all-to-all-start.5 = ((bf16[4,128,2048]{2,1,0:T(8,128)(2,1)}), bf16[4,128,2048]{2,1,0:T(8,128)(2,1)}, u32[]{:S(2)}, u32[]{:S(2)}) async-start(bf16[4,128,2048]{2,1,0:T(8,128)(2,1)} %broadcast_in_dim.71), calls=%async_computation.5 | async-start | bytes 4194304 | tf_op jit(solution)/shard_map/all_to_all | solution.py:333
  720.5 269.7 %reduce-scatter.5.cloned.1.call-start = ((), (), s32[]{:S(2)}) async-start(), calls=%async_computation.17 | async-start | bytes 2359296 | tf_op jit(solution)/shard_map/reduce_scatter | solution.py:700
  745.1 68.1 %collective-permute-start.68 = (bf16[1408,256]{1,0:T(8,128)(2,1)}, bf16[1408,256]{1,0:T(8,128)(2,1)}, u32[]{:S(2)}, u32[]{:S(2)}) collective-permute-start(bf16[1408,256]{1,0:T(8,128)(2,1)} %get-tuple-element.423), channel_id=1, source_target_pairs={{0,8},{8,0},{16,24},{24,16},{1,9},{9,1},{17,25},{25,17},{2,10},{10... | collective-permute-start | bytes 2162696 | tf_op jit(solution)/shard_map/ppermute | solution.py:308
  746.2 71.8 %collective-permute-start.69 = (bf16[1408,256]{1,0:T(8,128)(2,1)}, bf16[1408,256]{1,0:T(8,128)(2,1)}, u32[]{:S(2)}, u32[]{:S(2)}) collective-permute-start(bf16[1408,256]{1,0:T(8,128)(2,1)} %get-tuple-element.422), channel_id=1, source_target_pairs={{0,16},{8,24},{16,0},{24,8},{1,17},{9,25},{17,1},{25,9},{2,18},{10... | collective-permute-start | bytes 2162696 | tf_op jit(solution)/shard_map/ppermute | solution.py:308
  788.9 203.2 %reduce-scatter.3.cloned.1.call-start = ((), (), s32[]{:S(2)}) async-start(), calls=%async_computation.16 | async-start | bytes 7077888 | tf_op jit(solution)/shard_map/reduce_scatter | solution.py:701
  827.2 81.4 %collective-permute-start.70 = (bf16[1408,256]{1,0:T(8,128)(2,1)}, bf16[1408,256]{1,0:T(8,128)(2,1)}, u32[]{:S(2)}, u32[]{:S(2)}) collective-permute-start(bf16[1408,256]{1,0:T(8,128)(2,1)} %get-tuple-element.421), channel_id=1, source_target_pairs={{0,24},{8,16},{16,8},{24,0},{1,25},{9,17},{17,9},{25,1},{2,26},{10... | collective-permute-start | bytes 2162696 | tf_op jit(solution)/shard_map/ppermute | solution.py:308
  849.4 58.7 %all-to-all-start.6 = ((bf16[4,128,2048]{2,1,0:T(8,128)(2,1)}), bf16[4,128,2048]{2,1,0:T(8,128)(2,1)S(1)}, u32[]{:S(2)}, u32[]{:S(2)}) async-start(bf16[4,128,2048]{2,1,0:T(8,128)(2,1)} %bitcast.631), calls=%async_computation.6 | async-start | bytes 4194304 | tf_op jit(solution)/shard_map/all_to_all | solution.py:338
  910.6 53.3 %collective-permute-start.74 = (bf16[64,2048]{1,0:T(8,128)(2,1)}, bf16[64,2048]{1,0:T(8,128)(2,1)}, u32[]{:S(2)}, u32[]{:S(2)}) collective-permute-start(bf16[64,2048]{1,0:T(8,128)(2,1)} %get-tuple-element.493), channel_id=1, source_target_pairs={{0,16},{8,24},{16,0},{24,8},{1,17},{9,25},{17,1},{25,9},{2,18},{10... | collective-permute-start | bytes 786440 | tf_op jit(solution)/shard_map/ppermute | solution.py:308
  (168 other events, 2454.7 us)
Sparse Core Ops, SparseCore 0:
  10.2 88.1 all-gather.2
  100.0 43.8 all-gather.4
  789.1 41.5 reduce-scatter.4
  832.8 118.1 reduce-scatter.2

commit v10 on v8

--- a/solution.py
+++ b/solution.py
@@ -499,7 +499,6 @@
         axis = ("x", "y")[part % 2]
         value = gather_joined(cot_all[part], axis, ("y", "x").index(axis))
         cot_all[part] = value.reshape(n_c, n_g, n_c, sub, dim // n_c)
-
     own_inputs = lax.dynamic_slice_in_dim(inputs, at_c * own_rows, own_rows, 0)
     own_blocks[0][2:], attention = tie(own_blocks[0][2:], attention)
     hidden = own_inputs + attention
@@ -677,21 +676,23 @@
     qkv_grad = jnp.concatenate(
         [part.reshape(span, width) for part in (query_grad, key_grad, value_grad)], axis=1
     )
-    qkv_grad, out_parts, moved_gu[2:3] = tie(qkv_grad, out_parts, moved_gu[2:3])
+    qkv_grad, moved_gu[2:3] = tie(qkv_grad, moved_gu[2:3])
     qkv_sum = dot(normed_1, qkv_grad, ((0,), (0,)))
     normed_grad_1 = col_sum(dot(qkv_grad, qkv, ((1,), (1,))), n_c)
-    normed_grad_1, moved_gu[3:] = tie(normed_grad_1, moved_gu[3:])
+    normed_grad_1, moved_gu[3:], out_parts = tie(normed_grad_1, moved_gu[3:], out_parts)
     gate_e, up_e = (place_e(value) for value in place_slices(moved_gu, 2))
     own_scale = lax.dynamic_slice_in_dim(first_scale, at_c * own_rows, own_rows, 0)
     rows_part, gain_1_sum = norm_back(normed_grad_1, own_inputs * own_scale, own_scale, gain_1)
     token_rows = (hidden_grad + rows_part).astype(BF16)
-    token_grad = rows_to_features(token_rows, n_c).astype(F32)
-
-    out_rows = [chips_last(part, token_rows[:16, :128]) for part in out_parts]
+    token_moved = rows_to_features(token_rows, n_c)
+    token_grad = token_moved.astype(F32)
+
+    out_rows = [chips_last(part, token_moved[:, :16, :128]) for part in out_parts]
     out_rows = jnp.concatenate(out_rows, axis=0)
     result = rows_to_features((hidden + out_rows).astype(BF16), n_c)
 
     sums = jnp.stack([gain_1_sum, gain_2_sum, logit_sum]).reshape(3, n_row, d_own)
+    sums, result = tie(sums, result)
     sums = jnp.broadcast_to(sums.transpose(1, 0, 2)[:, None], (n_row, n_c, 3, d_own))
     sums = lax.all_to_all(sums.reshape(n_row * n_c, 3, d_own), ALL, 0, 0, tiled=True)
     sums = jnp.sum(sums, axis=0)

time: 1000 us -> 1000 us (level)
  starting transfers between devices: 154 us -> 123 us
  waiting for transfers between devices: 375 us -> 393 us
    ppermute x60, waiting for transfers between devices: 301 us -> 332 us  [shift_by(): lax.ppermute(value, axis, [(i, i ^ shift) for i in range(lax.axis_size(ax...]
    ppermute x60, starting transfers between devices: 113 us -> 84.4 us  [shift_by(): lax.ppermute(value, axis, [(i, i ^ shift) for i in range(lax.axis_size(ax...]
    all_to_all x2, waiting for transfers between devices: 15.1 us -> 0.01 us  [col_sum(): lax.all_to_all(parts, COL, 0, 0, tiled=True).astype(F32)]
    unnamed x228 -> x234, local copies, waits for them, and re-layouts: 36.7 us -> 39.9 us
  transfers between devices with their start and end apart: 88 -> 88, of which waited for: 34 -> 29; matrix products, arithmetic and copies ran while one was open for 25% -> 26% of each run, Pallas kernels for 16% -> 16%
where the time goes in v10:
time: 1000 us; the launch traced here: 994 us
  waiting for transfers between devices  393 us (39%)
  Pallas kernels  160 us (16%)
  local copies, waits for them, and re-layouts  136 us (14%)
  starting transfers between devices  123 us (12%)
  other arithmetic  110 us (11%)
  matrix products  42.2 us (4%)
  between operations  16.3 us (2%)
  blocking collectives  15.1 us (2%)
    ppermute x60, waiting for transfers between devices, shift_by(): lax.ppermute(value, axis, [(i, i ^ shift) for i in range(lax.axis_size(ax...  332 us
    pallas_call x4, Pallas kernels, ffn_pass(): pl.pallas_call(functools.partial(ffn_kernel, sizes, groups), grid_spec=pl...  112 us
    ppermute x60, starting transfers between devices, shift_by(): lax.ppermute(value, axis, [(i, i ^ shift) for i in range(lax.axis_size(ax...  84.4 us
    pallas_call x3, Pallas kernels, weight_grad(): pl.pallas_call(functools.partial(grad_kernel, parts, kinds, f_pad), grid_...  47.3 us
    unnamed x234, local copies, waits for them, and re-layouts  39.9 us
    dot_general x6, matrix products, dot(): lax.dot_general(left, right, (dims, ((), ())), preferred_element_type=F32)  31.9 us
    all_to_all x1, waiting for transfers between devices, shards(): lax.all_to_all(jnp.broadcast_to(small[None], (n_row,) + small.shape), ROW...  22.3 us
    squeeze x16, other arithmetic, scatter_axis(): return lax.index_in_dim(value, 0, at, keepdims=False)  21.6 us
  transfers between devices with their start and end apart: 88, of which 29 were waited for; matrix products, arithmetic and copies ran while one was open for 26% of the time, Pallas kernels for 16%

profile of v10, /device:TPU:0, one launch (start us, length us, event | category | flops | bytes accessed | tf_op | source)
XLA Modules:
  0.0 994.3 jit_solution(18442128219999256562)
XLA Ops:
  39.9 12.7 %all-to-all-done.1 = bf16[4,512,512]{2,1,0:T(8,128)(2,1)S(1)} async-done(((bf16[4,512,512]{2,1,0:T(8,128)(2,1)}), bf16[4,512,512]{2,1,0:T(8,128)(2,1)S(1)}, u32[]{:S(2)}, u32[]{:S(2)}) %all-to-all-start.1) | async-done | bytes 2097184 | tf_op jit(solution)/shard_map/all_to_all | solution.py:333
  61.3 22.3 %all-to-all-done.2 = f32[8,24,256]{2,1,0:T(8,128)S(1)} async-done(((f32[8,24,256]{2,1,0:T(8,128)}), f32[8,24,256]{2,1,0:T(8,128)S(1)}, u32[]{:S(2)}, u32[]{:S(2)}) %all-to-all-start.2) | async-done | bytes 196640 | tf_op jit(solution)/shard_map/all_to_all | solution.py:404
  83.6 18.6 %all-gather.3.cloned.1.call-done = bf16[2048,1536]{1,0:T(8,128)(2,1)} async-done(((bf16[256,1536]{1,0:T(8,128)(2,1)}), bf16[2048,1536]{1,0:T(8,128)(2,1)}) %all-gather.3.cloned.1.call-update) | async-done | bytes 6291472 | tf_op jit(solution)/shard_map/all_gather | solution.py:431
  127.5 30.9 %collective-permute-done.3 = bf16[2,4,2,64,512]{4,3,2,1,0:T(8,128)(2,1)} collective-permute-done((bf16[2,4,2,64,512]{4,3,2,1,0:T(8,128)(2,1)}, bf16[2,4,2,64,512]{4,3,2,1,0:T(8,128)(2,1)}, u32[]{:S(2)}, u32[]{:S(2)}) %collective-permute-start.3) | collective-permute-done | bytes 1048608 | tf_op jit(solution)/shard_map/ppermute | solution.py:308
  177.5 39.1 %collective-permute-done.5 = bf16[1,1,4,4,64,512]{5,4,3,2,1,0:T(8,128)(2,1)S(1)} collective-permute-done((bf16[1,1,4,4,64,512]{5,4,3,2,1,0:T(8,128)(2,1)}, bf16[1,1,4,4,64,512]{5,4,3,2,1,0:T(8,128)(2,1)S(1)}, u32[]{:S(2)}, u32[]{:S(2)}) %collective-permute-start.5) | collective-permute-done | bytes 1048608 | tf_op jit(solution)/shard_map/ppermute | solution.py:308
  258.0 14.2 %collective-permute-done.9.refs_1_ = bf16[1408,256]{1,0:T(8,128)(2,1)S(1)} collective-permute-done((bf16[1408,256]{1,0:T(8,128)(2,1)S(1)}, bf16[1408,256]{1,0:T(8,128)(2,1)S(1)}, u32[]{:S(2)}, u32[]{:S(2)}) %collective-permute-start.9) | collective-permute-done | bytes 720928 | tf_op jit(solution)/shard_map/ppermute | solution.py:308
  289.5 16.0 %collective-permute-done.10 = bf16[4,1,1,64,1024]{4,3,0,2,1:T(8,128)(2,1)} collective-permute-done((bf16[4,1,1,64,1024]{4,3,0,2,1:T(8,128)(2,1)}, bf16[4,1,1,64,1024]{4,3,0,2,1:T(8,128)(2,1)}, u32[]{:S(2)}, u32[]{:S(2)}) %collective-permute-start.10) | collective-permute-done | bytes 524320 | tf_op jit(solution)/shard_map/ppermute | solution.py:308
  369.7 21.2 %ffn_pass.5 = (bf16[1024,2048]{1,0:T(8,128)(2,1)}, bf16[1024,2048]{1,0:T(8,128)(2,1)}, bf16[352,1024]{1,0:T(8,128)(2,1)}, bf16[368,1024]{1,0:T(8,128)(2,1)}, bf16[352,1024]{1,0:T(8,128)(2,1)}) custom-call(s32[3]{0:T(128)} %pad_add_fusion.meta, bf16[1024,2048]{1,0:T(8,128)(2,1)} %pad_maximum_fusion.rows_ref.refs_6_.refs_4_, ...), custom_call_target="tpu_custom_call" | custom-call | flops 8858370048 | bytes 23265280 | tf_op jit(solution)/shard_map/ffn_pass/pallas_call | solution.py:172
  411.2 21.0 %ffn_pass.4 = (bf16[1024,2048]{1,0:T(8,128)(2,1)}, bf16[1024,2048]{1,0:T(8,128)(2,1)}, bf16[352,1024]{1,0:T(8,128)(2,1)}, bf16[368,1024]{1,0:T(8,128)(2,1)}, bf16[352,1024]{1,0:T(8,128)(2,1)}) custom-call(s32[3]{0:T(128)} %pad_add_fusion.meta, bf16[1024,2048]{1,0:T(8,128)(2,1)} %pad_maximum_fusion.3.rows_ref.refs_7_.refs_5_, ...), custom_call_target="tpu_custom_call" | custom-call | flops 8858370048 | bytes 23265280 | tf_op jit(solution)/shard_map/ffn_pass/pallas_call | solution.py:172
  432.9 16.6 %weight_grad.3 = (bf16[2,4,1056,256]{3,2,1,0:T(8,128)(2,1)}, f32[8,2048]{1,0:T(8,128)}) custom-call(s32[3]{0:T(128)} %pad_add_fusion.meta, bf16[368,1024]{1,0:T(8,128)(2,1)} %get-tuple-element.221.refs_0_, bf16[368,1024]{1,0:T(8,128)(2,1)} %get-tuple-element.222.refs_1_, bf16[352,1024]{1,0:T(8,128)(2,1)} %get-tuple-element.223.refs_2_, ...), custom_call_target="tpu_custom_call" | custom-call | flops 8858370048 | bytes 17039360 | tf_op jit(solution)/shard_map/weight_grad/pallas_call | solution.py:271
  455.7 34.9 %ffn_pass.6 = (bf16[1024,2048]{1,0:T(8,128)(2,1)}, bf16[1024,2048]{1,0:T(8,128)(2,1)}, bf16[704,1024]{1,0:T(8,128)(2,1)}, bf16[704,1024]{1,0:T(8,128)(2,1)}, bf16[704,1024]{1,0:T(8,128)(2,1)}) custom-call(s32[3]{0:T(128)} %pad_add_fusion.meta, bf16[1024,2048]{1,0:T(8,128)(2,1)} %pad_maximum_fusion.rows_ref.refs_6_.refs_4_, ...), custom_call_target="tpu_custom_call" | custom-call | flops 17716740096 | bytes 46530560 | tf_op jit(solution)/shard_map/ffn_pass/pallas_call | solution.py:172
  507.9 35.1 %ffn_pass.7 = (bf16[1024,2048]{1,0:T(8,128)(2,1)}, bf16[1024,2048]{1,0:T(8,128)(2,1)}, bf16[704,1024]{1,0:T(8,128)(2,1)}, bf16[704,1024]{1,0:T(8,128)(2,1)}, bf16[704,1024]{1,0:T(8,128)(2,1)}) custom-call(s32[3]{0:T(128)} %pad_add_fusion.meta, bf16[1024,2048]{1,0:T(8,128)(2,1)} %pad_maximum_fusion.3.rows_ref.refs_7_.refs_5_, ...), custom_call_target="tpu_custom_call" | custom-call | flops 17716740096 | bytes 46530560 | tf_op jit(solution)/shard_map/ffn_pass/pallas_call | solution.py:172
  558.5 12.4 %weight_grad.4 = bf16[2,4,704,256]{3,2,1,0:T(8,128)(2,1)} custom-call(s32[3]{0:T(128)} %pad_add_fusion.meta, bf16[704,1024]{1,0:T(8,128)(2,1)} %get-tuple-element.247.refs_0_, bf16[704,1024]{1,0:T(8,128)(2,1)} %get-tuple-element.248.refs_1_, bf16[4,4,4,64,512]{4,3,2,1,0:T(8,128)(2,1)} %bitcast.585, bf16[4,4,4,64,512]{4,3,2,1,0:T(8,128)(2,1)} %bitcast.580), custom_call_target="tpu_custom_call" | custom-call | flops 5905580032 | bytes 14155776 | tf_op jit(solution)/shard_map/weight_grad/pallas_call | solution.py:271
  577.5 10.7 %collective-permute-done.49 = bf16[4,1,2,64,1024]{4,3,0,2,1:T(8,128)(2,1)} collective-permute-done((bf16[4,1,2,64,1024]{4,3,0,2,1:T(8,128)(2,1)}, bf16[4,1,2,64,1024]{4,3,0,2,1:T(8,128)(2,1)}, u32[]{:S(2)}, u32[]{:S(2)}) %collective-permute-start.49) | collective-permute-done | bytes 1048608 | tf_op jit(solution)/shard_map/ppermute | solution.py:308
  594.7 18.3 %weight_grad.5 = bf16[2,4,1408,256]{3,2,1,0:T(8,128)(2,1)} custom-call(s32[3]{0:T(128)} %pad_add_fusion.meta, bf16[704,1024]{1,0:T(8,128)(2,1)} %get-tuple-element.254.refs_0_, bf16[704,1024]{1,0:T(8,128)(2,1)} %get-tuple-element.255.refs_1_, bf16[704,1024]{1,0:T(8,128)(2,1)} %get-tuple-element.256.refs_2_, bf16[704,1024]{1,0:T(8,128)(2,1)} %get-tuple-element.257.refs_3_, ...), custom_call_target="tpu_custom_call" | custom-call | flops 11811160064 | bytes 19922944 | tf_op jit(solution)/shard_map/weight_grad/pallas_call | solution.py:271
  617.2 12.3 %collective-permute-done.50 = bf16[2,64,2048]{2,1,0:T(8,128)(2,1)S(1)} collective-permute-done((bf16[2,64,2048]{2,1,0:T(8,128)(2,1)S(1)}, bf16[2,64,2048]{2,1,0:T(8,128)(2,1)S(1)}, u32[]{:S(2)}, u32[]{:S(2)}) %collective-permute-start.50) | collective-permute-done | bytes 524320 | tf_op jit(solution)/shard_map/ppermute | solution.py:308
  631.2 9.7 collective-permute-done.54
  652.5 10.2 %collective-permute-done.56 = bf16[64,2048]{1,0:T(8,128)(2,1)S(1)} collective-permute-done((bf16[64,2048]{1,0:T(8,128)(2,1)S(1)}, bf16[64,2048]{1,0:T(8,128)(2,1)S(1)}, u32[]{:S(2)}, u32[]{:S(2)}) %collective-permute-start.56) | collective-permute-done | bytes 262176 | tf_op jit(solution)/shard_map/ppermute | solution.py:308
  675.9 21.0 %collective-permute-done.59 = bf16[64,2048]{1,0:T(8,128)(2,1)S(1)} collective-permute-done((bf16[64,2048]{1,0:T(8,128)(2,1)S(1)}, bf16[64,2048]{1,0:T(8,128)(2,1)S(1)}, u32[]{:S(2)}, u32[]{:S(2)}) %collective-permute-start.59) | collective-permute-done | bytes 262176 | tf_op jit(solution)/shard_map/ppermute | solution.py:308
  717.0 10.5 %collective-permute-start.62 = (bf16[704,256]{1,0:T(8,128)(2,1)S(1)}, bf16[704,256]{1,0:T(8,128)(2,1)}, u32[]{:S(2)}, u32[]{:S(2)}) collective-permute-start(bf16[704,256]{1,0:T(8,128)(2,1)S(1)} %get-tuple-element.467), channel_id=1, source_target_pairs={{0,16},{8,24},{16,0},{24,8},{1,17},{9,25},{17,1},{25,9},{2,18},{10... | collective-permute-start | bytes 1081352 | tf_op jit(solution)/shard_map/ppermute | solution.py:308
  731.1 36.6 %collective-permute-done.62 = bf16[704,256]{1,0:T(8,128)(2,1)} collective-permute-done((bf16[704,256]{1,0:T(8,128)(2,1)S(1)}, bf16[704,256]{1,0:T(8,128)(2,1)}, u32[]{:S(2)}, u32[]{:S(2)}) %collective-permute-start.62) | collective-permute-done | bytes 360480 | tf_op jit(solution)/shard_map/ppermute | solution.py:308
  860.0 22.2 %collective-permute-done.71 = bf16[2,64,2048]{2,1,0:T(8,128)(2,1)S(1)} collective-permute-done((bf16[2,64,2048]{2,1,0:T(8,128)(2,1)S(1)}, bf16[2,64,2048]{2,1,0:T(8,128)(2,1)S(1)}, u32[]{:S(2)}, u32[]{:S(2)}) %collective-permute-start.71) | collective-permute-done | bytes 524320 | tf_op jit(solution)/shard_map/ppermute | solution.py:308
  883.2 20.7 %collective-permute-done.72 = bf16[2,64,2048]{2,1,0:T(8,128)(2,1)S(1)} collective-permute-done((bf16[2,64,2048]{2,1,0:T(8,128)(2,1)S(1)}, bf16[2,64,2048]{2,1,0:T(8,128)(2,1)S(1)}, u32[]{:S(2)}, u32[]{:S(2)}) %collective-permute-start.72) | collective-permute-done | bytes 524320 | tf_op jit(solution)/shard_map/ppermute | solution.py:308
  925.2 14.5 %collective-permute-done.73 = bf16[64,2048]{1,0:T(8,128)(2,1)S(1)} collective-permute-done((bf16[64,2048]{1,0:T(8,128)(2,1)}, bf16[64,2048]{1,0:T(8,128)(2,1)S(1)}, u32[]{:S(2)}, u32[]{:S(2)}) %collective-permute-start.73) | collective-permute-done | bytes 262176 | tf_op jit(solution)/shard_map/ppermute | solution.py:308
  (643 shorter events, 496.4 us)
Async XLA Ops:
  7.2 95.1 %all-gather.3.cloned.1.call-start = ((), (), s32[]{:S(2)}) async-start(), calls=%async_computation.14 | async-start | bytes 7077888 | tf_op jit(solution)/shard_map/all_gather | solution.py:431
  17.8 84.6 %collective-permute-start = (bf16[1,4,2,64,512]{4,3,2,1,0:T(8,128)(2,1)}, bf16[1,4,2,64,512]{4,3,2,1,0:T(8,128)(2,1)}, u32[]{:S(2)}, u32[]{:S(2)}) collective-permute-start(bf16[1,4,2,64,512]{4,3,2,1,0:T(8,128)(2,1)} %bitcast.15), channel_id=1, source_target_pairs={{0,16},{8,24},{16,0},{24,8},{1,17},{9,25},{17,1},{25,9},{2,18},{10... | collective-permute-start | bytes 1572872 | tf_op jit(solution)/shard_map/ppermute | solution.py:308
  27.3 133.0 %all-gather.5.cloned.1.call-start = ((), (), s32[]{:S(2)}) async-start(), calls=%async_computation.15 | async-start | bytes 2359296 | tf_op jit(solution)/shard_map/all_gather | solution.py:434
  104.3 56.0 %collective-permute-start.4 = (bf16[1056,256]{1,0:T(8,128)(2,1)}, bf16[1056,256]{1,0:T(8,128)(2,1)}, u32[]{:S(2)}, u32[]{:S(2)}) collective-permute-start(bf16[1056,256]{1,0:T(8,128)(2,1)} %get-tuple-element.191), channel_id=1, source_target_pairs={{0,8},{8,0},{16,24},{24,16},{1,9},{9,1},{17,25},{25,17},{2,10},{10... | collective-permute-start | bytes 1622024 | tf_op jit(solution)/shard_map/ppermute | solution.py:308
  106.1 52.2 %collective-permute-start.3 = (bf16[2,4,2,64,512]{4,3,2,1,0:T(8,128)(2,1)}, bf16[2,4,2,64,512]{4,3,2,1,0:T(8,128)(2,1)}, u32[]{:S(2)}, u32[]{:S(2)}) collective-permute-start(bf16[2,4,2,64,512]{4,3,2,1,0:T(8,128)(2,1)} %constant_dynamic-update-slice_fusion), channel_id=1, source_target_pairs={{0,8},{8,0},{16,24},{24,16},{1,9},{9,1},{17,25},{25,17},{2,10},{10... | collective-permute-start | bytes 3145736 | tf_op jit(solution)/shard_map/ppermute | solution.py:308
  164.5 57.5 %all-to-all-start.4 = ((bf16[4,128,2048]{2,1,0:T(8,128)(2,1)}), bf16[4,128,2048]{2,1,0:T(8,128)(2,1)}, u32[]{:S(2)}, u32[]{:S(2)}) async-start(bf16[4,128,2048]{2,1,0:T(8,128)(2,1)} %bitcast.629), calls=%async_computation.4 | async-start | bytes 4194304 | tf_op jit(solution)/shard_map/all_to_all | solution.py:338
  174.9 49.3 %collective-permute-start.1 = (bf16[1056,256]{1,0:T(8,128)(2,1)}, bf16[1056,256]{1,0:T(8,128)(2,1)}, u32[]{:S(2)}, u32[]{:S(2)}) collective-permute-start(bf16[1056,256]{1,0:T(8,128)(2,1)} %get-tuple-element.187), channel_id=1, source_target_pairs={{0,16},{8,24},{16,0},{24,8},{1,17},{9,25},{17,1},{25,9},{2,18},{10... | collective-permute-start | bytes 1622024 | tf_op jit(solution)/shard_map/ppermute | solution.py:308
  246.5 67.7 %collective-permute-start.17 = (bf16[2,1,4,4,64,512]{5,4,3,2,0,1:T(8,128)(2,1)S(1)}, bf16[2,1,4,4,64,512]{5,4,3,2,0,1:T(8,128)(2,1)}, u32[]{:S(2)}, u32[]{:S(2)}) collective-permute-start(bf16[2,1,4,4,64,512]{5,4,3,2,0,1:T(8,128)(2,1)S(1)} %maximum_bitcast_fusion), channel_id=1, source_target_pairs={{0,1},{1,0},{2,3},{3,2},{4,5},{5,4},{6,7},{7,6},{8,9},{9,8},{10,11... | collective-permute-start | bytes 6291464 | tf_op jit(solution)/shard_map/ppermute | solution.py:308
  247.5 68.7 %collective-permute-start.18 = (bf16[1,2,4,4,64,512]{5,4,3,2,1,0:T(8,128)(2,1)}, bf16[1,2,4,4,64,512]{5,4,3,2,1,0:T(8,128)(2,1)}, u32[]{:S(2)}, u32[]{:S(2)}) collective-permute-start(bf16[1,2,4,4,64,512]{5,4,3,2,1,0:T(8,128)(2,1)} %maximum_bitcast_fusion.1), channel_id=1, source_target_pairs={{0,2},{2,0},{1,3},{3,1},{4,6},{6,4},{5,7},{7,5},{8,10},{10,8},{9,1... | collective-permute-start | bytes 6291464 | tf_op jit(solution)/shard_map/ppermute | solution.py:308
  367.9 81.5 %collective-permute-start.25 = (bf16[1408,256]{1,0:T(8,128)(2,1)}, bf16[1408,256]{1,0:T(8,128)(2,1)}, u32[]{:S(2)}, u32[]{:S(2)}) collective-permute-start(bf16[1408,256]{1,0:T(8,128)(2,1)} %get-tuple-element.430.refs_0_), channel_id=1, source_target_pairs={{0,4},{4,0},{1,5},{5,1},{2,6},{6,2},{3,7},{7,3},{8,12},{12,8},{9,1... | collective-permute-start | bytes 2162696 | tf_op jit(solution)/shard_map/ppermute | solution.py:302
  368.0 64.3 %collective-permute-start.30 = (bf16[704,256]{1,0:T(8,128)(2,1)}, bf16[704,256]{1,0:T(8,128)(2,1)}, u32[]{:S(2)}, u32[]{:S(2)}) collective-permute-start(bf16[704,256]{1,0:T(8,128)(2,1)} %get-tuple-element.469), channel_id=1, source_target_pairs={{0,24},{8,16},{16,8},{24,0},{1,25},{9,17},{17,9},{25,1},{2,26},{10... | collective-permute-start | bytes 1081352 | tf_op jit(solution)/shard_map/ppermute | solution.py:308
  455.0 50.8 %collective-permute-start.41 = (bf16[4,1056,256]{2,1,0:T(8,128)(2,1)S(1)}, bf16[4,1056,256]{2,1,0:T(8,128)(2,1)}, u32[]{:S(2)}, u32[]{:S(2)}) collective-permute-start(bf16[4,1056,256]{2,1,0:T(8,128)(2,1)S(1)} %get-tuple-element.409), channel_id=1, source_target_pairs={{0,4},{4,0},{1,5},{5,1},{2,6},{6,2},{3,7},{7,3},{8,12},{12,8},{9,1... | collective-permute-start | bytes 6488072 | tf_op jit(solution)/shard_map/ppermute | solution.py:302
  497.6 146.7 %collective-permute-start.40 = (bf16[4,1,2,64,1024]{4,3,0,2,1:T(8,128)(2,1)}, bf16[4,1,2,64,1024]{4,3,0,2,1:T(8,128)(2,1)}, u32[]{:S(2)}, u32[]{:S(2)}) collective-permute-start(bf16[4,1,2,64,1024]{4,3,0,2,1:T(8,128)(2,1)} %slice_bitcast_fusion.16), channel_id=1, source_target_pairs={{0,2},{2,0},{1,3},{3,1},{4,6},{6,4},{5,7},{7,5},{8,10},{10,8},{9,1... | collective-permute-start | bytes 3145736 | tf_op jit(solution)/shard_map/ppermute | solution.py:308
  572.4 58.8 %collective-permute-start.55 = (bf16[1056,256]{1,0:T(8,128)(2,1)}, bf16[1056,256]{1,0:T(8,128)(2,1)}, u32[]{:S(2)}, u32[]{:S(2)}) collective-permute-start(bf16[1056,256]{1,0:T(8,128)(2,1)} %get-tuple-element.447), channel_id=1, source_target_pairs={{0,16},{8,24},{16,0},{24,8},{1,17},{9,25},{17,1},{25,9},{2,18},{10... | collective-permute-start | bytes 1622024 | tf_op jit(solution)/shard_map/ppermute | solution.py:308
  643.1 62.8 %collective-permute-start.39 = (bf16[4,2,1,64,1024]{4,3,0,1,2:T(8,128)(2,1)}, bf16[4,2,1,64,1024]{4,3,0,1,2:T(8,128)(2,1)}, u32[]{:S(2)}, u32[]{:S(2)}) collective-permute-start(bf16[4,2,1,64,1024]{4,3,0,1,2:T(8,128)(2,1)} %slice_bitcast_fusion.18), channel_id=1, source_target_pairs={{0,1},{1,0},{2,3},{3,2},{4,5},{5,4},{6,7},{7,6},{8,9},{9,8},{10,11... | collective-permute-start | bytes 3145736 | tf_op jit(solution)/shard_map/ppermute | solution.py:308
  650.7 58.0 %collective-permute-start.43 = (bf16[4,1,2,64,1024]{4,3,0,2,1:T(8,128)(2,1)}, bf16[4,1,2,64,1024]{4,3,0,2,1:T(8,128)(2,1)}, u32[]{:S(2)}, u32[]{:S(2)}) collective-permute-start(bf16[4,1,2,64,1024]{4,3,0,2,1:T(8,128)(2,1)} %slice_bitcast_fusion.12), channel_id=1, source_target_pairs={{0,2},{2,0},{1,3},{3,1},{4,6},{6,4},{5,7},{7,5},{8,10},{10,8},{9,1... | collective-permute-start | bytes 3145736 | tf_op jit(solution)/shard_map/ppermute | solution.py:308
  701.4 66.2 %all-to-all-start.5 = ((bf16[4,128,2048]{2,1,0:T(8,128)(2,1)}), bf16[4,128,2048]{2,1,0:T(8,128)(2,1)}, u32[]{:S(2)}, u32[]{:S(2)}) async-start(bf16[4,128,2048]{2,1,0:T(8,128)(2,1)} %broadcast_in_dim.71), calls=%async_computation.5 | async-start | bytes 4194304 | tf_op jit(solution)/shard_map/all_to_all | solution.py:333
  705.9 276.5 %reduce-scatter.5.cloned.1.call-start = ((), (), s32[]{:S(2)}) async-start(), calls=%async_computation.17 | async-start | bytes 2359296 | tf_op jit(solution)/shard_map/reduce_scatter | solution.py:700
  717.0 50.7 %collective-permute-start.62 = (bf16[704,256]{1,0:T(8,128)(2,1)S(1)}, bf16[704,256]{1,0:T(8,128)(2,1)}, u32[]{:S(2)}, u32[]{:S(2)}) collective-permute-start(bf16[704,256]{1,0:T(8,128)(2,1)S(1)} %get-tuple-element.467), channel_id=1, source_target_pairs={{0,16},{8,24},{16,0},{24,8},{1,17},{9,25},{17,1},{25,9},{2,18},{10... | collective-permute-start | bytes 1081352 | tf_op jit(solution)/shard_map/ppermute | solution.py:308
  729.0 91.0 %collective-permute-start.69 = (bf16[1408,256]{1,0:T(8,128)(2,1)}, bf16[1408,256]{1,0:T(8,128)(2,1)}, u32[]{:S(2)}, u32[]{:S(2)}) collective-permute-start(bf16[1408,256]{1,0:T(8,128)(2,1)} %get-tuple-element.428), channel_id=1, source_target_pairs={{0,16},{8,24},{16,0},{24,8},{1,17},{9,25},{17,1},{25,9},{2,18},{10... | collective-permute-start | bytes 2162696 | tf_op jit(solution)/shard_map/ppermute | solution.py:308
  730.9 84.3 %collective-permute-start.68 = (bf16[1408,256]{1,0:T(8,128)(2,1)}, bf16[1408,256]{1,0:T(8,128)(2,1)}, u32[]{:S(2)}, u32[]{:S(2)}) collective-permute-start(bf16[1408,256]{1,0:T(8,128)(2,1)} %get-tuple-element.429), channel_id=1, source_target_pairs={{0,8},{8,0},{16,24},{24,16},{1,9},{9,1},{17,25},{25,17},{2,10},{10... | collective-permute-start | bytes 2162696 | tf_op jit(solution)/shard_map/ppermute | solution.py:308
  787.4 197.0 %reduce-scatter.3.cloned.1.call-start = ((), (), s32[]{:S(2)}) async-start(), calls=%async_computation.16 | async-start | bytes 7077888 | tf_op jit(solution)/shard_map/reduce_scatter | solution.py:701
  829.2 76.0 %collective-permute-start.70 = (bf16[1408,256]{1,0:T(8,128)(2,1)}, bf16[1408,256]{1,0:T(8,128)(2,1)}, u32[]{:S(2)}, u32[]{:S(2)}) collective-permute-start(bf16[1408,256]{1,0:T(8,128)(2,1)} %get-tuple-element.427), channel_id=1, source_target_pairs={{0,24},{8,16},{16,8},{24,0},{1,25},{9,17},{17,9},{25,1},{2,26},{10... | collective-permute-start | bytes 2162696 | tf_op jit(solution)/shard_map/ppermute | solution.py:308
  849.5 55.3 %all-to-all-start.6 = ((bf16[4,128,2048]{2,1,0:T(8,128)(2,1)}), bf16[4,128,2048]{2,1,0:T(8,128)(2,1)S(1)}, u32[]{:S(2)}, u32[]{:S(2)}) async-start(bf16[4,128,2048]{2,1,0:T(8,128)(2,1)} %bitcast.630), calls=%async_computation.6 | async-start | bytes 4194304 | tf_op jit(solution)/shard_map/all_to_all | solution.py:338
  (170 other events, 2535.5 us)
Sparse Core Ops, SparseCore 0:
  10.2 91.9 all-gather.2
  103.8 42.8 all-gather.4
  787.5 34.3 reduce-scatter.4
  828.3 111.4 reduce-scatter.2
